TPU v7x, 256 devices: a whole 4x4x8 slice. The times are simulated.
256 devices in a mesh: depth: 16 (over z, y_hi), lat: 16 (over y_lo, x, core).
Axes of the slice: x: 4, y: 4 (y_hi: 2, y_lo: 2; y = y_hi * 2 + y_lo), z: 8, core: 2. Of those that a mesh axis runs over, the one named last changes fastest.
Arguments:
- object_slices: float32 [16, 2, 2048, 2048], P('depth', None, 'lat'), as said below
- probe: float32 [2, 2, 256, 256], replicated, may hold values from -2.7 to 2.7
- positions: int32 [64, 2], P('lat'), may hold values from 0 to 2047, as said below
- measured: float32 [64, 256, 256], P('lat'), may hold values from 0 to 0.8
Outputs:
- object_grad: float32 [16, 2, 2048, 2048], P('depth', None, 'lat')
Inputs may be any that keep to these rules, and one draw needn't show every extreme that they name: Rows 4 l ... 4 l + 3 are the positions of lat index l: their row offset lies in [l * 128, (l + 1) * 128) and their column offset in [0, 1792]. `object_slices`: each cell's magnitude, sqrt(real part squared plus imaginary part squared), lies between 0.9 and 1.
All inputs are finite; a program needn't handle non-finite values.
Results may differ from a plain program's by a relative error of at most 0.039.
Values may be sent and summed in bfloat16 or wider, within the bound.
No kernel may reach another device: no remote copies, remote signals or barrier semaphores. Data moves between devices by JAX's collectives and lax.ppermute only.
A program may use at most 64 MiB of HBM per device.

v0:
```python
import math

import jax
import jax.numpy as jnp
from jax import lax
from jax.sharding import PartitionSpec as P

fresnel = 0.5


def shifted(block, axis, distance):
    devices = range(lax.axis_size(axis))
    route = [((i - distance) % len(devices), i) for i in devices]
    return lax.ppermute(block, axis, route)


def from_behind(block, axis, distance):
    devices = range(lax.axis_size(axis))
    route = [(i - distance, i) for i in devices if i - distance in devices]
    return lax.ppermute(block, axis, route)


def stack_block(real_part, imag_part):
    return jnp.stack([jnp.stack([real_part, -imag_part]), jnp.stack([imag_part, real_part])])


def make_tables(pixels):
    highest = lax.Precision.HIGHEST
    steps_idx = jnp.arange(pixels, dtype=jnp.int32)
    product = steps_idx[:, None] * steps_idx[None, :] % pixels
    angle = 2.0 * math.pi / pixels * product.astype(jnp.float32)
    scale = 1.0 / math.sqrt(pixels)
    d_real = jnp.cos(angle) * scale
    d_imag = -jnp.sin(angle) * scale
    freq = jnp.where(steps_idx < pixels // 2, steps_idx, steps_idx - pixels).astype(jnp.float32)
    theta = math.pi * fresnel / pixels * freq * freq
    h_real = jnp.cos(theta)
    h_imag = -jnp.sin(theta)
    a_real = d_real * h_real[None, :] + d_imag * h_imag[None, :]
    a_imag = d_real * h_imag[None, :] - d_imag * h_real[None, :]
    k_real = jnp.dot(a_real, d_real, precision=highest) - jnp.dot(a_imag, d_imag, precision=highest)
    k_imag = jnp.dot(a_real, d_imag, precision=highest) + jnp.dot(a_imag, d_real, precision=highest)
    return (
        stack_block(k_real, k_imag),
        stack_block(k_real.T, -k_imag.T),
        stack_block(d_real, d_imag),
        stack_block(d_real, -d_imag),
    )


def transform(table, wave):
    highest = lax.Precision.HIGHEST
    middle = jnp.einsum("srij,mrjk->msik", table, wave.astype(jnp.float32), precision=highest)
    return jnp.einsum("mrik,srlk->msil", middle, table, precision=highest)


def multiply(object_patch, wave_in):
    real_part = object_patch[0] * wave_in[:, 0] - object_patch[1] * wave_in[:, 1]
    imag_part = object_patch[0] * wave_in[:, 1] + object_patch[1] * wave_in[:, 0]
    return jnp.stack([real_part, imag_part], axis=1)


def conj_multiply(object_patch, wave_in):
    real_part = object_patch[0] * wave_in[:, 0] + object_patch[1] * wave_in[:, 1]
    imag_part = object_patch[0] * wave_in[:, 1] - object_patch[1] * wave_in[:, 0]
    return jnp.stack([real_part, imag_part], axis=1)


def conj_sum(wave_in, grad_lit):
    real_part = wave_in[:, 0] * grad_lit[:, 0] + wave_in[:, 1] * grad_lit[:, 1]
    imag_part = wave_in[:, 0] * grad_lit[:, 1] - wave_in[:, 1] * grad_lit[:, 0]
    return jnp.stack([jnp.sum(real_part, axis=0), jnp.sum(imag_part, axis=0)])


def on_device(object_slices, probe, positions, measured):
    pixels = probe.shape[-1]
    tile_rows = object_slices.shape[2]
    local_count = positions.shape[0]
    depth_size = lax.axis_size("depth")
    my_section = lax.axis_index("depth")
    prop_table, prop_adjoint, far_table, far_adjoint = make_tables(pixels)
    own_tile = object_slices[0]
    next_tile = shifted(own_tile, "lat", -1)
    after_tile = shifted(own_tile, "lat", -2)
    extended = jnp.concatenate([own_tile, next_tile, after_tile], axis=1)
    start_wave = probe.astype(jnp.bfloat16)
    zero_wave = jnp.zeros(probe.shape, jnp.bfloat16)
    saved_init = jnp.zeros((local_count,) + probe.shape, jnp.bfloat16)
    accum_init = jnp.zeros(extended.shape, jnp.float32)

    def corner(which):
        place = lax.dynamic_index_in_dim(positions, which, 0, False)
        return (place[0] % tile_rows, place[1])

    def forward_work(which, incoming, saved, seeds):
        in_wave = jnp.where(my_section == 0, start_wave, incoming)
        row_start, col_start = corner(which)
        patch_block = lax.dynamic_slice(extended, (0, row_start, col_start), (2, pixels, pixels))
        lit_wave = multiply(patch_block, in_wave.astype(jnp.float32))
        out_wave = transform(prop_table, lit_wave).astype(jnp.bfloat16)
        saved = lax.dynamic_update_index_in_dim(saved, in_wave, which, 0)
        target = lax.dynamic_index_in_dim(measured, which, 0, False)

        def far_field(wave_in):
            far_wave = transform(far_table, wave_in)
            residual = jnp.sum(far_wave * far_wave, axis=(0, 1)) - target
            return transform(far_adjoint, residual * far_wave).astype(jnp.bfloat16)

        seed_wave = lax.cond(
            my_section == depth_size - 1, far_field, lambda wave_in: zero_wave, out_wave
        )
        seeds = lax.dynamic_update_index_in_dim(seeds, seed_wave, which, 0)
        return (out_wave, saved, seeds)

    def backward_work(which, incoming, saved, seeds, accumulated):
        seed_wave = lax.dynamic_index_in_dim(seeds, which, 0, False)
        grad_in = jnp.where(my_section == depth_size - 1, seed_wave, incoming)
        row_start, col_start = corner(which)
        patch_block = lax.dynamic_slice(extended, (0, row_start, col_start), (2, pixels, pixels))
        grad_lit = transform(prop_adjoint, grad_in)
        in_wave = lax.dynamic_index_in_dim(saved, which, 0, False).astype(jnp.float32)
        grad_term = conj_sum(in_wave, grad_lit)
        current = lax.dynamic_slice(accumulated, (0, row_start, col_start), (2, pixels, pixels))
        accumulated = lax.dynamic_update_slice(
            accumulated, current + grad_term, (0, row_start, col_start)
        )
        out_wave = conj_multiply(patch_block, grad_lit).astype(jnp.bfloat16)
        return (out_wave, accumulated)

    def forward_guarded(which, incoming, saved, seeds):
        active = (which >= 0) & (which < local_count)
        clipped = jnp.clip(which, 0, local_count - 1)
        return lax.cond(
            active,
            lambda operands: forward_work(clipped, operands[0], operands[1], operands[2]),
            lambda operands: (zero_wave, operands[1], operands[2]),
            (incoming, saved, seeds),
        )

    def backward_guarded(which, incoming, saved, seeds, accumulated):
        active = (which >= 0) & (which < local_count)
        clipped = jnp.clip(which, 0, local_count - 1)
        return lax.cond(
            active,
            lambda operands: backward_work(clipped, operands[0], saved, seeds, operands[1]),
            lambda operands: (zero_wave, operands[1]),
            (incoming, accumulated),
        )

    def forward_turn(step_now, carried):
        incoming, saved, seeds = carried
        out_wave, saved, seeds = forward_guarded(step_now - my_section, incoming, saved, seeds)
        incoming = from_behind(out_wave, "depth", 1)
        return (incoming, saved, seeds)

    _, saved, seeds = lax.fori_loop(
        0, local_count + depth_size - 1, forward_turn, (zero_wave, saved_init, saved_init)
    )

    def backward_turn(step_now, carried):
        incoming, accumulated = carried
        which = step_now - (depth_size - 1 - my_section)
        out_wave, accumulated = backward_guarded(which, incoming, saved, seeds, accumulated)
        incoming = from_behind(out_wave, "depth", -1)
        return (incoming, accumulated)

    _, accumulated = lax.fori_loop(
        0, local_count + depth_size - 1, backward_turn, (zero_wave, accum_init)
    )
    from_before = shifted(accumulated[:, tile_rows : 2 * tile_rows], "lat", 1)
    from_earlier = shifted(accumulated[:, 2 * tile_rows :], "lat", 2)
    total = accumulated[:, :tile_rows] + from_before + from_earlier
    return total[None]


def solution(mesh):
    return jax.shard_map(
        on_device,
        mesh=mesh,
        in_specs=(P("depth", None, "lat", None), P(), P("lat", None), P("lat", None, None)),
        out_specs=P("depth", None, "lat", None),
        check_vma=False,
    )
```

profile of v0, /device:TPU:9, one launch (start us, length us, event | category | flops | bytes accessed | tf_op | source)
XLA Modules:
  0.0 1382.0 jit_solution(10981202098822569407)
XLA Ops:
  15.2 31.7 %collective-permute-done.3 = f32[2,128,2048]{2,1,0:T(8,128)} collective-permute-done((f32[2,128,2048]{2,1,0:T(8,128)}, f32[2,128,2048]{2,1,0:T(8,128)}, u32[]{:S(2)}, u32[]{:S(2)}) %collective-permute-start.3) | collective-permute-done | bytes 2097184 | tf_op jit(solution)/shard_map/ppermute | solution.py:14
  47.0 23.2 %collective-permute-done.2 = f32[2,128,2048]{2,1,0:T(8,128)} collective-permute-done((f32[2,128,2048]{2,1,0:T(8,128)}, f32[2,128,2048]{2,1,0:T(8,128)}, u32[]{:S(2)}, u32[]{:S(2)}) %collective-permute-start.2) | collective-permute-done | bytes 2097184 | tf_op jit(solution)/shard_map/ppermute | solution.py:14
  79.7 422.8 %while.36 = (s32[]{:T(128)}, bf16[2,2,256,256]{3,2,1,0:T(8,128)(2,1)}, bf16[4,2,2,256,256]{4,3,2,1,0:T(8,128)(2,1)}, bf16[4,2,2,256,256]{4,3,2,1,0:T(8,128)(2,1)...) while((s32[]{:T(128)}, ...), condition=%wide.region_6.7_spmd, body=%wide.region_0.6_spmd.sunk | while | flops 9666822144 | bytes 33293520 | solution.py:156
  79.7 14.7 %conditional.5 = (bf16[2,2,256,256]{3,2,1,0:T(8,128)(2,1)}, bf16[4,2,2,256,256]{4,3,2,1,0:T(8,128)(2,1)}, bf16[4,2,2,256,256]{4,3,2,1,0:T(8,128)(2,1)}) conditional(s32[]{:T(128)} %convert_element_type.183, (bf16[4,2,2,256,256]{4,3,2,1,0:T(8,128)(2,1)}, bf16[4,2,2,256,256]{4,3,2,1,0:T(8,128)(2,1)}) %tuple.117, (s32[]{:T(128)}, s32[4,2]{0,1:T(2,128)S(1)}, ...), branch_computations={%region_1.1_spmd, %region_2.5_spmd} | conditional | flops 9666822144 | bytes 31196036 | solution.py:133
  96.5 10.2 collective-permute-done
  106.8 14.7 %conditional.5 = (bf16[2,2,256,256]{3,2,1,0:T(8,128)(2,1)}, bf16[4,2,2,256,256]{4,3,2,1,0:T(8,128)(2,1)}, bf16[4,2,2,256,256]{4,3,2,1,0:T(8,128)(2,1)}) conditional(s32[]{:T(128)} %convert_element_type.183, (bf16[4,2,2,256,256]{4,3,2,1,0:T(8,128)(2,1)}, bf16[4,2,2,256,256]{4,3,2,1,0:T(8,128)(2,1)}) %tuple.117, (s32[]{:T(128)}, s32[4,2]{0,1:T(2,128)S(1)}, ...), branch_computations={%region_1.1_spmd, %region_2.5_spmd} | conditional | flops 9666822144 | bytes 31196036 | solution.py:133
  121.5 6.4 collective-permute-start
  127.9 9.3 collective-permute-done
  137.2 14.7 %conditional.5 = (bf16[2,2,256,256]{3,2,1,0:T(8,128)(2,1)}, bf16[4,2,2,256,256]{4,3,2,1,0:T(8,128)(2,1)}, bf16[4,2,2,256,256]{4,3,2,1,0:T(8,128)(2,1)}) conditional(s32[]{:T(128)} %convert_element_type.183, (bf16[4,2,2,256,256]{4,3,2,1,0:T(8,128)(2,1)}, bf16[4,2,2,256,256]{4,3,2,1,0:T(8,128)(2,1)}) %tuple.117, (s32[]{:T(128)}, s32[4,2]{0,1:T(2,128)S(1)}, ...), branch_computations={%region_1.1_spmd, %region_2.5_spmd} | conditional | flops 9666822144 | bytes 31196036 | solution.py:133
  158.3 8.4 collective-permute-done
  166.7 14.7 %conditional.5 = (bf16[2,2,256,256]{3,2,1,0:T(8,128)(2,1)}, bf16[4,2,2,256,256]{4,3,2,1,0:T(8,128)(2,1)}, bf16[4,2,2,256,256]{4,3,2,1,0:T(8,128)(2,1)}) conditional(s32[]{:T(128)} %convert_element_type.183, (bf16[4,2,2,256,256]{4,3,2,1,0:T(8,128)(2,1)}, bf16[4,2,2,256,256]{4,3,2,1,0:T(8,128)(2,1)}) %tuple.117, (s32[]{:T(128)}, s32[4,2]{0,1:T(2,128)S(1)}, ...), branch_computations={%region_1.1_spmd, %region_2.5_spmd} | conditional | flops 9666822144 | bytes 31196036 | solution.py:133
  187.9 7.5 collective-permute-done
  196.2 20.3 %collective-permute-start = (bf16[2,2,256,256]{3,2,1,0:T(8,128)(2,1)}, bf16[2,2,256,256]{3,2,1,0:T(8,128)(2,1)}, u32[]{:S(2)}, u32[]{:S(2)}) collective-permute-start(bf16[2,2,256,256]{3,2,1,0:T(8,128)(2,1)} %get-tuple-element.791), channel_id=1, source_target_pairs={{0,16},{16,32},{32,48},{48,64},{64,80},{80,96},{96,112},{112,128},... | collective-permute-start | bytes 1572872 | tf_op jit(solution)/shard_map/while/body/eval_jaxpr/ppermute | solution.py:20
  216.5 6.5 collective-permute-done
  223.8 6.7 collective-permute-start
  237.2 21.2 %collective-permute-start = (bf16[2,2,256,256]{3,2,1,0:T(8,128)(2,1)}, bf16[2,2,256,256]{3,2,1,0:T(8,128)(2,1)}, u32[]{:S(2)}, u32[]{:S(2)}) collective-permute-start(bf16[2,2,256,256]{3,2,1,0:T(8,128)(2,1)} %get-tuple-element.791), channel_id=1, source_target_pairs={{0,16},{16,32},{32,48},{48,64},{64,80},{80,96},{96,112},{112,128},... | collective-permute-start | bytes 1572872 | tf_op jit(solution)/shard_map/while/body/eval_jaxpr/ppermute | solution.py:20
  264.9 7.3 collective-permute-start
  278.7 16.0 %collective-permute-start = (bf16[2,2,256,256]{3,2,1,0:T(8,128)(2,1)}, bf16[2,2,256,256]{3,2,1,0:T(8,128)(2,1)}, u32[]{:S(2)}, u32[]{:S(2)}) collective-permute-start(bf16[2,2,256,256]{3,2,1,0:T(8,128)(2,1)} %get-tuple-element.791), channel_id=1, source_target_pairs={{0,16},{16,32},{32,48},{48,64},{64,80},{80,96},{96,112},{112,128},... | collective-permute-start | bytes 1572872 | tf_op jit(solution)/shard_map/while/body/eval_jaxpr/ppermute | solution.py:20
  301.1 7.0 collective-permute-start
  314.6 18.4 %collective-permute-start = (bf16[2,2,256,256]{3,2,1,0:T(8,128)(2,1)}, bf16[2,2,256,256]{3,2,1,0:T(8,128)(2,1)}, u32[]{:S(2)}, u32[]{:S(2)}) collective-permute-start(bf16[2,2,256,256]{3,2,1,0:T(8,128)(2,1)} %get-tuple-element.791), channel_id=1, source_target_pairs={{0,16},{16,32},{32,48},{48,64},{64,80},{80,96},{96,112},{112,128},... | collective-permute-start | bytes 1572872 | tf_op jit(solution)/shard_map/while/body/eval_jaxpr/ppermute | solution.py:20
  339.5 7.6 collective-permute-start
  347.1 7.0 collective-permute-done
  355.0 13.7 collective-permute-start
  375.1 13.1 collective-permute-start
  388.2 9.2 collective-permute-done
  398.3 8.7 collective-permute-start
  407.0 7.7 collective-permute-done
  415.5 14.3 %collective-permute-start = (bf16[2,2,256,256]{3,2,1,0:T(8,128)(2,1)}, bf16[2,2,256,256]{3,2,1,0:T(8,128)(2,1)}, u32[]{:S(2)}, u32[]{:S(2)}) collective-permute-start(bf16[2,2,256,256]{3,2,1,0:T(8,128)(2,1)} %get-tuple-element.791), channel_id=1, source_target_pairs={{0,16},{16,32},{32,48},{48,64},{64,80},{80,96},{96,112},{112,128},... | collective-permute-start | bytes 1572872 | tf_op jit(solution)/shard_map/while/body/eval_jaxpr/ppermute | solution.py:20
  429.9 9.8 collective-permute-done
  440.6 7.3 collective-permute-start
  447.9 11.0 collective-permute-done
  459.7 14.1 %collective-permute-start = (bf16[2,2,256,256]{3,2,1,0:T(8,128)(2,1)}, bf16[2,2,256,256]{3,2,1,0:T(8,128)(2,1)}, u32[]{:S(2)}, u32[]{:S(2)}) collective-permute-start(bf16[2,2,256,256]{3,2,1,0:T(8,128)(2,1)} %get-tuple-element.791), channel_id=1, source_target_pairs={{0,16},{16,32},{32,48},{48,64},{64,80},{80,96},{96,112},{112,128},... | collective-permute-start | bytes 1572872 | tf_op jit(solution)/shard_map/while/body/eval_jaxpr/ppermute | solution.py:20
  473.8 11.1 collective-permute-done
  485.8 6.8 collective-permute-start
  492.6 10.0 collective-permute-done
  506.0 706.8 %while.37 = (s32[]{:T(128)}, bf16[2,2,256,256]{3,2,1,0:T(8,128)(2,1)S(1)}, f32[2,384,2048]{2,1,0:T(8,128)}, s32[]{:T(128)}, s32[4,2]{0,1:T(2,128)S(1)}, /*index=...) while((s32[]{:T(128)}, ...), condition=%wide.region_12.13_spmd, body=%wide.region_7.12_spmd.sunk | while | flops 3224240128 | bytes 18350660 | solution.py:167
  507.3 21.1 %collective-permute-done.1 = bf16[2,2,256,256]{3,2,1,0:T(8,128)(2,1)S(1)} collective-permute-done((bf16[2,2,256,256]{3,2,1,0:T(8,128)(2,1)S(1)}, bf16[2,2,256,256]{3,2,1,0:T(8,128)(2,1)S(1)}, u32[]{:S(2)}, u32[]{:S(2)}) %collective-permute-start.1) | collective-permute-done | bytes 524320 | tf_op jit(solution)/shard_map/while/body/eval_jaxpr/ppermute | solution.py:20
  529.8 12.1 collective-permute-done.1
  543.3 23.0 %collective-permute-done.1 = bf16[2,2,256,256]{3,2,1,0:T(8,128)(2,1)S(1)} collective-permute-done((bf16[2,2,256,256]{3,2,1,0:T(8,128)(2,1)S(1)}, bf16[2,2,256,256]{3,2,1,0:T(8,128)(2,1)S(1)}, u32[]{:S(2)}, u32[]{:S(2)}) %collective-permute-start.1) | collective-permute-done | bytes 524320 | tf_op jit(solution)/shard_map/while/body/eval_jaxpr/ppermute | solution.py:20
  567.7 15.0 %collective-permute-done.1 = bf16[2,2,256,256]{3,2,1,0:T(8,128)(2,1)S(1)} collective-permute-done((bf16[2,2,256,256]{3,2,1,0:T(8,128)(2,1)S(1)}, bf16[2,2,256,256]{3,2,1,0:T(8,128)(2,1)S(1)}, u32[]{:S(2)}, u32[]{:S(2)}) %collective-permute-start.1) | collective-permute-done | bytes 524320 | tf_op jit(solution)/shard_map/while/body/eval_jaxpr/ppermute | solution.py:20
  584.0 15.7 %collective-permute-done.1 = bf16[2,2,256,256]{3,2,1,0:T(8,128)(2,1)S(1)} collective-permute-done((bf16[2,2,256,256]{3,2,1,0:T(8,128)(2,1)S(1)}, bf16[2,2,256,256]{3,2,1,0:T(8,128)(2,1)S(1)}, u32[]{:S(2)}, u32[]{:S(2)}) %collective-permute-start.1) | collective-permute-done | bytes 524320 | tf_op jit(solution)/shard_map/while/body/eval_jaxpr/ppermute | solution.py:20
  601.0 20.5 %collective-permute-done.1 = bf16[2,2,256,256]{3,2,1,0:T(8,128)(2,1)S(1)} collective-permute-done((bf16[2,2,256,256]{3,2,1,0:T(8,128)(2,1)S(1)}, bf16[2,2,256,256]{3,2,1,0:T(8,128)(2,1)S(1)}, u32[]{:S(2)}, u32[]{:S(2)}) %collective-permute-start.1) | collective-permute-done | bytes 524320 | tf_op jit(solution)/shard_map/while/body/eval_jaxpr/ppermute | solution.py:20
  622.9 15.9 %collective-permute-done.1 = bf16[2,2,256,256]{3,2,1,0:T(8,128)(2,1)S(1)} collective-permute-done((bf16[2,2,256,256]{3,2,1,0:T(8,128)(2,1)S(1)}, bf16[2,2,256,256]{3,2,1,0:T(8,128)(2,1)S(1)}, u32[]{:S(2)}, u32[]{:S(2)}) %collective-permute-start.1) | collective-permute-done | bytes 524320 | tf_op jit(solution)/shard_map/while/body/eval_jaxpr/ppermute | solution.py:20
  640.1 19.3 %collective-permute-done.1 = bf16[2,2,256,256]{3,2,1,0:T(8,128)(2,1)S(1)} collective-permute-done((bf16[2,2,256,256]{3,2,1,0:T(8,128)(2,1)S(1)}, bf16[2,2,256,256]{3,2,1,0:T(8,128)(2,1)S(1)}, u32[]{:S(2)}, u32[]{:S(2)}) %collective-permute-start.1) | collective-permute-done | bytes 524320 | tf_op jit(solution)/shard_map/while/body/eval_jaxpr/ppermute | solution.py:20
  660.8 16.9 %collective-permute-done.1 = bf16[2,2,256,256]{3,2,1,0:T(8,128)(2,1)S(1)} collective-permute-done((bf16[2,2,256,256]{3,2,1,0:T(8,128)(2,1)S(1)}, bf16[2,2,256,256]{3,2,1,0:T(8,128)(2,1)S(1)}, u32[]{:S(2)}, u32[]{:S(2)}) %collective-permute-start.1) | collective-permute-done | bytes 524320 | tf_op jit(solution)/shard_map/while/body/eval_jaxpr/ppermute | solution.py:20
  679.0 17.1 %collective-permute-done.1 = bf16[2,2,256,256]{3,2,1,0:T(8,128)(2,1)S(1)} collective-permute-done((bf16[2,2,256,256]{3,2,1,0:T(8,128)(2,1)S(1)}, bf16[2,2,256,256]{3,2,1,0:T(8,128)(2,1)S(1)}, u32[]{:S(2)}, u32[]{:S(2)}) %collective-permute-start.1) | collective-permute-done | bytes 524320 | tf_op jit(solution)/shard_map/while/body/eval_jaxpr/ppermute | solution.py:20
  697.5 15.2 %collective-permute-done.1 = bf16[2,2,256,256]{3,2,1,0:T(8,128)(2,1)S(1)} collective-permute-done((bf16[2,2,256,256]{3,2,1,0:T(8,128)(2,1)S(1)}, bf16[2,2,256,256]{3,2,1,0:T(8,128)(2,1)S(1)}, u32[]{:S(2)}, u32[]{:S(2)}) %collective-permute-start.1) | collective-permute-done | bytes 524320 | tf_op jit(solution)/shard_map/while/body/eval_jaxpr/ppermute | solution.py:20
  714.0 26.9 %collective-permute-done.1 = bf16[2,2,256,256]{3,2,1,0:T(8,128)(2,1)S(1)} collective-permute-done((bf16[2,2,256,256]{3,2,1,0:T(8,128)(2,1)S(1)}, bf16[2,2,256,256]{3,2,1,0:T(8,128)(2,1)S(1)}, u32[]{:S(2)}, u32[]{:S(2)}) %collective-permute-start.1) | collective-permute-done | bytes 524320 | tf_op jit(solution)/shard_map/while/body/eval_jaxpr/ppermute | solution.py:20
  742.3 12.6 collective-permute-done.1
  756.3 39.7 %collective-permute-done.1 = bf16[2,2,256,256]{3,2,1,0:T(8,128)(2,1)S(1)} collective-permute-done((bf16[2,2,256,256]{3,2,1,0:T(8,128)(2,1)S(1)}, bf16[2,2,256,256]{3,2,1,0:T(8,128)(2,1)S(1)}, u32[]{:S(2)}, u32[]{:S(2)}) %collective-permute-start.1) | collective-permute-done | bytes 524320 | tf_op jit(solution)/shard_map/while/body/eval_jaxpr/ppermute | solution.py:20
  797.4 268.2 %collective-permute-done.1 = bf16[2,2,256,256]{3,2,1,0:T(8,128)(2,1)S(1)} collective-permute-done((bf16[2,2,256,256]{3,2,1,0:T(8,128)(2,1)S(1)}, bf16[2,2,256,256]{3,2,1,0:T(8,128)(2,1)S(1)}, u32[]{:S(2)}, u32[]{:S(2)}) %collective-permute-start.1) | collective-permute-done | bytes 524320 | tf_op jit(solution)/shard_map/while/body/eval_jaxpr/ppermute | solution.py:20
  1065.6 19.3 %conditional.6 = (bf16[2,2,256,256]{3,2,1,0:T(8,128)(2,1)S(1)}, f32[2,384,2048]{2,1,0:T(8,128)}) conditional(s32[]{:T(128)} %convert_element_type.184, f32[2,384,2048]{2,1,0:T(8,128)} %get-tuple-element.876, (s32[]{:T(128)}, s32[4,2]{0,1:T(2,128)S(1)}, f32[2,384,2048]{2,1,0:T(8,128)}, s32[]{:T(128)}, bf16[4,2,2,256,256]{4,3,2,1,0:T(8,128)(2,1)}, ...), branch_computations={%region_8.8_spmd, %region_9.11_spmd} | conditional | flops 3224240128 | bytes 16253235 | solution.py:143
  1078.4 6.5 dynamic_update_slice.12
  1086.2 15.2 %collective-permute-done.1 = bf16[2,2,256,256]{3,2,1,0:T(8,128)(2,1)S(1)} collective-permute-done((bf16[2,2,256,256]{3,2,1,0:T(8,128)(2,1)S(1)}, bf16[2,2,256,256]{3,2,1,0:T(8,128)(2,1)S(1)}, u32[]{:S(2)}, u32[]{:S(2)}) %collective-permute-start.1) | collective-permute-done | bytes 524320 | tf_op jit(solution)/shard_map/while/body/eval_jaxpr/ppermute | solution.py:20
  1101.4 18.9 %conditional.6 = (bf16[2,2,256,256]{3,2,1,0:T(8,128)(2,1)S(1)}, f32[2,384,2048]{2,1,0:T(8,128)}) conditional(s32[]{:T(128)} %convert_element_type.184, f32[2,384,2048]{2,1,0:T(8,128)} %get-tuple-element.876, (s32[]{:T(128)}, s32[4,2]{0,1:T(2,128)S(1)}, f32[2,384,2048]{2,1,0:T(8,128)}, s32[]{:T(128)}, bf16[4,2,2,256,256]{4,3,2,1,0:T(8,128)(2,1)}, ...), branch_computations={%region_8.8_spmd, %region_9.11_spmd} | conditional | flops 3224240128 | bytes 16253235 | solution.py:143
  1121.6 14.4 %collective-permute-done.1 = bf16[2,2,256,256]{3,2,1,0:T(8,128)(2,1)S(1)} collective-permute-done((bf16[2,2,256,256]{3,2,1,0:T(8,128)(2,1)S(1)}, bf16[2,2,256,256]{3,2,1,0:T(8,128)(2,1)S(1)}, u32[]{:S(2)}, u32[]{:S(2)}) %collective-permute-start.1) | collective-permute-done | bytes 524320 | tf_op jit(solution)/shard_map/while/body/eval_jaxpr/ppermute | solution.py:20
  1136.0 19.3 %conditional.6 = (bf16[2,2,256,256]{3,2,1,0:T(8,128)(2,1)S(1)}, f32[2,384,2048]{2,1,0:T(8,128)}) conditional(s32[]{:T(128)} %convert_element_type.184, f32[2,384,2048]{2,1,0:T(8,128)} %get-tuple-element.876, (s32[]{:T(128)}, s32[4,2]{0,1:T(2,128)S(1)}, f32[2,384,2048]{2,1,0:T(8,128)}, s32[]{:T(128)}, bf16[4,2,2,256,256]{4,3,2,1,0:T(8,128)(2,1)}, ...), branch_computations={%region_8.8_spmd, %region_9.11_spmd} | conditional | flops 3224240128 | bytes 16253235 | solution.py:143
  1148.8 6.5 dynamic_update_slice.12
  1156.6 22.2 %collective-permute-done.1 = bf16[2,2,256,256]{3,2,1,0:T(8,128)(2,1)S(1)} collective-permute-done((bf16[2,2,256,256]{3,2,1,0:T(8,128)(2,1)S(1)}, bf16[2,2,256,256]{3,2,1,0:T(8,128)(2,1)S(1)}, u32[]{:S(2)}, u32[]{:S(2)}) %collective-permute-start.1) | collective-permute-done | bytes 524320 | tf_op jit(solution)/shard_map/while/body/eval_jaxpr/ppermute | solution.py:20
  1178.7 18.9 %conditional.6 = (bf16[2,2,256,256]{3,2,1,0:T(8,128)(2,1)S(1)}, f32[2,384,2048]{2,1,0:T(8,128)}) conditional(s32[]{:T(128)} %convert_element_type.184, f32[2,384,2048]{2,1,0:T(8,128)} %get-tuple-element.876, (s32[]{:T(128)}, s32[4,2]{0,1:T(2,128)S(1)}, f32[2,384,2048]{2,1,0:T(8,128)}, s32[]{:T(128)}, bf16[4,2,2,256,256]{4,3,2,1,0:T(8,128)(2,1)}, ...), branch_computations={%region_8.8_spmd, %region_9.11_spmd} | conditional | flops 3224240128 | bytes 16253235 | solution.py:143
  1199.0 13.8 %collective-permute-done.1 = bf16[2,2,256,256]{3,2,1,0:T(8,128)(2,1)S(1)} collective-permute-done((bf16[2,2,256,256]{3,2,1,0:T(8,128)(2,1)S(1)}, bf16[2,2,256,256]{3,2,1,0:T(8,128)(2,1)S(1)}, u32[]{:S(2)}, u32[]{:S(2)}) %collective-permute-start.1) | collective-permute-done | bytes 524320 | tf_op jit(solution)/shard_map/while/body/eval_jaxpr/ppermute | solution.py:20
  1215.3 36.1 %collective-permute-start.4 = (f32[2,128,2048]{2,1,0:T(8,128)S(1)}, f32[2,128,2048]{2,1,0:T(8,128)S(1)}, u32[]{:S(2)}, u32[]{:S(2)}) collective-permute-start(f32[2,128,2048]{2,1,0:T(8,128)S(1)} %get-tuple-element.646), channel_id=1, source_target_pairs={{15,0},{0,1},{1,2},{2,3},{3,4},{4,5},{5,6},{6,7},{7,8},{8,9},{9,10... | collective-permute-start | bytes 6291464 | tf_op jit(solution)/shard_map/ppermute | solution.py:14
  1255.4 55.1 %collective-permute-done.4 = f32[2,128,2048]{2,1,0:T(8,128)S(1)} collective-permute-done((f32[2,128,2048]{2,1,0:T(8,128)S(1)}, f32[2,128,2048]{2,1,0:T(8,128)S(1)}, u32[]{:S(2)}, u32[]{:S(2)}) %collective-permute-start.4) | collective-permute-done | bytes 2097184 | tf_op jit(solution)/shard_map/ppermute | solution.py:14
  1310.4 68.2 %collective-permute-done.5 = f32[2,128,2048]{2,1,0:T(8,128)S(1)} collective-permute-done((f32[2,128,2048]{2,1,0:T(8,128)S(1)}, f32[2,128,2048]{2,1,0:T(8,128)S(1)}, u32[]{:S(2)}, u32[]{:S(2)}) %collective-permute-start.5) | collective-permute-done | bytes 2097184 | tf_op jit(solution)/shard_map/ppermute | solution.py:14
  (202 shorter events, 237.9 us)
Async XLA Ops:
  0.0 47.0 %collective-permute-start.3 = (f32[2,128,2048]{2,1,0:T(8,128)}, f32[2,128,2048]{2,1,0:T(8,128)}, u32[]{:S(2)}, u32[]{:S(2)}) collective-permute-start(f32[2,128,2048]{2,1,0:T(8,128)} %bitcast.176), channel_id=1, source_target_pairs={{2,0},{3,1},{4,2},{5,3},{6,4},{7,5},{8,6},{9,7},{10,8},{11,9},{12,... | collective-permute-start | bytes 6291464 | tf_op jit(solution)/shard_map/ppermute | solution.py:14
  2.4 67.8 %collective-permute-start.2 = (f32[2,128,2048]{2,1,0:T(8,128)}, f32[2,128,2048]{2,1,0:T(8,128)}, u32[]{:S(2)}, u32[]{:S(2)}) collective-permute-start(f32[2,128,2048]{2,1,0:T(8,128)} %bitcast.177), channel_id=1, source_target_pairs={{1,0},{2,1},{3,2},{4,3},{5,4},{6,5},{7,6},{8,7},{9,8},{10,9},{11,1... | collective-permute-start | bytes 6291464 | tf_op jit(solution)/shard_map/ppermute | solution.py:14
  3.4 3.0 copy-start.2
  14.0 56.1 %copy-start.1 = (f32[1,2,128,2048]{3,2,1,0:T(8,128)S(1)}, f32[1,2,128,2048]{3,2,1,0:T(8,128)}, u32[]{:S(2)}) copy-start(f32[1,2,128,2048]{3,2,1,0:T(8,128)} %param.14) | copy-start | bytes 6291460
  76.7 3.0 copy-start.3
  94.4 12.3 collective-permute-start
  121.5 15.8 %collective-permute-start = (bf16[2,2,256,256]{3,2,1,0:T(8,128)(2,1)}, bf16[2,2,256,256]{3,2,1,0:T(8,128)(2,1)}, u32[]{:S(2)}, u32[]{:S(2)}) collective-permute-start(bf16[2,2,256,256]{3,2,1,0:T(8,128)(2,1)} %get-tuple-element.791), channel_id=1, source_target_pairs={{0,16},{16,32},{32,48},{48,64},{64,80},{80,96},{96,112},{112,128},... | collective-permute-start | bytes 1572872 | tf_op jit(solution)/shard_map/while/body/eval_jaxpr/ppermute | solution.py:20
  151.9 14.8 %collective-permute-start = (bf16[2,2,256,256]{3,2,1,0:T(8,128)(2,1)}, bf16[2,2,256,256]{3,2,1,0:T(8,128)(2,1)}, u32[]{:S(2)}, u32[]{:S(2)}) collective-permute-start(bf16[2,2,256,256]{3,2,1,0:T(8,128)(2,1)} %get-tuple-element.791), channel_id=1, source_target_pairs={{0,16},{16,32},{32,48},{48,64},{64,80},{80,96},{96,112},{112,128},... | collective-permute-start | bytes 1572872 | tf_op jit(solution)/shard_map/while/body/eval_jaxpr/ppermute | solution.py:20
  181.4 13.9 %collective-permute-start = (bf16[2,2,256,256]{3,2,1,0:T(8,128)(2,1)}, bf16[2,2,256,256]{3,2,1,0:T(8,128)(2,1)}, u32[]{:S(2)}, u32[]{:S(2)}) collective-permute-start(bf16[2,2,256,256]{3,2,1,0:T(8,128)(2,1)} %get-tuple-element.791), channel_id=1, source_target_pairs={{0,16},{16,32},{32,48},{48,64},{64,80},{80,96},{96,112},{112,128},... | collective-permute-start | bytes 1572872 | tf_op jit(solution)/shard_map/while/body/eval_jaxpr/ppermute | solution.py:20
  196.2 26.8 %collective-permute-start = (bf16[2,2,256,256]{3,2,1,0:T(8,128)(2,1)}, bf16[2,2,256,256]{3,2,1,0:T(8,128)(2,1)}, u32[]{:S(2)}, u32[]{:S(2)}) collective-permute-start(bf16[2,2,256,256]{3,2,1,0:T(8,128)(2,1)} %get-tuple-element.791), channel_id=1, source_target_pairs={{0,16},{16,32},{32,48},{48,64},{64,80},{80,96},{96,112},{112,128},... | collective-permute-start | bytes 1572872 | tf_op jit(solution)/shard_map/while/body/eval_jaxpr/ppermute | solution.py:20
  223.8 12.5 collective-permute-start
  237.2 26.9 %collective-permute-start = (bf16[2,2,256,256]{3,2,1,0:T(8,128)(2,1)}, bf16[2,2,256,256]{3,2,1,0:T(8,128)(2,1)}, u32[]{:S(2)}, u32[]{:S(2)}) collective-permute-start(bf16[2,2,256,256]{3,2,1,0:T(8,128)(2,1)} %get-tuple-element.791), channel_id=1, source_target_pairs={{0,16},{16,32},{32,48},{48,64},{64,80},{80,96},{96,112},{112,128},... | collective-permute-start | bytes 1572872 | tf_op jit(solution)/shard_map/while/body/eval_jaxpr/ppermute | solution.py:20
  264.9 12.9 collective-permute-start
  278.7 21.6 %collective-permute-start = (bf16[2,2,256,256]{3,2,1,0:T(8,128)(2,1)}, bf16[2,2,256,256]{3,2,1,0:T(8,128)(2,1)}, u32[]{:S(2)}, u32[]{:S(2)}) collective-permute-start(bf16[2,2,256,256]{3,2,1,0:T(8,128)(2,1)} %get-tuple-element.791), channel_id=1, source_target_pairs={{0,16},{16,32},{32,48},{48,64},{64,80},{80,96},{96,112},{112,128},... | collective-permute-start | bytes 1572872 | tf_op jit(solution)/shard_map/while/body/eval_jaxpr/ppermute | solution.py:20
  301.1 12.6 collective-permute-start
  314.6 24.0 %collective-permute-start = (bf16[2,2,256,256]{3,2,1,0:T(8,128)(2,1)}, bf16[2,2,256,256]{3,2,1,0:T(8,128)(2,1)}, u32[]{:S(2)}, u32[]{:S(2)}) collective-permute-start(bf16[2,2,256,256]{3,2,1,0:T(8,128)(2,1)} %get-tuple-element.791), channel_id=1, source_target_pairs={{0,16},{16,32},{32,48},{48,64},{64,80},{80,96},{96,112},{112,128},... | collective-permute-start | bytes 1572872 | tf_op jit(solution)/shard_map/while/body/eval_jaxpr/ppermute | solution.py:20
  339.5 14.7 %collective-permute-start = (bf16[2,2,256,256]{3,2,1,0:T(8,128)(2,1)}, bf16[2,2,256,256]{3,2,1,0:T(8,128)(2,1)}, u32[]{:S(2)}, u32[]{:S(2)}) collective-permute-start(bf16[2,2,256,256]{3,2,1,0:T(8,128)(2,1)} %get-tuple-element.791), channel_id=1, source_target_pairs={{0,16},{16,32},{32,48},{48,64},{64,80},{80,96},{96,112},{112,128},... | collective-permute-start | bytes 1572872 | tf_op jit(solution)/shard_map/while/body/eval_jaxpr/ppermute | solution.py:20
  355.0 19.3 %collective-permute-start = (bf16[2,2,256,256]{3,2,1,0:T(8,128)(2,1)}, bf16[2,2,256,256]{3,2,1,0:T(8,128)(2,1)}, u32[]{:S(2)}, u32[]{:S(2)}) collective-permute-start(bf16[2,2,256,256]{3,2,1,0:T(8,128)(2,1)} %get-tuple-element.791), channel_id=1, source_target_pairs={{0,16},{16,32},{32,48},{48,64},{64,80},{80,96},{96,112},{112,128},... | collective-permute-start | bytes 1572872 | tf_op jit(solution)/shard_map/while/body/eval_jaxpr/ppermute | solution.py:20
  375.1 22.3 %collective-permute-start = (bf16[2,2,256,256]{3,2,1,0:T(8,128)(2,1)}, bf16[2,2,256,256]{3,2,1,0:T(8,128)(2,1)}, u32[]{:S(2)}, u32[]{:S(2)}) collective-permute-start(bf16[2,2,256,256]{3,2,1,0:T(8,128)(2,1)} %get-tuple-element.791), channel_id=1, source_target_pairs={{0,16},{16,32},{32,48},{48,64},{64,80},{80,96},{96,112},{112,128},... | collective-permute-start | bytes 1572872 | tf_op jit(solution)/shard_map/while/body/eval_jaxpr/ppermute | solution.py:20
  398.3 16.4 %collective-permute-start = (bf16[2,2,256,256]{3,2,1,0:T(8,128)(2,1)}, bf16[2,2,256,256]{3,2,1,0:T(8,128)(2,1)}, u32[]{:S(2)}, u32[]{:S(2)}) collective-permute-start(bf16[2,2,256,256]{3,2,1,0:T(8,128)(2,1)} %get-tuple-element.791), channel_id=1, source_target_pairs={{0,16},{16,32},{32,48},{48,64},{64,80},{80,96},{96,112},{112,128},... | collective-permute-start | bytes 1572872 | tf_op jit(solution)/shard_map/while/body/eval_jaxpr/ppermute | solution.py:20
  415.5 24.2 %collective-permute-start = (bf16[2,2,256,256]{3,2,1,0:T(8,128)(2,1)}, bf16[2,2,256,256]{3,2,1,0:T(8,128)(2,1)}, u32[]{:S(2)}, u32[]{:S(2)}) collective-permute-start(bf16[2,2,256,256]{3,2,1,0:T(8,128)(2,1)} %get-tuple-element.791), channel_id=1, source_target_pairs={{0,16},{16,32},{32,48},{48,64},{64,80},{80,96},{96,112},{112,128},... | collective-permute-start | bytes 1572872 | tf_op jit(solution)/shard_map/while/body/eval_jaxpr/ppermute | solution.py:20
  440.6 18.3 %collective-permute-start = (bf16[2,2,256,256]{3,2,1,0:T(8,128)(2,1)}, bf16[2,2,256,256]{3,2,1,0:T(8,128)(2,1)}, u32[]{:S(2)}, u32[]{:S(2)}) collective-permute-start(bf16[2,2,256,256]{3,2,1,0:T(8,128)(2,1)} %get-tuple-element.791), channel_id=1, source_target_pairs={{0,16},{16,32},{32,48},{48,64},{64,80},{80,96},{96,112},{112,128},... | collective-permute-start | bytes 1572872 | tf_op jit(solution)/shard_map/while/body/eval_jaxpr/ppermute | solution.py:20
  459.7 25.2 %collective-permute-start = (bf16[2,2,256,256]{3,2,1,0:T(8,128)(2,1)}, bf16[2,2,256,256]{3,2,1,0:T(8,128)(2,1)}, u32[]{:S(2)}, u32[]{:S(2)}) collective-permute-start(bf16[2,2,256,256]{3,2,1,0:T(8,128)(2,1)} %get-tuple-element.791), channel_id=1, source_target_pairs={{0,16},{16,32},{32,48},{48,64},{64,80},{80,96},{96,112},{112,128},... | collective-permute-start | bytes 1572872 | tf_op jit(solution)/shard_map/while/body/eval_jaxpr/ppermute | solution.py:20
  485.8 16.8 %collective-permute-start = (bf16[2,2,256,256]{3,2,1,0:T(8,128)(2,1)}, bf16[2,2,256,256]{3,2,1,0:T(8,128)(2,1)}, u32[]{:S(2)}, u32[]{:S(2)}) collective-permute-start(bf16[2,2,256,256]{3,2,1,0:T(8,128)(2,1)} %get-tuple-element.791), channel_id=1, source_target_pairs={{0,16},{16,32},{32,48},{48,64},{64,80},{80,96},{96,112},{112,128},... | collective-permute-start | bytes 1572872 | tf_op jit(solution)/shard_map/while/body/eval_jaxpr/ppermute | solution.py:20
  506.0 22.4 %collective-permute-start.1 = (bf16[2,2,256,256]{3,2,1,0:T(8,128)(2,1)S(1)}, bf16[2,2,256,256]{3,2,1,0:T(8,128)(2,1)S(1)}, u32[]{:S(2)}, u32[]{:S(2)}) collective-permute-start(bf16[2,2,256,256]{3,2,1,0:T(8,128)(2,1)S(1)} %get-tuple-element.804), channel_id=1, source_target_pairs={{16,0},{32,16},{48,32},{64,48},{80,64},{96,80},{112,96},{128,112},... | collective-permute-start | bytes 1572872 | tf_op jit(solution)/shard_map/while/body/eval_jaxpr/ppermute | solution.py:20
  528.5 13.4 collective-permute-start.1
  542.0 24.3 %collective-permute-start.1 = (bf16[2,2,256,256]{3,2,1,0:T(8,128)(2,1)S(1)}, bf16[2,2,256,256]{3,2,1,0:T(8,128)(2,1)S(1)}, u32[]{:S(2)}, u32[]{:S(2)}) collective-permute-start(bf16[2,2,256,256]{3,2,1,0:T(8,128)(2,1)S(1)} %get-tuple-element.804), channel_id=1, source_target_pairs={{16,0},{32,16},{48,32},{64,48},{80,64},{96,80},{112,96},{128,112},... | collective-permute-start | bytes 1572872 | tf_op jit(solution)/shard_map/while/body/eval_jaxpr/ppermute | solution.py:20
  566.3 16.3 %collective-permute-start.1 = (bf16[2,2,256,256]{3,2,1,0:T(8,128)(2,1)S(1)}, bf16[2,2,256,256]{3,2,1,0:T(8,128)(2,1)S(1)}, u32[]{:S(2)}, u32[]{:S(2)}) collective-permute-start(bf16[2,2,256,256]{3,2,1,0:T(8,128)(2,1)S(1)} %get-tuple-element.804), channel_id=1, source_target_pairs={{16,0},{32,16},{48,32},{64,48},{80,64},{96,80},{112,96},{128,112},... | collective-permute-start | bytes 1572872 | tf_op jit(solution)/shard_map/while/body/eval_jaxpr/ppermute | solution.py:20
  582.7 17.0 %collective-permute-start.1 = (bf16[2,2,256,256]{3,2,1,0:T(8,128)(2,1)S(1)}, bf16[2,2,256,256]{3,2,1,0:T(8,128)(2,1)S(1)}, u32[]{:S(2)}, u32[]{:S(2)}) collective-permute-start(bf16[2,2,256,256]{3,2,1,0:T(8,128)(2,1)S(1)} %get-tuple-element.804), channel_id=1, source_target_pairs={{16,0},{32,16},{48,32},{64,48},{80,64},{96,80},{112,96},{128,112},... | collective-permute-start | bytes 1572872 | tf_op jit(solution)/shard_map/while/body/eval_jaxpr/ppermute | solution.py:20
  599.7 21.8 %collective-permute-start.1 = (bf16[2,2,256,256]{3,2,1,0:T(8,128)(2,1)S(1)}, bf16[2,2,256,256]{3,2,1,0:T(8,128)(2,1)S(1)}, u32[]{:S(2)}, u32[]{:S(2)}) collective-permute-start(bf16[2,2,256,256]{3,2,1,0:T(8,128)(2,1)S(1)} %get-tuple-element.804), channel_id=1, source_target_pairs={{16,0},{32,16},{48,32},{64,48},{80,64},{96,80},{112,96},{128,112},... | collective-permute-start | bytes 1572872 | tf_op jit(solution)/shard_map/while/body/eval_jaxpr/ppermute | solution.py:20
  621.6 17.2 %collective-permute-start.1 = (bf16[2,2,256,256]{3,2,1,0:T(8,128)(2,1)S(1)}, bf16[2,2,256,256]{3,2,1,0:T(8,128)(2,1)S(1)}, u32[]{:S(2)}, u32[]{:S(2)}) collective-permute-start(bf16[2,2,256,256]{3,2,1,0:T(8,128)(2,1)S(1)} %get-tuple-element.804), channel_id=1, source_target_pairs={{16,0},{32,16},{48,32},{64,48},{80,64},{96,80},{112,96},{128,112},... | collective-permute-start | bytes 1572872 | tf_op jit(solution)/shard_map/while/body/eval_jaxpr/ppermute | solution.py:20
  638.8 20.6 %collective-permute-start.1 = (bf16[2,2,256,256]{3,2,1,0:T(8,128)(2,1)S(1)}, bf16[2,2,256,256]{3,2,1,0:T(8,128)(2,1)S(1)}, u32[]{:S(2)}, u32[]{:S(2)}) collective-permute-start(bf16[2,2,256,256]{3,2,1,0:T(8,128)(2,1)S(1)} %get-tuple-element.804), channel_id=1, source_target_pairs={{16,0},{32,16},{48,32},{64,48},{80,64},{96,80},{112,96},{128,112},... | collective-permute-start | bytes 1572872 | tf_op jit(solution)/shard_map/while/body/eval_jaxpr/ppermute | solution.py:20
  659.5 18.2 %collective-permute-start.1 = (bf16[2,2,256,256]{3,2,1,0:T(8,128)(2,1)S(1)}, bf16[2,2,256,256]{3,2,1,0:T(8,128)(2,1)S(1)}, u32[]{:S(2)}, u32[]{:S(2)}) collective-permute-start(bf16[2,2,256,256]{3,2,1,0:T(8,128)(2,1)S(1)} %get-tuple-element.804), channel_id=1, source_target_pairs={{16,0},{32,16},{48,32},{64,48},{80,64},{96,80},{112,96},{128,112},... | collective-permute-start | bytes 1572872 | tf_op jit(solution)/shard_map/while/body/eval_jaxpr/ppermute | solution.py:20
  677.7 18.4 %collective-permute-start.1 = (bf16[2,2,256,256]{3,2,1,0:T(8,128)(2,1)S(1)}, bf16[2,2,256,256]{3,2,1,0:T(8,128)(2,1)S(1)}, u32[]{:S(2)}, u32[]{:S(2)}) collective-permute-start(bf16[2,2,256,256]{3,2,1,0:T(8,128)(2,1)S(1)} %get-tuple-element.804), channel_id=1, source_target_pairs={{16,0},{32,16},{48,32},{64,48},{80,64},{96,80},{112,96},{128,112},... | collective-permute-start | bytes 1572872 | tf_op jit(solution)/shard_map/while/body/eval_jaxpr/ppermute | solution.py:20
  696.2 16.5 %collective-permute-start.1 = (bf16[2,2,256,256]{3,2,1,0:T(8,128)(2,1)S(1)}, bf16[2,2,256,256]{3,2,1,0:T(8,128)(2,1)S(1)}, u32[]{:S(2)}, u32[]{:S(2)}) collective-permute-start(bf16[2,2,256,256]{3,2,1,0:T(8,128)(2,1)S(1)} %get-tuple-element.804), channel_id=1, source_target_pairs={{16,0},{32,16},{48,32},{64,48},{80,64},{96,80},{112,96},{128,112},... | collective-permute-start | bytes 1572872 | tf_op jit(solution)/shard_map/while/body/eval_jaxpr/ppermute | solution.py:20
  712.7 28.2 %collective-permute-start.1 = (bf16[2,2,256,256]{3,2,1,0:T(8,128)(2,1)S(1)}, bf16[2,2,256,256]{3,2,1,0:T(8,128)(2,1)S(1)}, u32[]{:S(2)}, u32[]{:S(2)}) collective-permute-start(bf16[2,2,256,256]{3,2,1,0:T(8,128)(2,1)S(1)} %get-tuple-element.804), channel_id=1, source_target_pairs={{16,0},{32,16},{48,32},{64,48},{80,64},{96,80},{112,96},{128,112},... | collective-permute-start | bytes 1572872 | tf_op jit(solution)/shard_map/while/body/eval_jaxpr/ppermute | solution.py:20
  741.0 13.9 %collective-permute-start.1 = (bf16[2,2,256,256]{3,2,1,0:T(8,128)(2,1)S(1)}, bf16[2,2,256,256]{3,2,1,0:T(8,128)(2,1)S(1)}, u32[]{:S(2)}, u32[]{:S(2)}) collective-permute-start(bf16[2,2,256,256]{3,2,1,0:T(8,128)(2,1)S(1)} %get-tuple-element.804), channel_id=1, source_target_pairs={{16,0},{32,16},{48,32},{64,48},{80,64},{96,80},{112,96},{128,112},... | collective-permute-start | bytes 1572872 | tf_op jit(solution)/shard_map/while/body/eval_jaxpr/ppermute | solution.py:20
  755.0 41.0 %collective-permute-start.1 = (bf16[2,2,256,256]{3,2,1,0:T(8,128)(2,1)S(1)}, bf16[2,2,256,256]{3,2,1,0:T(8,128)(2,1)S(1)}, u32[]{:S(2)}, u32[]{:S(2)}) collective-permute-start(bf16[2,2,256,256]{3,2,1,0:T(8,128)(2,1)S(1)} %get-tuple-element.804), channel_id=1, source_target_pairs={{16,0},{32,16},{48,32},{64,48},{80,64},{96,80},{112,96},{128,112},... | collective-permute-start | bytes 1572872 | tf_op jit(solution)/shard_map/while/body/eval_jaxpr/ppermute | solution.py:20
  796.1 269.5 %collective-permute-start.1 = (bf16[2,2,256,256]{3,2,1,0:T(8,128)(2,1)S(1)}, bf16[2,2,256,256]{3,2,1,0:T(8,128)(2,1)S(1)}, u32[]{:S(2)}, u32[]{:S(2)}) collective-permute-start(bf16[2,2,256,256]{3,2,1,0:T(8,128)(2,1)S(1)} %get-tuple-element.804), channel_id=1, source_target_pairs={{16,0},{32,16},{48,32},{64,48},{80,64},{96,80},{112,96},{128,112},... | collective-permute-start | bytes 1572872 | tf_op jit(solution)/shard_map/while/body/eval_jaxpr/ppermute | solution.py:20
  1084.9 16.5 %collective-permute-start.1 = (bf16[2,2,256,256]{3,2,1,0:T(8,128)(2,1)S(1)}, bf16[2,2,256,256]{3,2,1,0:T(8,128)(2,1)S(1)}, u32[]{:S(2)}, u32[]{:S(2)}) collective-permute-start(bf16[2,2,256,256]{3,2,1,0:T(8,128)(2,1)S(1)} %get-tuple-element.804), channel_id=1, source_target_pairs={{16,0},{32,16},{48,32},{64,48},{80,64},{96,80},{112,96},{128,112},... | collective-permute-start | bytes 1572872 | tf_op jit(solution)/shard_map/while/body/eval_jaxpr/ppermute | solution.py:20
  1120.3 15.7 %collective-permute-start.1 = (bf16[2,2,256,256]{3,2,1,0:T(8,128)(2,1)S(1)}, bf16[2,2,256,256]{3,2,1,0:T(8,128)(2,1)S(1)}, u32[]{:S(2)}, u32[]{:S(2)}) collective-permute-start(bf16[2,2,256,256]{3,2,1,0:T(8,128)(2,1)S(1)} %get-tuple-element.804), channel_id=1, source_target_pairs={{16,0},{32,16},{48,32},{64,48},{80,64},{96,80},{112,96},{128,112},... | collective-permute-start | bytes 1572872 | tf_op jit(solution)/shard_map/while/body/eval_jaxpr/ppermute | solution.py:20
  1155.3 23.5 %collective-permute-start.1 = (bf16[2,2,256,256]{3,2,1,0:T(8,128)(2,1)S(1)}, bf16[2,2,256,256]{3,2,1,0:T(8,128)(2,1)S(1)}, u32[]{:S(2)}, u32[]{:S(2)}) collective-permute-start(bf16[2,2,256,256]{3,2,1,0:T(8,128)(2,1)S(1)} %get-tuple-element.804), channel_id=1, source_target_pairs={{16,0},{32,16},{48,32},{64,48},{80,64},{96,80},{112,96},{128,112},... | collective-permute-start | bytes 1572872 | tf_op jit(solution)/shard_map/while/body/eval_jaxpr/ppermute | solution.py:20
  1197.7 15.1 %collective-permute-start.1 = (bf16[2,2,256,256]{3,2,1,0:T(8,128)(2,1)S(1)}, bf16[2,2,256,256]{3,2,1,0:T(8,128)(2,1)S(1)}, u32[]{:S(2)}, u32[]{:S(2)}) collective-permute-start(bf16[2,2,256,256]{3,2,1,0:T(8,128)(2,1)S(1)} %get-tuple-element.804), channel_id=1, source_target_pairs={{16,0},{32,16},{48,32},{64,48},{80,64},{96,80},{112,96},{128,112},... | collective-permute-start | bytes 1572872 | tf_op jit(solution)/shard_map/while/body/eval_jaxpr/ppermute | solution.py:20
  1215.3 95.1 %collective-permute-start.4 = (f32[2,128,2048]{2,1,0:T(8,128)S(1)}, f32[2,128,2048]{2,1,0:T(8,128)S(1)}, u32[]{:S(2)}, u32[]{:S(2)}) collective-permute-start(f32[2,128,2048]{2,1,0:T(8,128)S(1)} %get-tuple-element.646), channel_id=1, source_target_pairs={{15,0},{0,1},{1,2},{2,3},{3,4},{4,5},{5,6},{6,7},{7,8},{8,9},{9,10... | collective-permute-start | bytes 6291464 | tf_op jit(solution)/shard_map/ppermute | solution.py:14
  1251.4 127.2 %collective-permute-start.5 = (f32[2,128,2048]{2,1,0:T(8,128)S(1)}, f32[2,128,2048]{2,1,0:T(8,128)S(1)}, u32[]{:S(2)}, u32[]{:S(2)}) collective-permute-start(f32[2,128,2048]{2,1,0:T(8,128)S(1)} %get-tuple-element.647), channel_id=1, source_target_pairs={{14,0},{15,1},{0,2},{1,3},{2,4},{3,5},{4,6},{5,7},{6,8},{7,9},{8,1... | collective-permute-start | bytes 6291464 | tf_op jit(solution)/shard_map/ppermute | solution.py:14
where the time goes:
time: 1360 us; the launch traced here: 1380 us
  waiting for transfers between devices  930 us (68%)
  starting transfers between devices  272 us (20%)
  local copies, waits for them, and re-layouts  68 us (5%)
  other arithmetic  40.3 us (3%)
  matrix products  39.7 us (3%)
  loops' own time  31.7 us (2%)
    ppermute x38, waiting for transfers between devices, from_behind(): return lax.ppermute(block, axis, route)  752 us
    ppermute x38, starting transfers between devices, from_behind(): return lax.ppermute(block, axis, route)  229 us
    ppermute x4, waiting for transfers between devices, shifted(): return lax.ppermute(block, axis, route)  178 us
    ppermute x4, starting transfers between devices, shifted(): return lax.ppermute(block, axis, route)  43.4 us
  transfers between devices with their start and end apart: 42, of which 42 were waited for; matrix products, arithmetic and copies ran while one was open for 1% of the time, Pallas kernels for 0%

commit v1 on v0

v1 whole, which is shorter than its diff:
```python
import functools

import jax
import jax.numpy as jnp
import numpy as np
from jax import lax
from jax.experimental import pallas as pl
from jax.experimental.pallas import tpu as pltpu
from jax.sharding import PartitionSpec as P

BF = jnp.bfloat16
F32 = jnp.float32
ANY = pl.BlockSpec(memory_space=pl.ANY)
SMEM = pl.BlockSpec(memory_space=pltpu.MemorySpace.SMEM)
VMEM = pl.BlockSpec(memory_space=pltpu.MemorySpace.VMEM)


@functools.lru_cache
def base_tables(n):
    k = np.arange(n)
    d = np.exp(-2j * np.pi * ((k[:, None] * k[None, :]) % n) / n) / np.sqrt(n)
    q = np.where(k < n // 2, k, k - n).astype(np.float64)
    h = np.exp(-1j * np.pi * 0.5 * q * q / n)
    prop = (np.conj(d) * h[None, :]) @ d
    return np.stack([prop.real, prop.imag, d.real, d.imag]).astype(np.float32)


def tables_kernel(scales, base, out, *, n, slices):
    s = pl.program_id(0)
    which = jnp.where(s < slices, 0, 2)
    re = base[which]
    im = base[which + 1]
    for side, sign in ((0, 1.0), (1, -1.0)):
        scale = scales[side, s]
        a = (re * scale).astype(BF)
        b = im * (scale * sign)
        out[0, side, 0:n, 0:n] = a
        out[0, side, n:2 * n, n:2 * n] = a
        out[0, side, 0:n, n:2 * n] = (-b).astype(BF)
        out[0, side, n:2 * n, 0:n] = b.astype(BF)


def make_tables(n, slices):
    a = 2.0 ** ((np.arange(slices) + 0.5) / slices)
    scales = np.concatenate([np.stack([a, 1.0 / a]), np.ones((2, 1))], axis=1).astype(np.float32)
    return pl.pallas_call(
        functools.partial(tables_kernel, n=n, slices=slices),
        grid=(slices + 1,),
        out_shape=jax.ShapeDtypeStruct((slices + 1, 2, 2 * n, 2 * n), BF),
        in_specs=[SMEM, pl.BlockSpec((4, n, n), lambda s: (0, 0, 0))],
        out_specs=pl.BlockSpec((1, 2, 2 * n, 2 * n), lambda s: (s, 0, 0, 0)),
    )(jnp.asarray(scales), jnp.asarray(base_tables(n)))


def chain_kernel(info, probe, target, m0, m1, m2, m3, tabs_hbm, out_hbm,
                 patch, tabs, inc, cur, lhs, mid, outv, psem, tsem, osem, *, n, slices):
    team, inner = info[1], info[2]
    messages = (m0, m1, m2, m3)
    per = slices // 4

    def patch_copy(s):
        rel = lax.rem(s // per - team + 4, 4)
        entry = jnp.bitwise_xor(lax.rem(s, per), inner)
        return rel, entry

    def table_copy(s):
        return pltpu.make_async_copy(tabs_hbm.at[s], tabs.at[s], tsem.at[s])

    def out_copy(s):
        return pltpu.make_async_copy(outv.at[s], out_hbm.at[s], osem.at[s])

    def to_lhs(m, re, im):
        lhs[0:n, m * n:(m + 1) * n] = re.astype(BF)
        lhs[n:2 * n, m * n:(m + 1) * n] = im.astype(BF)

    def transform(left, right):
        for m in range(2):
            u = jnp.dot(left, lhs[:, m * n:(m + 1) * n], preferred_element_type=F32).astype(BF)
            mid[m * n:(m + 1) * n, 0:n] = u[0:n]
            mid[m * n:(m + 1) * n, n:2 * n] = u[n:2 * n]
        return jnp.dot(mid[...], right, preferred_element_type=F32)

    @pl.when(info[0] == 1)
    def _():
        for s in range(slices):
            table_copy(s).start()
            rel, entry = patch_copy(s)
            for r in range(4):
                @pl.when(rel == r)
                def _():
                    pltpu.make_async_copy(messages[r].at[entry], patch.at[s], psem.at[s]).start()
        table_copy(slices).start()
        for m in range(2):
            for c in range(2):
                x = pltpu.roll(probe[m, c], info[3], 0)
                x = pltpu.roll(x, info[4], 1)
                cur[m * n:(m + 1) * n, c * n:(c + 1) * n] = x.astype(BF).astype(F32)

        def forward(s, carry):
            table_copy(s).wait()
            pltpu.make_async_copy(m0.at[0], patch.at[s], psem.at[s]).wait()
            pr = patch[s, 0].astype(F32)
            pi = patch[s, 1].astype(F32)
            for m in range(2):
                wr = cur[m * n:(m + 1) * n, 0:n]
                wi = cur[m * n:(m + 1) * n, n:2 * n]
                to_lhs(m, pr * wr - pi * wi, pr * wi + pi * wr)
            inc[s] = cur[...].astype(BF)
            cur[...] = transform(tabs[s, 0], tabs[s, 1])
            return carry

        lax.fori_loop(0, slices, forward, 0)
        table_copy(slices).wait()
        for m in range(2):
            to_lhs(m, cur[m * n:(m + 1) * n, 0:n], cur[m * n:(m + 1) * n, n:2 * n])
        cur[...] = transform(tabs[slices, 0], tabs[slices, 1])
        f = [[cur[m * n:(m + 1) * n, c * n:(c + 1) * n] for c in range(2)] for m in range(2)]
        resid = (f[0][0] * f[0][0] + f[0][1] * f[0][1]) + (f[1][0] * f[1][0] + f[1][1] * f[1][1]) - target[...]
        for m in range(2):
            to_lhs(m, resid * f[m][0], resid * f[m][1])
        cur[...] = transform(tabs[slices, 1], tabs[slices, 0])
        for m in range(2):
            to_lhs(m, cur[m * n:(m + 1) * n, 0:n], cur[m * n:(m + 1) * n, n:2 * n])

        def backward(back, carry):
            s = slices - 1 - back
            cur[...] = transform(tabs[s, 1], tabs[s, 0])
            pr = patch[s, 0].astype(F32)
            pi = patch[s, 1].astype(F32)
            tr = jnp.zeros((n, n), F32)
            ti = jnp.zeros((n, n), F32)
            for m in range(2):
                gr = cur[m * n:(m + 1) * n, 0:n]
                gi = cur[m * n:(m + 1) * n, n:2 * n]
                wr = inc[s, m * n:(m + 1) * n, 0:n].astype(F32)
                wi = inc[s, m * n:(m + 1) * n, n:2 * n].astype(F32)
                tr += wr * gr + wi * gi
                ti += wr * gi - wi * gr
                to_lhs(m, pr * gr + pi * gi, pr * gi - pi * gr)
            outv[s, 0] = tr.astype(BF)
            outv[s, 1] = ti.astype(BF)
            out_copy(s).start()
            return carry

        lax.fori_loop(0, slices, backward, 0)
        for s in range(slices):
            out_copy(s).wait()


def chain(info, probe, target, messages, tables):
    n = target.shape[-1]
    slices = tables.shape[0] - 1
    return pl.pallas_call(
        functools.partial(chain_kernel, n=n, slices=slices),
        out_shape=jax.ShapeDtypeStruct((slices, 2, n, n), BF),
        in_specs=[SMEM, VMEM, VMEM] + [ANY] * 5,
        out_specs=ANY,
        scratch_shapes=[
            pltpu.VMEM((slices, 2, n, n), BF),
            pltpu.VMEM((slices + 1, 2, 2 * n, 2 * n), BF),
            pltpu.VMEM((slices, 2 * n, 2 * n), BF),
            pltpu.VMEM((2 * n, 2 * n), F32),
            pltpu.VMEM((2 * n, 2 * n), BF),
            pltpu.VMEM((2 * n, 2 * n), BF),
            pltpu.VMEM((slices, 2, n, n), BF),
            pltpu.SemaphoreType.DMA((slices,)),
            pltpu.SemaphoreType.DMA((slices + 1,)),
            pltpu.SemaphoreType.DMA((slices,)),
        ],
        compiler_params=pltpu.CompilerParams(vmem_limit_bytes=58 << 20),
    )(info, probe, target, *messages, tables)


def window(ref, lead, offset, n):
    width = ref.shape[-1]
    start = pl.multiple_of((offset // n) * n, n)
    after = pl.multiple_of(jnp.minimum(start + n, width - n), n)
    lane = lax.broadcasted_iota(jnp.int32, (ref.shape[-2], n), 1)
    first = ref[lead, :, pl.ds(start, n)].astype(F32)
    second = ref[lead, :, pl.ds(after, n)].astype(F32)
    return jnp.where(lane >= offset % n, first, second)


def own_windows_kernel(places, tile, tile_bf, wins, *, n):
    tile_bf[...] = tile[...].astype(BF)
    for p in range(wins.shape[0]):
        for c in range(2):
            wins[p, c] = window(tile, c, places[p, 1], n).astype(BF)


def own_windows(places, tile, n):
    count = places.shape[0]
    return pl.pallas_call(
        functools.partial(own_windows_kernel, n=n),
        out_shape=(jax.ShapeDtypeStruct(tile.shape, BF), jax.ShapeDtypeStruct((count, 2, tile.shape[1], n), BF)),
        in_specs=[SMEM, VMEM],
        out_specs=(VMEM, VMEM),
        compiler_params=pltpu.CompilerParams(vmem_limit_bytes=40 << 20),
    )(places, tile)


def merge_kernel(places, behind, tile, ahead, out, *, n):
    rows = tile.shape[1]
    row = lax.broadcasted_iota(jnp.int32, (rows, n), 0)
    for p in range(out.shape[0]):
        for c in range(2):
            far = window(ahead, c, places[p, 1], n)
            near = behind[p, c].astype(F32)
            out[p, c, 0:rows] = jnp.where(row >= places[p, 0] % rows, near, far).astype(BF)
            out[p, c, rows:2 * rows] = window(tile, c, places[p, 1], n).astype(BF)


def merge(places, behind, tile, ahead, n):
    count = places.shape[0]
    return pl.pallas_call(
        functools.partial(merge_kernel, n=n),
        out_shape=jax.ShapeDtypeStruct((count, 2, 2 * tile.shape[1], n), BF),
        in_specs=[SMEM, VMEM, VMEM, VMEM],
        out_specs=VMEM,
        compiler_params=pltpu.CompilerParams(vmem_limit_bytes=40 << 20),
    )(places, behind, tile, ahead)


def gather_kernel(own_places, mid_places, far_places, from_own, from_mid, from_far, out, *, n):
    rows = out.shape[1]
    width = out.shape[-1]
    row = lax.broadcasted_iota(jnp.int32, (rows, n), 0)
    lane = lax.broadcasted_iota(jnp.int32, (rows, n), 1)
    out[...] = jnp.zeros_like(out)
    for places, terms, kind in ((own_places, from_own, 0), (mid_places, from_mid, 1), (far_places, from_far, 2)):
        for p in range(places.shape[0]):
            shift = places[p, 0] % rows
            offset = places[p, 1]
            start = pl.multiple_of((offset // n) * n, n)
            after = pl.multiple_of(jnp.minimum(start + n, width - n), n)
            for c in range(2):
                if kind == 1:
                    term = terms[p, c, rows:2 * rows].astype(F32)
                else:
                    term = terms[p, c].astype(F32)
                    keep = row >= shift if kind == 0 else row < shift
                    term = jnp.where(keep, term, 0.0)
                here = lane >= offset % n
                out[c, :, pl.ds(start, n)] += jnp.where(here, term, 0.0)
                out[c, :, pl.ds(after, n)] += jnp.where(here, 0.0, term)


def gather_terms(own_places, mid_places, far_places, from_own, from_mid, from_far, rows, width):
    n = from_mid.shape[-1]
    return pl.pallas_call(
        functools.partial(gather_kernel, n=n),
        out_shape=jax.ShapeDtypeStruct((2, rows, width), F32),
        in_specs=[SMEM, SMEM, SMEM, VMEM, VMEM, VMEM],
        out_specs=VMEM,
        compiler_params=pltpu.CompilerParams(vmem_limit_bytes=40 << 20),
    )(own_places, mid_places, far_places, from_own, from_mid, from_far)


def shifted(block, distance):
    size = lax.axis_size("lat")
    return lax.ppermute(block, "lat", [(i, (i + distance) % size) for i in range(size)])


def team_of(position, lat):
    return (position + 2 * (lat % 2)) % 4


def permute(block, route):
    depth, lat = lax.axis_size("depth"), lax.axis_size("lat")
    pairs = []
    for d in range(depth):
        for m in range(lat):
            to = route(d, m)
            if to is not None:
                pairs.append((d * lat + m, to * lat + m))
    return lax.ppermute(block, ("depth", "lat"), pairs)


def pick(block, index):
    return lax.dynamic_index_in_dim(block, index, 0, False)


def on_device(object_slices, probe, positions, measured):
    n = probe.shape[-1]
    rows, width = object_slices.shape[2:]
    depth_size = lax.axis_size("depth")
    d = lax.axis_index("depth")
    m = lax.axis_index("lat")
    team, inner = d // 4, d % 4
    tile = object_slices[0]

    mid_places = shifted(positions, 1)
    tile_bf, mine = own_windows(positions, tile, n)
    ahead = shifted(tile_bf, -1)
    behind = shifted(mine, 1)
    target = shifted(pick(measured, inner), 1)
    patches = merge(mid_places, behind, tile_bf, ahead, n)

    parts = [pick(patches, inner)]
    for k in (1, 2, 3):
        parts.append(permute(pick(patches, inner ^ k), lambda a, b: (a ^ k)))
    message = jnp.stack(parts)
    messages = [message]
    for k in (1, 2, 3):
        def route(a, b):
            goal = team_of(a % 4, b)
            return goal * 4 + a % 4 if (goal + k) % 4 == a // 4 else None
        messages.append(permute(message, route))

    home = team_of(inner, m)
    place = pick(mid_places, inner)
    info = jnp.stack([(home == team).astype(jnp.int32), team, inner, place[0] % rows, place[1] % n]).astype(jnp.int32)
    tables = make_tables(n, depth_size)
    terms = chain(info, probe, target, messages, tables)

    terms = terms.reshape(4, 4, 2, n, n)
    block = pick(terms, team)
    for k in (1, 2, 3):
        def route(a, b):
            return ((a // 4 + k) % 4) * 4 + a % 4 if team_of(a % 4, b) == a // 4 else None
        got = permute(pick(terms, (team + k) % 4), route)
        block = jnp.where((home + k) % 4 == team, got, block)
    collected = jnp.zeros((4, 2, n, n), BF)
    collected = lax.dynamic_update_index_in_dim(collected, pick(block, inner), inner, 0)
    for k in (1, 2, 3):
        got = permute(pick(block, inner ^ k), lambda a, b: (a ^ k))
        collected = lax.dynamic_update_index_in_dim(collected, got, inner ^ k, 0)

    mixed = collected[:, :, :rows]
    from_own = shifted(mixed, -1)
    from_far = shifted(mixed, 1)
    far_places = shifted(positions, 2)
    total = gather_terms(positions, mid_places, far_places, from_own, collected, from_far, rows, width)
    return total[None]


def solution(mesh):
    return jax.shard_map(
        on_device,
        mesh=mesh,
        in_specs=(P("depth", None, "lat", None), P(), P("lat", None), P("lat", None, None)),
        out_specs=P("depth", None, "lat", None),
        check_vma=False,
    )
```

time: 1360 us -> 187 us (0.14)
  the two profiles are of different devices: /device:TPU:9 before, /device:TPU:1 now
where the time goes in v1:
time: 187 us
  waiting for transfers between devices  95.5 us (51%)
  starting transfers between devices  57.3 us (31%)
  Pallas kernels  19 us (10%)
  local copies, waits for them, and re-layouts  9.48 us (5%)
  between operations  3.89 us (2%)
    ppermute x12, waiting for transfers between devices, permute(): return lax.ppermute(block, ('depth', 'lat'), pairs)  77 us
    ppermute x12, starting transfers between devices, permute(): return lax.ppermute(block, ('depth', 'lat'), pairs)  40.8 us
    ppermute x7, waiting for transfers between devices, shifted(): lax.ppermute(block, 'lat', [(i, (i + distance) % size) for i in range(siz...  18.5 us
    ppermute x7, starting transfers between devices, shifted(): lax.ppermute(block, 'lat', [(i, (i + distance) % size) for i in range(siz...  16.5 us
    pallas_call x1, Pallas kernels, make_tables(): pl.pallas_call(functools.partial(tables_kernel, n=n, slices=slices), grid...  11.3 us
    squeeze x3, local copies, waits for them, and re-layouts, pick(): return lax.dynamic_index_in_dim(block, index, 0, False)  4.42 us
  transfers between devices with their start and end apart: 19, of which 9 were waited for; matrix products, arithmetic and copies ran while one was open for 1% of the time, Pallas kernels for 6%

profile of v1, /device:TPU:1, one launch (start us, length us, event | category | flops | bytes accessed | tf_op | source)
XLA Modules:
  0.0 187.0 jit_solution(4758713016210557410)
XLA Ops:
  0.0 0.0 copy-start
  0.0 0.9 copy.10.places.own_places
  0.9 0.0 copy-start.1
  0.9 1.6 copy-done.1
  2.4 1.6 shard_map.64
  4.1 3.2 %collective-permute-start.4 = (bf16[2,128,2048]{2,1,0:T(8,128)(2,1)S(1)}, bf16[2,128,2048]{2,1,0:T(8,128)(2,1)S(1)}, u32[]{:S(2)}, u32[]{:S(2)}) collective-permute-start(bf16[2,128,2048]{2,1,0:T(8,128)(2,1)S(1)} %get-tuple-element.8.tile), channel_id=1, source_target_pairs={{0,15},{1,0},{2,1},{3,2},{4,3},{5,4},{6,5},{7,6},{8,7},{9,8},{10,9... | collective-permute-start | bytes 3145736 | tf_op jit(solution)/shard_map/ppermute | solution.py:261
  7.3 0.0 collective-permute-start.3
  7.3 0.0 collective-permute-start
  7.3 6.4 %collective-permute-done.places.mid_places = s32[4,2]{1,0:T(4,128)S(1)} collective-permute-done((s32[4,2]{1,0:T(4,128)S(1)}, s32[4,2]{1,0:T(4,128)S(1)}, u32[]{:S(2)}, u32[]{:S(2)}) %collective-permute-start) | collective-permute-done | bytes 64 | tf_op jit(solution)/shard_map/ppermute | solution.py:261
  13.7 0.0 collective-permute-done.3.behind
  13.7 5.7 %collective-permute-done.4.ahead = bf16[2,128,2048]{2,1,0:T(8,128)(2,1)S(1)} collective-permute-done((bf16[2,128,2048]{2,1,0:T(8,128)(2,1)S(1)}, bf16[2,128,2048]{2,1,0:T(8,128)(2,1)S(1)}, u32[]{:S(2)}, u32[]{:S(2)}) %collective-permute-start.4) | collective-permute-done | bytes 1048608 | tf_op jit(solution)/shard_map/ppermute | solution.py:261
  19.4 1.4 shard_map.65
  20.8 0.1 constant_dynamic-slice_fusion
  20.9 2.7 %collective-permute-start.5 = (bf16[2,256,256]{2,1,0:T(8,128)(2,1)S(1)}, bf16[2,256,256]{2,1,0:T(8,128)(2,1)S(1)}, u32[]{:S(2)}, u32[]{:S(2)}) collective-permute-start(bf16[2,256,256]{2,1,0:T(8,128)(2,1)S(1)} %get-tuple-element.19), channel_id=1, source_target_pairs={{0,16},{1,17},{2,18},{3,19},{4,20},{5,21},{6,22},{7,23},{8,24},{9,... | collective-permute-start | bytes 786440 | tf_op jit(solution)/shard_map/ppermute | solution.py:276
  23.6 1.6 collective-permute-start.6
  25.3 0.0 collective-permute-start.7
  25.3 3.3 %collective-permute-done.5 = bf16[2,256,256]{2,1,0:T(8,128)(2,1)S(1)} collective-permute-done((bf16[2,256,256]{2,1,0:T(8,128)(2,1)S(1)}, bf16[2,256,256]{2,1,0:T(8,128)(2,1)S(1)}, u32[]{:S(2)}, u32[]{:S(2)}) %collective-permute-start.5) | collective-permute-done | bytes 262176 | tf_op jit(solution)/shard_map/ppermute | solution.py:276
  28.6 1.2 collective-permute-done.6
  29.8 6.2 %collective-permute-done.7 = bf16[2,256,256]{2,1,0:T(8,128)(2,1)S(1)} collective-permute-done((bf16[2,256,256]{2,1,0:T(8,128)(2,1)S(1)}, bf16[2,256,256]{2,1,0:T(8,128)(2,1)S(1)}, u32[]{:S(2)}, u32[]{:S(2)}) %collective-permute-start.7) | collective-permute-done | bytes 262176 | tf_op jit(solution)/shard_map/ppermute | solution.py:276
  36.1 0.1 pad_maximum_fusion.m0
  36.2 0.0 copy-start.2
  36.2 0.7 collective-permute-start.10
  37.0 1.6 collective-permute-start.8
  38.6 9.1 %collective-permute-start.9 = (bf16[4,2,256,256]{3,2,1,0:T(8,128)(2,1)S(1)}, bf16[4,2,256,256]{3,2,1,0:T(8,128)(2,1)}, u32[]{:S(2)}, u32[]{:S(2)}) collective-permute-start(bf16[4,2,256,256]{3,2,1,0:T(8,128)(2,1)S(1)} %pad_maximum_fusion.m0), channel_id=1, source_target_pairs={{1,129},{3,131},{5,133},{7,135},{9,137},{11,139},{13,141},{15,143}... | collective-permute-start | bytes 3145736 | tf_op jit(solution)/shard_map/ppermute | solution.py:276
  47.7 0.0 copy-done
  47.7 0.7 dynamic-slice_bitcast_fusion.9
  48.4 0.0 collective-permute-start.2
  48.4 11.3 %shard_map.66.tabs_hbm = bf16[17,2,512,512]{3,2,1,0:T(8,128)(2,1)} custom-call(f32[2,17]{1,0:T(2,128)} %constant.143.clone.scales, f32[4,256,256]{2,1,0:T(8,128)} %constant.144.clone.base), custom_call_target="tpu_custom_call" | custom-call | tf_op jit(solution)/shard_map/pallas_call | solution.py:46
  59.7 0.0 copy-done.2
  59.7 0.6 fusion.2
  64.1 0.6 stack.40.info
  64.7 0.0 collective-permute-done.2.target
  64.7 0.0 copy-start.4
  64.7 0.0 collective-permute-done.10.m3
  64.7 0.0 copy-start.3
  64.7 0.0 collective-permute-done.8.m1
  64.7 0.0 collective-permute-done.9.m2
  64.7 0.7 copy-done.4
  65.4 0.4 copy-done.3
  65.8 1.7 shard_map.67
  67.6 3.6 %dynamic-slice_bitcast_fusion = (bf16[4,2,256,256]{3,2,1,0:T(8,128)(2,1)}, bf16[4,2,256,256]{3,2,1,0:T(8,128)(2,1)}, bf16[4,2,256,256]{3,2,1,0:T(8,128)(2,1)}) fusion(bf16[4,4,2,256,256]{4,3,2,1,0:T(8,128)(2,1)} %bitcast.46, s32[]{:T(128)S(6)} %select_n.131, s32[]{:T(128)S(6)} %select_n.127, s32[]{:T(128)S(6)} %select_n.123), kind=kLoop, calls=%fused_computation.4 | loop fusion | bytes 6291468 | tf_op jit(solution)/shard_map/jit(dynamic_index_in_dim)/squeeze | solution.py:280
  71.2 0.7 collective-permute-start.11
  71.9 1.3 collective-permute-start.12
  73.2 1.7 collective-permute-start.13
  74.9 0.0 collective-permute-done.11
  74.9 59.7 %collective-permute-done.12 = bf16[4,2,256,256]{3,2,1,0:T(8,128)(2,1)S(1)} collective-permute-done((bf16[4,2,256,256]{3,2,1,0:T(8,128)(2,1)}, bf16[4,2,256,256]{3,2,1,0:T(8,128)(2,1)S(1)}, u32[]{:S(2)}, u32[]{:S(2)}) %collective-permute-start.12) | collective-permute-done | bytes 1048608 | tf_op jit(solution)/shard_map/ppermute | solution.py:276
  134.6 0.0 collective-permute-done.13
  134.6 1.6 fusion.1
  136.1 0.1 broadcast_in_dim.17
  136.2 0.1 dynamic-slice_bitcast_fusion.3
  136.3 14.6 %collective-permute-start.14 = (bf16[2,256,256]{2,1,0:T(8,128)(2,1)S(1)}, bf16[2,256,256]{2,1,0:T(8,128)(2,1)S(1)}, u32[]{:S(2)}, u32[]{:S(2)}) collective-permute-start(bf16[2,256,256]{2,1,0:T(8,128)(2,1)S(1)} %get-tuple-element.14), channel_id=1, source_target_pairs={{0,16},{1,17},{2,18},{3,19},{4,20},{5,21},{6,22},{7,23},{8,24},{9,... | collective-permute-start | bytes 786440 | tf_op jit(solution)/shard_map/ppermute | solution.py:276
  150.9 4.0 %collective-permute-start.15 = (bf16[2,256,256]{2,1,0:T(8,128)(2,1)S(1)}, bf16[2,256,256]{2,1,0:T(8,128)(2,1)S(1)}, u32[]{:S(2)}, u32[]{:S(2)}) collective-permute-start(bf16[2,256,256]{2,1,0:T(8,128)(2,1)S(1)} %get-tuple-element.13), channel_id=1, source_target_pairs={{0,32},{1,33},{2,34},{3,35},{4,36},{5,37},{6,38},{7,39},{8,40},{9,... | collective-permute-start | bytes 786440 | tf_op jit(solution)/shard_map/ppermute | solution.py:276
  155.0 2.6 %collective-permute-start.16 = (bf16[2,256,256]{2,1,0:T(8,128)(2,1)S(1)}, bf16[2,256,256]{2,1,0:T(8,128)(2,1)S(1)}, u32[]{:S(2)}, u32[]{:S(2)}) collective-permute-start(bf16[2,256,256]{2,1,0:T(8,128)(2,1)S(1)} %get-tuple-element.12), channel_id=1, source_target_pairs={{0,48},{1,49},{2,50},{3,51},{4,52},{5,53},{6,54},{7,55},{8,56},{9,... | collective-permute-start | bytes 786440 | tf_op jit(solution)/shard_map/ppermute | solution.py:276
  157.6 0.0 collective-permute-done.14
  157.6 1.1 collective-permute-done.15
  158.8 5.5 %collective-permute-done.16 = bf16[2,256,256]{2,1,0:T(8,128)(2,1)S(1)} collective-permute-done((bf16[2,256,256]{2,1,0:T(8,128)(2,1)S(1)}, bf16[2,256,256]{2,1,0:T(8,128)(2,1)S(1)}, u32[]{:S(2)}, u32[]{:S(2)}) %collective-permute-start.16) | collective-permute-done | bytes 262176 | tf_op jit(solution)/shard_map/ppermute | solution.py:276
  164.3 9.2 %collective-permute-start.17 = (bf16[4,2,128,256]{3,2,1,0:T(8,128)(2,1)S(1)}, bf16[4,2,128,256]{3,2,1,0:T(8,128)(2,1)S(1)}, u32[]{:S(2)}, u32[]{:S(2)}) collective-permute-start(bf16[4,2,128,256]{3,2,1,0:T(8,128)(2,1)S(1)} %slice.14), channel_id=1, source_target_pairs={{0,15},{1,0},{2,1},{3,2},{4,3},{5,4},{6,5},{7,6},{8,7},{9,8},{10,9... | collective-permute-start | bytes 1572872 | tf_op jit(solution)/shard_map/ppermute | solution.py:261
  173.5 2.8 %collective-permute-start.18 = (bf16[4,2,128,256]{3,2,1,0:T(8,128)(2,1)S(1)}, bf16[4,2,128,256]{3,2,1,0:T(8,128)(2,1)S(1)}, u32[]{:S(2)}, u32[]{:S(2)}) collective-permute-start(bf16[4,2,128,256]{3,2,1,0:T(8,128)(2,1)S(1)} %slice.14), channel_id=1, source_target_pairs={{0,1},{1,2},{2,3},{3,4},{4,5},{5,6},{6,7},{7,8},{8,9},{9,10},{10,1... | collective-permute-start | bytes 1572872 | tf_op jit(solution)/shard_map/ppermute | solution.py:261
  176.4 1.2 collective-permute-start.1
  177.6 6.4 %collective-permute-done.1.far_places = s32[4,2]{1,0:T(4,128)S(1)} collective-permute-done((s32[4,2]{1,0:T(4,128)S(1)}, s32[4,2]{1,0:T(4,128)S(1)}, u32[]{:S(2)}, u32[]{:S(2)}) %collective-permute-start.1) | collective-permute-done | bytes 64 | tf_op jit(solution)/shard_map/ppermute | solution.py:261
  184.0 0.0 collective-permute-done.17.from_own
  184.0 0.0 collective-permute-done.18.from_far
  184.0 3.0 %shard_map.68 = f32[2,128,2048]{2,1,0:T(8,128)} custom-call(s32[4,2]{1,0:T(4,128)S(1)} %copy.10.places.own_places, s32[4,2]{1,0:T(4,128)S(1)} %collective-permute-done.places.mid_places, s32[4,2]{1,0:T(4,128)S(1)} %collective-permute-done.1.far_places, bf16[4,2,128,256]{3,2,1,0:T(8,128)(2,1)S(1)} %collective-permute-done.17.from_own, ...), custom_call_target="tpu_custom_call" | custom-call | tf_op jit(solution)/shard_map/pallas_call | solution.py:250
  (5 shorter events, 0.1 us)
Async XLA Ops:
  0.0 47.7 %copy-start = (f32[4,256,256]{2,1,0:T(8,128)S(1)}, f32[4,256,256]{2,1,0:T(8,128)}, u32[]{:S(2)}) copy-start(f32[4,256,256]{2,1,0:T(8,128)} %param.9) | copy-start | bytes 3145732
  0.9 1.6 copy-start.1
  4.1 15.4 %collective-permute-start.4 = (bf16[2,128,2048]{2,1,0:T(8,128)(2,1)S(1)}, bf16[2,128,2048]{2,1,0:T(8,128)(2,1)S(1)}, u32[]{:S(2)}, u32[]{:S(2)}) collective-permute-start(bf16[2,128,2048]{2,1,0:T(8,128)(2,1)S(1)} %get-tuple-element.8.tile), channel_id=1, source_target_pairs={{0,15},{1,0},{2,1},{3,2},{4,3},{5,4},{6,5},{7,6},{8,7},{9,8},{10,9... | collective-permute-start | bytes 3145736 | tf_op jit(solution)/shard_map/ppermute | solution.py:261
  7.3 6.4 %collective-permute-start.3 = (bf16[4,2,128,256]{3,2,1,0:T(8,128)(2,1)}, bf16[4,2,128,256]{3,2,1,0:T(8,128)(2,1)}, u32[]{:S(2)}, u32[]{:S(2)}) collective-permute-start(bf16[4,2,128,256]{3,2,1,0:T(8,128)(2,1)} %get-tuple-element.7), channel_id=1, source_target_pairs={{0,1},{1,2},{2,3},{3,4},{4,5},{5,6},{6,7},{7,8},{8,9},{9,10},{10,1... | collective-permute-start | bytes 1572872 | tf_op jit(solution)/shard_map/ppermute | solution.py:261
  7.3 6.4 %collective-permute-start = (s32[4,2]{1,0:T(4,128)S(1)}, s32[4,2]{1,0:T(4,128)S(1)}, u32[]{:S(2)}, u32[]{:S(2)}) collective-permute-start(s32[4,2]{1,0:T(4,128)S(1)} %copy.10.places.own_places), channel_id=1, source_target_pairs={{0,1},{1,2},{2,3},{3,4},{4,5},{5,6},{6,7},{7,8},{8,9},{9,10},{10,1... | collective-permute-start | bytes 104 | tf_op jit(solution)/shard_map/ppermute | solution.py:261
  20.9 7.7 %collective-permute-start.5 = (bf16[2,256,256]{2,1,0:T(8,128)(2,1)S(1)}, bf16[2,256,256]{2,1,0:T(8,128)(2,1)S(1)}, u32[]{:S(2)}, u32[]{:S(2)}) collective-permute-start(bf16[2,256,256]{2,1,0:T(8,128)(2,1)S(1)} %get-tuple-element.19), channel_id=1, source_target_pairs={{0,16},{1,17},{2,18},{3,19},{4,20},{5,21},{6,22},{7,23},{8,24},{9,... | collective-permute-start | bytes 786440 | tf_op jit(solution)/shard_map/ppermute | solution.py:276
  23.6 6.2 %collective-permute-start.6 = (bf16[2,256,256]{2,1,0:T(8,128)(2,1)S(1)}, bf16[2,256,256]{2,1,0:T(8,128)(2,1)S(1)}, u32[]{:S(2)}, u32[]{:S(2)}) collective-permute-start(bf16[2,256,256]{2,1,0:T(8,128)(2,1)S(1)} %get-tuple-element.18), channel_id=1, source_target_pairs={{0,32},{1,33},{2,34},{3,35},{4,36},{5,37},{6,38},{7,39},{8,40},{9,... | collective-permute-start | bytes 786440 | tf_op jit(solution)/shard_map/ppermute | solution.py:276
  25.3 10.8 %collective-permute-start.7 = (bf16[2,256,256]{2,1,0:T(8,128)(2,1)S(1)}, bf16[2,256,256]{2,1,0:T(8,128)(2,1)S(1)}, u32[]{:S(2)}, u32[]{:S(2)}) collective-permute-start(bf16[2,256,256]{2,1,0:T(8,128)(2,1)S(1)} %get-tuple-element.17), channel_id=1, source_target_pairs={{0,48},{1,49},{2,50},{3,51},{4,52},{5,53},{6,54},{7,55},{8,56},{9,... | collective-permute-start | bytes 786440 | tf_op jit(solution)/shard_map/ppermute | solution.py:276
  36.2 23.5 %copy-start.2 = (bf16[4,2,256,256]{3,2,1,0:T(8,128)(2,1)}, bf16[4,2,256,256]{3,2,1,0:T(8,128)(2,1)S(1)}, u32[]{:S(2)}) copy-start(bf16[4,2,256,256]{3,2,1,0:T(8,128)(2,1)S(1)} %pad_maximum_fusion.m0) | copy-start | bytes 3145732
  36.2 28.5 %collective-permute-start.10 = (bf16[4,2,256,256]{3,2,1,0:T(8,128)(2,1)S(1)}, bf16[4,2,256,256]{3,2,1,0:T(8,128)(2,1)S(1)}, u32[]{:S(2)}, u32[]{:S(2)}) collective-permute-start(bf16[4,2,256,256]{3,2,1,0:T(8,128)(2,1)S(1)} %pad_maximum_fusion.m0), channel_id=1, source_target_pairs={{16,80},{18,82},{20,84},{22,86},{24,88},{26,90},{28,92},{30,94},{4... | collective-permute-start | bytes 3145736 | tf_op jit(solution)/shard_map/ppermute | solution.py:276
  37.0 27.7 %collective-permute-start.8 = (bf16[4,2,256,256]{3,2,1,0:T(8,128)(2,1)S(1)}, bf16[4,2,256,256]{3,2,1,0:T(8,128)(2,1)}, u32[]{:S(2)}, u32[]{:S(2)}) collective-permute-start(bf16[4,2,256,256]{3,2,1,0:T(8,128)(2,1)S(1)} %pad_maximum_fusion.m0), channel_id=1, source_target_pairs={{17,209},{19,211},{21,213},{23,215},{25,217},{27,219},{29,221},{31... | collective-permute-start | bytes 3145736 | tf_op jit(solution)/shard_map/ppermute | solution.py:276
  38.6 26.1 %collective-permute-start.9 = (bf16[4,2,256,256]{3,2,1,0:T(8,128)(2,1)S(1)}, bf16[4,2,256,256]{3,2,1,0:T(8,128)(2,1)}, u32[]{:S(2)}, u32[]{:S(2)}) collective-permute-start(bf16[4,2,256,256]{3,2,1,0:T(8,128)(2,1)S(1)} %pad_maximum_fusion.m0), channel_id=1, source_target_pairs={{1,129},{3,131},{5,133},{7,135},{9,137},{11,139},{13,141},{15,143}... | collective-permute-start | bytes 3145736 | tf_op jit(solution)/shard_map/ppermute | solution.py:276
  48.4 16.3 %collective-permute-start.2 = (f32[256,256]{1,0:T(8,128)}, f32[256,256]{1,0:T(8,128)S(1)}, u32[]{:S(2)}, u32[]{:S(2)}) collective-permute-start(f32[256,256]{1,0:T(8,128)} %dynamic-slice_bitcast_fusion.9), channel_id=1, source_target_pairs={{0,1},{1,2},{2,3},{3,4},{4,5},{5,6},{6,7},{7,8},{8,9},{9,10},{10,1... | collective-permute-start | bytes 786440 | tf_op jit(solution)/shard_map/ppermute | solution.py:261
  64.7 0.7 copy-start.4
  64.7 1.2 copy-start.3
  71.2 3.7 %collective-permute-start.11 = (bf16[4,2,256,256]{3,2,1,0:T(8,128)(2,1)}, bf16[4,2,256,256]{3,2,1,0:T(8,128)(2,1)S(1)}, u32[]{:S(2)}, u32[]{:S(2)}) collective-permute-start(bf16[4,2,256,256]{3,2,1,0:T(8,128)(2,1)} %get-tuple-element.11), channel_id=1, source_target_pairs={{0,192},{2,194},{4,196},{6,198},{8,200},{10,202},{12,204},{14,206}... | collective-permute-start | bytes 3145736 | tf_op jit(solution)/shard_map/ppermute | solution.py:276
  71.9 62.6 %collective-permute-start.12 = (bf16[4,2,256,256]{3,2,1,0:T(8,128)(2,1)}, bf16[4,2,256,256]{3,2,1,0:T(8,128)(2,1)S(1)}, u32[]{:S(2)}, u32[]{:S(2)}) collective-permute-start(bf16[4,2,256,256]{3,2,1,0:T(8,128)(2,1)} %get-tuple-element.10), channel_id=1, source_target_pairs={{0,128},{2,130},{4,132},{6,134},{8,136},{10,138},{12,140},{14,142}... | collective-permute-start | bytes 3145736 | tf_op jit(solution)/shard_map/ppermute | solution.py:276
  73.2 61.3 %collective-permute-start.13 = (bf16[4,2,256,256]{3,2,1,0:T(8,128)(2,1)}, bf16[4,2,256,256]{3,2,1,0:T(8,128)(2,1)}, u32[]{:S(2)}, u32[]{:S(2)}) collective-permute-start(bf16[4,2,256,256]{3,2,1,0:T(8,128)(2,1)} %get-tuple-element.9), channel_id=1, source_target_pairs={{0,64},{2,66},{4,68},{6,70},{8,72},{10,74},{12,76},{14,78},{33,97}... | collective-permute-start | bytes 3145736 | tf_op jit(solution)/shard_map/ppermute | solution.py:276
  136.3 21.3 %collective-permute-start.14 = (bf16[2,256,256]{2,1,0:T(8,128)(2,1)S(1)}, bf16[2,256,256]{2,1,0:T(8,128)(2,1)S(1)}, u32[]{:S(2)}, u32[]{:S(2)}) collective-permute-start(bf16[2,256,256]{2,1,0:T(8,128)(2,1)S(1)} %get-tuple-element.14), channel_id=1, source_target_pairs={{0,16},{1,17},{2,18},{3,19},{4,20},{5,21},{6,22},{7,23},{8,24},{9,... | collective-permute-start | bytes 786440 | tf_op jit(solution)/shard_map/ppermute | solution.py:276
  150.9 7.8 %collective-permute-start.15 = (bf16[2,256,256]{2,1,0:T(8,128)(2,1)S(1)}, bf16[2,256,256]{2,1,0:T(8,128)(2,1)S(1)}, u32[]{:S(2)}, u32[]{:S(2)}) collective-permute-start(bf16[2,256,256]{2,1,0:T(8,128)(2,1)S(1)} %get-tuple-element.13), channel_id=1, source_target_pairs={{0,32},{1,33},{2,34},{3,35},{4,36},{5,37},{6,38},{7,39},{8,40},{9,... | collective-permute-start | bytes 786440 | tf_op jit(solution)/shard_map/ppermute | solution.py:276
  155.0 9.3 %collective-permute-start.16 = (bf16[2,256,256]{2,1,0:T(8,128)(2,1)S(1)}, bf16[2,256,256]{2,1,0:T(8,128)(2,1)S(1)}, u32[]{:S(2)}, u32[]{:S(2)}) collective-permute-start(bf16[2,256,256]{2,1,0:T(8,128)(2,1)S(1)} %get-tuple-element.12), channel_id=1, source_target_pairs={{0,48},{1,49},{2,50},{3,51},{4,52},{5,53},{6,54},{7,55},{8,56},{9,... | collective-permute-start | bytes 786440 | tf_op jit(solution)/shard_map/ppermute | solution.py:276
  164.3 19.6 %collective-permute-start.17 = (bf16[4,2,128,256]{3,2,1,0:T(8,128)(2,1)S(1)}, bf16[4,2,128,256]{3,2,1,0:T(8,128)(2,1)S(1)}, u32[]{:S(2)}, u32[]{:S(2)}) collective-permute-start(bf16[4,2,128,256]{3,2,1,0:T(8,128)(2,1)S(1)} %slice.14), channel_id=1, source_target_pairs={{0,15},{1,0},{2,1},{3,2},{4,3},{5,4},{6,5},{7,6},{8,7},{9,8},{10,9... | collective-permute-start | bytes 1572872 | tf_op jit(solution)/shard_map/ppermute | solution.py:261
  173.5 10.4 %collective-permute-start.18 = (bf16[4,2,128,256]{3,2,1,0:T(8,128)(2,1)S(1)}, bf16[4,2,128,256]{3,2,1,0:T(8,128)(2,1)S(1)}, u32[]{:S(2)}, u32[]{:S(2)}) collective-permute-start(bf16[4,2,128,256]{3,2,1,0:T(8,128)(2,1)S(1)} %slice.14), channel_id=1, source_target_pairs={{0,1},{1,2},{2,3},{3,4},{4,5},{5,6},{6,7},{7,8},{8,9},{9,10},{10,1... | collective-permute-start | bytes 1572872 | tf_op jit(solution)/shard_map/ppermute | solution.py:261
  176.4 7.6 %collective-permute-start.1 = (s32[4,2]{1,0:T(4,128)S(1)}, s32[4,2]{1,0:T(4,128)S(1)}, u32[]{:S(2)}, u32[]{:S(2)}) collective-permute-start(s32[4,2]{1,0:T(4,128)S(1)} %copy.10.places.own_places), channel_id=1, source_target_pairs={{0,2},{1,3},{2,4},{3,5},{4,6},{5,7},{6,8},{7,9},{8,10},{9,11},{10,... | collective-permute-start | bytes 104 | tf_op jit(solution)/shard_map/ppermute | solution.py:261

commit v2 on v1

--- a/solution.py
+++ b/solution.py
@@ -52,22 +52,13 @@
     )(jnp.asarray(scales), jnp.asarray(base_tables(n)))
 
 
-def chain_kernel(info, probe, target, m0, m1, m2, m3, tabs_hbm, out_hbm,
-                 patch, tabs, inc, cur, lhs, mid, outv, psem, tsem, osem, *, n, slices):
-    team, inner = info[1], info[2]
+def chain_kernel(plan, places, probe, target, m0, m1, m2, m3, tabs_hbm, o0, o1, o2, o3,
+                 patch, tabs, inc, cur, lhs, mid, outv, psem, tsem, osem, *, n, slices, rows):
     messages = (m0, m1, m2, m3)
-    per = slices // 4
-
-    def patch_copy(s):
-        rel = lax.rem(s // per - team + 4, 4)
-        entry = jnp.bitwise_xor(lax.rem(s, per), inner)
-        return rel, entry
+    outs = (o0, o1, o2, o3)
 
     def table_copy(s):
         return pltpu.make_async_copy(tabs_hbm.at[s], tabs.at[s], tsem.at[s])
-
-    def out_copy(s):
-        return pltpu.make_async_copy(outv.at[s], out_hbm.at[s], osem.at[s])
 
     def to_lhs(m, re, im):
         lhs[0:n, m * n:(m + 1) * n] = re.astype(BF)
@@ -80,20 +71,21 @@
             mid[m * n:(m + 1) * n, n:2 * n] = u[n:2 * n]
         return jnp.dot(mid[...], right, preferred_element_type=F32)
 
-    @pl.when(info[0] == 1)
+    @pl.when(plan[HANDLER] == 1)
     def _():
         for s in range(slices):
             table_copy(s).start()
-            rel, entry = patch_copy(s)
             for r in range(4):
-                @pl.when(rel == r)
+                @pl.when(plan[REL + s] == r)
                 def _():
-                    pltpu.make_async_copy(messages[r].at[entry], patch.at[s], psem.at[s]).start()
+                    pltpu.make_async_copy(messages[r].at[plan[ENTRY + s]], patch.at[s], psem.at[s]).start()
         table_copy(slices).start()
+        row_shift = lax.rem(places[plan[POSITION], 0], rows)
+        col_shift = lax.rem(places[plan[POSITION], 1], n)
         for m in range(2):
             for c in range(2):
-                x = pltpu.roll(probe[m, c], info[3], 0)
-                x = pltpu.roll(x, info[4], 1)
+                x = pltpu.roll(probe[m, c], row_shift, 0)
+                x = pltpu.roll(x, col_shift, 1)
                 cur[m * n:(m + 1) * n, c * n:(c + 1) * n] = x.astype(BF).astype(F32)
 
         def forward(s, carry):
@@ -139,22 +131,26 @@
                 to_lhs(m, pr * gr + pi * gi, pr * gi - pi * gr)
             outv[s, 0] = tr.astype(BF)
             outv[s, 1] = ti.astype(BF)
-            out_copy(s).start()
+            for r in range(4):
+                @pl.when(plan[REL + s] == r)
+                def _():
+                    pltpu.make_async_copy(outv.at[s], outs[r].at[plan[ENTRY + s]], osem.at[s]).start()
             return carry
 
         lax.fori_loop(0, slices, backward, 0)
         for s in range(slices):
-            out_copy(s).wait()
-
-
-def chain(info, probe, target, messages, tables):
+            pltpu.make_async_copy(outv.at[s], o0.at[0], osem.at[s]).wait()
+
+
+def chain(plan, places, probe, target, messages, tables, rows):
     n = target.shape[-1]
     slices = tables.shape[0] - 1
-    return pl.pallas_call(
-        functools.partial(chain_kernel, n=n, slices=slices),
-        out_shape=jax.ShapeDtypeStruct((slices, 2, n, n), BF),
-        in_specs=[SMEM, VMEM, VMEM] + [ANY] * 5,
-        out_specs=ANY,
+    piece = jax.ShapeDtypeStruct(messages[0].shape, BF)
+    return pl.pallas_call(
+        functools.partial(chain_kernel, n=n, slices=slices, rows=rows),
+        out_shape=(piece,) * 4,
+        in_specs=[SMEM, SMEM, VMEM, VMEM] + [ANY] * 5,
+        out_specs=(ANY,) * 4,
         scratch_shapes=[
             pltpu.VMEM((slices, 2, n, n), BF),
             pltpu.VMEM((slices + 1, 2, 2 * n, 2 * n), BF),
@@ -168,7 +164,7 @@
             pltpu.SemaphoreType.DMA((slices,)),
         ],
         compiler_params=pltpu.CompilerParams(vmem_limit_bytes=58 << 20),
-    )(info, probe, target, *messages, tables)
+    )(plan, places, probe, target, *messages, tables)
 
 
 def window(ref, lead, offset, n):
@@ -199,61 +195,63 @@
     )(places, tile)
 
 
-def merge_kernel(places, behind, tile, ahead, out, *, n):
+def merge_kernel(plan, places, behind, tile, ahead, *outs, n):
     rows = tile.shape[1]
     row = lax.broadcasted_iota(jnp.int32, (rows, n), 0)
-    for p in range(out.shape[0]):
+    for k in range(4):
+        p = plan[ORDER + k]
         for c in range(2):
             far = window(ahead, c, places[p, 1], n)
             near = behind[p, c].astype(F32)
-            out[p, c, 0:rows] = jnp.where(row >= places[p, 0] % rows, near, far).astype(BF)
-            out[p, c, rows:2 * rows] = window(tile, c, places[p, 1], n).astype(BF)
-
-
-def merge(places, behind, tile, ahead, n):
-    count = places.shape[0]
+            outs[k][c, 0:rows] = jnp.where(row >= places[p, 0] % rows, near, far).astype(BF)
+            outs[k][c, rows:2 * rows] = window(tile, c, places[p, 1], n).astype(BF)
+
+
+def merge(plan, places, behind, tile, ahead, n):
     return pl.pallas_call(
         functools.partial(merge_kernel, n=n),
-        out_shape=jax.ShapeDtypeStruct((count, 2, 2 * tile.shape[1], n), BF),
-        in_specs=[SMEM, VMEM, VMEM, VMEM],
-        out_specs=VMEM,
+        out_shape=(jax.ShapeDtypeStruct((2, 2 * tile.shape[1], n), BF),) * 4,
+        in_specs=[SMEM, SMEM, VMEM, VMEM, VMEM],
+        out_specs=(VMEM,) * 4,
         compiler_params=pltpu.CompilerParams(vmem_limit_bytes=40 << 20),
-    )(places, behind, tile, ahead)
-
-
-def gather_kernel(own_places, mid_places, far_places, from_own, from_mid, from_far, out, *, n):
+    )(plan, places, behind, tile, ahead)
+
+
+def gather_kernel(plan, own_places, mid_places, far_places, from_own, m0, m1, m2, m3, from_far, out, *, n):
     rows = out.shape[1]
     width = out.shape[-1]
     row = lax.broadcasted_iota(jnp.int32, (rows, n), 0)
     lane = lax.broadcasted_iota(jnp.int32, (rows, n), 1)
     out[...] = jnp.zeros_like(out)
-    for places, terms, kind in ((own_places, from_own, 0), (mid_places, from_mid, 1), (far_places, from_far, 2)):
-        for p in range(places.shape[0]):
+    mids = (m0, m1, m2, m3)
+    for places, kind, order in ((own_places, 0, OTHER), (mid_places, 1, ORDER), (far_places, 2, OTHER)):
+        for k in range(4):
+            p = plan[order + k]
             shift = places[p, 0] % rows
             offset = places[p, 1]
             start = pl.multiple_of((offset // n) * n, n)
             after = pl.multiple_of(jnp.minimum(start + n, width - n), n)
             for c in range(2):
-                if kind == 1:
-                    term = terms[p, c, rows:2 * rows].astype(F32)
+                if kind == 0:
+                    term = jnp.where(row >= shift, from_own[k, c].astype(F32), 0.0)
+                elif kind == 1:
+                    term = mids[k][c, rows:2 * rows].astype(F32)
                 else:
-                    term = terms[p, c].astype(F32)
-                    keep = row >= shift if kind == 0 else row < shift
-                    term = jnp.where(keep, term, 0.0)
+                    term = jnp.where(row < shift, from_far[k, c].astype(F32), 0.0)
                 here = lane >= offset % n
                 out[c, :, pl.ds(start, n)] += jnp.where(here, term, 0.0)
                 out[c, :, pl.ds(after, n)] += jnp.where(here, 0.0, term)
 
 
-def gather_terms(own_places, mid_places, far_places, from_own, from_mid, from_far, rows, width):
-    n = from_mid.shape[-1]
+def gather_terms(plan, own_places, mid_places, far_places, from_own, mids, from_far, rows, width):
+    n = from_own.shape[-1]
     return pl.pallas_call(
         functools.partial(gather_kernel, n=n),
         out_shape=jax.ShapeDtypeStruct((2, rows, width), F32),
-        in_specs=[SMEM, SMEM, SMEM, VMEM, VMEM, VMEM],
+        in_specs=[SMEM] * 4 + [VMEM] * 6,
         out_specs=VMEM,
         compiler_params=pltpu.CompilerParams(vmem_limit_bytes=40 << 20),
-    )(own_places, mid_places, far_places, from_own, from_mid, from_far)
+    )(plan, own_places, mid_places, far_places, from_own, *mids, from_far)
 
 
 def shifted(block, distance):
@@ -261,8 +259,53 @@
     return lax.ppermute(block, "lat", [(i, (i + distance) % size) for i in range(size)])
 
 
-def team_of(position, lat):
-    return (position + 2 * (lat % 2)) % 4
+HANDLER, POSITION, SOURCE, ORDER, OTHER, REL, ENTRY = 0, 1, 2, 3, 7, 11, 27
+GOAL = (((0, 0), (1, 1), (2, 0), (3, 1)), ((1, 2), (0, 3), (3, 2), (2, 3)))
+
+
+def meet(c, team, j):
+    goal, inner = GOAL[c][j]
+    flip = inner ^ 2
+    if c == 0:
+        return inner if (team - goal) % 4 in (0, 1) else flip
+    return inner if (team - goal) % 4 in (0, 3) else flip
+
+
+def place_of(c, d):
+    v = (d + 2 * c) % 16
+    return v // 4, v % 4
+
+
+def position_at(c, team, inner):
+    found = [j for j in range(4) if meet(c, team, j) == inner]
+    assert len(found) == 1
+    return found[0]
+
+
+def device_of(c, team, inner):
+    return (4 * team + inner - 2 * c) % 16
+
+
+@functools.lru_cache
+def make_plan():
+    out = np.zeros((2, 16, 48), np.int32)
+    for c in range(2):
+        for d in range(16):
+            team, inner = place_of(c, d)
+            j = position_at(c, team, inner)
+            row = out[c, d]
+            row[HANDLER] = GOAL[c][j] == (team, inner)
+            row[POSITION] = j
+            row[SOURCE] = (team - GOAL[c][j][0]) % 4
+            other = place_of(1 - c, d)
+            for k in range(4):
+                row[ORDER + k] = position_at(c, team, inner ^ k)
+                row[OTHER + k] = position_at(1 - c, other[0], other[1] ^ k)
+            for s in range(16):
+                there, at = place_of(c, s)
+                row[REL + s] = (there - team) % 4
+                row[ENTRY + s] = at ^ meet(c, there, j)
+    return out
 
 
 def permute(block, route):
@@ -270,14 +313,29 @@
     pairs = []
     for d in range(depth):
         for m in range(lat):
-            to = route(d, m)
+            to = route(m % 2, *place_of(m % 2, d))
             if to is not None:
-                pairs.append((d * lat + m, to * lat + m))
+                pairs.append((d * lat + m, device_of(m % 2, *to) * lat + m))
     return lax.ppermute(block, ("depth", "lat"), pairs)
 
 
-def pick(block, index):
-    return lax.dynamic_index_in_dim(block, index, 0, False)
+def within(block, k):
+    return permute(block, lambda c, team, inner: (team, inner ^ k))
+
+
+def towards(block, k):
+    def route(c, team, inner):
+        goal = GOAL[c][position_at(c, team, inner)]
+        return goal if (team - goal[0]) % 4 == k else None
+    return permute(block, route)
+
+
+def away(block, k):
+    def route(c, team, inner):
+        j = position_at(c, team, inner)
+        there = (team + k) % 4
+        return (there, meet(c, there, j)) if GOAL[c][j] == (team, inner) else None
+    return permute(block, route)
 
 
 def on_device(object_slices, probe, positions, measured):
@@ -286,51 +344,33 @@
     depth_size = lax.axis_size("depth")
     d = lax.axis_index("depth")
     m = lax.axis_index("lat")
-    team, inner = d // 4, d % 4
+    plan = lax.dynamic_slice(jnp.asarray(make_plan()), (m % 2, d, 0), (1, 1, 48)).reshape(48)
     tile = object_slices[0]
 
     mid_places = shifted(positions, 1)
+    far_places = shifted(positions, 2)
     tile_bf, mine = own_windows(positions, tile, n)
     ahead = shifted(tile_bf, -1)
     behind = shifted(mine, 1)
-    target = shifted(pick(measured, inner), 1)
-    patches = merge(mid_places, behind, tile_bf, ahead, n)
-
-    parts = [pick(patches, inner)]
+    target = shifted(lax.dynamic_index_in_dim(measured, plan[OTHER], 0, False), 1)
+    tables = make_tables(n, depth_size)
+    mid_places, far_places, ahead, behind, target, tables = lax.optimization_barrier(
+        (mid_places, far_places, ahead, behind, target, tables))
+    parts = merge(plan, mid_places, behind, tile_bf, ahead, n)
+
+    message = jnp.stack([parts[0]] + [within(parts[k], k) for k in (1, 2, 3)])
+    messages = [message] + [towards(message, k) for k in (1, 2, 3)]
+    terms = chain(plan, mid_places, probe, target, messages, tables, rows)
+
+    block = terms[0]
     for k in (1, 2, 3):
-        parts.append(permute(pick(patches, inner ^ k), lambda a, b: (a ^ k)))
-    message = jnp.stack(parts)
-    messages = [message]
-    for k in (1, 2, 3):
-        def route(a, b):
-            goal = team_of(a % 4, b)
-            return goal * 4 + a % 4 if (goal + k) % 4 == a // 4 else None
-        messages.append(permute(message, route))
-
-    home = team_of(inner, m)
-    place = pick(mid_places, inner)
-    info = jnp.stack([(home == team).astype(jnp.int32), team, inner, place[0] % rows, place[1] % n]).astype(jnp.int32)
-    tables = make_tables(n, depth_size)
-    terms = chain(info, probe, target, messages, tables)
-
-    terms = terms.reshape(4, 4, 2, n, n)
-    block = pick(terms, team)
-    for k in (1, 2, 3):
-        def route(a, b):
-            return ((a // 4 + k) % 4) * 4 + a % 4 if team_of(a % 4, b) == a // 4 else None
-        got = permute(pick(terms, (team + k) % 4), route)
-        block = jnp.where((home + k) % 4 == team, got, block)
-    collected = jnp.zeros((4, 2, n, n), BF)
-    collected = lax.dynamic_update_index_in_dim(collected, pick(block, inner), inner, 0)
-    for k in (1, 2, 3):
-        got = permute(pick(block, inner ^ k), lambda a, b: (a ^ k))
-        collected = lax.dynamic_update_index_in_dim(collected, got, inner ^ k, 0)
-
-    mixed = collected[:, :, :rows]
+        block = jnp.where(plan[SOURCE] == k, away(terms[k], k), block)
+    mids = [block[0]] + [within(block[k], k) for k in (1, 2, 3)]
+
+    mixed = jnp.stack([x[:, :rows] for x in mids])
     from_own = shifted(mixed, -1)
     from_far = shifted(mixed, 1)
-    far_places = shifted(positions, 2)
-    total = gather_terms(positions, mid_places, far_places, from_own, collected, from_far, rows, width)
+    total = gather_terms(plan, positions, mid_places, far_places, from_own, mids, from_far, rows, width)
     return total[None]
 
 

time: 187 us -> 171 us (0.914)
  the two profiles are of different devices: /device:TPU:1 before, /device:TPU:96 now
where the time goes in v2:
time: 171 us
  waiting for transfers between devices  98.5 us (58%)
  starting transfers between devices  41.7 us (24%)
  Pallas kernels  19 us (11%)
  local copies, waits for them, and re-layouts  6.39 us (4%)
  between operations  3.82 us (2%)
    ppermute x12, waiting for transfers between devices, permute(): return lax.ppermute(block, ('depth', 'lat'), pairs)  88.2 us
    ppermute x12, starting transfers between devices, permute(): return lax.ppermute(block, ('depth', 'lat'), pairs)  37.5 us
    pallas_call x1, Pallas kernels, make_tables(): pl.pallas_call(functools.partial(tables_kernel, n=n, slices=slices), grid...  11.2 us
    ppermute x7, waiting for transfers between devices, shifted(): lax.ppermute(block, 'lat', [(i, (i + distance) % size) for i in range(siz...  10.3 us
    ppermute x7, starting transfers between devices, shifted(): lax.ppermute(block, 'lat', [(i, (i + distance) % size) for i in range(siz...  4.19 us
    unnamed x23, local copies, waits for them, and re-layouts  3.56 us
  transfers between devices with their start and end apart: 19, of which 9 were waited for; matrix products, arithmetic and copies ran while one was open for 2% of the time, Pallas kernels for 7%

profile of v2, /device:TPU:96, one launch (start us, length us, event | category | flops | bytes accessed | tf_op | source)
XLA Modules:
  0.0 171.0 jit_solution(10791788583274348397)
XLA Ops:
  0.0 0.0 copy-start
  0.0 0.9 copy.11.places.own_places
  0.9 1.6 copy-done.1
  2.4 1.6 shard_map.73
  4.1 3.2 %collective-permute-start.2 = (bf16[2,128,2048]{2,1,0:T(8,128)(2,1)S(1)}, bf16[2,128,2048]{2,1,0:T(8,128)(2,1)S(1)}, u32[]{:S(2)}, u32[]{:S(2)}) collective-permute-start(bf16[2,128,2048]{2,1,0:T(8,128)(2,1)S(1)} %get-tuple-element.21.tile), channel_id=1, source_target_pairs={{0,15},{1,0},{2,1},{3,2},{4,3},{5,4},{6,5},{7,6},{8,7},{9,8},{10,9... | collective-permute-start | bytes 3145736 | tf_op jit(solution)/shard_map/ppermute | solution.py:259
  7.3 0.0 collective-permute-start.3
  7.3 0.7 constant_dynamic-slice_fusion
  8.0 0.6 fusion
  10.4 0.0 copy-done
  10.4 0.7 dynamic-slice_bitcast_fusion
  11.2 0.0 collective-permute-start.4
  11.2 0.0 collective-permute-start
  11.2 0.4 collective-permute-start.1
  11.6 11.2 %shard_map.74.tabs_hbm = bf16[17,2,512,512]{3,2,1,0:T(8,128)(2,1)} custom-call(f32[2,17]{1,0:T(2,128)} %constant.43.clone.scales, f32[4,256,256]{2,1,0:T(8,128)} %constant.44.clone.base), custom_call_target="tpu_custom_call" | custom-call | tf_op jit(solution)/shard_map/pallas_call | solution.py:46
  22.7 0.7 fusion.1.plan
  23.4 0.0 collective-permute-done.places.mid_places
  23.4 0.0 collective-permute-done.1.far_places
  23.4 0.0 collective-permute-done.4.target
  23.5 0.0 copy-start.10
  23.5 0.0 collective-permute-done.3.behind
  23.5 0.0 collective-permute-done.2.ahead
  23.5 1.5 shard_map.75
  25.0 2.8 %collective-permute-start.7 = (bf16[2,256,256]{2,1,0:T(8,128)(2,1)S(1)}, bf16[2,256,256]{2,1,0:T(8,128)(2,1)S(1)}, u32[]{:S(2)}, u32[]{:S(2)}) collective-permute-start(bf16[2,256,256]{2,1,0:T(8,128)(2,1)S(1)} %get-tuple-element.31), channel_id=1, source_target_pairs={{0,48},{1,241},{2,50},{3,243},{4,52},{5,245},{6,54},{7,247},{8,56}... | collective-permute-start | bytes 786440 | tf_op jit(solution)/shard_map/ppermute | solution.py:319
  27.8 1.9 %collective-permute-start.6 = (bf16[2,256,256]{2,1,0:T(8,128)(2,1)S(1)}, bf16[2,256,256]{2,1,0:T(8,128)(2,1)S(1)}, u32[]{:S(2)}, u32[]{:S(2)}) collective-permute-start(bf16[2,256,256]{2,1,0:T(8,128)(2,1)S(1)} %get-tuple-element.30), channel_id=1, source_target_pairs={{0,32},{1,225},{2,34},{3,227},{4,36},{5,229},{6,38},{7,231},{8,40}... | collective-permute-start | bytes 786440 | tf_op jit(solution)/shard_map/ppermute | solution.py:319
  29.7 0.3 collective-permute-start.5
  30.1 5.6 %collective-permute-done.7 = bf16[2,256,256]{2,1,0:T(8,128)(2,1)S(1)} collective-permute-done((bf16[2,256,256]{2,1,0:T(8,128)(2,1)S(1)}, bf16[2,256,256]{2,1,0:T(8,128)(2,1)S(1)}, u32[]{:S(2)}, u32[]{:S(2)}) %collective-permute-start.7) | collective-permute-done | bytes 262176 | tf_op jit(solution)/shard_map/ppermute | solution.py:319
  35.7 2.1 %collective-permute-done.6 = bf16[2,256,256]{2,1,0:T(8,128)(2,1)S(1)} collective-permute-done((bf16[2,256,256]{2,1,0:T(8,128)(2,1)S(1)}, bf16[2,256,256]{2,1,0:T(8,128)(2,1)S(1)}, u32[]{:S(2)}, u32[]{:S(2)}) %collective-permute-start.6) | collective-permute-done | bytes 262176 | tf_op jit(solution)/shard_map/ppermute | solution.py:319
  37.8 4.5 %collective-permute-done.5 = bf16[2,256,256]{2,1,0:T(8,128)(2,1)S(1)} collective-permute-done((bf16[2,256,256]{2,1,0:T(8,128)(2,1)S(1)}, bf16[2,256,256]{2,1,0:T(8,128)(2,1)S(1)}, u32[]{:S(2)}, u32[]{:S(2)}) %collective-permute-start.5) | collective-permute-done | bytes 262176 | tf_op jit(solution)/shard_map/ppermute | solution.py:319
  42.2 0.1 pad_maximum_fusion.m0
  42.4 0.0 copy-done.4
  42.4 0.0 copy-done.2
  42.4 0.0 copy-done.10
  42.4 0.0 copy-start.6
  42.4 0.7 collective-permute-start.8
  43.1 0.7 collective-permute-start.9
  43.9 6.2 %collective-permute-start.10 = (bf16[4,2,256,256]{3,2,1,0:T(8,128)(2,1)S(1)}, bf16[4,2,256,256]{3,2,1,0:T(8,128)(2,1)S(1)}, u32[]{:S(2)}, u32[]{:S(2)}) collective-permute-start(bf16[4,2,256,256]{3,2,1,0:T(8,128)(2,1)S(1)} %pad_maximum_fusion.m0), channel_id=1, source_target_pairs={{1,65},{3,67},{5,69},{7,71},{9,73},{11,75},{13,77},{15,79},{48,80}... | collective-permute-start | bytes 3145736 | tf_op jit(solution)/shard_map/ppermute | solution.py:319
  50.1 0.0 collective-permute-done.8.m1
  50.1 0.0 copy-start.7
  50.1 0.0 collective-permute-done.9.m2
  50.2 0.0 copy-start.8
  50.2 23.4 %collective-permute-done.10.m3 = bf16[4,2,256,256]{3,2,1,0:T(8,128)(2,1)S(1)} collective-permute-done((bf16[4,2,256,256]{3,2,1,0:T(8,128)(2,1)S(1)}, bf16[4,2,256,256]{3,2,1,0:T(8,128)(2,1)S(1)}, u32[]{:S(2)}, u32[]{:S(2)}) %collective-permute-start.10) | collective-permute-done | bytes 1048608 | tf_op jit(solution)/shard_map/ppermute | solution.py:319
  73.6 0.0 copy-done.6
  73.6 1.1 copy-done.9
  74.7 1.7 %shard_map.76 = (bf16[4,2,256,256]{3,2,1,0:T(8,128)(2,1)}, bf16[4,2,256,256]{3,2,1,0:T(8,128)(2,1)}, bf16[4,2,256,256]{3,2,1,0:T(8,128)(2,1)}, bf16[4,2,256,256]{3,2,1,0:T(8,128)(2,1)}) custom-call(s32[48]{0:T(128)} %copy-done.4, s32[4,2]{1,0:T(4,128)} %copy-done.2, f32[2,2,256,256]{3,2,1,0:T(8,128)} %probe.1, f32[256,256]{1,0:T(8,128)} %copy-done.10, ...), custom_call_target="tpu_custom_call" | custom-call | tf_op jit(solution)/shard_map/pallas_call | solution.py:149
  76.4 1.3 collective-permute-start.11
  77.7 0.7 collective-permute-start.12
  78.5 0.7 collective-permute-start.13
  80.9 44.8 %collective-permute-done.11 = bf16[4,2,256,256]{3,2,1,0:T(8,128)(2,1)S(1)} collective-permute-done((bf16[4,2,256,256]{3,2,1,0:T(8,128)(2,1)}, bf16[4,2,256,256]{3,2,1,0:T(8,128)(2,1)S(1)}, u32[]{:S(2)}, u32[]{:S(2)}) %collective-permute-start.11) | collective-permute-done | bytes 1048608 | tf_op jit(solution)/shard_map/ppermute | solution.py:319
  125.7 0.0 collective-permute-done.12
  125.7 0.0 collective-permute-done.13
  125.7 1.4 select_select_fusion
  127.1 0.1 slice_bitcast_fusion.3
  127.2 14.0 %collective-permute-start.16 = (bf16[2,256,256]{2,1,0:T(8,128)(2,1)S(1)}, bf16[2,256,256]{2,1,0:T(8,128)(2,1)S(1)}, u32[]{:S(2)}, u32[]{:S(2)}) collective-permute-start(bf16[2,256,256]{2,1,0:T(8,128)(2,1)S(1)} %get-tuple-element.38), channel_id=1, source_target_pairs={{0,48},{1,241},{2,50},{3,243},{4,52},{5,245},{6,54},{7,247},{8,56}... | collective-permute-start | bytes 786440 | tf_op jit(solution)/shard_map/ppermute | solution.py:319
  141.2 8.0 %collective-permute-start.15 = (bf16[2,256,256]{2,1,0:T(8,128)(2,1)S(1)}, bf16[2,256,256]{2,1,0:T(8,128)(2,1)S(1)}, u32[]{:S(2)}, u32[]{:S(2)}) collective-permute-start(bf16[2,256,256]{2,1,0:T(8,128)(2,1)S(1)} %get-tuple-element.39), channel_id=1, source_target_pairs={{0,32},{1,225},{2,34},{3,227},{4,36},{5,229},{6,38},{7,231},{8,40}... | collective-permute-start | bytes 786440 | tf_op jit(solution)/shard_map/ppermute | solution.py:319
  149.2 0.0 collective-permute-start.14
  149.2 0.0 collective-permute-done.16.m3
  149.2 7.2 %collective-permute-done.15.m2 = bf16[2,256,256]{2,1,0:T(8,128)(2,1)S(1)} collective-permute-done((bf16[2,256,256]{2,1,0:T(8,128)(2,1)S(1)}, bf16[2,256,256]{2,1,0:T(8,128)(2,1)S(1)}, u32[]{:S(2)}, u32[]{:S(2)}) %collective-permute-start.15) | collective-permute-done | bytes 262176 | tf_op jit(solution)/shard_map/ppermute | solution.py:319
  156.4 0.7 collective-permute-done.14.m1
  157.1 0.1 pad_maximum_fusion.1
  157.2 0.1 collective-permute-start.17
  157.2 0.5 collective-permute-start.18
  157.7 6.2 %collective-permute-done.17.from_own = bf16[4,2,128,256]{3,2,1,0:T(8,128)(2,1)S(1)} collective-permute-done((bf16[4,2,128,256]{3,2,1,0:T(8,128)(2,1)S(1)}, bf16[4,2,128,256]{3,2,1,0:T(8,128)(2,1)S(1)}, u32[]{:S(2)}, u32[]{:S(2)}) %collective-permute-start.17) | collective-permute-done | bytes 524320 | tf_op jit(solution)/shard_map/ppermute | solution.py:259
  163.9 4.1 %collective-permute-done.18.from_far = bf16[4,2,128,256]{3,2,1,0:T(8,128)(2,1)S(1)} collective-permute-done((bf16[4,2,128,256]{3,2,1,0:T(8,128)(2,1)S(1)}, bf16[4,2,128,256]{3,2,1,0:T(8,128)(2,1)S(1)}, u32[]{:S(2)}, u32[]{:S(2)}) %collective-permute-start.18) | collective-permute-done | bytes 524320 | tf_op jit(solution)/shard_map/ppermute | solution.py:259
  168.0 3.0 %shard_map.77 = f32[2,128,2048]{2,1,0:T(8,128)} custom-call(s32[48]{0:T(128)S(1)} %copy-done.5, s32[4,2]{1,0:T(4,128)S(1)} %copy.11.places.own_places, s32[4,2]{1,0:T(4,128)S(1)} %copy-done.3, s32[4,2]{1,0:T(4,128)S(1)} %collective-permute-done.1.far_places, bf16[4,2,128,256]{3,2,1,0:T(8,128)(2,1)S(1)} %collective-permute-done.17.from_own, ...), custom_call_target="tpu_custom_call" | custom-call | tf_op jit(solution)/shard_map/pallas_call | solution.py:248
  (14 shorter events, 0.1 us)
Async XLA Ops:
  0.0 10.4 %copy-start = (f32[4,256,256]{2,1,0:T(8,128)S(1)}, f32[4,256,256]{2,1,0:T(8,128)}, u32[]{:S(2)}) copy-start(f32[4,256,256]{2,1,0:T(8,128)} %param.10) | copy-start | bytes 3145732
  0.9 1.6 copy-start.1
  4.1 19.4 %collective-permute-start.2 = (bf16[2,128,2048]{2,1,0:T(8,128)(2,1)S(1)}, bf16[2,128,2048]{2,1,0:T(8,128)(2,1)S(1)}, u32[]{:S(2)}, u32[]{:S(2)}) collective-permute-start(bf16[2,128,2048]{2,1,0:T(8,128)(2,1)S(1)} %get-tuple-element.21.tile), channel_id=1, source_target_pairs={{0,15},{1,0},{2,1},{3,2},{4,3},{5,4},{6,5},{7,6},{8,7},{9,8},{10,9... | collective-permute-start | bytes 3145736 | tf_op jit(solution)/shard_map/ppermute | solution.py:259
  7.3 16.2 %collective-permute-start.3 = (bf16[4,2,128,256]{3,2,1,0:T(8,128)(2,1)}, bf16[4,2,128,256]{3,2,1,0:T(8,128)(2,1)}, u32[]{:S(2)}, u32[]{:S(2)}) collective-permute-start(bf16[4,2,128,256]{3,2,1,0:T(8,128)(2,1)} %get-tuple-element.22), channel_id=1, source_target_pairs={{0,1},{1,2},{2,3},{3,4},{4,5},{5,6},{6,7},{7,8},{8,9},{9,10},{10,1... | collective-permute-start | bytes 1572872 | tf_op jit(solution)/shard_map/ppermute | solution.py:259
  11.2 12.3 %collective-permute-start.4 = (f32[256,256]{1,0:T(8,128)}, f32[256,256]{1,0:T(8,128)S(1)}, u32[]{:S(2)}, u32[]{:S(2)}) collective-permute-start(f32[256,256]{1,0:T(8,128)} %dynamic-slice_bitcast_fusion), channel_id=1, source_target_pairs={{0,1},{1,2},{2,3},{3,4},{4,5},{5,6},{6,7},{7,8},{8,9},{9,10},{10,1... | collective-permute-start | bytes 786440 | tf_op jit(solution)/shard_map/ppermute | solution.py:259
  11.2 12.3 %collective-permute-start = (s32[4,2]{1,0:T(4,128)S(1)}, s32[4,2]{1,0:T(4,128)S(1)}, u32[]{:S(2)}, u32[]{:S(2)}) collective-permute-start(s32[4,2]{1,0:T(4,128)S(1)} %copy.11.places.own_places), channel_id=1, source_target_pairs={{0,1},{1,2},{2,3},{3,4},{4,5},{5,6},{6,7},{7,8},{8,9},{9,10},{10,1... | collective-permute-start | bytes 104 | tf_op jit(solution)/shard_map/ppermute | solution.py:259
  11.2 12.3 %collective-permute-start.1 = (s32[4,2]{1,0:T(4,128)S(1)}, s32[4,2]{1,0:T(4,128)S(1)}, u32[]{:S(2)}, u32[]{:S(2)}) collective-permute-start(s32[4,2]{1,0:T(4,128)S(1)} %copy.11.places.own_places), channel_id=1, source_target_pairs={{0,2},{1,3},{2,4},{3,5},{4,6},{5,7},{6,8},{7,9},{8,10},{9,11},{10,... | collective-permute-start | bytes 104 | tf_op jit(solution)/shard_map/ppermute | solution.py:259
  23.4 18.9 %copy-start.4 = (s32[48]{0:T(128)}, s32[48]{0:T(128)S(1)}, u32[]{:S(2)}) copy-start(s32[48]{0:T(128)S(1)} %fusion.1.plan) | copy-start | bytes 580
  23.4 18.9 %copy-start.2 = (s32[4,2]{1,0:T(4,128)}, s32[4,2]{1,0:T(4,128)S(1)}, u32[]{:S(2)}) copy-start(s32[4,2]{1,0:T(4,128)S(1)} %collective-permute-done.places.mid_places) | copy-start | bytes 100
  23.5 18.9 %copy-start.10 = (f32[256,256]{1,0:T(8,128)}, f32[256,256]{1,0:T(8,128)S(1)}, u32[]{:S(2)}) copy-start(f32[256,256]{1,0:T(8,128)S(1)} %collective-permute-done.4.target) | copy-start | bytes 786436
  25.0 10.7 %collective-permute-start.7 = (bf16[2,256,256]{2,1,0:T(8,128)(2,1)S(1)}, bf16[2,256,256]{2,1,0:T(8,128)(2,1)S(1)}, u32[]{:S(2)}, u32[]{:S(2)}) collective-permute-start(bf16[2,256,256]{2,1,0:T(8,128)(2,1)S(1)} %get-tuple-element.31), channel_id=1, source_target_pairs={{0,48},{1,241},{2,50},{3,243},{4,52},{5,245},{6,54},{7,247},{8,56}... | collective-permute-start | bytes 786440 | tf_op jit(solution)/shard_map/ppermute | solution.py:319
  27.8 9.9 %collective-permute-start.6 = (bf16[2,256,256]{2,1,0:T(8,128)(2,1)S(1)}, bf16[2,256,256]{2,1,0:T(8,128)(2,1)S(1)}, u32[]{:S(2)}, u32[]{:S(2)}) collective-permute-start(bf16[2,256,256]{2,1,0:T(8,128)(2,1)S(1)} %get-tuple-element.30), channel_id=1, source_target_pairs={{0,32},{1,225},{2,34},{3,227},{4,36},{5,229},{6,38},{7,231},{8,40}... | collective-permute-start | bytes 786440 | tf_op jit(solution)/shard_map/ppermute | solution.py:319
  29.7 12.5 %collective-permute-start.5 = (bf16[2,256,256]{2,1,0:T(8,128)(2,1)S(1)}, bf16[2,256,256]{2,1,0:T(8,128)(2,1)S(1)}, u32[]{:S(2)}, u32[]{:S(2)}) collective-permute-start(bf16[2,256,256]{2,1,0:T(8,128)(2,1)S(1)} %get-tuple-element.29), channel_id=1, source_target_pairs={{0,16},{1,17},{2,18},{3,19},{4,20},{5,21},{6,22},{7,23},{8,24},{9,... | collective-permute-start | bytes 786440 | tf_op jit(solution)/shard_map/ppermute | solution.py:319
  42.4 31.2 %copy-start.6 = (bf16[4,2,256,256]{3,2,1,0:T(8,128)(2,1)}, bf16[4,2,256,256]{3,2,1,0:T(8,128)(2,1)S(1)}, u32[]{:S(2)}) copy-start(bf16[4,2,256,256]{3,2,1,0:T(8,128)(2,1)S(1)} %pad_maximum_fusion.m0) | copy-start | bytes 3145732
  42.4 7.7 %collective-permute-start.8 = (bf16[4,2,256,256]{3,2,1,0:T(8,128)(2,1)S(1)}, bf16[4,2,256,256]{3,2,1,0:T(8,128)(2,1)S(1)}, u32[]{:S(2)}, u32[]{:S(2)}) collective-permute-start(bf16[4,2,256,256]{3,2,1,0:T(8,128)(2,1)S(1)} %pad_maximum_fusion.m0), channel_id=1, source_target_pairs={{16,208},{18,210},{20,212},{22,214},{24,216},{26,218},{28,220},{30... | collective-permute-start | bytes 3145736 | tf_op jit(solution)/shard_map/ppermute | solution.py:319
  43.1 7.0 %collective-permute-start.9 = (bf16[4,2,256,256]{3,2,1,0:T(8,128)(2,1)S(1)}, bf16[4,2,256,256]{3,2,1,0:T(8,128)(2,1)S(1)}, u32[]{:S(2)}, u32[]{:S(2)}) collective-permute-start(bf16[4,2,256,256]{3,2,1,0:T(8,128)(2,1)S(1)} %pad_maximum_fusion.m0), channel_id=1, source_target_pairs={{32,128},{33,193},{34,130},{35,195},{36,132},{37,197},{38,134},{39... | collective-permute-start | bytes 3145736 | tf_op jit(solution)/shard_map/ppermute | solution.py:319
  43.9 29.7 %collective-permute-start.10 = (bf16[4,2,256,256]{3,2,1,0:T(8,128)(2,1)S(1)}, bf16[4,2,256,256]{3,2,1,0:T(8,128)(2,1)S(1)}, u32[]{:S(2)}, u32[]{:S(2)}) collective-permute-start(bf16[4,2,256,256]{3,2,1,0:T(8,128)(2,1)S(1)} %pad_maximum_fusion.m0), channel_id=1, source_target_pairs={{1,65},{3,67},{5,69},{7,71},{9,73},{11,75},{13,77},{15,79},{48,80}... | collective-permute-start | bytes 3145736 | tf_op jit(solution)/shard_map/ppermute | solution.py:319
  50.1 23.5 %copy-start.7 = (bf16[4,2,256,256]{3,2,1,0:T(8,128)(2,1)}, bf16[4,2,256,256]{3,2,1,0:T(8,128)(2,1)S(1)}, u32[]{:S(2)}) copy-start(bf16[4,2,256,256]{3,2,1,0:T(8,128)(2,1)S(1)} %collective-permute-done.8.m1) | copy-start | bytes 3145732
  50.2 23.4 %copy-start.8 = (bf16[4,2,256,256]{3,2,1,0:T(8,128)(2,1)}, bf16[4,2,256,256]{3,2,1,0:T(8,128)(2,1)S(1)}, u32[]{:S(2)}) copy-start(bf16[4,2,256,256]{3,2,1,0:T(8,128)(2,1)S(1)} %collective-permute-done.9.m2) | copy-start | bytes 3145732
  73.6 1.1 copy-start.9
  76.4 49.3 %collective-permute-start.11 = (bf16[4,2,256,256]{3,2,1,0:T(8,128)(2,1)}, bf16[4,2,256,256]{3,2,1,0:T(8,128)(2,1)S(1)}, u32[]{:S(2)}, u32[]{:S(2)}) collective-permute-start(bf16[4,2,256,256]{3,2,1,0:T(8,128)(2,1)} %get-tuple-element.33), channel_id=1, source_target_pairs={{0,224},{2,226},{4,228},{6,230},{8,232},{10,234},{12,236},{14,238}... | collective-permute-start | bytes 3145736 | tf_op jit(solution)/shard_map/ppermute | solution.py:319
  77.7 48.0 %collective-permute-start.12 = (bf16[4,2,256,256]{3,2,1,0:T(8,128)(2,1)}, bf16[4,2,256,256]{3,2,1,0:T(8,128)(2,1)S(1)}, u32[]{:S(2)}, u32[]{:S(2)}) collective-permute-start(bf16[4,2,256,256]{3,2,1,0:T(8,128)(2,1)} %get-tuple-element.34), channel_id=1, source_target_pairs={{0,160},{2,162},{4,164},{6,166},{8,168},{10,170},{12,172},{14,174}... | collective-permute-start | bytes 3145736 | tf_op jit(solution)/shard_map/ppermute | solution.py:319
  78.5 47.2 %collective-permute-start.13 = (bf16[4,2,256,256]{3,2,1,0:T(8,128)(2,1)}, bf16[4,2,256,256]{3,2,1,0:T(8,128)(2,1)S(1)}, u32[]{:S(2)}, u32[]{:S(2)}) collective-permute-start(bf16[4,2,256,256]{3,2,1,0:T(8,128)(2,1)} %get-tuple-element.35), channel_id=1, source_target_pairs={{0,64},{2,66},{4,68},{6,70},{8,72},{10,74},{12,76},{14,78},{17,49}... | collective-permute-start | bytes 3145736 | tf_op jit(solution)/shard_map/ppermute | solution.py:319
  127.1 40.9 %copy-start.3 = (s32[4,2]{1,0:T(4,128)S(1)}, s32[4,2]{1,0:T(4,128)}, u32[]{:S(2)}) copy-start(s32[4,2]{1,0:T(4,128)} %copy-done.2) | copy-start | bytes 100
  127.1 40.9 %copy-start.5 = (s32[48]{0:T(128)S(1)}, s32[48]{0:T(128)}, u32[]{:S(2)}) copy-start(s32[48]{0:T(128)} %copy-done.4) | copy-start | bytes 580
  127.2 22.0 %collective-permute-start.16 = (bf16[2,256,256]{2,1,0:T(8,128)(2,1)S(1)}, bf16[2,256,256]{2,1,0:T(8,128)(2,1)S(1)}, u32[]{:S(2)}, u32[]{:S(2)}) collective-permute-start(bf16[2,256,256]{2,1,0:T(8,128)(2,1)S(1)} %get-tuple-element.38), channel_id=1, source_target_pairs={{0,48},{1,241},{2,50},{3,243},{4,52},{5,245},{6,54},{7,247},{8,56}... | collective-permute-start | bytes 786440 | tf_op jit(solution)/shard_map/ppermute | solution.py:319
  141.2 15.2 %collective-permute-start.15 = (bf16[2,256,256]{2,1,0:T(8,128)(2,1)S(1)}, bf16[2,256,256]{2,1,0:T(8,128)(2,1)S(1)}, u32[]{:S(2)}, u32[]{:S(2)}) collective-permute-start(bf16[2,256,256]{2,1,0:T(8,128)(2,1)S(1)} %get-tuple-element.39), channel_id=1, source_target_pairs={{0,32},{1,225},{2,34},{3,227},{4,36},{5,229},{6,38},{7,231},{8,40}... | collective-permute-start | bytes 786440 | tf_op jit(solution)/shard_map/ppermute | solution.py:319
  149.2 7.9 %collective-permute-start.14 = (bf16[2,256,256]{2,1,0:T(8,128)(2,1)S(1)}, bf16[2,256,256]{2,1,0:T(8,128)(2,1)S(1)}, u32[]{:S(2)}, u32[]{:S(2)}) collective-permute-start(bf16[2,256,256]{2,1,0:T(8,128)(2,1)S(1)} %get-tuple-element.40), channel_id=1, source_target_pairs={{0,16},{1,17},{2,18},{3,19},{4,20},{5,21},{6,22},{7,23},{8,24},{9,... | collective-permute-start | bytes 786440 | tf_op jit(solution)/shard_map/ppermute | solution.py:319
  157.2 6.8 %collective-permute-start.17 = (bf16[4,2,128,256]{3,2,1,0:T(8,128)(2,1)S(1)}, bf16[4,2,128,256]{3,2,1,0:T(8,128)(2,1)S(1)}, u32[]{:S(2)}, u32[]{:S(2)}) collective-permute-start(bf16[4,2,128,256]{3,2,1,0:T(8,128)(2,1)S(1)} %pad_maximum_fusion.1), channel_id=1, source_target_pairs={{0,15},{1,0},{2,1},{3,2},{4,3},{5,4},{6,5},{7,6},{8,7},{9,8},{10,9... | collective-permute-start | bytes 1572872 | tf_op jit(solution)/shard_map/ppermute | solution.py:259
  157.2 10.8 %collective-permute-start.18 = (bf16[4,2,128,256]{3,2,1,0:T(8,128)(2,1)S(1)}, bf16[4,2,128,256]{3,2,1,0:T(8,128)(2,1)S(1)}, u32[]{:S(2)}, u32[]{:S(2)}) collective-permute-start(bf16[4,2,128,256]{3,2,1,0:T(8,128)(2,1)S(1)} %pad_maximum_fusion.1), channel_id=1, source_target_pairs={{0,1},{1,2},{2,3},{3,4},{4,5},{5,6},{6,7},{7,8},{8,9},{9,10},{10,1... | collective-permute-start | bytes 1572872 | tf_op jit(solution)/shard_map/ppermute | solution.py:259

commit v3 on v2

--- a/solution.py
+++ b/solution.py
@@ -52,24 +52,43 @@
     )(jnp.asarray(scales), jnp.asarray(base_tables(n)))
 
 
-def chain_kernel(plan, places, probe, target, m0, m1, m2, m3, tabs_hbm, o0, o1, o2, o3,
-                 patch, tabs, inc, cur, lhs, mid, outv, psem, tsem, osem, *, n, slices, rows):
-    messages = (m0, m1, m2, m3)
-    outs = (o0, o1, o2, o3)
+def chain_kernel(plan, places, probe, target, *refs, n, slices, rows):
+    near_in, far_in, tabs_hbm, near_out, far_out = refs[0:4], refs[4:8], refs[8], refs[9:13], refs[13:17]
+    (patch, tabs, inc, lhs0, lhs1, mid0, mid1, outv, psem, tsem, osem) = refs[17:]
+    lhs, mid = (lhs0, lhs1), (mid0, mid1)
+    half = n // 2
 
     def table_copy(s):
         return pltpu.make_async_copy(tabs_hbm.at[s], tabs.at[s], tsem.at[s])
 
-    def to_lhs(m, re, im):
-        lhs[0:n, m * n:(m + 1) * n] = re.astype(BF)
-        lhs[n:2 * n, m * n:(m + 1) * n] = im.astype(BF)
+    def patch_wait(s):
+        for h in range(2):
+            pltpu.make_async_copy(near_in[0].at[0], patch.at[s, :, pl.ds(h * half, half)], psem.at[h, s]).wait()
+
+    def put(m, re, im):
+        lhs[m][0:n] = re.astype(BF)
+        lhs[m][n:2 * n] = im.astype(BF)
+
+    def first(m, left):
+        u = jnp.dot(left, lhs[m][...], preferred_element_type=F32)
+        mid[m][:, 0:n] = u[0:n].astype(BF)
+        mid[m][:, n:2 * n] = u[n:2 * n].astype(BF)
+
+    def second(m, right):
+        v = jnp.dot(mid[m][...], right, preferred_element_type=F32)
+        return v[:, 0:n], v[:, n:2 * n]
 
     def transform(left, right):
-        for m in range(2):
-            u = jnp.dot(left, lhs[:, m * n:(m + 1) * n], preferred_element_type=F32).astype(BF)
-            mid[m * n:(m + 1) * n, 0:n] = u[0:n]
-            mid[m * n:(m + 1) * n, n:2 * n] = u[n:2 * n]
-        return jnp.dot(mid[...], right, preferred_element_type=F32)
+        first(0, left)
+        first(1, left)
+        return second(0, right), second(1, right)
+
+    def enter(s, m, wr, wi):
+        inc[s, m, 0] = wr.astype(BF)
+        inc[s, m, 1] = wi.astype(BF)
+        pr = patch[s, 0].astype(F32)
+        pi = patch[s, 1].astype(F32)
+        put(m, pr * wr - pi * wi, pr * wi + pi * wr)
 
     @pl.when(plan[HANDLER] == 1)
     def _():
@@ -78,93 +97,97 @@
             for r in range(4):
                 @pl.when(plan[REL + s] == r)
                 def _():
-                    pltpu.make_async_copy(messages[r].at[plan[ENTRY + s]], patch.at[s], psem.at[s]).start()
+                    for h, group in enumerate((near_in, far_in)):
+                        pltpu.make_async_copy(group[r].at[plan[ENTRY + s]], patch.at[s, :, pl.ds(h * half, half)], psem.at[h, s]).start()
         table_copy(slices).start()
         row_shift = lax.rem(places[plan[POSITION], 0], rows)
         col_shift = lax.rem(places[plan[POSITION], 1], n)
+        rolled = []
         for m in range(2):
             for c in range(2):
                 x = pltpu.roll(probe[m, c], row_shift, 0)
-                x = pltpu.roll(x, col_shift, 1)
-                cur[m * n:(m + 1) * n, c * n:(c + 1) * n] = x.astype(BF).astype(F32)
+                rolled.append(pltpu.roll(x, col_shift, 1).astype(BF).astype(F32))
+        patch_wait(0)
+        for m in range(2):
+            enter(0, m, rolled[2 * m], rolled[2 * m + 1])
 
         def forward(s, carry):
             table_copy(s).wait()
-            pltpu.make_async_copy(m0.at[0], patch.at[s], psem.at[s]).wait()
-            pr = patch[s, 0].astype(F32)
-            pi = patch[s, 1].astype(F32)
-            for m in range(2):
-                wr = cur[m * n:(m + 1) * n, 0:n]
-                wi = cur[m * n:(m + 1) * n, n:2 * n]
-                to_lhs(m, pr * wr - pi * wi, pr * wi + pi * wr)
-            inc[s] = cur[...].astype(BF)
-            cur[...] = transform(tabs[s, 0], tabs[s, 1])
+            patch_wait(s + 1)
+            first(0, tabs[s, 0])
+            first(1, tabs[s, 0])
+            enter(s + 1, 0, *second(0, tabs[s, 1]))
+            enter(s + 1, 1, *second(1, tabs[s, 1]))
             return carry
 
-        lax.fori_loop(0, slices, forward, 0)
+        lax.fori_loop(0, slices - 1, forward, 0)
+        table_copy(slices - 1).wait()
         table_copy(slices).wait()
+        f = transform(tabs[slices - 1, 0], tabs[slices - 1, 1])
         for m in range(2):
-            to_lhs(m, cur[m * n:(m + 1) * n, 0:n], cur[m * n:(m + 1) * n, n:2 * n])
-        cur[...] = transform(tabs[slices, 0], tabs[slices, 1])
-        f = [[cur[m * n:(m + 1) * n, c * n:(c + 1) * n] for c in range(2)] for m in range(2)]
+            put(m, *f[m])
+        f = transform(tabs[slices, 0], tabs[slices, 1])
         resid = (f[0][0] * f[0][0] + f[0][1] * f[0][1]) + (f[1][0] * f[1][0] + f[1][1] * f[1][1]) - target[...]
         for m in range(2):
-            to_lhs(m, resid * f[m][0], resid * f[m][1])
-        cur[...] = transform(tabs[slices, 1], tabs[slices, 0])
+            put(m, resid * f[m][0], resid * f[m][1])
+        f = transform(tabs[slices, 1], tabs[slices, 0])
         for m in range(2):
-            to_lhs(m, cur[m * n:(m + 1) * n, 0:n], cur[m * n:(m + 1) * n, n:2 * n])
+            put(m, *f[m])
 
         def backward(back, carry):
             s = slices - 1 - back
-            cur[...] = transform(tabs[s, 1], tabs[s, 0])
-            pr = patch[s, 0].astype(F32)
-            pi = patch[s, 1].astype(F32)
-            tr = jnp.zeros((n, n), F32)
-            ti = jnp.zeros((n, n), F32)
+            tr = ti = None
+            first(0, tabs[s, 1])
+            first(1, tabs[s, 1])
             for m in range(2):
-                gr = cur[m * n:(m + 1) * n, 0:n]
-                gi = cur[m * n:(m + 1) * n, n:2 * n]
-                wr = inc[s, m * n:(m + 1) * n, 0:n].astype(F32)
-                wi = inc[s, m * n:(m + 1) * n, n:2 * n].astype(F32)
-                tr += wr * gr + wi * gi
-                ti += wr * gi - wi * gr
-                to_lhs(m, pr * gr + pi * gi, pr * gi - pi * gr)
+                gr, gi = second(m, tabs[s, 0])
+                pr = patch[s, 0].astype(F32)
+                pi = patch[s, 1].astype(F32)
+                put(m, pr * gr + pi * gi, pr * gi - pi * gr)
+                wr = inc[s, m, 0].astype(F32)
+                wi = inc[s, m, 1].astype(F32)
+                ar = wr * gr + wi * gi
+                ai = wr * gi - wi * gr
+                tr, ti = (ar, ai) if tr is None else (tr + ar, ti + ai)
             outv[s, 0] = tr.astype(BF)
             outv[s, 1] = ti.astype(BF)
             for r in range(4):
                 @pl.when(plan[REL + s] == r)
                 def _():
-                    pltpu.make_async_copy(outv.at[s], outs[r].at[plan[ENTRY + s]], osem.at[s]).start()
+                    for h, group in enumerate((near_out, far_out)):
+                        pltpu.make_async_copy(outv.at[s, :, pl.ds(h * half, half)], group[r].at[plan[ENTRY + s]], osem.at[h, s]).start()
             return carry
 
         lax.fori_loop(0, slices, backward, 0)
         for s in range(slices):
-            pltpu.make_async_copy(outv.at[s], o0.at[0], osem.at[s]).wait()
-
-
-def chain(plan, places, probe, target, messages, tables, rows):
+            for h in range(2):
+                pltpu.make_async_copy(outv.at[s, :, pl.ds(h * half, half)], near_out[0].at[0], osem.at[h, s]).wait()
+
+
+def chain(plan, places, probe, target, near, far, tables, rows):
     n = target.shape[-1]
     slices = tables.shape[0] - 1
-    piece = jax.ShapeDtypeStruct(messages[0].shape, BF)
+    piece = jax.ShapeDtypeStruct(near[0].shape, BF)
     return pl.pallas_call(
         functools.partial(chain_kernel, n=n, slices=slices, rows=rows),
-        out_shape=(piece,) * 4,
-        in_specs=[SMEM, SMEM, VMEM, VMEM] + [ANY] * 5,
-        out_specs=(ANY,) * 4,
+        out_shape=(piece,) * 8,
+        in_specs=[SMEM, SMEM, VMEM, VMEM] + [ANY] * 9,
+        out_specs=(ANY,) * 8,
         scratch_shapes=[
             pltpu.VMEM((slices, 2, n, n), BF),
             pltpu.VMEM((slices + 1, 2, 2 * n, 2 * n), BF),
-            pltpu.VMEM((slices, 2 * n, 2 * n), BF),
-            pltpu.VMEM((2 * n, 2 * n), F32),
-            pltpu.VMEM((2 * n, 2 * n), BF),
-            pltpu.VMEM((2 * n, 2 * n), BF),
+            pltpu.VMEM((slices, 2, 2, n, n), BF),
+            pltpu.VMEM((2 * n, n), BF),
+            pltpu.VMEM((2 * n, n), BF),
+            pltpu.VMEM((n, 2 * n), BF),
+            pltpu.VMEM((n, 2 * n), BF),
             pltpu.VMEM((slices, 2, n, n), BF),
-            pltpu.SemaphoreType.DMA((slices,)),
+            pltpu.SemaphoreType.DMA((2, slices)),
             pltpu.SemaphoreType.DMA((slices + 1,)),
-            pltpu.SemaphoreType.DMA((slices,)),
+            pltpu.SemaphoreType.DMA((2, slices)),
         ],
         compiler_params=pltpu.CompilerParams(vmem_limit_bytes=58 << 20),
-    )(plan, places, probe, target, *messages, tables)
+    )(plan, places, probe, target, *near, *far, tables)
 
 
 def window(ref, lead, offset, n):
@@ -195,26 +218,42 @@
     )(places, tile)
 
 
-def merge_kernel(plan, places, behind, tile, ahead, *outs, n):
-    rows = tile.shape[1]
+def far_kernel(plan, places, tile, *outs, n):
+    for k in range(4):
+        p = plan[ORDER + k]
+        for c in range(2):
+            outs[k][c] = window(tile, c, places[p, 1], n).astype(BF)
+
+
+def far_parts(plan, places, tile, n):
+    return pl.pallas_call(
+        functools.partial(far_kernel, n=n),
+        out_shape=(jax.ShapeDtypeStruct((2, tile.shape[1], n), BF),) * 4,
+        in_specs=[SMEM, SMEM, VMEM],
+        out_specs=(VMEM,) * 4,
+        compiler_params=pltpu.CompilerParams(vmem_limit_bytes=40 << 20),
+    )(plan, places, tile)
+
+
+def near_kernel(plan, places, behind, ahead, *outs, n):
+    rows = ahead.shape[1]
     row = lax.broadcasted_iota(jnp.int32, (rows, n), 0)
     for k in range(4):
         p = plan[ORDER + k]
         for c in range(2):
-            far = window(ahead, c, places[p, 1], n)
-            near = behind[p, c].astype(F32)
-            outs[k][c, 0:rows] = jnp.where(row >= places[p, 0] % rows, near, far).astype(BF)
-            outs[k][c, rows:2 * rows] = window(tile, c, places[p, 1], n).astype(BF)
-
-
-def merge(plan, places, behind, tile, ahead, n):
-    return pl.pallas_call(
-        functools.partial(merge_kernel, n=n),
-        out_shape=(jax.ShapeDtypeStruct((2, 2 * tile.shape[1], n), BF),) * 4,
-        in_specs=[SMEM, SMEM, VMEM, VMEM, VMEM],
+            after = window(ahead, c, places[p, 1], n)
+            before = behind[p, c].astype(F32)
+            outs[k][c] = jnp.where(row >= places[p, 0] % rows, before, after).astype(BF)
+
+
+def near_parts(plan, places, behind, ahead, n):
+    return pl.pallas_call(
+        functools.partial(near_kernel, n=n),
+        out_shape=(jax.ShapeDtypeStruct((2, ahead.shape[1], n), BF),) * 4,
+        in_specs=[SMEM, SMEM, VMEM, VMEM],
         out_specs=(VMEM,) * 4,
         compiler_params=pltpu.CompilerParams(vmem_limit_bytes=40 << 20),
-    )(plan, places, behind, tile, ahead)
+    )(plan, places, behind, ahead)
 
 
 def gather_kernel(plan, own_places, mid_places, far_places, from_own, m0, m1, m2, m3, from_far, out, *, n):
@@ -235,7 +274,7 @@
                 if kind == 0:
                     term = jnp.where(row >= shift, from_own[k, c].astype(F32), 0.0)
                 elif kind == 1:
-                    term = mids[k][c, rows:2 * rows].astype(F32)
+                    term = mids[k][c].astype(F32)
                 else:
                     term = jnp.where(row < shift, from_far[k, c].astype(F32), 0.0)
                 here = lane >= offset % n
@@ -348,26 +387,34 @@
     tile = object_slices[0]
 
     mid_places = shifted(positions, 1)
-    far_places = shifted(positions, 2)
     tile_bf, mine = own_windows(positions, tile, n)
     ahead = shifted(tile_bf, -1)
     behind = shifted(mine, 1)
     target = shifted(lax.dynamic_index_in_dim(measured, plan[OTHER], 0, False), 1)
+    far_places = shifted(positions, 2)
+
+    far = far_parts(plan, mid_places, tile_bf, n)
+    far_got = [within(far[k], k) for k in (1, 2, 3)]
+    far, ahead, behind, target, far_places = lax.optimization_barrier((far, ahead, behind, target, far_places))
+    near = near_parts(plan, mid_places, behind, ahead, n)
+    near_got = [within(near[k], k) for k in (1, 2, 3)]
+    far_message = jnp.stack([far[0]] + far_got)
+    far_in = [far_message] + [towards(far_message, k) for k in (1, 2, 3)]
+    near_message = jnp.stack([near[0]] + near_got)
+    near_in = [near_message] + [towards(near_message, k) for k in (1, 2, 3)]
     tables = make_tables(n, depth_size)
-    mid_places, far_places, ahead, behind, target, tables = lax.optimization_barrier(
-        (mid_places, far_places, ahead, behind, target, tables))
-    parts = merge(plan, mid_places, behind, tile_bf, ahead, n)
-
-    message = jnp.stack([parts[0]] + [within(parts[k], k) for k in (1, 2, 3)])
-    messages = [message] + [towards(message, k) for k in (1, 2, 3)]
-    terms = chain(plan, mid_places, probe, target, messages, tables, rows)
-
-    block = terms[0]
-    for k in (1, 2, 3):
-        block = jnp.where(plan[SOURCE] == k, away(terms[k], k), block)
-    mids = [block[0]] + [within(block[k], k) for k in (1, 2, 3)]
-
-    mixed = jnp.stack([x[:, :rows] for x in mids])
+    terms = chain(plan, mid_places, probe, target, near_in, far_in, tables, rows)
+
+    def home(pieces):
+        block = pieces[0]
+        for k in (1, 2, 3):
+            block = jnp.where(plan[SOURCE] == k, away(pieces[k], k), block)
+        return block
+
+    near_block = home(terms[:4])
+    far_block = home(terms[4:])
+    mixed = jnp.stack([near_block[0]] + [within(near_block[k], k) for k in (1, 2, 3)])
+    mids = [far_block[0]] + [within(far_block[k], k) for k in (1, 2, 3)]
     from_own = shifted(mixed, -1)
     from_far = shifted(mixed, 1)
     total = gather_terms(plan, positions, mid_places, far_places, from_own, mids, from_far, rows, width)

time: 171 us -> 167 us (0.977)
  the two profiles are of different devices: /device:TPU:96 before, /device:TPU:1 now
where the time goes in v3:
time: 167 us
  starting transfers between devices  78 us (47%)
  waiting for transfers between devices  56.8 us (34%)
  Pallas kernels  19.9 us (12%)
  local copies, waits for them, and re-layouts  6.26 us (4%)
  between operations  4.29 us (3%)
    ppermute x24, starting transfers between devices, permute(): return lax.ppermute(block, ('depth', 'lat'), pairs)  54.1 us
    ppermute x24, waiting for transfers between devices, permute(): return lax.ppermute(block, ('depth', 'lat'), pairs)  53.9 us
    ppermute x7, starting transfers between devices, shifted(): lax.ppermute(block, 'lat', [(i, (i + distance) % size) for i in range(siz...  23.9 us
    pallas_call x1, Pallas kernels, make_tables(): pl.pallas_call(functools.partial(tables_kernel, n=n, slices=slices), grid...  11.1 us
    unnamed x25, local copies, waits for them, and re-layouts  4.12 us
  transfers between devices with their start and end apart: 31, of which 7 were waited for; matrix products, arithmetic and copies ran while one was open for 2% of the time, Pallas kernels for 8%

profile of v3, /device:TPU:1, one launch (start us, length us, event | category | flops | bytes accessed | tf_op | source)
XLA Modules:
  0.0 166.7 jit_solution(17812343939988806249)
XLA Ops:
  0.0 0.9 copy.11.places.own_places
  0.9 1.6 copy-done.1
  2.4 1.6 shard_map.73
  4.1 3.2 %collective-permute-start.1 = (bf16[2,128,2048]{2,1,0:T(8,128)(2,1)S(1)}, bf16[2,128,2048]{2,1,0:T(8,128)(2,1)S(1)}, u32[]{:S(2)}, u32[]{:S(2)}) collective-permute-start(bf16[2,128,2048]{2,1,0:T(8,128)(2,1)S(1)} %get-tuple-element.28.tile), channel_id=1, source_target_pairs={{0,15},{1,0},{2,1},{3,2},{4,3},{5,4},{6,5},{7,6},{8,7},{9,8},{10,9... | collective-permute-start | bytes 3145736 | tf_op jit(solution)/shard_map/ppermute | solution.py:298
  7.3 0.7 constant_dynamic-slice_fusion
  8.0 0.7 fusion.1
  10.7 0.1 collective-permute-start.3
  10.8 1.0 collective-permute-start
  11.8 1.2 collective-permute-start.4
  12.9 0.7 fusion.2.plan
  13.6 2.8 %collective-permute-done.places.mid_places = s32[4,2]{1,0:T(4,128)S(1)} collective-permute-done((s32[4,2]{1,0:T(4,128)S(1)}, s32[4,2]{1,0:T(4,128)S(1)}, u32[]{:S(2)}, u32[]{:S(2)}) %collective-permute-start) | collective-permute-done | bytes 64 | tf_op jit(solution)/shard_map/ppermute | solution.py:298
  16.5 0.7 shard_map.74
  17.2 7.7 %collective-permute-start.13 = (bf16[2,128,256]{2,1,0:T(8,128)(2,1)S(1)}, bf16[2,128,256]{2,1,0:T(8,128)(2,1)S(1)}, u32[]{:S(2)}, u32[]{:S(2)}) collective-permute-start(bf16[2,128,256]{2,1,0:T(8,128)(2,1)S(1)} %get-tuple-element.32), channel_id=1, source_target_pairs={{0,48},{1,241},{2,50},{3,243},{4,52},{5,245},{6,54},{7,247},{8,56}... | collective-permute-start | bytes 393224 | tf_op jit(solution)/shard_map/ppermute | solution.py:358
  24.9 0.0 collective-permute-done.4.far_places
  24.9 2.9 %collective-permute-start.12 = (bf16[2,128,256]{2,1,0:T(8,128)(2,1)S(1)}, bf16[2,128,256]{2,1,0:T(8,128)(2,1)S(1)}, u32[]{:S(2)}, u32[]{:S(2)}) collective-permute-start(bf16[2,128,256]{2,1,0:T(8,128)(2,1)S(1)} %get-tuple-element.31), channel_id=1, source_target_pairs={{0,32},{1,225},{2,34},{3,227},{4,36},{5,229},{6,38},{7,231},{8,40}... | collective-permute-start | bytes 393224 | tf_op jit(solution)/shard_map/ppermute | solution.py:358
  27.7 0.0 collective-permute-done.3.target
  27.7 2.6 %collective-permute-start.11 = (bf16[2,128,256]{2,1,0:T(8,128)(2,1)S(1)}, bf16[2,128,256]{2,1,0:T(8,128)(2,1)S(1)}, u32[]{:S(2)}, u32[]{:S(2)}) collective-permute-start(bf16[2,128,256]{2,1,0:T(8,128)(2,1)S(1)} %get-tuple-element.30), channel_id=1, source_target_pairs={{0,16},{1,17},{2,18},{3,19},{4,20},{5,21},{6,22},{7,23},{8,24},{9,... | collective-permute-start | bytes 393224 | tf_op jit(solution)/shard_map/ppermute | solution.py:358
  30.4 0.0 collective-permute-done.2.behind
  30.4 0.0 collective-permute-done.1.ahead
  30.4 0.0 collective-permute-done.13
  30.4 0.0 collective-permute-done.12
  30.4 2.7 %collective-permute-done.11 = bf16[2,128,256]{2,1,0:T(8,128)(2,1)S(1)} collective-permute-done((bf16[2,128,256]{2,1,0:T(8,128)(2,1)S(1)}, bf16[2,128,256]{2,1,0:T(8,128)(2,1)S(1)}, u32[]{:S(2)}, u32[]{:S(2)}) %collective-permute-start.11) | collective-permute-done | bytes 131104 | tf_op jit(solution)/shard_map/ppermute | solution.py:358
  33.1 0.1 pad_maximum_fusion.1.refs_4_
  33.1 0.7 collective-permute-start.14
  33.9 1.3 shard_map.75
  35.2 2.5 %collective-permute-start.7 = (bf16[2,128,256]{2,1,0:T(8,128)(2,1)S(1)}, bf16[2,128,256]{2,1,0:T(8,128)(2,1)S(1)}, u32[]{:S(2)}, u32[]{:S(2)}) collective-permute-start(bf16[2,128,256]{2,1,0:T(8,128)(2,1)S(1)} %get-tuple-element.41), channel_id=1, source_target_pairs={{0,48},{1,241},{2,50},{3,243},{4,52},{5,245},{6,54},{7,247},{8,56}... | collective-permute-start | bytes 393224 | tf_op jit(solution)/shard_map/ppermute | solution.py:358
  37.7 3.8 %collective-permute-start.6 = (bf16[2,128,256]{2,1,0:T(8,128)(2,1)S(1)}, bf16[2,128,256]{2,1,0:T(8,128)(2,1)S(1)}, u32[]{:S(2)}, u32[]{:S(2)}) collective-permute-start(bf16[2,128,256]{2,1,0:T(8,128)(2,1)S(1)} %get-tuple-element.40), channel_id=1, source_target_pairs={{0,32},{1,225},{2,34},{3,227},{4,36},{5,229},{6,38},{7,231},{8,40}... | collective-permute-start | bytes 393224 | tf_op jit(solution)/shard_map/ppermute | solution.py:358
  41.4 0.0 collective-permute-start.5
  41.4 0.7 collective-permute-start.15
  42.1 0.5 collective-permute-done.7
  42.7 5.5 %collective-permute-start.16 = (bf16[4,2,128,256]{3,2,1,0:T(8,128)(2,1)S(1)}, bf16[4,2,128,256]{3,2,1,0:T(8,128)(2,1)}, u32[]{:S(2)}, u32[]{:S(2)}) collective-permute-start(bf16[4,2,128,256]{3,2,1,0:T(8,128)(2,1)S(1)} %pad_maximum_fusion.1.refs_4_), channel_id=1, source_target_pairs={{1,65},{3,67},{5,69},{7,71},{9,73},{11,75},{13,77},{15,79},{48,80}... | collective-permute-start | bytes 1572872 | tf_op jit(solution)/shard_map/ppermute | solution.py:358
  48.2 0.1 pad_maximum_fusion.refs_0_
  48.2 0.0 copy-start.7
  48.3 1.5 collective-permute-start.8
  49.7 1.4 collective-permute-start.9
  51.2 0.0 collective-permute-done.14.refs_5_
  51.2 0.8 copy-done.8
  52.0 3.0 %collective-permute-start.10 = (bf16[4,2,128,256]{3,2,1,0:T(8,128)(2,1)S(1)}, bf16[4,2,128,256]{3,2,1,0:T(8,128)(2,1)}, u32[]{:S(2)}, u32[]{:S(2)}) collective-permute-start(bf16[4,2,128,256]{3,2,1,0:T(8,128)(2,1)S(1)} %pad_maximum_fusion.refs_0_), channel_id=1, source_target_pairs={{1,65},{3,67},{5,69},{7,71},{9,73},{11,75},{13,77},{15,79},{48,80}... | collective-permute-start | bytes 1572872 | tf_op jit(solution)/shard_map/ppermute | solution.py:358
  55.0 11.1 %shard_map.76.refs_8_ = bf16[17,2,512,512]{3,2,1,0:T(8,128)(2,1)} custom-call(f32[2,17]{1,0:T(2,128)} %constant.43.clone.scales, f32[4,256,256]{2,1,0:T(8,128)} %constant.44.clone.base), custom_call_target="tpu_custom_call" | custom-call | tf_op jit(solution)/shard_map/pallas_call | solution.py:46
  66.1 0.0 collective-permute-done.15.refs_6_
  66.1 0.0 collective-permute-done.16.refs_7_
  66.2 0.8 copy-done.9
  67.0 2.2 %shard_map.77 = (bf16[4,2,128,256]{3,2,1,0:T(8,128)(2,1)}, bf16[4,2,128,256]{3,2,1,0:T(8,128)(2,1)}, bf16[4,2,128,256]{3,2,1,0:T(8,128)(2,1)}, bf16[4,2,128,256]...) custom-call(s32[48]{0:T(128)} %copy-done.4, ...), custom_call_target="tpu_custom_call" | custom-call | tf_op jit(solution)/shard_map/pallas_call | solution.py:171
  69.2 1.3 collective-permute-start.17
  70.5 0.7 collective-permute-start.18
  71.2 0.7 collective-permute-start.19
  73.8 1.3 collective-permute-start.24
  75.1 0.7 collective-permute-start.25
  75.8 36.8 %collective-permute-done.17 = bf16[4,2,128,256]{3,2,1,0:T(8,128)(2,1)S(1)} collective-permute-done((bf16[4,2,128,256]{3,2,1,0:T(8,128)(2,1)}, bf16[4,2,128,256]{3,2,1,0:T(8,128)(2,1)S(1)}, u32[]{:S(2)}, u32[]{:S(2)}) %collective-permute-start.17) | collective-permute-done | bytes 524320 | tf_op jit(solution)/shard_map/ppermute | solution.py:358
  112.6 0.7 collective-permute-start.26
  113.3 1.2 select_select_fusion.1
  114.6 4.2 %collective-permute-start.22 = (bf16[2,128,256]{2,1,0:T(8,128)(2,1)S(1)}, bf16[2,128,256]{2,1,0:T(8,128)(2,1)S(1)}, u32[]{:S(2)}, u32[]{:S(2)}) collective-permute-start(bf16[2,128,256]{2,1,0:T(8,128)(2,1)S(1)} %get-tuple-element.56), channel_id=1, source_target_pairs={{0,48},{1,241},{2,50},{3,243},{4,52},{5,245},{6,54},{7,247},{8,56}... | collective-permute-start | bytes 393224 | tf_op jit(solution)/shard_map/ppermute | solution.py:358
  118.8 3.1 %collective-permute-start.21 = (bf16[2,128,256]{2,1,0:T(8,128)(2,1)S(1)}, bf16[2,128,256]{2,1,0:T(8,128)(2,1)S(1)}, u32[]{:S(2)}, u32[]{:S(2)}) collective-permute-start(bf16[2,128,256]{2,1,0:T(8,128)(2,1)S(1)} %get-tuple-element.57), channel_id=1, source_target_pairs={{0,32},{1,225},{2,34},{3,227},{4,36},{5,229},{6,38},{7,231},{8,40}... | collective-permute-start | bytes 393224 | tf_op jit(solution)/shard_map/ppermute | solution.py:358
  121.9 2.1 %collective-permute-done.22 = bf16[2,128,256]{2,1,0:T(8,128)(2,1)S(1)} collective-permute-done((bf16[2,128,256]{2,1,0:T(8,128)(2,1)S(1)}, bf16[2,128,256]{2,1,0:T(8,128)(2,1)S(1)}, u32[]{:S(2)}, u32[]{:S(2)}) %collective-permute-start.22) | collective-permute-done | bytes 131104 | tf_op jit(solution)/shard_map/ppermute | solution.py:358
  124.0 3.9 %collective-permute-start.20 = (bf16[2,128,256]{2,1,0:T(8,128)(2,1)S(1)}, bf16[2,128,256]{2,1,0:T(8,128)(2,1)S(1)}, u32[]{:S(2)}, u32[]{:S(2)}) collective-permute-start(bf16[2,128,256]{2,1,0:T(8,128)(2,1)S(1)} %get-tuple-element.58), channel_id=1, source_target_pairs={{0,16},{1,17},{2,18},{3,19},{4,20},{5,21},{6,22},{7,23},{8,24},{9,... | collective-permute-start | bytes 393224 | tf_op jit(solution)/shard_map/ppermute | solution.py:358
  127.8 2.4 %collective-permute-done.20 = bf16[2,128,256]{2,1,0:T(8,128)(2,1)S(1)} collective-permute-done((bf16[2,128,256]{2,1,0:T(8,128)(2,1)S(1)}, bf16[2,128,256]{2,1,0:T(8,128)(2,1)S(1)}, u32[]{:S(2)}, u32[]{:S(2)}) %collective-permute-start.20) | collective-permute-done | bytes 131104 | tf_op jit(solution)/shard_map/ppermute | solution.py:358
  130.2 0.1 pad_maximum_fusion.2
  130.3 18.4 %collective-permute-start.23 = (bf16[4,2,128,256]{3,2,1,0:T(8,128)(2,1)S(1)}, bf16[4,2,128,256]{3,2,1,0:T(8,128)(2,1)S(1)}, u32[]{:S(2)}, u32[]{:S(2)}) collective-permute-start(bf16[4,2,128,256]{3,2,1,0:T(8,128)(2,1)S(1)} %pad_maximum_fusion.2), channel_id=1, source_target_pairs={{0,15},{1,0},{2,1},{3,2},{4,3},{5,4},{6,5},{7,6},{8,7},{9,8},{10,9... | collective-permute-start | bytes 1572872 | tf_op jit(solution)/shard_map/ppermute | solution.py:298
  148.8 0.1 select_select_fusion
  148.9 0.1 collective-permute-start.27
  149.0 0.5 collective-permute-start.28
  149.5 4.9 %collective-permute-start.29 = (bf16[2,128,256]{2,1,0:T(8,128)(2,1)S(1)}, bf16[2,128,256]{2,1,0:T(8,128)(2,1)S(1)}, u32[]{:S(2)}, u32[]{:S(2)}) collective-permute-start(bf16[2,128,256]{2,1,0:T(8,128)(2,1)S(1)} %get-tuple-element.51), channel_id=1, source_target_pairs={{0,48},{1,241},{2,50},{3,243},{4,52},{5,245},{6,54},{7,247},{8,56}... | collective-permute-start | bytes 393224 | tf_op jit(solution)/shard_map/ppermute | solution.py:358
  154.4 9.4 %collective-permute-done.27.m1 = bf16[2,128,256]{2,1,0:T(8,128)(2,1)S(1)} collective-permute-done((bf16[2,128,256]{2,1,0:T(8,128)(2,1)S(1)}, bf16[2,128,256]{2,1,0:T(8,128)(2,1)S(1)}, u32[]{:S(2)}, u32[]{:S(2)}) %collective-permute-start.27) | collective-permute-done | bytes 131104 | tf_op jit(solution)/shard_map/ppermute | solution.py:358
  163.8 3.0 %shard_map.78 = f32[2,128,2048]{2,1,0:T(8,128)} custom-call(s32[48]{0:T(128)S(1)} %copy-done.5, s32[4,2]{1,0:T(4,128)S(1)} %copy.11.places.own_places, s32[4,2]{1,0:T(4,128)S(1)} %copy-done.3, s32[4,2]{1,0:T(4,128)S(1)} %collective-permute-done.4.far_places, bf16[4,2,128,256]{3,2,1,0:T(8,128)(2,1)S(1)} %collective-permute-done.23.from_own, ...), custom_call_target="tpu_custom_call" | custom-call | tf_op jit(solution)/shard_map/pallas_call | solution.py:287
  (40 shorter events, 0.2 us)
Async XLA Ops:
  0.0 10.7 %copy-start = (f32[4,256,256]{2,1,0:T(8,128)S(1)}, f32[4,256,256]{2,1,0:T(8,128)}, u32[]{:S(2)}) copy-start(f32[4,256,256]{2,1,0:T(8,128)} %param.10) | copy-start | bytes 3145732
  0.9 1.6 copy-start.1
  4.1 26.3 %collective-permute-start.1 = (bf16[2,128,2048]{2,1,0:T(8,128)(2,1)S(1)}, bf16[2,128,2048]{2,1,0:T(8,128)(2,1)S(1)}, u32[]{:S(2)}, u32[]{:S(2)}) collective-permute-start(bf16[2,128,2048]{2,1,0:T(8,128)(2,1)S(1)} %get-tuple-element.28.tile), channel_id=1, source_target_pairs={{0,15},{1,0},{2,1},{3,2},{4,3},{5,4},{6,5},{7,6},{8,7},{9,8},{10,9... | collective-permute-start | bytes 3145736 | tf_op jit(solution)/shard_map/ppermute | solution.py:298
  7.3 23.1 %collective-permute-start.2 = (bf16[4,2,128,256]{3,2,1,0:T(8,128)(2,1)}, bf16[4,2,128,256]{3,2,1,0:T(8,128)(2,1)}, u32[]{:S(2)}, u32[]{:S(2)}) collective-permute-start(bf16[4,2,128,256]{3,2,1,0:T(8,128)(2,1)} %get-tuple-element.33), channel_id=1, source_target_pairs={{0,1},{1,2},{2,3},{3,4},{4,5},{5,6},{6,7},{7,8},{8,9},{9,10},{10,1... | collective-permute-start | bytes 1572872 | tf_op jit(solution)/shard_map/ppermute | solution.py:298
  10.7 17.0 %collective-permute-start.3 = (f32[256,256]{1,0:T(8,128)S(1)}, f32[256,256]{1,0:T(8,128)S(1)}, u32[]{:S(2)}, u32[]{:S(2)}) collective-permute-start(f32[256,256]{1,0:T(8,128)S(1)} %dynamic-slice_bitcast_fusion), channel_id=1, source_target_pairs={{0,1},{1,2},{2,3},{3,4},{4,5},{5,6},{6,7},{7,8},{8,9},{9,10},{10,1... | collective-permute-start | bytes 786440 | tf_op jit(solution)/shard_map/ppermute | solution.py:298
  10.8 5.7 %collective-permute-start = (s32[4,2]{1,0:T(4,128)S(1)}, s32[4,2]{1,0:T(4,128)S(1)}, u32[]{:S(2)}, u32[]{:S(2)}) collective-permute-start(s32[4,2]{1,0:T(4,128)S(1)} %copy.11.places.own_places), channel_id=1, source_target_pairs={{0,1},{1,2},{2,3},{3,4},{4,5},{5,6},{6,7},{7,8},{8,9},{9,10},{10,1... | collective-permute-start | bytes 104 | tf_op jit(solution)/shard_map/ppermute | solution.py:298
  11.8 13.1 %collective-permute-start.4 = (s32[4,2]{1,0:T(4,128)S(1)}, s32[4,2]{1,0:T(4,128)S(1)}, u32[]{:S(2)}, u32[]{:S(2)}) collective-permute-start(s32[4,2]{1,0:T(4,128)S(1)} %copy.11.places.own_places), channel_id=1, source_target_pairs={{0,2},{1,3},{2,4},{3,5},{4,6},{5,7},{6,8},{7,9},{8,10},{9,11},{10,... | collective-permute-start | bytes 104 | tf_op jit(solution)/shard_map/ppermute | solution.py:298
  13.6 34.6 %copy-start.4 = (s32[48]{0:T(128)}, s32[48]{0:T(128)S(1)}, u32[]{:S(2)}) copy-start(s32[48]{0:T(128)S(1)} %fusion.2.plan) | copy-start | bytes 580
  16.5 31.8 %copy-start.2 = (s32[4,2]{1,0:T(4,128)}, s32[4,2]{1,0:T(4,128)S(1)}, u32[]{:S(2)}) copy-start(s32[4,2]{1,0:T(4,128)S(1)} %collective-permute-done.places.mid_places) | copy-start | bytes 100
  17.2 13.2 %collective-permute-start.13 = (bf16[2,128,256]{2,1,0:T(8,128)(2,1)S(1)}, bf16[2,128,256]{2,1,0:T(8,128)(2,1)S(1)}, u32[]{:S(2)}, u32[]{:S(2)}) collective-permute-start(bf16[2,128,256]{2,1,0:T(8,128)(2,1)S(1)} %get-tuple-element.32), channel_id=1, source_target_pairs={{0,48},{1,241},{2,50},{3,243},{4,52},{5,245},{6,54},{7,247},{8,56}... | collective-permute-start | bytes 393224 | tf_op jit(solution)/shard_map/ppermute | solution.py:358
  24.9 5.5 %collective-permute-start.12 = (bf16[2,128,256]{2,1,0:T(8,128)(2,1)S(1)}, bf16[2,128,256]{2,1,0:T(8,128)(2,1)S(1)}, u32[]{:S(2)}, u32[]{:S(2)}) collective-permute-start(bf16[2,128,256]{2,1,0:T(8,128)(2,1)S(1)} %get-tuple-element.31), channel_id=1, source_target_pairs={{0,32},{1,225},{2,34},{3,227},{4,36},{5,229},{6,38},{7,231},{8,40}... | collective-permute-start | bytes 393224 | tf_op jit(solution)/shard_map/ppermute | solution.py:358
  27.7 38.4 %copy-start.11 = (f32[256,256]{1,0:T(8,128)}, f32[256,256]{1,0:T(8,128)S(1)}, u32[]{:S(2)}) copy-start(f32[256,256]{1,0:T(8,128)S(1)} %collective-permute-done.3.target) | copy-start | bytes 786436
  27.7 5.3 %collective-permute-start.11 = (bf16[2,128,256]{2,1,0:T(8,128)(2,1)S(1)}, bf16[2,128,256]{2,1,0:T(8,128)(2,1)S(1)}, u32[]{:S(2)}, u32[]{:S(2)}) collective-permute-start(bf16[2,128,256]{2,1,0:T(8,128)(2,1)S(1)} %get-tuple-element.30), channel_id=1, source_target_pairs={{0,16},{1,17},{2,18},{3,19},{4,20},{5,21},{6,22},{7,23},{8,24},{9,... | collective-permute-start | bytes 393224 | tf_op jit(solution)/shard_map/ppermute | solution.py:358
  33.1 33.0 %copy-start.6 = (bf16[4,2,128,256]{3,2,1,0:T(8,128)(2,1)}, bf16[4,2,128,256]{3,2,1,0:T(8,128)(2,1)S(1)}, u32[]{:S(2)}) copy-start(bf16[4,2,128,256]{3,2,1,0:T(8,128)(2,1)S(1)} %pad_maximum_fusion.1.refs_4_) | copy-start | bytes 1572868
  33.1 18.0 %collective-permute-start.14 = (bf16[4,2,128,256]{3,2,1,0:T(8,128)(2,1)S(1)}, bf16[4,2,128,256]{3,2,1,0:T(8,128)(2,1)S(1)}, u32[]{:S(2)}, u32[]{:S(2)}) collective-permute-start(bf16[4,2,128,256]{3,2,1,0:T(8,128)(2,1)S(1)} %pad_maximum_fusion.1.refs_4_), channel_id=1, source_target_pairs={{16,208},{18,210},{20,212},{22,214},{24,216},{26,218},{28,220},{30... | collective-permute-start | bytes 1572872 | tf_op jit(solution)/shard_map/ppermute | solution.py:358
  35.2 7.5 %collective-permute-start.7 = (bf16[2,128,256]{2,1,0:T(8,128)(2,1)S(1)}, bf16[2,128,256]{2,1,0:T(8,128)(2,1)S(1)}, u32[]{:S(2)}, u32[]{:S(2)}) collective-permute-start(bf16[2,128,256]{2,1,0:T(8,128)(2,1)S(1)} %get-tuple-element.41), channel_id=1, source_target_pairs={{0,48},{1,241},{2,50},{3,243},{4,52},{5,245},{6,54},{7,247},{8,56}... | collective-permute-start | bytes 393224 | tf_op jit(solution)/shard_map/ppermute | solution.py:358
  37.7 10.5 %collective-permute-start.6 = (bf16[2,128,256]{2,1,0:T(8,128)(2,1)S(1)}, bf16[2,128,256]{2,1,0:T(8,128)(2,1)S(1)}, u32[]{:S(2)}, u32[]{:S(2)}) collective-permute-start(bf16[2,128,256]{2,1,0:T(8,128)(2,1)S(1)} %get-tuple-element.40), channel_id=1, source_target_pairs={{0,32},{1,225},{2,34},{3,227},{4,36},{5,229},{6,38},{7,231},{8,40}... | collective-permute-start | bytes 393224 | tf_op jit(solution)/shard_map/ppermute | solution.py:358
  41.4 6.7 %collective-permute-start.5 = (bf16[2,128,256]{2,1,0:T(8,128)(2,1)S(1)}, bf16[2,128,256]{2,1,0:T(8,128)(2,1)S(1)}, u32[]{:S(2)}, u32[]{:S(2)}) collective-permute-start(bf16[2,128,256]{2,1,0:T(8,128)(2,1)S(1)} %get-tuple-element.39), channel_id=1, source_target_pairs={{0,16},{1,17},{2,18},{3,19},{4,20},{5,21},{6,22},{7,23},{8,24},{9,... | collective-permute-start | bytes 393224 | tf_op jit(solution)/shard_map/ppermute | solution.py:358
  41.4 24.7 %collective-permute-start.15 = (bf16[4,2,128,256]{3,2,1,0:T(8,128)(2,1)S(1)}, bf16[4,2,128,256]{3,2,1,0:T(8,128)(2,1)S(1)}, u32[]{:S(2)}, u32[]{:S(2)}) collective-permute-start(bf16[4,2,128,256]{3,2,1,0:T(8,128)(2,1)S(1)} %pad_maximum_fusion.1.refs_4_), channel_id=1, source_target_pairs={{32,128},{33,193},{34,130},{35,195},{36,132},{37,197},{38,134},{39... | collective-permute-start | bytes 1572872 | tf_op jit(solution)/shard_map/ppermute | solution.py:358
  42.7 23.5 %collective-permute-start.16 = (bf16[4,2,128,256]{3,2,1,0:T(8,128)(2,1)S(1)}, bf16[4,2,128,256]{3,2,1,0:T(8,128)(2,1)}, u32[]{:S(2)}, u32[]{:S(2)}) collective-permute-start(bf16[4,2,128,256]{3,2,1,0:T(8,128)(2,1)S(1)} %pad_maximum_fusion.1.refs_4_), channel_id=1, source_target_pairs={{1,65},{3,67},{5,69},{7,71},{9,73},{11,75},{13,77},{15,79},{48,80}... | collective-permute-start | bytes 1572872 | tf_op jit(solution)/shard_map/ppermute | solution.py:358
  48.2 17.9 %copy-start.7 = (bf16[4,2,128,256]{3,2,1,0:T(8,128)(2,1)}, bf16[4,2,128,256]{3,2,1,0:T(8,128)(2,1)S(1)}, u32[]{:S(2)}) copy-start(bf16[4,2,128,256]{3,2,1,0:T(8,128)(2,1)S(1)} %pad_maximum_fusion.refs_0_) | copy-start | bytes 1572868
  48.3 17.9 %collective-permute-start.8 = (bf16[4,2,128,256]{3,2,1,0:T(8,128)(2,1)S(1)}, bf16[4,2,128,256]{3,2,1,0:T(8,128)(2,1)}, u32[]{:S(2)}, u32[]{:S(2)}) collective-permute-start(bf16[4,2,128,256]{3,2,1,0:T(8,128)(2,1)S(1)} %pad_maximum_fusion.refs_0_), channel_id=1, source_target_pairs={{16,208},{18,210},{20,212},{22,214},{24,216},{26,218},{28,220},{30... | collective-permute-start | bytes 1572872 | tf_op jit(solution)/shard_map/ppermute | solution.py:358
  49.7 16.4 %collective-permute-start.9 = (bf16[4,2,128,256]{3,2,1,0:T(8,128)(2,1)S(1)}, bf16[4,2,128,256]{3,2,1,0:T(8,128)(2,1)}, u32[]{:S(2)}, u32[]{:S(2)}) collective-permute-start(bf16[4,2,128,256]{3,2,1,0:T(8,128)(2,1)S(1)} %pad_maximum_fusion.refs_0_), channel_id=1, source_target_pairs={{32,128},{33,193},{34,130},{35,195},{36,132},{37,197},{38,134},{39... | collective-permute-start | bytes 1572872 | tf_op jit(solution)/shard_map/ppermute | solution.py:358
  51.2 0.8 copy-start.8
  52.0 14.1 %collective-permute-start.10 = (bf16[4,2,128,256]{3,2,1,0:T(8,128)(2,1)S(1)}, bf16[4,2,128,256]{3,2,1,0:T(8,128)(2,1)}, u32[]{:S(2)}, u32[]{:S(2)}) collective-permute-start(bf16[4,2,128,256]{3,2,1,0:T(8,128)(2,1)S(1)} %pad_maximum_fusion.refs_0_), channel_id=1, source_target_pairs={{1,65},{3,67},{5,69},{7,71},{9,73},{11,75},{13,77},{15,79},{48,80}... | collective-permute-start | bytes 1572872 | tf_op jit(solution)/shard_map/ppermute | solution.py:358
  66.1 0.8 copy-start.9
  69.2 43.4 %collective-permute-start.17 = (bf16[4,2,128,256]{3,2,1,0:T(8,128)(2,1)}, bf16[4,2,128,256]{3,2,1,0:T(8,128)(2,1)S(1)}, u32[]{:S(2)}, u32[]{:S(2)}) collective-permute-start(bf16[4,2,128,256]{3,2,1,0:T(8,128)(2,1)} %get-tuple-element.43), channel_id=1, source_target_pairs={{0,224},{2,226},{4,228},{6,230},{8,232},{10,234},{12,236},{14,238}... | collective-permute-start | bytes 1572872 | tf_op jit(solution)/shard_map/ppermute | solution.py:358
  70.5 42.8 %collective-permute-start.18 = (bf16[4,2,128,256]{3,2,1,0:T(8,128)(2,1)}, bf16[4,2,128,256]{3,2,1,0:T(8,128)(2,1)S(1)}, u32[]{:S(2)}, u32[]{:S(2)}) collective-permute-start(bf16[4,2,128,256]{3,2,1,0:T(8,128)(2,1)} %get-tuple-element.44), channel_id=1, source_target_pairs={{0,160},{2,162},{4,164},{6,166},{8,168},{10,170},{12,172},{14,174}... | collective-permute-start | bytes 1572872 | tf_op jit(solution)/shard_map/ppermute | solution.py:358
  71.2 42.1 %collective-permute-start.19 = (bf16[4,2,128,256]{3,2,1,0:T(8,128)(2,1)}, bf16[4,2,128,256]{3,2,1,0:T(8,128)(2,1)S(1)}, u32[]{:S(2)}, u32[]{:S(2)}) collective-permute-start(bf16[4,2,128,256]{3,2,1,0:T(8,128)(2,1)} %get-tuple-element.45), channel_id=1, source_target_pairs={{0,64},{2,66},{4,68},{6,70},{8,72},{10,74},{12,76},{14,78},{17,49}... | collective-permute-start | bytes 1572872 | tf_op jit(solution)/shard_map/ppermute | solution.py:358
  73.8 75.0 %collective-permute-start.24 = (bf16[4,2,128,256]{3,2,1,0:T(8,128)(2,1)}, bf16[4,2,128,256]{3,2,1,0:T(8,128)(2,1)S(1)}, u32[]{:S(2)}, u32[]{:S(2)}) collective-permute-start(bf16[4,2,128,256]{3,2,1,0:T(8,128)(2,1)} %get-tuple-element.47), channel_id=1, source_target_pairs={{0,224},{2,226},{4,228},{6,230},{8,232},{10,234},{12,236},{14,238}... | collective-permute-start | bytes 1572872 | tf_op jit(solution)/shard_map/ppermute | solution.py:358
  75.1 73.7 %collective-permute-start.25 = (bf16[4,2,128,256]{3,2,1,0:T(8,128)(2,1)}, bf16[4,2,128,256]{3,2,1,0:T(8,128)(2,1)S(1)}, u32[]{:S(2)}, u32[]{:S(2)}) collective-permute-start(bf16[4,2,128,256]{3,2,1,0:T(8,128)(2,1)} %get-tuple-element.48), channel_id=1, source_target_pairs={{0,160},{2,162},{4,164},{6,166},{8,168},{10,170},{12,172},{14,174}... | collective-permute-start | bytes 1572872 | tf_op jit(solution)/shard_map/ppermute | solution.py:358
  112.6 36.1 %collective-permute-start.26 = (bf16[4,2,128,256]{3,2,1,0:T(8,128)(2,1)}, bf16[4,2,128,256]{3,2,1,0:T(8,128)(2,1)S(1)}, u32[]{:S(2)}, u32[]{:S(2)}) collective-permute-start(bf16[4,2,128,256]{3,2,1,0:T(8,128)(2,1)} %get-tuple-element.49), channel_id=1, source_target_pairs={{0,64},{2,66},{4,68},{6,70},{8,72},{10,74},{12,76},{14,78},{17,49}... | collective-permute-start | bytes 1572872 | tf_op jit(solution)/shard_map/ppermute | solution.py:358
  113.3 35.4 %copy-start.10 = (bf16[4,2,128,256]{3,2,1,0:T(8,128)(2,1)S(1)}, bf16[4,2,128,256]{3,2,1,0:T(8,128)(2,1)}, u32[]{:S(2)}) copy-start(bf16[4,2,128,256]{3,2,1,0:T(8,128)(2,1)} %get-tuple-element.50) | copy-start | bytes 1572868
  114.6 9.4 %collective-permute-start.22 = (bf16[2,128,256]{2,1,0:T(8,128)(2,1)S(1)}, bf16[2,128,256]{2,1,0:T(8,128)(2,1)S(1)}, u32[]{:S(2)}, u32[]{:S(2)}) collective-permute-start(bf16[2,128,256]{2,1,0:T(8,128)(2,1)S(1)} %get-tuple-element.56), channel_id=1, source_target_pairs={{0,48},{1,241},{2,50},{3,243},{4,52},{5,245},{6,54},{7,247},{8,56}... | collective-permute-start | bytes 393224 | tf_op jit(solution)/shard_map/ppermute | solution.py:358
  118.8 9.0 %collective-permute-start.21 = (bf16[2,128,256]{2,1,0:T(8,128)(2,1)S(1)}, bf16[2,128,256]{2,1,0:T(8,128)(2,1)S(1)}, u32[]{:S(2)}, u32[]{:S(2)}) collective-permute-start(bf16[2,128,256]{2,1,0:T(8,128)(2,1)S(1)} %get-tuple-element.57), channel_id=1, source_target_pairs={{0,32},{1,225},{2,34},{3,227},{4,36},{5,229},{6,38},{7,231},{8,40}... | collective-permute-start | bytes 393224 | tf_op jit(solution)/shard_map/ppermute | solution.py:358
  124.0 6.2 %collective-permute-start.20 = (bf16[2,128,256]{2,1,0:T(8,128)(2,1)S(1)}, bf16[2,128,256]{2,1,0:T(8,128)(2,1)S(1)}, u32[]{:S(2)}, u32[]{:S(2)}) collective-permute-start(bf16[2,128,256]{2,1,0:T(8,128)(2,1)S(1)} %get-tuple-element.58), channel_id=1, source_target_pairs={{0,16},{1,17},{2,18},{3,19},{4,20},{5,21},{6,22},{7,23},{8,24},{9,... | collective-permute-start | bytes 393224 | tf_op jit(solution)/shard_map/ppermute | solution.py:358
  130.3 33.5 %copy-start.3 = (s32[4,2]{1,0:T(4,128)S(1)}, s32[4,2]{1,0:T(4,128)}, u32[]{:S(2)}) copy-start(s32[4,2]{1,0:T(4,128)} %copy-done.2) | copy-start | bytes 100
  130.3 33.5 %copy-start.5 = (s32[48]{0:T(128)S(1)}, s32[48]{0:T(128)}, u32[]{:S(2)}) copy-start(s32[48]{0:T(128)} %copy-done.4) | copy-start | bytes 580
  130.3 33.5 %collective-permute-start.23 = (bf16[4,2,128,256]{3,2,1,0:T(8,128)(2,1)S(1)}, bf16[4,2,128,256]{3,2,1,0:T(8,128)(2,1)S(1)}, u32[]{:S(2)}, u32[]{:S(2)}) collective-permute-start(bf16[4,2,128,256]{3,2,1,0:T(8,128)(2,1)S(1)} %pad_maximum_fusion.2), channel_id=1, source_target_pairs={{0,15},{1,0},{2,1},{3,2},{4,3},{5,4},{6,5},{7,6},{8,7},{9,8},{10,9... | collective-permute-start | bytes 1572872 | tf_op jit(solution)/shard_map/ppermute | solution.py:298
  148.7 15.0 %collective-permute-start.30 = (bf16[4,2,128,256]{3,2,1,0:T(8,128)(2,1)S(1)}, bf16[4,2,128,256]{3,2,1,0:T(8,128)(2,1)S(1)}, u32[]{:S(2)}, u32[]{:S(2)}) collective-permute-start(bf16[4,2,128,256]{3,2,1,0:T(8,128)(2,1)S(1)} %pad_maximum_fusion.2), channel_id=1, source_target_pairs={{0,1},{1,2},{2,3},{3,4},{4,5},{5,6},{6,7},{7,8},{8,9},{9,10},{10,1... | collective-permute-start | bytes 1572872 | tf_op jit(solution)/shard_map/ppermute | solution.py:298
  148.9 14.8 %collective-permute-start.27 = (bf16[2,128,256]{2,1,0:T(8,128)(2,1)S(1)}, bf16[2,128,256]{2,1,0:T(8,128)(2,1)S(1)}, u32[]{:S(2)}, u32[]{:S(2)}) collective-permute-start(bf16[2,128,256]{2,1,0:T(8,128)(2,1)S(1)} %get-tuple-element.53), channel_id=1, source_target_pairs={{0,16},{1,17},{2,18},{3,19},{4,20},{5,21},{6,22},{7,23},{8,24},{9,... | collective-permute-start | bytes 393224 | tf_op jit(solution)/shard_map/ppermute | solution.py:358
  149.0 14.7 %collective-permute-start.28 = (bf16[2,128,256]{2,1,0:T(8,128)(2,1)S(1)}, bf16[2,128,256]{2,1,0:T(8,128)(2,1)S(1)}, u32[]{:S(2)}, u32[]{:S(2)}) collective-permute-start(bf16[2,128,256]{2,1,0:T(8,128)(2,1)S(1)} %get-tuple-element.52), channel_id=1, source_target_pairs={{0,32},{1,225},{2,34},{3,227},{4,36},{5,229},{6,38},{7,231},{8,40}... | collective-permute-start | bytes 393224 | tf_op jit(solution)/shard_map/ppermute | solution.py:358
  149.5 14.3 %collective-permute-start.29 = (bf16[2,128,256]{2,1,0:T(8,128)(2,1)S(1)}, bf16[2,128,256]{2,1,0:T(8,128)(2,1)S(1)}, u32[]{:S(2)}, u32[]{:S(2)}) collective-permute-start(bf16[2,128,256]{2,1,0:T(8,128)(2,1)S(1)} %get-tuple-element.51), channel_id=1, source_target_pairs={{0,48},{1,241},{2,50},{3,243},{4,52},{5,245},{6,54},{7,247},{8,56}... | collective-permute-start | bytes 393224 | tf_op jit(solution)/shard_map/ppermute | solution.py:358

commit v4 on v3

--- a/solution.py
+++ b/solution.py
@@ -52,9 +52,9 @@
     )(jnp.asarray(scales), jnp.asarray(base_tables(n)))
 
 
-def chain_kernel(plan, places, probe, target, *refs, n, slices, rows):
-    near_in, far_in, tabs_hbm, near_out, far_out = refs[0:4], refs[4:8], refs[8], refs[9:13], refs[13:17]
-    (patch, tabs, inc, lhs0, lhs1, mid0, mid1, outv, psem, tsem, osem) = refs[17:]
+def chain_kernel(plan, places, probe, behind, *refs, n, slices, rows):
+    near_in, far_in, tabs_hbm, outs = refs[0:4], refs[4:8], refs[8], refs[9:13]
+    (patch, tabs, inc, lhs0, lhs1, mid0, mid1, outv, target, psem, tsem, osem, gsem) = refs[13:]
     lhs, mid = (lhs0, lhs1), (mid0, mid1)
     half = n // 2
 
@@ -92,6 +92,8 @@
 
     @pl.when(plan[HANDLER] == 1)
     def _():
+        target_copy = pltpu.make_async_copy(behind.at[pl.ds(behind.shape[0] - 2, 2)], target, gsem)
+        target_copy.start()
         for s in range(slices):
             table_copy(s).start()
             for r in range(4):
@@ -127,7 +129,9 @@
         for m in range(2):
             put(m, *f[m])
         f = transform(tabs[slices, 0], tabs[slices, 1])
-        resid = (f[0][0] * f[0][0] + f[0][1] * f[0][1]) + (f[1][0] * f[1][0] + f[1][1] * f[1][1]) - target[...]
+        target_copy.wait()
+        wanted = [target[0, h].astype(F32) + target[1, h].astype(F32) for h in range(2)]
+        resid = (f[0][0] * f[0][0] + f[0][1] * f[0][1]) + (f[1][0] * f[1][0] + f[1][1] * f[1][1]) - jnp.concatenate(wanted, axis=0)
         for m in range(2):
             put(m, resid * f[m][0], resid * f[m][1])
         f = transform(tabs[slices, 1], tabs[slices, 0])
@@ -154,25 +158,23 @@
             for r in range(4):
                 @pl.when(plan[REL + s] == r)
                 def _():
-                    for h, group in enumerate((near_out, far_out)):
-                        pltpu.make_async_copy(outv.at[s, :, pl.ds(h * half, half)], group[r].at[plan[ENTRY + s]], osem.at[h, s]).start()
+                    pltpu.make_async_copy(outv.at[s], outs[r].at[plan[ENTRY + s]], osem.at[s]).start()
             return carry
 
         lax.fori_loop(0, slices, backward, 0)
         for s in range(slices):
-            for h in range(2):
-                pltpu.make_async_copy(outv.at[s, :, pl.ds(h * half, half)], near_out[0].at[0], osem.at[h, s]).wait()
-
-
-def chain(plan, places, probe, target, near, far, tables, rows):
-    n = target.shape[-1]
+            pltpu.make_async_copy(outv.at[s], outs[0].at[0], osem.at[s]).wait()
+
+
+def chain(plan, places, probe, behind, near, far, tables, rows):
+    n = probe.shape[-1]
     slices = tables.shape[0] - 1
-    piece = jax.ShapeDtypeStruct(near[0].shape, BF)
+    piece = jax.ShapeDtypeStruct((slices // 4, 2, n, n), BF)
     return pl.pallas_call(
         functools.partial(chain_kernel, n=n, slices=slices, rows=rows),
-        out_shape=(piece,) * 8,
-        in_specs=[SMEM, SMEM, VMEM, VMEM] + [ANY] * 9,
-        out_specs=(ANY,) * 8,
+        out_shape=(piece,) * 4,
+        in_specs=[SMEM, SMEM, VMEM] + [ANY] * 10,
+        out_specs=(ANY,) * 4,
         scratch_shapes=[
             pltpu.VMEM((slices, 2, n, n), BF),
             pltpu.VMEM((slices + 1, 2, 2 * n, 2 * n), BF),
@@ -182,12 +184,14 @@
             pltpu.VMEM((n, 2 * n), BF),
             pltpu.VMEM((n, 2 * n), BF),
             pltpu.VMEM((slices, 2, n, n), BF),
+            pltpu.VMEM((2, 2, n // 2, n), BF),
             pltpu.SemaphoreType.DMA((2, slices)),
             pltpu.SemaphoreType.DMA((slices + 1,)),
-            pltpu.SemaphoreType.DMA((2, slices)),
+            pltpu.SemaphoreType.DMA((slices,)),
+            pltpu.SemaphoreType.DMA,
         ],
         compiler_params=pltpu.CompilerParams(vmem_limit_bytes=58 << 20),
-    )(plan, places, probe, target, *near, *far, tables)
+    )(plan, places, probe, behind, *near, *far, tables)
 
 
 def window(ref, lead, offset, n):
@@ -200,22 +204,32 @@
     return jnp.where(lane >= offset % n, first, second)
 
 
-def own_windows_kernel(places, tile, tile_bf, wins, *, n):
+def own_windows_kernel(plan, places, tile, measured, tile_bf, wins, target, sem, *, n):
+    copy = pltpu.make_async_copy(measured.at[plan[OTHER]], target, sem)
+    copy.start()
+    rows = tile.shape[1]
     tile_bf[...] = tile[...].astype(BF)
-    for p in range(wins.shape[0]):
+    for p in range(places.shape[0]):
         for c in range(2):
             wins[p, c] = window(tile, c, places[p, 1], n).astype(BF)
-
-
-def own_windows(places, tile, n):
+    copy.wait()
+    for c in range(2):
+        x = target[c * rows:(c + 1) * rows]
+        high = x.astype(BF)
+        wins[places.shape[0], c] = high
+        wins[places.shape[0] + 1, c] = (x - high.astype(F32)).astype(BF)
+
+
+def own_windows(plan, places, tile, measured, n):
     count = places.shape[0]
     return pl.pallas_call(
         functools.partial(own_windows_kernel, n=n),
-        out_shape=(jax.ShapeDtypeStruct(tile.shape, BF), jax.ShapeDtypeStruct((count, 2, tile.shape[1], n), BF)),
-        in_specs=[SMEM, VMEM],
+        out_shape=(jax.ShapeDtypeStruct(tile.shape, BF), jax.ShapeDtypeStruct((count + 2, 2, tile.shape[1], n), BF)),
+        in_specs=[SMEM, SMEM, VMEM, ANY],
         out_specs=(VMEM, VMEM),
+        scratch_shapes=[pltpu.VMEM((n, n), F32), pltpu.SemaphoreType.DMA],
         compiler_params=pltpu.CompilerParams(vmem_limit_bytes=40 << 20),
-    )(places, tile)
+    )(plan, places, tile, measured)
 
 
 def far_kernel(plan, places, tile, *outs, n):
@@ -387,15 +401,15 @@
     tile = object_slices[0]
 
     mid_places = shifted(positions, 1)
-    tile_bf, mine = own_windows(positions, tile, n)
+    far_places = shifted(positions, 2)
+    tile_bf, mine = own_windows(plan, positions, tile, measured, n)
+    tile_bf, mine, mid_places, far_places = lax.optimization_barrier((tile_bf, mine, mid_places, far_places))
     ahead = shifted(tile_bf, -1)
     behind = shifted(mine, 1)
-    target = shifted(lax.dynamic_index_in_dim(measured, plan[OTHER], 0, False), 1)
-    far_places = shifted(positions, 2)
 
     far = far_parts(plan, mid_places, tile_bf, n)
     far_got = [within(far[k], k) for k in (1, 2, 3)]
-    far, ahead, behind, target, far_places = lax.optimization_barrier((far, ahead, behind, target, far_places))
+    far, ahead, behind = lax.optimization_barrier((far, ahead, behind))
     near = near_parts(plan, mid_places, behind, ahead, n)
     near_got = [within(near[k], k) for k in (1, 2, 3)]
     far_message = jnp.stack([far[0]] + far_got)
@@ -403,18 +417,13 @@
     near_message = jnp.stack([near[0]] + near_got)
     near_in = [near_message] + [towards(near_message, k) for k in (1, 2, 3)]
     tables = make_tables(n, depth_size)
-    terms = chain(plan, mid_places, probe, target, near_in, far_in, tables, rows)
-
-    def home(pieces):
-        block = pieces[0]
-        for k in (1, 2, 3):
-            block = jnp.where(plan[SOURCE] == k, away(pieces[k], k), block)
-        return block
-
-    near_block = home(terms[:4])
-    far_block = home(terms[4:])
-    mixed = jnp.stack([near_block[0]] + [within(near_block[k], k) for k in (1, 2, 3)])
-    mids = [far_block[0]] + [within(far_block[k], k) for k in (1, 2, 3)]
+    terms = chain(plan, mid_places, probe, behind, near_in, far_in, tables, rows)
+
+    block = terms[0]
+    for k in (1, 2, 3):
+        block = jnp.where(plan[SOURCE] == k, away(terms[k], k), block)
+    mixed = jnp.stack([block[0, :, :rows]] + [within(block[k, :, :rows], k) for k in (1, 2, 3)])
+    mids = [block[0, :, rows:]] + [within(block[k, :, rows:], k) for k in (1, 2, 3)]
     from_own = shifted(mixed, -1)
     from_far = shifted(mixed, 1)
     total = gather_terms(plan, positions, mid_places, far_places, from_own, mids, from_far, rows, width)

time: 167 us -> 169 us (1.012)
  waiting for transfers between devices: 56.8 us -> 71.3 us
  starting transfers between devices: 78 us -> 67.8 us
  between operations: 4.29 us -> 2.16 us
    ppermute x24 -> x21, waiting for transfers between devices: 53.9 us -> 67.9 us  [permute(): return lax.ppermute(block, ('depth', 'lat'), pairs)]
    ppermute x24 -> x21, starting transfers between devices: 54.1 us -> 47.3 us  [permute(): return lax.ppermute(block, ('depth', 'lat'), pairs)]
    ppermute x7 -> x6, starting transfers between devices: 23.9 us -> 20.4 us  [shifted(): lax.ppermute(block, 'lat', [(i, (i + distance) % size) for i in range(siz...]
  transfers between devices with their start and end apart: 31 -> 27, of which waited for: 7 -> 11; matrix products, arithmetic and copies ran while one was open for 2% -> 1% of each run, Pallas kernels for 8% -> 8%
where the time goes in v4:
time: 169 us; the launch traced here: 168 us
  waiting for transfers between devices  71.3 us (42%)
  starting transfers between devices  67.8 us (40%)
  Pallas kernels  18.5 us (11%)
  local copies, waits for them, and re-layouts  6.69 us (4%)
  between operations  2.16 us (1%)
    ppermute x21, waiting for transfers between devices, permute(): return lax.ppermute(block, ('depth', 'lat'), pairs)  67.9 us
    ppermute x21, starting transfers between devices, permute(): return lax.ppermute(block, ('depth', 'lat'), pairs)  47.3 us
    ppermute x6, starting transfers between devices, shifted(): lax.ppermute(block, 'lat', [(i, (i + distance) % size) for i in range(siz...  20.4 us
    pallas_call x1, Pallas kernels, make_tables(): pl.pallas_call(functools.partial(tables_kernel, n=n, slices=slices), grid...  11.1 us
    unnamed x25, local copies, waits for them, and re-layouts  4.62 us
  transfers between devices with their start and end apart: 27, of which 11 were waited for; matrix products, arithmetic and copies ran while one was open for 1% of the time, Pallas kernels for 8%

profile of v4, /device:TPU:1, one launch (start us, length us, event | category | flops | bytes accessed | tf_op | source)
XLA Modules:
  0.0 168.1 jit_solution(17879850463484461510)
XLA Ops:
  0.0 0.8 copy.11.places.own_places
  0.8 2.6 %collective-permute-start = (s32[4,2]{1,0:T(4,128)S(1)}, s32[4,2]{1,0:T(4,128)S(1)}, u32[]{:S(2)}, u32[]{:S(2)}) collective-permute-start(s32[4,2]{1,0:T(4,128)S(1)} %copy.11.places.own_places), channel_id=1, source_target_pairs={{0,1},{1,2},{2,3},{3,4},{4,5},{5,6},{6,7},{7,8},{8,9},{9,10},{10,1... | collective-permute-start | bytes 104 | tf_op jit(solution)/shard_map/ppermute | solution.py:312
  3.4 1.2 collective-permute-start.1
  4.6 0.7 fusion.plan
  5.3 1.6 copy-done.1
  6.9 1.2 copy-done.2
  8.1 0.9 shard_map.73
  9.0 0.0 collective-permute-done.places.mid_places
  9.0 0.7 collective-permute-start.2
  9.7 1.1 collective-permute-start.3
  10.8 0.7 shard_map.74
  11.6 8.3 %collective-permute-start.12 = (bf16[2,128,256]{2,1,0:T(8,128)(2,1)S(1)}, bf16[2,128,256]{2,1,0:T(8,128)(2,1)S(1)}, u32[]{:S(2)}, u32[]{:S(2)}) collective-permute-start(bf16[2,128,256]{2,1,0:T(8,128)(2,1)S(1)} %get-tuple-element.34), channel_id=1, source_target_pairs={{0,48},{1,241},{2,50},{3,243},{4,52},{5,245},{6,54},{7,247},{8,56}... | collective-permute-start | bytes 393224 | tf_op jit(solution)/shard_map/ppermute | solution.py:372
  19.8 0.0 collective-permute-start.11
  19.8 0.4 collective-permute-start.10
  20.2 3.4 %collective-permute-done.2.ahead = bf16[2,128,2048]{2,1,0:T(8,128)(2,1)S(1)} collective-permute-done((bf16[2,128,2048]{2,1,0:T(8,128)(2,1)S(1)}, bf16[2,128,2048]{2,1,0:T(8,128)(2,1)S(1)}, u32[]{:S(2)}, u32[]{:S(2)}) %collective-permute-start.2) | collective-permute-done | bytes 1048608 | tf_op jit(solution)/shard_map/ppermute | solution.py:312
  23.6 0.6 collective-permute-done.12
  24.2 0.9 collective-permute-done.11
  25.2 7.5 %collective-permute-done.10 = bf16[2,128,256]{2,1,0:T(8,128)(2,1)S(1)} collective-permute-done((bf16[2,128,256]{2,1,0:T(8,128)(2,1)S(1)}, bf16[2,128,256]{2,1,0:T(8,128)(2,1)S(1)}, u32[]{:S(2)}, u32[]{:S(2)}) %collective-permute-start.10) | collective-permute-done | bytes 131104 | tf_op jit(solution)/shard_map/ppermute | solution.py:372
  32.7 0.1 pad_maximum_fusion.1.refs_4_
  32.8 0.7 collective-permute-start.13
  33.5 0.8 shard_map.75
  34.3 6.0 %collective-permute-start.6 = (bf16[2,128,256]{2,1,0:T(8,128)(2,1)S(1)}, bf16[2,128,256]{2,1,0:T(8,128)(2,1)S(1)}, u32[]{:S(2)}, u32[]{:S(2)}) collective-permute-start(bf16[2,128,256]{2,1,0:T(8,128)(2,1)S(1)} %get-tuple-element.41), channel_id=1, source_target_pairs={{0,48},{1,241},{2,50},{3,243},{4,52},{5,245},{6,54},{7,247},{8,56}... | collective-permute-start | bytes 393224 | tf_op jit(solution)/shard_map/ppermute | solution.py:372
  40.3 0.0 collective-permute-start.5
  40.3 2.4 %collective-permute-start.4 = (bf16[2,128,256]{2,1,0:T(8,128)(2,1)S(1)}, bf16[2,128,256]{2,1,0:T(8,128)(2,1)S(1)}, u32[]{:S(2)}, u32[]{:S(2)}) collective-permute-start(bf16[2,128,256]{2,1,0:T(8,128)(2,1)S(1)} %get-tuple-element.39), channel_id=1, source_target_pairs={{0,16},{1,17},{2,18},{3,19},{4,20},{5,21},{6,22},{7,23},{8,24},{9,... | collective-permute-start | bytes 393224 | tf_op jit(solution)/shard_map/ppermute | solution.py:372
  42.7 0.7 collective-permute-start.14
  43.4 0.0 collective-permute-done.6
  43.4 1.3 collective-permute-start.15
  44.7 0.7 collective-permute-done.5
  45.5 0.2 collective-permute-done.4
  45.6 0.1 pad_maximum_fusion.refs_0_
  45.7 1.5 collective-permute-start.7
  47.2 1.5 collective-permute-start.8
  48.7 2.1 %collective-permute-start.9 = (bf16[4,2,128,256]{3,2,1,0:T(8,128)(2,1)S(1)}, bf16[4,2,128,256]{3,2,1,0:T(8,128)(2,1)}, u32[]{:S(2)}, u32[]{:S(2)}) collective-permute-start(bf16[4,2,128,256]{3,2,1,0:T(8,128)(2,1)S(1)} %pad_maximum_fusion.refs_0_), channel_id=1, source_target_pairs={{1,65},{3,67},{5,69},{7,71},{9,73},{11,75},{13,77},{15,79},{48,80}... | collective-permute-start | bytes 1572872 | tf_op jit(solution)/shard_map/ppermute | solution.py:372
  50.7 11.1 %shard_map.76.refs_8_ = bf16[17,2,512,512]{3,2,1,0:T(8,128)(2,1)} custom-call(f32[2,17]{1,0:T(2,128)} %constant.38.clone.scales, f32[4,256,256]{2,1,0:T(8,128)} %constant.39.clone.base), custom_call_target="tpu_custom_call" | custom-call | tf_op jit(solution)/shard_map/pallas_call | solution.py:46
  61.9 0.0 collective-permute-done.15.refs_7_
  61.9 0.0 collective-permute-done.7.refs_1_
  61.9 0.0 collective-permute-done.9.refs_3_
  61.9 0.8 copy-done.10
  62.7 0.2 copy-done.11
  62.9 2.0 %shard_map.77 = (bf16[4,2,256,256]{3,2,1,0:T(8,128)(2,1)}, bf16[4,2,256,256]{3,2,1,0:T(8,128)(2,1)}, bf16[4,2,256,256]{3,2,1,0:T(8,128)(2,1)}, bf16[4,2,256,256]{3,2,1,0:T(8,128)(2,1)}) custom-call(s32[48]{0:T(128)} %copy-done.5, s32[4,2]{1,0:T(4,128)} %copy-done.3, f32[2,2,256,256]{3,2,1,0:T(8,128)} %probe.1, bf16[6,2,128,256]{3,2,1,0:T(8,128)(2,1)} %copy-done, ...), custom_call_target="tpu_custom_call" | custom-call | tf_op jit(solution)/shard_map/pallas_call | solution.py:173
  65.0 1.3 collective-permute-start.16
  66.3 0.7 collective-permute-start.17
  67.0 0.7 collective-permute-start.18
  67.7 0.7 constant_dynamic-slice_fusion
  68.4 0.6 slice.30
  70.9 45.2 %collective-permute-done.16 = bf16[4,2,256,256]{3,2,1,0:T(8,128)(2,1)S(1)} collective-permute-done((bf16[4,2,256,256]{3,2,1,0:T(8,128)(2,1)}, bf16[4,2,256,256]{3,2,1,0:T(8,128)(2,1)S(1)}, u32[]{:S(2)}, u32[]{:S(2)}) %collective-permute-start.16) | collective-permute-done | bytes 1048608 | tf_op jit(solution)/shard_map/ppermute | solution.py:372
  116.1 1.5 select_select_fusion
  117.6 0.1 slice_bitcast_fusion
  117.6 5.7 %collective-permute-start.21 = (bf16[2,128,256]{2,1,0:T(8,128)(2,1)S(1)}, bf16[2,128,256]{2,1,0:T(8,128)(2,1)S(1)}, u32[]{:S(2)}, u32[]{:S(2)}) collective-permute-start(bf16[2,128,256]{2,1,0:T(8,128)(2,1)S(1)} %get-tuple-element.51), channel_id=1, source_target_pairs={{0,48},{1,241},{2,50},{3,243},{4,52},{5,245},{6,54},{7,247},{8,56}... | collective-permute-start | bytes 393224 | tf_op jit(solution)/shard_map/ppermute | solution.py:372
  123.3 7.4 %collective-permute-start.20 = (bf16[2,128,256]{2,1,0:T(8,128)(2,1)S(1)}, bf16[2,128,256]{2,1,0:T(8,128)(2,1)S(1)}, u32[]{:S(2)}, u32[]{:S(2)}) collective-permute-start(bf16[2,128,256]{2,1,0:T(8,128)(2,1)S(1)} %get-tuple-element.52), channel_id=1, source_target_pairs={{0,32},{1,225},{2,34},{3,227},{4,36},{5,229},{6,38},{7,231},{8,40}... | collective-permute-start | bytes 393224 | tf_op jit(solution)/shard_map/ppermute | solution.py:372
  130.7 1.4 collective-permute-start.19
  132.1 1.8 %collective-permute-done.21 = bf16[2,128,256]{2,1,0:T(8,128)(2,1)S(1)} collective-permute-done((bf16[2,128,256]{2,1,0:T(8,128)(2,1)S(1)}, bf16[2,128,256]{2,1,0:T(8,128)(2,1)S(1)}, u32[]{:S(2)}, u32[]{:S(2)}) %collective-permute-start.21) | collective-permute-done | bytes 131104 | tf_op jit(solution)/shard_map/ppermute | solution.py:372
  133.9 0.6 collective-permute-done.20
  134.5 1.6 collective-permute-done.19
  136.0 0.1 pad_maximum_fusion.2
  136.1 14.8 %collective-permute-start.22 = (bf16[4,2,128,256]{3,2,1,0:T(8,128)(2,1)S(1)}, bf16[4,2,128,256]{3,2,1,0:T(8,128)(2,1)S(1)}, u32[]{:S(2)}, u32[]{:S(2)}) collective-permute-start(bf16[4,2,128,256]{3,2,1,0:T(8,128)(2,1)S(1)} %pad_maximum_fusion.2), channel_id=1, source_target_pairs={{0,15},{1,0},{2,1},{3,2},{4,3},{5,4},{6,5},{7,6},{8,7},{9,8},{10,9... | collective-permute-start | bytes 1572872 | tf_op jit(solution)/shard_map/ppermute | solution.py:312
  150.9 0.0 collective-permute-start.26
  150.9 2.6 %collective-permute-start.23 = (bf16[2,128,256]{2,1,0:T(8,128)(2,1)S(1)}, bf16[2,128,256]{2,1,0:T(8,128)(2,1)S(1)}, u32[]{:S(2)}, u32[]{:S(2)}) collective-permute-start(bf16[2,128,256]{2,1,0:T(8,128)(2,1)S(1)} %get-tuple-element.49), channel_id=1, source_target_pairs={{0,16},{1,17},{2,18},{3,19},{4,20},{5,21},{6,22},{7,23},{8,24},{9,... | collective-permute-start | bytes 393224 | tf_op jit(solution)/shard_map/ppermute | solution.py:372
  153.5 0.0 collective-permute-start.24
  153.5 2.8 %collective-permute-start.25 = (bf16[2,128,256]{2,1,0:T(8,128)(2,1)S(1)}, bf16[2,128,256]{2,1,0:T(8,128)(2,1)S(1)}, u32[]{:S(2)}, u32[]{:S(2)}) collective-permute-start(bf16[2,128,256]{2,1,0:T(8,128)(2,1)S(1)} %get-tuple-element.47), channel_id=1, source_target_pairs={{0,48},{1,241},{2,50},{3,243},{4,52},{5,245},{6,54},{7,247},{8,56}... | collective-permute-start | bytes 393224 | tf_op jit(solution)/shard_map/ppermute | solution.py:372
  156.3 8.8 %collective-permute-done.23.m1 = bf16[2,128,256]{2,1,0:T(8,128)(2,1)S(1)} collective-permute-done((bf16[2,128,256]{2,1,0:T(8,128)(2,1)S(1)}, bf16[2,128,256]{2,1,0:T(8,128)(2,1)S(1)}, u32[]{:S(2)}, u32[]{:S(2)}) %collective-permute-start.23) | collective-permute-done | bytes 131104 | tf_op jit(solution)/shard_map/ppermute | solution.py:372
  165.1 0.0 collective-permute-done.24.m2
  165.1 0.0 collective-permute-done.25.m3
  165.1 3.0 %shard_map.78 = f32[2,128,2048]{2,1,0:T(8,128)} custom-call(s32[48]{0:T(128)S(1)} %copy-done.6, s32[4,2]{1,0:T(4,128)S(1)} %copy.11.places.own_places, s32[4,2]{1,0:T(4,128)S(1)} %copy-done.4, s32[4,2]{1,0:T(4,128)S(1)} %collective-permute-done.1.far_places, bf16[4,2,128,256]{3,2,1,0:T(8,128)(2,1)S(1)} %collective-permute-done.22.from_own, ...), custom_call_target="tpu_custom_call" | custom-call | tf_op jit(solution)/shard_map/pallas_call | solution.py:301
  (29 shorter events, 0.1 us)
Async XLA Ops:
  0.8 8.2 %collective-permute-start = (s32[4,2]{1,0:T(4,128)S(1)}, s32[4,2]{1,0:T(4,128)S(1)}, u32[]{:S(2)}, u32[]{:S(2)}) collective-permute-start(s32[4,2]{1,0:T(4,128)S(1)} %copy.11.places.own_places), channel_id=1, source_target_pairs={{0,1},{1,2},{2,3},{3,4},{4,5},{5,6},{6,7},{7,8},{8,9},{9,10},{10,1... | collective-permute-start | bytes 104 | tf_op jit(solution)/shard_map/ppermute | solution.py:312
  3.4 5.6 %collective-permute-start.1 = (s32[4,2]{1,0:T(4,128)S(1)}, s32[4,2]{1,0:T(4,128)S(1)}, u32[]{:S(2)}, u32[]{:S(2)}) collective-permute-start(s32[4,2]{1,0:T(4,128)S(1)} %copy.11.places.own_places), channel_id=1, source_target_pairs={{0,2},{1,3},{2,4},{3,5},{4,6},{5,7},{6,8},{7,9},{8,10},{9,11},{10,... | collective-permute-start | bytes 104 | tf_op jit(solution)/shard_map/ppermute | solution.py:312
  5.3 28.2 %copy-start.5 = (s32[48]{0:T(128)}, s32[48]{0:T(128)S(1)}, u32[]{:S(2)}) copy-start(s32[48]{0:T(128)S(1)} %fusion.plan) | copy-start | bytes 580
  5.3 1.6 copy-start.1
  6.9 1.2 copy-start.2
  9.0 36.7 %copy-start.3 = (s32[4,2]{1,0:T(4,128)}, s32[4,2]{1,0:T(4,128)S(1)}, u32[]{:S(2)}) copy-start(s32[4,2]{1,0:T(4,128)S(1)} %collective-permute-done.places.mid_places) | copy-start | bytes 100
  9.0 14.6 %collective-permute-start.2 = (bf16[2,128,2048]{2,1,0:T(8,128)(2,1)S(1)}, bf16[2,128,2048]{2,1,0:T(8,128)(2,1)S(1)}, u32[]{:S(2)}, u32[]{:S(2)}) collective-permute-start(bf16[2,128,2048]{2,1,0:T(8,128)(2,1)S(1)} %get-tuple-element.30.tile), channel_id=1, source_target_pairs={{0,15},{1,0},{2,1},{3,2},{4,3},{5,4},{6,5},{7,6},{8,7},{9,8},{10,9... | collective-permute-start | bytes 3145736 | tf_op jit(solution)/shard_map/ppermute | solution.py:312
  9.7 10.5 %collective-permute-start.3 = (bf16[6,2,128,256]{3,2,1,0:T(8,128)(2,1)S(1)}, bf16[6,2,128,256]{3,2,1,0:T(8,128)(2,1)S(1)}, u32[]{:S(2)}, u32[]{:S(2)}) collective-permute-start(bf16[6,2,128,256]{3,2,1,0:T(8,128)(2,1)S(1)} %get-tuple-element.35), channel_id=1, source_target_pairs={{0,1},{1,2},{2,3},{3,4},{4,5},{5,6},{6,7},{7,8},{8,9},{9,10},{10,1... | collective-permute-start | bytes 2359304 | tf_op jit(solution)/shard_map/ppermute | solution.py:312
  11.6 12.7 %collective-permute-start.12 = (bf16[2,128,256]{2,1,0:T(8,128)(2,1)S(1)}, bf16[2,128,256]{2,1,0:T(8,128)(2,1)S(1)}, u32[]{:S(2)}, u32[]{:S(2)}) collective-permute-start(bf16[2,128,256]{2,1,0:T(8,128)(2,1)S(1)} %get-tuple-element.34), channel_id=1, source_target_pairs={{0,48},{1,241},{2,50},{3,243},{4,52},{5,245},{6,54},{7,247},{8,56}... | collective-permute-start | bytes 393224 | tf_op jit(solution)/shard_map/ppermute | solution.py:372
  19.8 5.3 %collective-permute-start.11 = (bf16[2,128,256]{2,1,0:T(8,128)(2,1)S(1)}, bf16[2,128,256]{2,1,0:T(8,128)(2,1)S(1)}, u32[]{:S(2)}, u32[]{:S(2)}) collective-permute-start(bf16[2,128,256]{2,1,0:T(8,128)(2,1)S(1)} %get-tuple-element.33), channel_id=1, source_target_pairs={{0,32},{1,225},{2,34},{3,227},{4,36},{5,229},{6,38},{7,231},{8,40}... | collective-permute-start | bytes 393224 | tf_op jit(solution)/shard_map/ppermute | solution.py:372
  19.8 12.9 %collective-permute-start.10 = (bf16[2,128,256]{2,1,0:T(8,128)(2,1)S(1)}, bf16[2,128,256]{2,1,0:T(8,128)(2,1)S(1)}, u32[]{:S(2)}, u32[]{:S(2)}) collective-permute-start(bf16[2,128,256]{2,1,0:T(8,128)(2,1)S(1)} %get-tuple-element.32), channel_id=1, source_target_pairs={{0,16},{1,17},{2,18},{3,19},{4,20},{5,21},{6,22},{7,23},{8,24},{9,... | collective-permute-start | bytes 393224 | tf_op jit(solution)/shard_map/ppermute | solution.py:372
  20.2 41.6 %copy-start = (bf16[6,2,128,256]{3,2,1,0:T(8,128)(2,1)}, bf16[6,2,128,256]{3,2,1,0:T(8,128)(2,1)S(1)}, u32[]{:S(2)}) copy-start(bf16[6,2,128,256]{3,2,1,0:T(8,128)(2,1)S(1)} %collective-permute-done.3.behind) | copy-start | bytes 2359300
  32.8 29.1 %copy-start.7 = (bf16[4,2,128,256]{3,2,1,0:T(8,128)(2,1)}, bf16[4,2,128,256]{3,2,1,0:T(8,128)(2,1)S(1)}, u32[]{:S(2)}) copy-start(bf16[4,2,128,256]{3,2,1,0:T(8,128)(2,1)S(1)} %pad_maximum_fusion.1.refs_4_) | copy-start | bytes 1572868
  32.8 15.9 %collective-permute-start.13 = (bf16[4,2,128,256]{3,2,1,0:T(8,128)(2,1)S(1)}, bf16[4,2,128,256]{3,2,1,0:T(8,128)(2,1)S(1)}, u32[]{:S(2)}, u32[]{:S(2)}) collective-permute-start(bf16[4,2,128,256]{3,2,1,0:T(8,128)(2,1)S(1)} %pad_maximum_fusion.1.refs_4_), channel_id=1, source_target_pairs={{16,208},{18,210},{20,212},{22,214},{24,216},{26,218},{28,220},{30... | collective-permute-start | bytes 1572872 | tf_op jit(solution)/shard_map/ppermute | solution.py:372
  34.3 9.1 %collective-permute-start.6 = (bf16[2,128,256]{2,1,0:T(8,128)(2,1)S(1)}, bf16[2,128,256]{2,1,0:T(8,128)(2,1)S(1)}, u32[]{:S(2)}, u32[]{:S(2)}) collective-permute-start(bf16[2,128,256]{2,1,0:T(8,128)(2,1)S(1)} %get-tuple-element.41), channel_id=1, source_target_pairs={{0,48},{1,241},{2,50},{3,243},{4,52},{5,245},{6,54},{7,247},{8,56}... | collective-permute-start | bytes 393224 | tf_op jit(solution)/shard_map/ppermute | solution.py:372
  40.3 5.2 %collective-permute-start.5 = (bf16[2,128,256]{2,1,0:T(8,128)(2,1)S(1)}, bf16[2,128,256]{2,1,0:T(8,128)(2,1)S(1)}, u32[]{:S(2)}, u32[]{:S(2)}) collective-permute-start(bf16[2,128,256]{2,1,0:T(8,128)(2,1)S(1)} %get-tuple-element.40), channel_id=1, source_target_pairs={{0,32},{1,225},{2,34},{3,227},{4,36},{5,229},{6,38},{7,231},{8,40}... | collective-permute-start | bytes 393224 | tf_op jit(solution)/shard_map/ppermute | solution.py:372
  40.3 5.3 %collective-permute-start.4 = (bf16[2,128,256]{2,1,0:T(8,128)(2,1)S(1)}, bf16[2,128,256]{2,1,0:T(8,128)(2,1)S(1)}, u32[]{:S(2)}, u32[]{:S(2)}) collective-permute-start(bf16[2,128,256]{2,1,0:T(8,128)(2,1)S(1)} %get-tuple-element.39), channel_id=1, source_target_pairs={{0,16},{1,17},{2,18},{3,19},{4,20},{5,21},{6,22},{7,23},{8,24},{9,... | collective-permute-start | bytes 393224 | tf_op jit(solution)/shard_map/ppermute | solution.py:372
  42.7 19.1 %collective-permute-start.14 = (bf16[4,2,128,256]{3,2,1,0:T(8,128)(2,1)S(1)}, bf16[4,2,128,256]{3,2,1,0:T(8,128)(2,1)S(1)}, u32[]{:S(2)}, u32[]{:S(2)}) collective-permute-start(bf16[4,2,128,256]{3,2,1,0:T(8,128)(2,1)S(1)} %pad_maximum_fusion.1.refs_4_), channel_id=1, source_target_pairs={{32,128},{33,193},{34,130},{35,195},{36,132},{37,197},{38,134},{39... | collective-permute-start | bytes 1572872 | tf_op jit(solution)/shard_map/ppermute | solution.py:372
  43.4 18.5 %collective-permute-start.15 = (bf16[4,2,128,256]{3,2,1,0:T(8,128)(2,1)S(1)}, bf16[4,2,128,256]{3,2,1,0:T(8,128)(2,1)S(1)}, u32[]{:S(2)}, u32[]{:S(2)}) collective-permute-start(bf16[4,2,128,256]{3,2,1,0:T(8,128)(2,1)S(1)} %pad_maximum_fusion.1.refs_4_), channel_id=1, source_target_pairs={{1,65},{3,67},{5,69},{7,71},{9,73},{11,75},{13,77},{15,79},{48,80}... | collective-permute-start | bytes 1572872 | tf_op jit(solution)/shard_map/ppermute | solution.py:372
  45.7 16.1 %copy-start.8 = (bf16[4,2,128,256]{3,2,1,0:T(8,128)(2,1)}, bf16[4,2,128,256]{3,2,1,0:T(8,128)(2,1)S(1)}, u32[]{:S(2)}) copy-start(bf16[4,2,128,256]{3,2,1,0:T(8,128)(2,1)S(1)} %pad_maximum_fusion.refs_0_) | copy-start | bytes 1572868
  45.7 16.2 %collective-permute-start.7 = (bf16[4,2,128,256]{3,2,1,0:T(8,128)(2,1)S(1)}, bf16[4,2,128,256]{3,2,1,0:T(8,128)(2,1)}, u32[]{:S(2)}, u32[]{:S(2)}) collective-permute-start(bf16[4,2,128,256]{3,2,1,0:T(8,128)(2,1)S(1)} %pad_maximum_fusion.refs_0_), channel_id=1, source_target_pairs={{16,208},{18,210},{20,212},{22,214},{24,216},{26,218},{28,220},{30... | collective-permute-start | bytes 1572872 | tf_op jit(solution)/shard_map/ppermute | solution.py:372
  47.2 14.7 %collective-permute-start.8 = (bf16[4,2,128,256]{3,2,1,0:T(8,128)(2,1)S(1)}, bf16[4,2,128,256]{3,2,1,0:T(8,128)(2,1)}, u32[]{:S(2)}, u32[]{:S(2)}) collective-permute-start(bf16[4,2,128,256]{3,2,1,0:T(8,128)(2,1)S(1)} %pad_maximum_fusion.refs_0_), channel_id=1, source_target_pairs={{32,128},{33,193},{34,130},{35,195},{36,132},{37,197},{38,134},{39... | collective-permute-start | bytes 1572872 | tf_op jit(solution)/shard_map/ppermute | solution.py:372
  48.7 13.2 %copy-start.9 = (bf16[4,2,128,256]{3,2,1,0:T(8,128)(2,1)}, bf16[4,2,128,256]{3,2,1,0:T(8,128)(2,1)S(1)}, u32[]{:S(2)}) copy-start(bf16[4,2,128,256]{3,2,1,0:T(8,128)(2,1)S(1)} %collective-permute-done.13.refs_5_) | copy-start | bytes 1572868
  48.7 13.3 %collective-permute-start.9 = (bf16[4,2,128,256]{3,2,1,0:T(8,128)(2,1)S(1)}, bf16[4,2,128,256]{3,2,1,0:T(8,128)(2,1)}, u32[]{:S(2)}, u32[]{:S(2)}) collective-permute-start(bf16[4,2,128,256]{3,2,1,0:T(8,128)(2,1)S(1)} %pad_maximum_fusion.refs_0_), channel_id=1, source_target_pairs={{1,65},{3,67},{5,69},{7,71},{9,73},{11,75},{13,77},{15,79},{48,80}... | collective-permute-start | bytes 1572872 | tf_op jit(solution)/shard_map/ppermute | solution.py:372
  61.9 0.9 copy-start.10
  61.9 1.0 copy-start.11
  65.0 51.1 %collective-permute-start.16 = (bf16[4,2,256,256]{3,2,1,0:T(8,128)(2,1)}, bf16[4,2,256,256]{3,2,1,0:T(8,128)(2,1)S(1)}, u32[]{:S(2)}, u32[]{:S(2)}) collective-permute-start(bf16[4,2,256,256]{3,2,1,0:T(8,128)(2,1)} %get-tuple-element.43), channel_id=1, source_target_pairs={{0,224},{2,226},{4,228},{6,230},{8,232},{10,234},{12,236},{14,238}... | collective-permute-start | bytes 3145736 | tf_op jit(solution)/shard_map/ppermute | solution.py:372
  66.3 49.8 %collective-permute-start.17 = (bf16[4,2,256,256]{3,2,1,0:T(8,128)(2,1)}, bf16[4,2,256,256]{3,2,1,0:T(8,128)(2,1)S(1)}, u32[]{:S(2)}, u32[]{:S(2)}) collective-permute-start(bf16[4,2,256,256]{3,2,1,0:T(8,128)(2,1)} %get-tuple-element.44), channel_id=1, source_target_pairs={{0,160},{2,162},{4,164},{6,166},{8,168},{10,170},{12,172},{14,174}... | collective-permute-start | bytes 3145736 | tf_op jit(solution)/shard_map/ppermute | solution.py:372
  67.0 49.1 %collective-permute-start.18 = (bf16[4,2,256,256]{3,2,1,0:T(8,128)(2,1)}, bf16[4,2,256,256]{3,2,1,0:T(8,128)(2,1)S(1)}, u32[]{:S(2)}, u32[]{:S(2)}) collective-permute-start(bf16[4,2,256,256]{3,2,1,0:T(8,128)(2,1)} %get-tuple-element.45), channel_id=1, source_target_pairs={{0,64},{2,66},{4,68},{6,70},{8,72},{10,74},{12,76},{14,78},{17,49}... | collective-permute-start | bytes 3145736 | tf_op jit(solution)/shard_map/ppermute | solution.py:372
  117.5 47.6 %copy-start.4 = (s32[4,2]{1,0:T(4,128)S(1)}, s32[4,2]{1,0:T(4,128)}, u32[]{:S(2)}) copy-start(s32[4,2]{1,0:T(4,128)} %copy-done.3) | copy-start | bytes 100
  117.5 47.6 %copy-start.6 = (s32[48]{0:T(128)S(1)}, s32[48]{0:T(128)}, u32[]{:S(2)}) copy-start(s32[48]{0:T(128)} %copy-done.5) | copy-start | bytes 580
  117.6 16.3 %collective-permute-start.21 = (bf16[2,128,256]{2,1,0:T(8,128)(2,1)S(1)}, bf16[2,128,256]{2,1,0:T(8,128)(2,1)S(1)}, u32[]{:S(2)}, u32[]{:S(2)}) collective-permute-start(bf16[2,128,256]{2,1,0:T(8,128)(2,1)S(1)} %get-tuple-element.51), channel_id=1, source_target_pairs={{0,48},{1,241},{2,50},{3,243},{4,52},{5,245},{6,54},{7,247},{8,56}... | collective-permute-start | bytes 393224 | tf_op jit(solution)/shard_map/ppermute | solution.py:372
  123.3 11.2 %collective-permute-start.20 = (bf16[2,128,256]{2,1,0:T(8,128)(2,1)S(1)}, bf16[2,128,256]{2,1,0:T(8,128)(2,1)S(1)}, u32[]{:S(2)}, u32[]{:S(2)}) collective-permute-start(bf16[2,128,256]{2,1,0:T(8,128)(2,1)S(1)} %get-tuple-element.52), channel_id=1, source_target_pairs={{0,32},{1,225},{2,34},{3,227},{4,36},{5,229},{6,38},{7,231},{8,40}... | collective-permute-start | bytes 393224 | tf_op jit(solution)/shard_map/ppermute | solution.py:372
  130.7 5.3 %collective-permute-start.19 = (bf16[2,128,256]{2,1,0:T(8,128)(2,1)S(1)}, bf16[2,128,256]{2,1,0:T(8,128)(2,1)S(1)}, u32[]{:S(2)}, u32[]{:S(2)}) collective-permute-start(bf16[2,128,256]{2,1,0:T(8,128)(2,1)S(1)} %get-tuple-element.53), channel_id=1, source_target_pairs={{0,16},{1,17},{2,18},{3,19},{4,20},{5,21},{6,22},{7,23},{8,24},{9,... | collective-permute-start | bytes 393224 | tf_op jit(solution)/shard_map/ppermute | solution.py:372
  136.1 29.0 %collective-permute-start.22 = (bf16[4,2,128,256]{3,2,1,0:T(8,128)(2,1)S(1)}, bf16[4,2,128,256]{3,2,1,0:T(8,128)(2,1)S(1)}, u32[]{:S(2)}, u32[]{:S(2)}) collective-permute-start(bf16[4,2,128,256]{3,2,1,0:T(8,128)(2,1)S(1)} %pad_maximum_fusion.2), channel_id=1, source_target_pairs={{0,15},{1,0},{2,1},{3,2},{4,3},{5,4},{6,5},{7,6},{8,7},{9,8},{10,9... | collective-permute-start | bytes 1572872 | tf_op jit(solution)/shard_map/ppermute | solution.py:312
  150.9 14.2 %collective-permute-start.26 = (bf16[4,2,128,256]{3,2,1,0:T(8,128)(2,1)S(1)}, bf16[4,2,128,256]{3,2,1,0:T(8,128)(2,1)S(1)}, u32[]{:S(2)}, u32[]{:S(2)}) collective-permute-start(bf16[4,2,128,256]{3,2,1,0:T(8,128)(2,1)S(1)} %pad_maximum_fusion.2), channel_id=1, source_target_pairs={{0,1},{1,2},{2,3},{3,4},{4,5},{5,6},{6,7},{7,8},{8,9},{9,10},{10,1... | collective-permute-start | bytes 1572872 | tf_op jit(solution)/shard_map/ppermute | solution.py:312
  150.9 14.2 %collective-permute-start.23 = (bf16[2,128,256]{2,1,0:T(8,128)(2,1)S(1)}, bf16[2,128,256]{2,1,0:T(8,128)(2,1)S(1)}, u32[]{:S(2)}, u32[]{:S(2)}) collective-permute-start(bf16[2,128,256]{2,1,0:T(8,128)(2,1)S(1)} %get-tuple-element.49), channel_id=1, source_target_pairs={{0,16},{1,17},{2,18},{3,19},{4,20},{5,21},{6,22},{7,23},{8,24},{9,... | collective-permute-start | bytes 393224 | tf_op jit(solution)/shard_map/ppermute | solution.py:372
  153.5 11.6 %collective-permute-start.24 = (bf16[2,128,256]{2,1,0:T(8,128)(2,1)S(1)}, bf16[2,128,256]{2,1,0:T(8,128)(2,1)S(1)}, u32[]{:S(2)}, u32[]{:S(2)}) collective-permute-start(bf16[2,128,256]{2,1,0:T(8,128)(2,1)S(1)} %get-tuple-element.48), channel_id=1, source_target_pairs={{0,32},{1,225},{2,34},{3,227},{4,36},{5,229},{6,38},{7,231},{8,40}... | collective-permute-start | bytes 393224 | tf_op jit(solution)/shard_map/ppermute | solution.py:372
  153.5 11.6 %collective-permute-start.25 = (bf16[2,128,256]{2,1,0:T(8,128)(2,1)S(1)}, bf16[2,128,256]{2,1,0:T(8,128)(2,1)S(1)}, u32[]{:S(2)}, u32[]{:S(2)}) collective-permute-start(bf16[2,128,256]{2,1,0:T(8,128)(2,1)S(1)} %get-tuple-element.47), channel_id=1, source_target_pairs={{0,48},{1,241},{2,50},{3,243},{4,52},{5,245},{6,54},{7,247},{8,56}... | collective-permute-start | bytes 393224 | tf_op jit(solution)/shard_map/ppermute | solution.py:372

commit v5 on v4

v5 whole, which is shorter than its diff:
```python
import functools

import jax
import jax.numpy as jnp
import numpy as np
from jax import lax
from jax.experimental import pallas as pl
from jax.experimental.pallas import tpu as pltpu
from jax.sharding import PartitionSpec as P

BF = jnp.bfloat16
F32 = jnp.float32
ANY = pl.BlockSpec(memory_space=pl.ANY)
SMEM = pl.BlockSpec(memory_space=pltpu.MemorySpace.SMEM)
FIRST = 64
SECOND = 32
LAG = 2
VMEM = pl.BlockSpec(memory_space=pltpu.MemorySpace.VMEM)


@functools.lru_cache
def base_tables(n):
    k = np.arange(n)
    d = np.exp(-2j * np.pi * ((k[:, None] * k[None, :]) % n) / n) / np.sqrt(n)
    q = np.where(k < n // 2, k, k - n).astype(np.float64)
    h = np.exp(-1j * np.pi * 0.5 * q * q / n)
    prop = (np.conj(d) * h[None, :]) @ d
    return np.stack([prop.real, prop.imag, d.real, d.imag]).astype(np.float32)


def tables_kernel(scales, base, out, *, n, slices):
    s = pl.program_id(0)
    which = jnp.where(s < slices, 0, 2)
    re = base[which]
    im = base[which + 1]
    for side, sign in ((0, 1.0), (1, -1.0)):
        scale = scales[side, s]
        a = (re * scale).astype(BF)
        b = im * (scale * sign)
        out[0, side, 0:n, 0:n] = a
        out[0, side, n:2 * n, n:2 * n] = a
        out[0, side, 0:n, n:2 * n] = (-b).astype(BF)
        out[0, side, n:2 * n, 0:n] = b.astype(BF)


def make_tables(n, slices):
    a = 2.0 ** ((np.arange(slices) + 0.5) / slices)
    scales = np.concatenate([np.stack([a, 1.0 / a]), np.ones((2, 1))], axis=1).astype(np.float32)
    return pl.pallas_call(
        functools.partial(tables_kernel, n=n, slices=slices),
        grid=(slices + 1,),
        out_shape=jax.ShapeDtypeStruct((slices + 1, 2, 2 * n, 2 * n), BF),
        in_specs=[SMEM, pl.BlockSpec((4, n, n), lambda s: (0, 0, 0))],
        out_specs=pl.BlockSpec((1, 2, 2 * n, 2 * n), lambda s: (s, 0, 0, 0)),
    )(jnp.asarray(scales), jnp.asarray(base_tables(n)))


def chain_kernel(*refs, n, slices, rows):
    accs = [pltpu.ACC(c)((size, n), F32)
            for size in (FIRST, SECOND) for _ in range(2) for c in range(2) for _ in range(n // size)]
    pl.run_scoped(lambda *scoped: chain_body(*refs, *scoped, n=n, slices=slices, rows=rows), *accs)


def chain_body(plan, places, probe, behind, *refs, n, slices, rows):
    ins, tabs_hbm, outs = refs[0:8], refs[8], refs[9:17]
    (patch, tabs, inc, lhs0, lhs1, mid0, mid1, outv, target, term, psem, tsem, osem, gsem) = refs[17:31]
    accs = list(refs[31:])
    first_acc = [[[accs.pop(0) for _ in range(n // FIRST)] for _ in range(2)] for _ in range(2)]
    second_acc = [[[accs.pop(0) for _ in range(n // SECOND)] for _ in range(2)] for _ in range(2)]
    lhs, mid = (lhs0, lhs1), (mid0, mid1)
    half = n // 2

    def table_copy(s):
        return pltpu.make_async_copy(tabs_hbm.at[s], tabs.at[s], tsem.at[s])

    def patch_wait(s):
        pltpu.make_async_copy(ins[0].at[0], patch.at[s], psem.at[s]).wait()

    def span(i, size):
        return pl.ds(i * size, size)

    def issue(m, accs, size, weights, rows_of, tasks=()):
        for c in range(2):
            for k in range(2):
                pltpu.matmul_push_rhs(weights(c, k), k, c)
        pieces = 2 * (n // size)
        todo = list(tasks)
        for j in range(pieces):
            k, i = divmod(j, n // size)
            for c in range(2):
                pltpu.matmul_acc_lhs(accs[m][c][i], rows_of(c, k, i), load_staged_rhs=k if i == 0 else None)
            left = max(1, pieces - 1 - max(j, LAG))
            take = 0 if j < LAG else -(-len(todo) // left)
            for task in todo[:take]:
                task()
            del todo[:take]
        for task in todo:
            task()

    def first(m, s, side, tasks=()):
        issue(m, first_acc, FIRST, lambda c, k: lhs[m][k * n:(k + 1) * n],
              lambda c, k, i: tabs[s, side, pl.ds(c * n + i * FIRST, FIRST), k * n:(k + 1) * n], tasks)

    def turn(m):
        def one(i, c):
            mid[m][span(i, FIRST), c * n:(c + 1) * n] = pltpu.matmul_pop(first_acc[m][c][i]).astype(BF)
        return [functools.partial(one, i, c) for i in range(n // FIRST) for c in range(2)]

    def second(m, s, side, tasks=()):
        issue(m, second_acc, SECOND, lambda c, k: tabs[s, side, k * n:(k + 1) * n, c * n:(c + 1) * n],
              lambda c, k, i: mid[m][span(i, SECOND), k * n:(k + 1) * n], tasks)

    def pop(m, i):
        return pltpu.matmul_pop(second_acc[m][0][i]), pltpu.matmul_pop(second_acc[m][1][i])

    def put(m, i, re, im):
        lhs[m][pl.ds(i * SECOND, SECOND)] = re.astype(BF)
        lhs[m][pl.ds(n + i * SECOND, SECOND)] = im.astype(BF)

    def enter(s, m, i, wr, wi):
        inc[s, m, 0, span(i, SECOND)] = wr.astype(BF)
        inc[s, m, 1, span(i, SECOND)] = wi.astype(BF)
        pr = patch[s, 0, span(i, SECOND)].astype(F32)
        pi = patch[s, 1, span(i, SECOND)].astype(F32)
        put(m, i, pr * wr - pi * wi, pr * wi + pi * wr)

    def leave(s, m, i, gr, gi):
        pr = patch[s, 0, span(i, SECOND)].astype(F32)
        pi = patch[s, 1, span(i, SECOND)].astype(F32)
        put(m, i, pr * gr + pi * gi, pr * gi - pi * gr)
        wr = inc[s, m, 0, span(i, SECOND)].astype(F32)
        wi = inc[s, m, 1, span(i, SECOND)].astype(F32)
        tr = wr * gr + wi * gi
        ti = wr * gi - wi * gr
        if m == 0:
            term[0, span(i, SECOND)] = tr
            term[1, span(i, SECOND)] = ti
        else:
            outv[s, 0, span(i, SECOND)] = (term[0, span(i, SECOND)] + tr).astype(BF)
            outv[s, 1, span(i, SECOND)] = (term[1, span(i, SECOND)] + ti).astype(BF)

    count = n // SECOND

    def uses(m, use):
        return [functools.partial(lambda i: use(m, i, *pop(m, i)), i) for i in range(count)]

    def run(tasks):
        for task in tasks:
            task()

    def step(s, side, use, after=None):
        second(0, s, side, turn(1))
        second(1, s, side, uses(0, use))
        if after is None:
            run(uses(1, use))
        else:
            first(0, *after, uses(1, use))
            first(1, *after, turn(0))

    @pl.when(plan[HANDLER] == 1)
    def _():
        target_copy = pltpu.make_async_copy(behind.at[pl.ds(behind.shape[0] - 2, 2)], target, gsem)
        target_copy.start()
        for s in range(slices):
            table_copy(s).start()
            for r in range(8):
                @pl.when(plan[REL + s] == r)
                def _():
                    pltpu.make_async_copy(ins[r].at[plan[ENTRY + s]], patch.at[s], psem.at[s]).start()
        table_copy(slices).start()
        row_shift = lax.rem(places[plan[POSITION], 0], rows)
        col_shift = lax.rem(places[plan[POSITION], 1], n)
        for m in range(2):
            for c in range(2):
                x = pltpu.roll(probe[m, c], row_shift, 0)
                term[c] = pltpu.roll(x, col_shift, 1).astype(BF).astype(F32)
            if m == 0:
                patch_wait(0)
                table_copy(0).wait()
            for i in range(count):
                enter(0, m, i, term[0, span(i, SECOND)], term[1, span(i, SECOND)])
            first(m, 0, 0)
        run(turn(0))

        def forward(s, carry):
            table_copy(s + 1).wait()
            patch_wait(s + 1)
            step(s, 1, lambda m, i, re, im: enter(s + 1, m, i, re, im), (s + 1, 0))
            return carry

        lax.fori_loop(0, slices - 1, forward, 0)
        table_copy(slices).wait()
        step(slices - 1, 1, put, (slices, 0))
        target_copy.wait()
        second(0, slices, 1, turn(1))
        second(1, slices, 1)
        for i in range(count):
            ar, ai = pop(0, i)
            br, bi = pop(1, i)
            h, at = divmod(i * SECOND, half)
            wanted = target[0, h, pl.ds(at, SECOND)].astype(F32) + target[1, h, pl.ds(at, SECOND)].astype(F32)
            resid = (ar * ar + ai * ai) + (br * br + bi * bi) - wanted
            put(0, i, resid * ar, resid * ai)
            put(1, i, resid * br, resid * bi)
        first(0, slices, 1)
        first(1, slices, 1, turn(0))
        step(slices, 0, put, (slices - 1, 1))

        def send(s):
            for r in range(8):
                @pl.when(plan[REL + s] == r)
                def _():
                    pltpu.make_async_copy(outv.at[s], outs[r].at[plan[ENTRY + s]], osem.at[s]).start()

        def backward(back, carry):
            s = slices - 1 - back
            step(s, 0, lambda m, i, re, im: leave(s, m, i, re, im), (s - 1, 1))
            send(s)
            return carry

        lax.fori_loop(0, slices - 1, backward, 0)
        step(0, 0, lambda m, i, re, im: leave(0, m, i, re, im))
        send(0)
        for s in range(slices):
            pltpu.make_async_copy(outv.at[s], outs[0].at[0], osem.at[s]).wait()


def chain(plan, places, probe, behind, messages, tables, rows):
    n = probe.shape[-1]
    slices = tables.shape[0] - 1
    piece = jax.ShapeDtypeStruct(messages[0].shape, BF)
    return pl.pallas_call(
        functools.partial(chain_kernel, n=n, slices=slices, rows=rows),
        out_shape=(piece,) * 8,
        in_specs=[SMEM, SMEM, VMEM] + [ANY] * 10,
        out_specs=(ANY,) * 8,
        scratch_shapes=[
            pltpu.VMEM((slices, 2, n, n), BF),
            pltpu.VMEM((slices + 1, 2, 2 * n, 2 * n), BF),
            pltpu.VMEM((slices, 2, 2, n, n), BF),
            pltpu.VMEM((2 * n, n), BF),
            pltpu.VMEM((2 * n, n), BF),
            pltpu.VMEM((n, 2 * n), BF),
            pltpu.VMEM((n, 2 * n), BF),
            pltpu.VMEM((slices, 2, n, n), BF),
            pltpu.VMEM((2, 2, n // 2, n), BF),
            pltpu.VMEM((2, n, n), F32),
            pltpu.SemaphoreType.DMA((slices,)),
            pltpu.SemaphoreType.DMA((slices + 1,)),
            pltpu.SemaphoreType.DMA((slices,)),
            pltpu.SemaphoreType.DMA,
        ],
        compiler_params=pltpu.CompilerParams(vmem_limit_bytes=58 << 20),
    )(plan, places, probe, behind, *messages, tables)


def window(ref, lead, offset, n):
    width = ref.shape[-1]
    start = pl.multiple_of((offset // n) * n, n)
    after = pl.multiple_of(jnp.minimum(start + n, width - n), n)
    lane = lax.broadcasted_iota(jnp.int32, (ref.shape[-2], n), 1)
    first = ref[lead, :, pl.ds(start, n)].astype(F32)
    second = ref[lead, :, pl.ds(after, n)].astype(F32)
    return jnp.where(lane >= offset % n, first, second)


def own_windows_kernel(plan, places, tile, measured, tile_bf, wins, target, sem, *, n):
    copy = pltpu.make_async_copy(measured.at[plan[OTHER]], target, sem)
    copy.start()
    rows = tile.shape[1]
    tile_bf[...] = tile[...].astype(BF)
    for p in range(places.shape[0]):
        for c in range(2):
            wins[p, c] = window(tile, c, places[p, 1], n).astype(BF)
    copy.wait()
    for c in range(2):
        x = target[c * rows:(c + 1) * rows]
        high = x.astype(BF)
        wins[places.shape[0], c] = high
        wins[places.shape[0] + 1, c] = (x - high.astype(F32)).astype(BF)


def own_windows(plan, places, tile, measured, n):
    count = places.shape[0]
    return pl.pallas_call(
        functools.partial(own_windows_kernel, n=n),
        out_shape=(jax.ShapeDtypeStruct(tile.shape, BF), jax.ShapeDtypeStruct((count + 2, 2, tile.shape[1], n), BF)),
        in_specs=[SMEM, SMEM, VMEM, ANY],
        out_specs=(VMEM, VMEM),
        scratch_shapes=[pltpu.VMEM((n, n), F32), pltpu.SemaphoreType.DMA],
        compiler_params=pltpu.CompilerParams(vmem_limit_bytes=40 << 20),
    )(plan, places, tile, measured)


def merge_kernel(plan, places, behind, tile, ahead, even, odd, given, *, n):
    rows = tile.shape[1]
    row = lax.broadcasted_iota(jnp.int32, (rows, n), 0)
    for k, out in enumerate((even.at[0], odd.at[0], given.at[0], given.at[1])):
        p = plan[ORDER + k]
        for c in range(2):
            after = window(ahead, c, places[p, 1], n)
            before = behind[p, c].astype(F32)
            out[c, 0:rows] = jnp.where(row >= places[p, 0] % rows, before, after).astype(BF)
            out[c, rows:2 * rows] = window(tile, c, places[p, 1], n).astype(BF)


def merge(plan, places, behind, tile, ahead, n):
    shape = (2, 2 * tile.shape[1], n)
    return pl.pallas_call(
        functools.partial(merge_kernel, n=n),
        out_shape=tuple(jax.ShapeDtypeStruct((k,) + shape, BF) for k in (1, 1, 2)),
        in_specs=[SMEM, SMEM, VMEM, VMEM, VMEM],
        out_specs=(VMEM,) * 3,
        compiler_params=pltpu.CompilerParams(vmem_limit_bytes=40 << 20),
    )(plan, places, behind, tile, ahead)


def gather_kernel(plan, own_places, mid_places, far_places, from_own, even, odd, given, from_far, out, *, n):
    rows = out.shape[1]
    width = out.shape[-1]
    row = lax.broadcasted_iota(jnp.int32, (rows, n), 0)
    lane = lax.broadcasted_iota(jnp.int32, (rows, n), 1)
    out[...] = jnp.zeros_like(out)
    mids = (even.at[0], odd.at[0], given.at[0], given.at[1])
    for places, kind, order in ((own_places, 0, OTHER), (mid_places, 1, ORDER), (far_places, 2, OTHER)):
        for k in range(4):
            p = plan[order + k]
            shift = places[p, 0] % rows
            offset = places[p, 1]
            start = pl.multiple_of((offset // n) * n, n)
            after = pl.multiple_of(jnp.minimum(start + n, width - n), n)
            for c in range(2):
                if kind == 0:
                    term = jnp.where(row >= shift, from_own[k, c].astype(F32), 0.0)
                elif kind == 1:
                    term = mids[k][c, rows:2 * rows].astype(F32)
                else:
                    term = jnp.where(row < shift, from_far[k, c].astype(F32), 0.0)
                here = lane >= offset % n
                out[c, :, pl.ds(start, n)] += jnp.where(here, term, 0.0)
                out[c, :, pl.ds(after, n)] += jnp.where(here, 0.0, term)


def gather_terms(plan, own_places, mid_places, far_places, from_own, mids, from_far, rows, width):
    n = from_own.shape[-1]
    return pl.pallas_call(
        functools.partial(gather_kernel, n=n),
        out_shape=jax.ShapeDtypeStruct((2, rows, width), F32),
        in_specs=[SMEM] * 4 + [VMEM] * 5,
        out_specs=VMEM,
        compiler_params=pltpu.CompilerParams(vmem_limit_bytes=40 << 20),
    )(plan, own_places, mid_places, far_places, from_own, *mids, from_far)


def shifted(block, distance):
    size = lax.axis_size("lat")
    return lax.ppermute(block, "lat", [(i, (i + distance) % size) for i in range(size)])


HANDLER, POSITION, EVEN, ODD, ORDER, OTHER, REL, ENTRY = 0, 1, 2, 3, 4, 8, 12, 28
GOAL = (((0, 0, 0), (1, 0, 1), (2, 0, 0), (3, 0, 1)), ((1, 1, 0), (0, 1, 1), (3, 1, 0), (2, 1, 1)))


def meet(c, team, j):
    goal, lo, _ = GOAL[c][j]
    return lo if (team - goal) % 4 in ((0, 1), (0, 3))[c] else 1 - lo


def place_of(c, d):
    v = (d + 2 * c) % 16
    return v // 4, v // 2 % 2, v % 2


def device_of(c, team, lo, y):
    return (4 * team + 2 * lo + y - 2 * c) % 16


def kept(c, team, lo):
    found = [(j, (team - GOAL[c][j][0]) % 4) for j in range(4) if meet(c, team, j) == lo]
    found.sort(key=lambda x: x[1] % 2)
    assert [k % 2 for _, k in found] == [0, 1]
    return found


@functools.lru_cache
def make_plan():
    out = np.zeros((2, 16, 48), np.int32)
    for c in range(2):
        for d in range(16):
            team, lo, y = place_of(c, d)
            row = out[c, d]
            (even, near), (odd, far) = kept(c, team, lo)
            row[EVEN] = 2 * near + (y ^ GOAL[c][even][2])
            row[ODD] = 2 * far + (y ^ GOAL[c][odd][2])
            j = even
            row[HANDLER] = GOAL[c][j] == (team, lo, y)
            row[POSITION] = j
            row[ORDER:ORDER + 4] = [even, odd] + [j for j, _ in kept(c, team, 1 - lo)]
            team2, lo2, _ = place_of(1 - c, d)
            row[OTHER:OTHER + 4] = [j for j, _ in kept(1 - c, team2, lo2) + kept(1 - c, team2, 1 - lo2)]
            for s in range(16):
                there, at, side = place_of(c, s)
                row[REL + s] = 2 * ((there - team) % 4) + (side ^ y)
                row[ENTRY + s] = at ^ meet(c, there, j)
    return out


def permute(block, route):
    depth, lat = lax.axis_size("depth"), lax.axis_size("lat")
    pairs = []
    for d in range(depth):
        for m in range(lat):
            to = route(m % 2, *place_of(m % 2, d))
            if to is not None:
                pairs.append((d * lat + m, device_of(m % 2, *to) * lat + m))
    return lax.ppermute(block, ("depth", "lat"), pairs)


def across(block):
    return permute(block, lambda c, team, lo, y: (team, 1 - lo, y))


def towards(block, k, e):
    def route(c, team, lo, y):
        for j, away in kept(c, team, lo):
            if away == k and y ^ e == GOAL[c][j][2]:
                return GOAL[c][j]
        return None
    return permute(block, route)


def away(block, k, e):
    def route(c, team, lo, y):
        for j in range(4):
            if GOAL[c][j] == (team, lo, y):
                there = (team + k) % 4
                return there, meet(c, there, j), y ^ e
        return None
    return permute(block, route)


def on_device(object_slices, probe, positions, measured):
    n = probe.shape[-1]
    rows, width = object_slices.shape[2:]
    depth_size = lax.axis_size("depth")
    d = lax.axis_index("depth")
    m = lax.axis_index("lat")
    plan = lax.dynamic_slice(jnp.asarray(make_plan()), (m % 2, d, 0), (1, 1, 48)).reshape(48)
    tile = object_slices[0]

    tile_bf, mine = own_windows(plan, positions, tile, measured, n)
    ahead = shifted(tile_bf, -1)
    behind = shifted(mine, 1)
    mid_places = shifted(positions, 1)
    far_places = shifted(positions, 2)
    mid_places, far_places, ahead, behind = lax.optimization_barrier((mid_places, far_places, ahead, behind))
    even, odd, given = merge(plan, mid_places, behind, tile_bf, ahead, n)

    got = across(given)
    kinds = (jnp.concatenate([even, got[0:1]]), jnp.concatenate([odd, got[1:2]]))
    order = [(2, 0), (1, 0), (3, 0), (2, 1), (1, 1), (3, 1), (0, 1)]
    messages = {(k, e): towards(kinds[k % 2], k, e) for k, e in order}
    messages[0, 0] = kinds[0]
    tables = make_tables(n, depth_size)
    slots = [(k, e) for k in range(4) for e in range(2)]
    terms = dict(zip(slots, chain(plan, mid_places, probe, behind, [messages[x] for x in slots], tables, rows)))

    got = {x: away(terms[x], *x) for x in order}
    even = terms[0, 0]
    for k, e in ((0, 1), (2, 0), (2, 1)):
        even = jnp.where(plan[EVEN] == 2 * k + e, got[k, e], even)
    odd = got[1, 0]
    for k, e in ((1, 1), (3, 0), (3, 1)):
        odd = jnp.where(plan[ODD] == 2 * k + e, got[k, e], odd)
    given = across(jnp.stack([even[1], odd[1]]))
    mixed = jnp.stack([even[0, :, :rows], odd[0, :, :rows], given[0, :, :rows], given[1, :, :rows]])
    from_own = shifted(mixed, -1)
    from_far = shifted(mixed, 1)
    total = gather_terms(plan, positions, mid_places, far_places, from_own, (even, odd, given), from_far, rows, width)
    return total[None]


def solution(mesh):
    return jax.shard_map(
        on_device,
        mesh=mesh,
        in_specs=(P("depth", None, "lat", None), P(), P("lat", None), P("lat", None, None)),
        out_specs=P("depth", None, "lat", None),
        check_vma=False,
    )
```

time: 169 us -> 172 us (1.018)
  the two profiles are of different devices: /device:TPU:1 before, /device:TPU:8 now
where the time goes in v5:
time: 172 us; the launch traced here: 171 us
  starting transfers between devices  64.4 us (37%)
  waiting for transfers between devices  49.9 us (29%)
  Pallas kernels  45.9 us (27%)
  local copies, waits for them, and re-layouts  5.77 us (3%)
  between operations  4.21 us (2%)
    ppermute x16, starting transfers between devices, permute(): return lax.ppermute(block, ('depth', 'lat'), pairs)  52 us
    pallas_call x1, Pallas kernels, chain(): pl.pallas_call(functools.partial(chain_kernel, n=n, slices=slices, rows=r...  30.1 us
    ppermute x16, waiting for transfers between devices, permute(): return lax.ppermute(block, ('depth', 'lat'), pairs)  26.7 us
    ppermute x6, waiting for transfers between devices, shifted(): lax.ppermute(block, 'lat', [(i, (i + distance) % size) for i in range(siz...  23.2 us
    ppermute x6, starting transfers between devices, shifted(): lax.ppermute(block, 'lat', [(i, (i + distance) % size) for i in range(siz...  12.4 us
    pallas_call x1, Pallas kernels, make_tables(): pl.pallas_call(functools.partial(tables_kernel, n=n, slices=slices), grid...  11.1 us
    unnamed x29, local copies, waits for them, and re-layouts  3.63 us
  transfers between devices with their start and end apart: 22, of which 10 were waited for; matrix products, arithmetic and copies ran while one was open for 1% of the time, Pallas kernels for 6%

profile of v5, /device:TPU:8, one launch (start us, length us, event | category | flops | bytes accessed | tf_op | source)
XLA Modules:
  0.0 171.4 jit_solution(13464232368503770879)
XLA Ops:
  0.0 0.8 copy.11.places.own_places
  0.8 0.7 fusion.2.plan.refs_0_
  1.5 1.6 copy-done.1
  3.1 1.2 copy-done.2
  4.3 0.9 shard_map.73
  5.2 2.2 %collective-permute-start.2 = (bf16[2,128,2048]{2,1,0:T(8,128)(2,1)S(1)}, bf16[2,128,2048]{2,1,0:T(8,128)(2,1)S(1)}, u32[]{:S(2)}, u32[]{:S(2)}) collective-permute-start(bf16[2,128,2048]{2,1,0:T(8,128)(2,1)S(1)} %get-tuple-element.22.tile), channel_id=1, source_target_pairs={{0,15},{1,0},{2,1},{3,2},{4,3},{5,4},{6,5},{7,6},{8,7},{9,8},{10,9... | collective-permute-start | bytes 3145736 | tf_op jit(solution)/shard_map/ppermute | solution.py:357
  7.3 0.0 collective-permute-start.3
  7.3 0.0 collective-permute-start
  7.3 1.1 collective-permute-start.1
  8.4 12.5 %collective-permute-done.places.refs_1_.mid_places = s32[4,2]{1,0:T(4,128)S(1)} collective-permute-done((s32[4,2]{1,0:T(4,128)S(1)}, s32[4,2]{1,0:T(4,128)S(1)}, u32[]{:S(2)}, u32[]{:S(2)}) %collective-permute-start) | collective-permute-done | bytes 64 | tf_op jit(solution)/shard_map/ppermute | solution.py:357
  20.9 0.0 collective-permute-done.1.far_places
  20.9 0.0 collective-permute-done.3.behind.refs_3_
  20.9 0.0 copy-start
  20.9 0.0 collective-permute-done.2.ahead
  20.9 0.9 shard_map.74
  21.9 2.0 %collective-permute-start.4 = (bf16[2,2,256,256]{3,2,1,0:T(8,128)(2,1)S(1)}, bf16[2,2,256,256]{3,2,1,0:T(8,128)(2,1)S(1)}, u32[]{:S(2)}, u32[]{:S(2)}) collective-permute-start(bf16[2,2,256,256]{3,2,1,0:T(8,128)(2,1)S(1)} %get-tuple-element.29), channel_id=1, source_target_pairs={{0,32},{1,225},{2,34},{3,227},{4,36},{5,229},{6,38},{7,231},{8,40}... | collective-permute-start | bytes 1572872 | tf_op jit(solution)/shard_map/ppermute | solution.py:416
  23.9 7.3 %collective-permute-done.4 = bf16[2,2,256,256]{3,2,1,0:T(8,128)(2,1)S(1)} collective-permute-done((bf16[2,2,256,256]{3,2,1,0:T(8,128)(2,1)S(1)}, bf16[2,2,256,256]{3,2,1,0:T(8,128)(2,1)S(1)}, u32[]{:S(2)}, u32[]{:S(2)}) %collective-permute-start.4) | collective-permute-done | bytes 524320 | tf_op jit(solution)/shard_map/ppermute | solution.py:416
  31.2 0.1 pad_maximum_fusion.refs_4_
  31.2 0.0 copy-done.3
  31.3 0.0 copy-done
  31.3 1.3 collective-permute-start.5
  32.6 0.8 pad_maximum_fusion.1
  33.4 1.3 collective-permute-start.6
  34.7 10.2 %collective-permute-start.7 = (bf16[2,2,256,256]{3,2,1,0:T(8,128)(2,1)}, bf16[2,2,256,256]{3,2,1,0:T(8,128)(2,1)S(1)}, u32[]{:S(2)}, u32[]{:S(2)}) collective-permute-start(bf16[2,2,256,256]{3,2,1,0:T(8,128)(2,1)} %pad_maximum_fusion.1), channel_id=1, source_target_pairs={{0,208},{2,210},{4,212},{6,214},{8,216},{10,218},{12,220},{14,222}... | collective-permute-start | bytes 1572872 | tf_op jit(solution)/shard_map/ppermute | solution.py:416
  44.9 1.3 collective-permute-start.8
  46.2 1.3 collective-permute-start.9
  47.5 1.9 %collective-permute-done.5.refs_5_ = bf16[2,2,256,256]{3,2,1,0:T(8,128)(2,1)S(1)} collective-permute-done((bf16[2,2,256,256]{3,2,1,0:T(8,128)(2,1)S(1)}, bf16[2,2,256,256]{3,2,1,0:T(8,128)(2,1)S(1)}, u32[]{:S(2)}, u32[]{:S(2)}) %collective-permute-start.5) | collective-permute-done | bytes 524320 | tf_op jit(solution)/shard_map/ppermute | solution.py:416
  49.5 1.3 collective-permute-start.10
  50.8 0.0 collective-permute-done.6.refs_6_
  50.8 1.3 collective-permute-start.11
  52.1 11.1 %shard_map.75.refs_12_ = bf16[17,2,512,512]{3,2,1,0:T(8,128)(2,1)} custom-call(f32[2,17]{1,0:T(2,128)} %constant.48.clone.scales, f32[4,256,256]{2,1,0:T(8,128)} %constant.49.clone.base), custom_call_target="tpu_custom_call" | custom-call | tf_op jit(solution)/shard_map/pallas_call | solution.py:49
  63.2 0.0 collective-permute-done.7.refs_7_
  63.2 7.1 %collective-permute-done.8.refs_8_ = bf16[2,2,256,256]{3,2,1,0:T(8,128)(2,1)S(1)} collective-permute-done((bf16[2,2,256,256]{3,2,1,0:T(8,128)(2,1)S(1)}, bf16[2,2,256,256]{3,2,1,0:T(8,128)(2,1)S(1)}, u32[]{:S(2)}, u32[]{:S(2)}) %collective-permute-start.8) | collective-permute-done | bytes 524320 | tf_op jit(solution)/shard_map/ppermute | solution.py:416
  70.3 0.0 collective-permute-done.9.refs_9_
  70.3 1.6 collective-permute-done.10.refs_10_
  71.9 0.0 collective-permute-done.11.refs_11_
  71.9 30.1 %shard_map.76 = (bf16[2,2,256,256]{3,2,1,0:T(8,128)(2,1)}, bf16[2,2,256,256]{3,2,1,0:T(8,128)(2,1)}, bf16[2,2,256,256]{3,2,1,0:T(8,128)(2,1)}, bf16[2,2,256,256]...) custom-call(s32[48]{0:T(128)} %copy-done.5, ...), custom_call_target="tpu_custom_call" | custom-call | tf_op jit(solution)/shard_map/pallas_call | solution.py:232
  102.0 1.5 collective-permute-start.15
  103.5 1.3 collective-permute-start.16
  104.8 6.0 %collective-permute-start.17 = (bf16[2,2,256,256]{3,2,1,0:T(8,128)(2,1)}, bf16[2,2,256,256]{3,2,1,0:T(8,128)(2,1)S(1)}, u32[]{:S(2)}, u32[]{:S(2)}) collective-permute-start(bf16[2,2,256,256]{3,2,1,0:T(8,128)(2,1)} %get-tuple-element.37), channel_id=1, source_target_pairs={{0,80},{2,82},{4,84},{6,86},{8,88},{10,90},{12,92},{14,94},{17,33}... | collective-permute-start | bytes 1572872 | tf_op jit(solution)/shard_map/ppermute | solution.py:416
  110.9 1.3 collective-permute-start.18
  112.2 1.3 collective-permute-start.12
  113.5 0.0 collective-permute-done.15
  113.5 11.8 %collective-permute-start.13 = (bf16[2,2,256,256]{3,2,1,0:T(8,128)(2,1)}, bf16[2,2,256,256]{3,2,1,0:T(8,128)(2,1)S(1)}, u32[]{:S(2)}, u32[]{:S(2)}) collective-permute-start(bf16[2,2,256,256]{3,2,1,0:T(8,128)(2,1)} %get-tuple-element.32), channel_id=1, source_target_pairs={{0,160},{2,162},{4,164},{6,166},{8,168},{10,170},{12,172},{14,174}... | collective-permute-start | bytes 1572872 | tf_op jit(solution)/shard_map/ppermute | solution.py:416
  125.4 0.0 collective-permute-done.16
  125.4 1.3 collective-permute-start.14
  126.7 0.7 constant_dynamic-slice_fusion
  127.4 0.6 fusion.1
  131.9 0.0 collective-permute-done.17
  131.9 0.0 collective-permute-done.18
  131.9 0.1 select_select_fusion.odd
  132.0 0.0 collective-permute-done.12
  132.0 0.3 collective-permute-done.13
  132.3 1.3 collective-permute-done.14
  133.7 0.1 select_select_fusion.1.even
  133.8 0.1 pad_maximum_fusion.2
  133.9 7.4 %collective-permute-start.19 = (bf16[2,2,256,256]{3,2,1,0:T(8,128)(2,1)S(1)}, bf16[2,2,256,256]{3,2,1,0:T(8,128)(2,1)S(1)}, u32[]{:S(2)}, u32[]{:S(2)}) collective-permute-start(bf16[2,2,256,256]{3,2,1,0:T(8,128)(2,1)S(1)} %pad_maximum_fusion.2), channel_id=1, source_target_pairs={{0,32},{1,225},{2,34},{3,227},{4,36},{5,229},{6,38},{7,231},{8,40}... | collective-permute-start | bytes 1572872 | tf_op jit(solution)/shard_map/ppermute | solution.py:416
  141.4 7.1 %collective-permute-done.19.given = bf16[2,2,256,256]{3,2,1,0:T(8,128)(2,1)S(1)} collective-permute-done((bf16[2,2,256,256]{3,2,1,0:T(8,128)(2,1)S(1)}, bf16[2,2,256,256]{3,2,1,0:T(8,128)(2,1)S(1)}, u32[]{:S(2)}, u32[]{:S(2)}) %collective-permute-start.19) | collective-permute-done | bytes 524320 | tf_op jit(solution)/shard_map/ppermute | solution.py:416
  148.5 0.1 pad_maximum_fusion.3
  148.6 9.1 %collective-permute-start.20 = (bf16[4,2,128,256]{3,2,1,0:T(8,128)(2,1)S(1)}, bf16[4,2,128,256]{3,2,1,0:T(8,128)(2,1)S(1)}, u32[]{:S(2)}, u32[]{:S(2)}) collective-permute-start(bf16[4,2,128,256]{3,2,1,0:T(8,128)(2,1)S(1)} %pad_maximum_fusion.3), channel_id=1, source_target_pairs={{0,15},{1,0},{2,1},{3,2},{4,3},{5,4},{6,5},{7,6},{8,7},{9,8},{10,9... | collective-permute-start | bytes 1572872 | tf_op jit(solution)/shard_map/ppermute | solution.py:357
  157.7 0.0 collective-permute-start.21
  157.7 6.7 %collective-permute-done.20.from_own = bf16[4,2,128,256]{3,2,1,0:T(8,128)(2,1)S(1)} collective-permute-done((bf16[4,2,128,256]{3,2,1,0:T(8,128)(2,1)S(1)}, bf16[4,2,128,256]{3,2,1,0:T(8,128)(2,1)S(1)}, u32[]{:S(2)}, u32[]{:S(2)}) %collective-permute-start.20) | collective-permute-done | bytes 524320 | tf_op jit(solution)/shard_map/ppermute | solution.py:357
  164.4 4.0 %collective-permute-done.21.from_far = bf16[4,2,128,256]{3,2,1,0:T(8,128)(2,1)S(1)} collective-permute-done((bf16[4,2,128,256]{3,2,1,0:T(8,128)(2,1)S(1)}, bf16[4,2,128,256]{3,2,1,0:T(8,128)(2,1)S(1)}, u32[]{:S(2)}, u32[]{:S(2)}) %collective-permute-start.21) | collective-permute-done | bytes 524320 | tf_op jit(solution)/shard_map/ppermute | solution.py:357
  168.4 3.0 %shard_map.77 = f32[2,128,2048]{2,1,0:T(8,128)} custom-call(s32[48]{0:T(128)S(1)} %copy-done.6, s32[4,2]{1,0:T(4,128)S(1)} %copy.11.places.own_places, s32[4,2]{1,0:T(4,128)S(1)} %copy-done.4, s32[4,2]{1,0:T(4,128)S(1)} %collective-permute-done.1.far_places, bf16[4,2,128,256]{3,2,1,0:T(8,128)(2,1)S(1)} %collective-permute-done.20.from_own, ...), custom_call_target="tpu_custom_call" | custom-call | tf_op jit(solution)/shard_map/pallas_call | solution.py:346
  (29 shorter events, 0.2 us)
Async XLA Ops:
  1.5 20.4 %copy-start.5 = (s32[48]{0:T(128)}, s32[48]{0:T(128)S(1)}, u32[]{:S(2)}) copy-start(s32[48]{0:T(128)S(1)} %fusion.2.plan.refs_0_) | copy-start | bytes 580
  1.5 1.6 copy-start.1
  3.1 1.2 copy-start.2
  5.2 15.8 %collective-permute-start.2 = (bf16[2,128,2048]{2,1,0:T(8,128)(2,1)S(1)}, bf16[2,128,2048]{2,1,0:T(8,128)(2,1)S(1)}, u32[]{:S(2)}, u32[]{:S(2)}) collective-permute-start(bf16[2,128,2048]{2,1,0:T(8,128)(2,1)S(1)} %get-tuple-element.22.tile), channel_id=1, source_target_pairs={{0,15},{1,0},{2,1},{3,2},{4,3},{5,4},{6,5},{7,6},{8,7},{9,8},{10,9... | collective-permute-start | bytes 3145736 | tf_op jit(solution)/shard_map/ppermute | solution.py:357
  7.3 13.6 %collective-permute-start.3 = (bf16[6,2,128,256]{3,2,1,0:T(8,128)(2,1)S(1)}, bf16[6,2,128,256]{3,2,1,0:T(8,128)(2,1)S(1)}, u32[]{:S(2)}, u32[]{:S(2)}) collective-permute-start(bf16[6,2,128,256]{3,2,1,0:T(8,128)(2,1)S(1)} %get-tuple-element.23), channel_id=1, source_target_pairs={{0,1},{1,2},{2,3},{3,4},{4,5},{5,6},{6,7},{7,8},{8,9},{9,10},{10,1... | collective-permute-start | bytes 2359304 | tf_op jit(solution)/shard_map/ppermute | solution.py:357
  7.3 13.6 %collective-permute-start = (s32[4,2]{1,0:T(4,128)S(1)}, s32[4,2]{1,0:T(4,128)S(1)}, u32[]{:S(2)}, u32[]{:S(2)}) collective-permute-start(s32[4,2]{1,0:T(4,128)S(1)} %copy.11.places.own_places), channel_id=1, source_target_pairs={{0,1},{1,2},{2,3},{3,4},{4,5},{5,6},{6,7},{7,8},{8,9},{9,10},{10,1... | collective-permute-start | bytes 104 | tf_op jit(solution)/shard_map/ppermute | solution.py:357
  7.3 13.6 %collective-permute-start.1 = (s32[4,2]{1,0:T(4,128)S(1)}, s32[4,2]{1,0:T(4,128)S(1)}, u32[]{:S(2)}, u32[]{:S(2)}) collective-permute-start(s32[4,2]{1,0:T(4,128)S(1)} %copy.11.places.own_places), channel_id=1, source_target_pairs={{0,2},{1,3},{2,4},{3,5},{4,6},{5,7},{6,8},{7,9},{8,10},{9,11},{10,... | collective-permute-start | bytes 104 | tf_op jit(solution)/shard_map/ppermute | solution.py:357
  20.9 10.4 %copy-start.3 = (s32[4,2]{1,0:T(4,128)}, s32[4,2]{1,0:T(4,128)S(1)}, u32[]{:S(2)}) copy-start(s32[4,2]{1,0:T(4,128)S(1)} %collective-permute-done.places.refs_1_.mid_places) | copy-start | bytes 100
  20.9 10.4 %copy-start = (bf16[6,2,128,256]{3,2,1,0:T(8,128)(2,1)}, bf16[6,2,128,256]{3,2,1,0:T(8,128)(2,1)S(1)}, u32[]{:S(2)}) copy-start(bf16[6,2,128,256]{3,2,1,0:T(8,128)(2,1)S(1)} %collective-permute-done.3.behind.refs_3_) | copy-start | bytes 2359300
  21.9 9.3 %collective-permute-start.4 = (bf16[2,2,256,256]{3,2,1,0:T(8,128)(2,1)S(1)}, bf16[2,2,256,256]{3,2,1,0:T(8,128)(2,1)S(1)}, u32[]{:S(2)}, u32[]{:S(2)}) collective-permute-start(bf16[2,2,256,256]{3,2,1,0:T(8,128)(2,1)S(1)} %get-tuple-element.29), channel_id=1, source_target_pairs={{0,32},{1,225},{2,34},{3,227},{4,36},{5,229},{6,38},{7,231},{8,40}... | collective-permute-start | bytes 1572872 | tf_op jit(solution)/shard_map/ppermute | solution.py:416
  31.3 31.9 %copy-start.7 = (bf16[2,2,256,256]{3,2,1,0:T(8,128)(2,1)}, bf16[2,2,256,256]{3,2,1,0:T(8,128)(2,1)S(1)}, u32[]{:S(2)}) copy-start(bf16[2,2,256,256]{3,2,1,0:T(8,128)(2,1)S(1)} %pad_maximum_fusion.refs_4_) | copy-start | bytes 1572868
  31.3 18.2 %collective-permute-start.5 = (bf16[2,2,256,256]{3,2,1,0:T(8,128)(2,1)S(1)}, bf16[2,2,256,256]{3,2,1,0:T(8,128)(2,1)S(1)}, u32[]{:S(2)}, u32[]{:S(2)}) collective-permute-start(bf16[2,2,256,256]{3,2,1,0:T(8,128)(2,1)S(1)} %pad_maximum_fusion.refs_4_), channel_id=1, source_target_pairs={{1,17},{3,19},{5,21},{7,23},{9,25},{11,27},{13,29},{15,31},{16,0},... | collective-permute-start | bytes 1572872 | tf_op jit(solution)/shard_map/ppermute | solution.py:416
  33.4 17.4 %collective-permute-start.6 = (bf16[2,2,256,256]{3,2,1,0:T(8,128)(2,1)}, bf16[2,2,256,256]{3,2,1,0:T(8,128)(2,1)S(1)}, u32[]{:S(2)}, u32[]{:S(2)}) collective-permute-start(bf16[2,2,256,256]{3,2,1,0:T(8,128)(2,1)} %pad_maximum_fusion.1), channel_id=1, source_target_pairs={{16,208},{18,210},{20,212},{22,214},{24,216},{26,218},{28,220},{30... | collective-permute-start | bytes 1572872 | tf_op jit(solution)/shard_map/ppermute | solution.py:416
  34.7 28.5 %collective-permute-start.7 = (bf16[2,2,256,256]{3,2,1,0:T(8,128)(2,1)}, bf16[2,2,256,256]{3,2,1,0:T(8,128)(2,1)S(1)}, u32[]{:S(2)}, u32[]{:S(2)}) collective-permute-start(bf16[2,2,256,256]{3,2,1,0:T(8,128)(2,1)} %pad_maximum_fusion.1), channel_id=1, source_target_pairs={{0,208},{2,210},{4,212},{6,214},{8,216},{10,218},{12,220},{14,222}... | collective-permute-start | bytes 1572872 | tf_op jit(solution)/shard_map/ppermute | solution.py:416
  44.9 25.4 %collective-permute-start.8 = (bf16[2,2,256,256]{3,2,1,0:T(8,128)(2,1)S(1)}, bf16[2,2,256,256]{3,2,1,0:T(8,128)(2,1)S(1)}, u32[]{:S(2)}, u32[]{:S(2)}) collective-permute-start(bf16[2,2,256,256]{3,2,1,0:T(8,128)(2,1)S(1)} %pad_maximum_fusion.refs_4_), channel_id=1, source_target_pairs={{32,128},{33,193},{34,130},{35,195},{36,132},{37,197},{38,134},{39... | collective-permute-start | bytes 1572872 | tf_op jit(solution)/shard_map/ppermute | solution.py:416
  46.2 24.1 %collective-permute-start.9 = (bf16[2,2,256,256]{3,2,1,0:T(8,128)(2,1)S(1)}, bf16[2,2,256,256]{3,2,1,0:T(8,128)(2,1)S(1)}, u32[]{:S(2)}, u32[]{:S(2)}) collective-permute-start(bf16[2,2,256,256]{3,2,1,0:T(8,128)(2,1)S(1)} %pad_maximum_fusion.refs_4_), channel_id=1, source_target_pairs={{48,128},{49,193},{50,130},{51,195},{52,132},{53,197},{54,134},{55... | collective-permute-start | bytes 1572872 | tf_op jit(solution)/shard_map/ppermute | solution.py:416
  49.5 13.7 %copy-start.8 = (bf16[2,2,256,256]{3,2,1,0:T(8,128)(2,1)}, bf16[2,2,256,256]{3,2,1,0:T(8,128)(2,1)S(1)}, u32[]{:S(2)}) copy-start(bf16[2,2,256,256]{3,2,1,0:T(8,128)(2,1)S(1)} %collective-permute-done.5.refs_5_) | copy-start | bytes 1572868
  49.5 22.4 %collective-permute-start.10 = (bf16[2,2,256,256]{3,2,1,0:T(8,128)(2,1)}, bf16[2,2,256,256]{3,2,1,0:T(8,128)(2,1)}, u32[]{:S(2)}, u32[]{:S(2)}) collective-permute-start(bf16[2,2,256,256]{3,2,1,0:T(8,128)(2,1)} %pad_maximum_fusion.1), channel_id=1, source_target_pairs={{1,65},{3,67},{5,69},{7,71},{9,73},{11,75},{13,77},{15,79},{48,80}... | collective-permute-start | bytes 1572872 | tf_op jit(solution)/shard_map/ppermute | solution.py:416
  50.8 12.4 %copy-start.9 = (bf16[2,2,256,256]{3,2,1,0:T(8,128)(2,1)}, bf16[2,2,256,256]{3,2,1,0:T(8,128)(2,1)S(1)}, u32[]{:S(2)}) copy-start(bf16[2,2,256,256]{3,2,1,0:T(8,128)(2,1)S(1)} %collective-permute-done.6.refs_6_) | copy-start | bytes 1572868
  50.8 21.1 %collective-permute-start.11 = (bf16[2,2,256,256]{3,2,1,0:T(8,128)(2,1)}, bf16[2,2,256,256]{3,2,1,0:T(8,128)(2,1)}, u32[]{:S(2)}, u32[]{:S(2)}) collective-permute-start(bf16[2,2,256,256]{3,2,1,0:T(8,128)(2,1)} %pad_maximum_fusion.1), channel_id=1, source_target_pairs={{17,65},{19,67},{21,69},{23,71},{25,73},{27,75},{29,77},{31,79},{3... | collective-permute-start | bytes 1572872 | tf_op jit(solution)/shard_map/ppermute | solution.py:416
  63.2 8.7 %copy-start.10 = (bf16[2,2,256,256]{3,2,1,0:T(8,128)(2,1)}, bf16[2,2,256,256]{3,2,1,0:T(8,128)(2,1)S(1)}, u32[]{:S(2)}) copy-start(bf16[2,2,256,256]{3,2,1,0:T(8,128)(2,1)S(1)} %collective-permute-done.7.refs_7_) | copy-start | bytes 1572868
  70.3 1.6 copy-start.11
  70.3 1.6 copy-start.12
  102.0 31.6 %copy-start.13 = (bf16[2,2,256,256]{3,2,1,0:T(8,128)(2,1)S(1)}, bf16[2,2,256,256]{3,2,1,0:T(8,128)(2,1)}, u32[]{:S(2)}) copy-start(bf16[2,2,256,256]{3,2,1,0:T(8,128)(2,1)} %get-tuple-element.34) | copy-start | bytes 1572868
  102.0 11.5 %collective-permute-start.15 = (bf16[2,2,256,256]{3,2,1,0:T(8,128)(2,1)}, bf16[2,2,256,256]{3,2,1,0:T(8,128)(2,1)S(1)}, u32[]{:S(2)}, u32[]{:S(2)}) collective-permute-start(bf16[2,2,256,256]{3,2,1,0:T(8,128)(2,1)} %get-tuple-element.35), channel_id=1, source_target_pairs={{0,240},{2,242},{4,244},{6,246},{8,248},{10,250},{12,252},{14,254}... | collective-permute-start | bytes 1572872 | tf_op jit(solution)/shard_map/ppermute | solution.py:416
  103.5 21.9 %collective-permute-start.16 = (bf16[2,2,256,256]{3,2,1,0:T(8,128)(2,1)}, bf16[2,2,256,256]{3,2,1,0:T(8,128)(2,1)S(1)}, u32[]{:S(2)}, u32[]{:S(2)}) collective-permute-start(bf16[2,2,256,256]{3,2,1,0:T(8,128)(2,1)} %get-tuple-element.36), channel_id=1, source_target_pairs={{0,224},{2,226},{4,228},{6,230},{8,232},{10,234},{12,236},{14,238}... | collective-permute-start | bytes 1572872 | tf_op jit(solution)/shard_map/ppermute | solution.py:416
  104.8 27.0 %collective-permute-start.17 = (bf16[2,2,256,256]{3,2,1,0:T(8,128)(2,1)}, bf16[2,2,256,256]{3,2,1,0:T(8,128)(2,1)S(1)}, u32[]{:S(2)}, u32[]{:S(2)}) collective-permute-start(bf16[2,2,256,256]{3,2,1,0:T(8,128)(2,1)} %get-tuple-element.37), channel_id=1, source_target_pairs={{0,80},{2,82},{4,84},{6,86},{8,88},{10,90},{12,92},{14,94},{17,33}... | collective-permute-start | bytes 1572872 | tf_op jit(solution)/shard_map/ppermute | solution.py:416
  110.9 21.0 %collective-permute-start.18 = (bf16[2,2,256,256]{3,2,1,0:T(8,128)(2,1)}, bf16[2,2,256,256]{3,2,1,0:T(8,128)(2,1)S(1)}, u32[]{:S(2)}, u32[]{:S(2)}) collective-permute-start(bf16[2,2,256,256]{3,2,1,0:T(8,128)(2,1)} %get-tuple-element.38), channel_id=1, source_target_pairs={{0,64},{2,66},{4,68},{6,70},{8,72},{10,74},{12,76},{14,78},{17,49}... | collective-permute-start | bytes 1572872 | tf_op jit(solution)/shard_map/ppermute | solution.py:416
  112.2 19.8 %collective-permute-start.12 = (bf16[2,2,256,256]{3,2,1,0:T(8,128)(2,1)}, bf16[2,2,256,256]{3,2,1,0:T(8,128)(2,1)S(1)}, u32[]{:S(2)}, u32[]{:S(2)}) collective-permute-start(bf16[2,2,256,256]{3,2,1,0:T(8,128)(2,1)} %get-tuple-element.31), channel_id=1, source_target_pairs={{0,176},{2,178},{4,180},{6,182},{8,184},{10,186},{12,188},{14,190}... | collective-permute-start | bytes 1572872 | tf_op jit(solution)/shard_map/ppermute | solution.py:416
  113.5 18.8 %collective-permute-start.13 = (bf16[2,2,256,256]{3,2,1,0:T(8,128)(2,1)}, bf16[2,2,256,256]{3,2,1,0:T(8,128)(2,1)S(1)}, u32[]{:S(2)}, u32[]{:S(2)}) collective-permute-start(bf16[2,2,256,256]{3,2,1,0:T(8,128)(2,1)} %get-tuple-element.32), channel_id=1, source_target_pairs={{0,160},{2,162},{4,164},{6,166},{8,168},{10,170},{12,172},{14,174}... | collective-permute-start | bytes 1572872 | tf_op jit(solution)/shard_map/ppermute | solution.py:416
  125.4 8.3 %collective-permute-start.14 = (bf16[2,2,256,256]{3,2,1,0:T(8,128)(2,1)}, bf16[2,2,256,256]{3,2,1,0:T(8,128)(2,1)S(1)}, u32[]{:S(2)}, u32[]{:S(2)}) collective-permute-start(bf16[2,2,256,256]{3,2,1,0:T(8,128)(2,1)} %get-tuple-element.33), channel_id=1, source_target_pairs={{0,16},{2,18},{4,20},{6,22},{8,24},{10,26},{12,28},{14,30},{17,1},... | collective-permute-start | bytes 1572872 | tf_op jit(solution)/shard_map/ppermute | solution.py:416
  133.8 34.7 %copy-start.4 = (s32[4,2]{1,0:T(4,128)S(1)}, s32[4,2]{1,0:T(4,128)}, u32[]{:S(2)}) copy-start(s32[4,2]{1,0:T(4,128)} %copy-done.3) | copy-start | bytes 100
  133.8 34.7 %copy-start.6 = (s32[48]{0:T(128)S(1)}, s32[48]{0:T(128)}, u32[]{:S(2)}) copy-start(s32[48]{0:T(128)} %copy-done.5) | copy-start | bytes 580
  133.9 14.6 %collective-permute-start.19 = (bf16[2,2,256,256]{3,2,1,0:T(8,128)(2,1)S(1)}, bf16[2,2,256,256]{3,2,1,0:T(8,128)(2,1)S(1)}, u32[]{:S(2)}, u32[]{:S(2)}) collective-permute-start(bf16[2,2,256,256]{3,2,1,0:T(8,128)(2,1)S(1)} %pad_maximum_fusion.2), channel_id=1, source_target_pairs={{0,32},{1,225},{2,34},{3,227},{4,36},{5,229},{6,38},{7,231},{8,40}... | collective-permute-start | bytes 1572872 | tf_op jit(solution)/shard_map/ppermute | solution.py:416
  148.6 15.8 %collective-permute-start.20 = (bf16[4,2,128,256]{3,2,1,0:T(8,128)(2,1)S(1)}, bf16[4,2,128,256]{3,2,1,0:T(8,128)(2,1)S(1)}, u32[]{:S(2)}, u32[]{:S(2)}) collective-permute-start(bf16[4,2,128,256]{3,2,1,0:T(8,128)(2,1)S(1)} %pad_maximum_fusion.3), channel_id=1, source_target_pairs={{0,15},{1,0},{2,1},{3,2},{4,3},{5,4},{6,5},{7,6},{8,7},{9,8},{10,9... | collective-permute-start | bytes 1572872 | tf_op jit(solution)/shard_map/ppermute | solution.py:357
  157.7 10.7 %collective-permute-start.21 = (bf16[4,2,128,256]{3,2,1,0:T(8,128)(2,1)S(1)}, bf16[4,2,128,256]{3,2,1,0:T(8,128)(2,1)S(1)}, u32[]{:S(2)}, u32[]{:S(2)}) collective-permute-start(bf16[4,2,128,256]{3,2,1,0:T(8,128)(2,1)S(1)} %pad_maximum_fusion.3), channel_id=1, source_target_pairs={{0,1},{1,2},{2,3},{3,4},{4,5},{5,6},{6,7},{7,8},{8,9},{9,10},{10,1... | collective-permute-start | bytes 1572872 | tf_op jit(solution)/shard_map/ppermute | solution.py:357

commit v6 on v5

--- a/solution.py
+++ b/solution.py
@@ -62,9 +62,9 @@
 
 
 def chain_body(plan, places, probe, behind, *refs, n, slices, rows):
-    ins, tabs_hbm, outs = refs[0:8], refs[8], refs[9:17]
-    (patch, tabs, inc, lhs0, lhs1, mid0, mid1, outv, target, term, psem, tsem, osem, gsem) = refs[17:31]
-    accs = list(refs[31:])
+    ins, tabs_hbm, near_out, far_out = refs[0:4], refs[4], refs[5:9], refs[9:13]
+    (patch, tabs, inc, lhs0, lhs1, mid0, mid1, outv, target, term, psem, tsem, osem, gsem) = refs[13:27]
+    accs = list(refs[27:])
     first_acc = [[[accs.pop(0) for _ in range(n // FIRST)] for _ in range(2)] for _ in range(2)]
     second_acc = [[[accs.pop(0) for _ in range(n // SECOND)] for _ in range(2)] for _ in range(2)]
     lhs, mid = (lhs0, lhs1), (mid0, mid1)
@@ -163,7 +163,7 @@
         target_copy.start()
         for s in range(slices):
             table_copy(s).start()
-            for r in range(8):
+            for r in range(4):
                 @pl.when(plan[REL + s] == r)
                 def _():
                     pltpu.make_async_copy(ins[r].at[plan[ENTRY + s]], patch.at[s], psem.at[s]).start()
@@ -207,10 +207,11 @@
         step(slices, 0, put, (slices - 1, 1))
 
         def send(s):
-            for r in range(8):
+            for r in range(4):
                 @pl.when(plan[REL + s] == r)
                 def _():
-                    pltpu.make_async_copy(outv.at[s], outs[r].at[plan[ENTRY + s]], osem.at[s]).start()
+                    for h, group in enumerate((near_out, far_out)):
+                        pltpu.make_async_copy(outv.at[s, :, pl.ds(h * half, half)], group[r].at[plan[ENTRY + s]], osem.at[h, s]).start()
 
         def backward(back, carry):
             s = slices - 1 - back
@@ -222,17 +223,18 @@
         step(0, 0, lambda m, i, re, im: leave(0, m, i, re, im))
         send(0)
         for s in range(slices):
-            pltpu.make_async_copy(outv.at[s], outs[0].at[0], osem.at[s]).wait()
+            for h in range(2):
+                pltpu.make_async_copy(outv.at[s, :, pl.ds(h * half, half)], near_out[0].at[0], osem.at[h, s]).wait()
 
 
 def chain(plan, places, probe, behind, messages, tables, rows):
     n = probe.shape[-1]
     slices = tables.shape[0] - 1
-    piece = jax.ShapeDtypeStruct(messages[0].shape, BF)
+    piece = jax.ShapeDtypeStruct((slices // 4, 2, n // 2, n), BF)
     return pl.pallas_call(
         functools.partial(chain_kernel, n=n, slices=slices, rows=rows),
         out_shape=(piece,) * 8,
-        in_specs=[SMEM, SMEM, VMEM] + [ANY] * 10,
+        in_specs=[SMEM, SMEM, VMEM] + [ANY] * 6,
         out_specs=(ANY,) * 8,
         scratch_shapes=[
             pltpu.VMEM((slices, 2, n, n), BF),
@@ -247,7 +249,7 @@
             pltpu.VMEM((2, n, n), F32),
             pltpu.SemaphoreType.DMA((slices,)),
             pltpu.SemaphoreType.DMA((slices + 1,)),
-            pltpu.SemaphoreType.DMA((slices,)),
+            pltpu.SemaphoreType.DMA((2, slices)),
             pltpu.SemaphoreType.DMA,
         ],
         compiler_params=pltpu.CompilerParams(vmem_limit_bytes=58 << 20),
@@ -264,15 +266,27 @@
     return jnp.where(lane >= offset % n, first, second)
 
 
-def own_windows_kernel(plan, places, tile, measured, tile_bf, wins, target, sem, *, n):
-    copy = pltpu.make_async_copy(measured.at[plan[OTHER]], target, sem)
-    copy.start()
-    rows = tile.shape[1]
-    tile_bf[...] = tile[...].astype(BF)
-    for p in range(places.shape[0]):
-        for c in range(2):
-            wins[p, c] = window(tile, c, places[p, 1], n).astype(BF)
-    copy.wait()
+def own_windows_kernel(places, tile_hbm, measured, tile_bf, wins, tile, target, sems, *, n, ahead_at, parts=4):
+    rows = tile_hbm.shape[1]
+    size = rows // parts
+    copies = [pltpu.make_async_copy(tile_hbm.at[:, pl.ds(q * size, size)], tile.at[:, pl.ds(q * size, size)], sems.at[q])
+              for q in range(parts)]
+    for copy in copies:
+        copy.start()
+    me = lax.axis_index("lat") % 2 * 16 + lax.axis_index("depth")
+    which = jnp.int32(0)
+    for at, position in enumerate(ahead_at):
+        which = jnp.where(me == at, jnp.int32(position), which)
+    wanted = pltpu.make_async_copy(measured.at[which], target, sems.at[parts])
+    wanted.start()
+    for q, copy in enumerate(copies):
+        copy.wait()
+        part = pl.ds(q * size, size)
+        tile_bf[:, part] = tile[:, part].astype(BF)
+        for p in range(places.shape[0]):
+            for c in range(2):
+                wins[p, c, part] = window(tile.at[:, part], c, places[p, 1], n).astype(BF)
+    wanted.wait()
     for c in range(2):
         x = target[c * rows:(c + 1) * rows]
         high = x.astype(BF)
@@ -280,48 +294,49 @@
         wins[places.shape[0] + 1, c] = (x - high.astype(F32)).astype(BF)
 
 
-def own_windows(plan, places, tile, measured, n):
+def own_windows(places, tile, measured, n):
     count = places.shape[0]
+    hbm = functools.partial(pltpu.with_memory_space_constraint, memory_space=pltpu.HBM)
+    ahead_at = tuple(int(x) for x in make_plan()[:, :, OTHER].ravel())
     return pl.pallas_call(
-        functools.partial(own_windows_kernel, n=n),
+        functools.partial(own_windows_kernel, n=n, ahead_at=ahead_at),
         out_shape=(jax.ShapeDtypeStruct(tile.shape, BF), jax.ShapeDtypeStruct((count + 2, 2, tile.shape[1], n), BF)),
-        in_specs=[SMEM, SMEM, VMEM, ANY],
+        in_specs=[SMEM, ANY, ANY],
         out_specs=(VMEM, VMEM),
-        scratch_shapes=[pltpu.VMEM((n, n), F32), pltpu.SemaphoreType.DMA],
+        scratch_shapes=[pltpu.VMEM(tile.shape, F32), pltpu.VMEM((n, n), F32), pltpu.SemaphoreType.DMA((5,))],
         compiler_params=pltpu.CompilerParams(vmem_limit_bytes=40 << 20),
-    )(plan, places, tile, measured)
-
-
-def merge_kernel(plan, places, behind, tile, ahead, even, odd, given, *, n):
+    )(places, hbm(tile), hbm(measured))
+
+
+def merge_kernel(plan, places, behind, tile, ahead, *outs, n):
     rows = tile.shape[1]
     row = lax.broadcasted_iota(jnp.int32, (rows, n), 0)
-    for k, out in enumerate((even.at[0], odd.at[0], given.at[0], given.at[1])):
+    for k in range(4):
         p = plan[ORDER + k]
         for c in range(2):
-            after = window(ahead, c, places[p, 1], n)
-            before = behind[p, c].astype(F32)
-            out[c, 0:rows] = jnp.where(row >= places[p, 0] % rows, before, after).astype(BF)
-            out[c, rows:2 * rows] = window(tile, c, places[p, 1], n).astype(BF)
+            far = window(ahead, c, places[p, 1], n)
+            near = behind[p, c].astype(F32)
+            outs[k][c, 0:rows] = jnp.where(row >= places[p, 0] % rows, near, far).astype(BF)
+            outs[k][c, rows:2 * rows] = window(tile, c, places[p, 1], n).astype(BF)
 
 
 def merge(plan, places, behind, tile, ahead, n):
-    shape = (2, 2 * tile.shape[1], n)
     return pl.pallas_call(
         functools.partial(merge_kernel, n=n),
-        out_shape=tuple(jax.ShapeDtypeStruct((k,) + shape, BF) for k in (1, 1, 2)),
+        out_shape=(jax.ShapeDtypeStruct((2, 2 * tile.shape[1], n), BF),) * 4,
         in_specs=[SMEM, SMEM, VMEM, VMEM, VMEM],
-        out_specs=(VMEM,) * 3,
+        out_specs=(VMEM,) * 4,
         compiler_params=pltpu.CompilerParams(vmem_limit_bytes=40 << 20),
     )(plan, places, behind, tile, ahead)
 
 
-def gather_kernel(plan, own_places, mid_places, far_places, from_own, even, odd, given, from_far, out, *, n):
+def gather_kernel(plan, own_places, mid_places, far_places, from_own, m0, m1, m2, m3, from_far, out, *, n):
     rows = out.shape[1]
     width = out.shape[-1]
     row = lax.broadcasted_iota(jnp.int32, (rows, n), 0)
     lane = lax.broadcasted_iota(jnp.int32, (rows, n), 1)
     out[...] = jnp.zeros_like(out)
-    mids = (even.at[0], odd.at[0], given.at[0], given.at[1])
+    mids = (m0, m1, m2, m3)
     for places, kind, order in ((own_places, 0, OTHER), (mid_places, 1, ORDER), (far_places, 2, OTHER)):
         for k in range(4):
             p = plan[order + k]
@@ -333,7 +348,7 @@
                 if kind == 0:
                     term = jnp.where(row >= shift, from_own[k, c].astype(F32), 0.0)
                 elif kind == 1:
-                    term = mids[k][c, rows:2 * rows].astype(F32)
+                    term = mids[k][c].astype(F32)
                 else:
                     term = jnp.where(row < shift, from_far[k, c].astype(F32), 0.0)
                 here = lane >= offset % n
@@ -346,7 +361,7 @@
     return pl.pallas_call(
         functools.partial(gather_kernel, n=n),
         out_shape=jax.ShapeDtypeStruct((2, rows, width), F32),
-        in_specs=[SMEM] * 4 + [VMEM] * 5,
+        in_specs=[SMEM] * 4 + [VMEM] * 6,
         out_specs=VMEM,
         compiler_params=pltpu.CompilerParams(vmem_limit_bytes=40 << 20),
     )(plan, own_places, mid_places, far_places, from_own, *mids, from_far)
@@ -357,29 +372,31 @@
     return lax.ppermute(block, "lat", [(i, (i + distance) % size) for i in range(size)])
 
 
-HANDLER, POSITION, EVEN, ODD, ORDER, OTHER, REL, ENTRY = 0, 1, 2, 3, 4, 8, 12, 28
-GOAL = (((0, 0, 0), (1, 0, 1), (2, 0, 0), (3, 0, 1)), ((1, 1, 0), (0, 1, 1), (3, 1, 0), (2, 1, 1)))
+HANDLER, POSITION, SOURCE, ORDER, OTHER, REL, ENTRY = 0, 1, 2, 3, 7, 11, 27
+GOAL = (((0, 0), (1, 1), (2, 0), (3, 1)), ((1, 2), (0, 3), (3, 2), (2, 3)))
 
 
 def meet(c, team, j):
-    goal, lo, _ = GOAL[c][j]
-    return lo if (team - goal) % 4 in ((0, 1), (0, 3))[c] else 1 - lo
+    goal, inner = GOAL[c][j]
+    flip = inner ^ 2
+    if c == 0:
+        return inner if (team - goal) % 4 in (0, 1) else flip
+    return inner if (team - goal) % 4 in (0, 3) else flip
 
 
 def place_of(c, d):
     v = (d + 2 * c) % 16
-    return v // 4, v // 2 % 2, v % 2
-
-
-def device_of(c, team, lo, y):
-    return (4 * team + 2 * lo + y - 2 * c) % 16
-
-
-def kept(c, team, lo):
-    found = [(j, (team - GOAL[c][j][0]) % 4) for j in range(4) if meet(c, team, j) == lo]
-    found.sort(key=lambda x: x[1] % 2)
-    assert [k % 2 for _, k in found] == [0, 1]
-    return found
+    return v // 4, v % 4
+
+
+def position_at(c, team, inner):
+    found = [j for j in range(4) if meet(c, team, j) == inner]
+    assert len(found) == 1
+    return found[0]
+
+
+def device_of(c, team, inner):
+    return (4 * team + inner - 2 * c) % 16
 
 
 @functools.lru_cache
@@ -387,20 +404,19 @@
     out = np.zeros((2, 16, 48), np.int32)
     for c in range(2):
         for d in range(16):
-            team, lo, y = place_of(c, d)
+            team, inner = place_of(c, d)
+            j = position_at(c, team, inner)
             row = out[c, d]
-            (even, near), (odd, far) = kept(c, team, lo)
-            row[EVEN] = 2 * near + (y ^ GOAL[c][even][2])
-            row[ODD] = 2 * far + (y ^ GOAL[c][odd][2])
-            j = even
-            row[HANDLER] = GOAL[c][j] == (team, lo, y)
+            row[HANDLER] = GOAL[c][j] == (team, inner)
             row[POSITION] = j
-            row[ORDER:ORDER + 4] = [even, odd] + [j for j, _ in kept(c, team, 1 - lo)]
-            team2, lo2, _ = place_of(1 - c, d)
-            row[OTHER:OTHER + 4] = [j for j, _ in kept(1 - c, team2, lo2) + kept(1 - c, team2, 1 - lo2)]
+            row[SOURCE] = (team - GOAL[c][j][0]) % 4
+            other = place_of(1 - c, d)
+            for k in range(4):
+                row[ORDER + k] = position_at(c, team, inner ^ k)
+                row[OTHER + k] = position_at(1 - c, other[0], other[1] ^ k)
             for s in range(16):
-                there, at, side = place_of(c, s)
-                row[REL + s] = 2 * ((there - team) % 4) + (side ^ y)
+                there, at = place_of(c, s)
+                row[REL + s] = (there - team) % 4
                 row[ENTRY + s] = at ^ meet(c, there, j)
     return out
 
@@ -416,26 +432,22 @@
     return lax.ppermute(block, ("depth", "lat"), pairs)
 
 
-def across(block):
-    return permute(block, lambda c, team, lo, y: (team, 1 - lo, y))
-
-
-def towards(block, k, e):
-    def route(c, team, lo, y):
-        for j, away in kept(c, team, lo):
-            if away == k and y ^ e == GOAL[c][j][2]:
-                return GOAL[c][j]
-        return None
+def within(block, k):
+    return permute(block, lambda c, team, inner: (team, inner ^ k))
+
+
+def towards(block, k):
+    def route(c, team, inner):
+        goal = GOAL[c][position_at(c, team, inner)]
+        return goal if (team - goal[0]) % 4 == k else None
     return permute(block, route)
 
 
-def away(block, k, e):
-    def route(c, team, lo, y):
-        for j in range(4):
-            if GOAL[c][j] == (team, lo, y):
-                there = (team + k) % 4
-                return there, meet(c, there, j), y ^ e
-        return None
+def away(block, k):
+    def route(c, team, inner):
+        j = position_at(c, team, inner)
+        there = (team + k) % 4
+        return (there, meet(c, there, j)) if GOAL[c][j] == (team, inner) else None
     return permute(block, route)
 
 
@@ -448,35 +460,32 @@
     plan = lax.dynamic_slice(jnp.asarray(make_plan()), (m % 2, d, 0), (1, 1, 48)).reshape(48)
     tile = object_slices[0]
 
-    tile_bf, mine = own_windows(plan, positions, tile, measured, n)
+    tile_bf, mine = own_windows(positions, tile, measured, n)
     ahead = shifted(tile_bf, -1)
     behind = shifted(mine, 1)
     mid_places = shifted(positions, 1)
     far_places = shifted(positions, 2)
     mid_places, far_places, ahead, behind = lax.optimization_barrier((mid_places, far_places, ahead, behind))
-    even, odd, given = merge(plan, mid_places, behind, tile_bf, ahead, n)
-
-    got = across(given)
-    kinds = (jnp.concatenate([even, got[0:1]]), jnp.concatenate([odd, got[1:2]]))
-    order = [(2, 0), (1, 0), (3, 0), (2, 1), (1, 1), (3, 1), (0, 1)]
-    messages = {(k, e): towards(kinds[k % 2], k, e) for k, e in order}
-    messages[0, 0] = kinds[0]
+    parts = merge(plan, mid_places, behind, tile_bf, ahead, n)
+
+    message = jnp.stack([parts[0]] + [within(parts[k], k) for k in (1, 2, 3)])
+    messages = [message] + [towards(message, k) for k in (1, 2, 3)]
     tables = make_tables(n, depth_size)
-    slots = [(k, e) for k in range(4) for e in range(2)]
-    terms = dict(zip(slots, chain(plan, mid_places, probe, behind, [messages[x] for x in slots], tables, rows)))
-
-    got = {x: away(terms[x], *x) for x in order}
-    even = terms[0, 0]
-    for k, e in ((0, 1), (2, 0), (2, 1)):
-        even = jnp.where(plan[EVEN] == 2 * k + e, got[k, e], even)
-    odd = got[1, 0]
-    for k, e in ((1, 1), (3, 0), (3, 1)):
-        odd = jnp.where(plan[ODD] == 2 * k + e, got[k, e], odd)
-    given = across(jnp.stack([even[1], odd[1]]))
-    mixed = jnp.stack([even[0, :, :rows], odd[0, :, :rows], given[0, :, :rows], given[1, :, :rows]])
+    terms = chain(plan, mid_places, probe, behind, messages, tables, rows)
+
+    def home(pieces):
+        block = pieces[0]
+        for k in (1, 2, 3):
+            block = jnp.where(plan[SOURCE] == k, away(pieces[k], k), block)
+        return block
+
+    near_block = home(terms[:4])
+    far_block = home(terms[4:])
+    mixed = jnp.stack([near_block[0]] + [within(near_block[k], k) for k in (1, 2, 3)])
+    mids = [far_block[0]] + [within(far_block[k], k) for k in (1, 2, 3)]
     from_own = shifted(mixed, -1)
     from_far = shifted(mixed, 1)
-    total = gather_terms(plan, positions, mid_places, far_places, from_own, (even, odd, given), from_far, rows, width)
+    total = gather_terms(plan, positions, mid_places, far_places, from_own, mids, from_far, rows, width)
     return total[None]
 
 

time: 172 us -> 158 us (0.919)
  the two profiles are of different devices: /device:TPU:8 before, /device:TPU:1 now
where the time goes in v6:
time: 158 us; the launch traced here: 156 us
  waiting for transfers between devices  79.2 us (50%)
  starting transfers between devices  49 us (31%)
  Pallas kernels  20 us (13%)
  local copies, waits for them, and re-layouts  3.78 us (2%)
  between operations  2.2 us (1%)
    ppermute x18, waiting for transfers between devices, permute(): return lax.ppermute(block, ('depth', 'lat'), pairs)  66.2 us
    ppermute x18, starting transfers between devices, permute(): return lax.ppermute(block, ('depth', 'lat'), pairs)  39.9 us
    ppermute x6, waiting for transfers between devices, shifted(): lax.ppermute(block, 'lat', [(i, (i + distance) % size) for i in range(siz...  13.1 us
    pallas_call x1, Pallas kernels, make_tables(): pl.pallas_call(functools.partial(tables_kernel, n=n, slices=slices), grid...  11.1 us
    ppermute x6, starting transfers between devices, shifted(): lax.ppermute(block, 'lat', [(i, (i + distance) % size) for i in range(siz...  9.08 us
  transfers between devices with their start and end apart: 24, of which 10 were waited for; matrix products, arithmetic and copies ran while one was open for 2% of the time, Pallas kernels for 7%

profile of v6, /device:TPU:1, one launch (start us, length us, event | category | flops | bytes accessed | tf_op | source)
XLA Modules:
  0.0 155.7 jit_solution(5717540918251968355)
XLA Ops:
  0.0 0.8 copy.11.places.own_places
  0.8 3.1 %shard_map.73 = (bf16[2,128,2048]{2,1,0:T(8,128)(2,1)S(1)}, bf16[6,2,128,256]{3,2,1,0:T(8,128)(2,1)}) custom-call(s32[4,2]{1,0:T(4,128)S(1)} %copy.11.places.own_places, f32[2,128,2048]{2,1,0:T(8,128)} %bitcast.29, f32[4,256,256]{2,1,0:T(8,128)} %measured.1), custom_call_target="tpu_custom_call" | custom-call | tf_op jit(solution)/shard_map/pallas_call | solution.py:301
  3.9 3.3 %collective-permute-start.2 = (bf16[2,128,2048]{2,1,0:T(8,128)(2,1)S(1)}, bf16[2,128,2048]{2,1,0:T(8,128)(2,1)S(1)}, u32[]{:S(2)}, u32[]{:S(2)}) collective-permute-start(bf16[2,128,2048]{2,1,0:T(8,128)(2,1)S(1)} %get-tuple-element.23.tile), channel_id=1, source_target_pairs={{0,15},{1,0},{2,1},{3,2},{4,3},{5,4},{6,5},{7,6},{8,7},{9,8},{10,9... | collective-permute-start | bytes 3145736 | tf_op jit(solution)/shard_map/ppermute | solution.py:372
  7.2 0.0 collective-permute-start.3
  7.2 0.0 collective-permute-start
  7.2 1.1 collective-permute-start.1
  8.3 0.7 fusion.1.plan.refs_0_
  9.0 7.5 %collective-permute-done.places.refs_1_.mid_places = s32[4,2]{1,0:T(4,128)S(1)} collective-permute-done((s32[4,2]{1,0:T(4,128)S(1)}, s32[4,2]{1,0:T(4,128)S(1)}, u32[]{:S(2)}, u32[]{:S(2)}) %collective-permute-start) | collective-permute-done | bytes 64 | tf_op jit(solution)/shard_map/ppermute | solution.py:372
  16.5 5.6 %collective-permute-done.1.far_places = s32[4,2]{1,0:T(4,128)S(1)} collective-permute-done((s32[4,2]{1,0:T(4,128)S(1)}, s32[4,2]{1,0:T(4,128)S(1)}, u32[]{:S(2)}, u32[]{:S(2)}) %collective-permute-start.1) | collective-permute-done | bytes 64 | tf_op jit(solution)/shard_map/ppermute | solution.py:372
  22.1 0.0 collective-permute-done.3.behind.refs_3_
  22.1 0.0 collective-permute-done.2.ahead
  22.1 0.9 shard_map.74
  23.0 8.0 %collective-permute-start.6 = (bf16[2,256,256]{2,1,0:T(8,128)(2,1)S(1)}, bf16[2,256,256]{2,1,0:T(8,128)(2,1)S(1)}, u32[]{:S(2)}, u32[]{:S(2)}) collective-permute-start(bf16[2,256,256]{2,1,0:T(8,128)(2,1)S(1)} %get-tuple-element.32), channel_id=1, source_target_pairs={{0,48},{1,241},{2,50},{3,243},{4,52},{5,245},{6,54},{7,247},{8,56}... | collective-permute-start | bytes 786440 | tf_op jit(solution)/shard_map/ppermute | solution.py:432
  31.0 0.0 collective-permute-start.5
  31.0 0.4 collective-permute-start.4
  31.4 3.6 %collective-permute-done.6 = bf16[2,256,256]{2,1,0:T(8,128)(2,1)S(1)} collective-permute-done((bf16[2,256,256]{2,1,0:T(8,128)(2,1)S(1)}, bf16[2,256,256]{2,1,0:T(8,128)(2,1)S(1)}, u32[]{:S(2)}, u32[]{:S(2)}) %collective-permute-start.6) | collective-permute-done | bytes 262176 | tf_op jit(solution)/shard_map/ppermute | solution.py:432
  35.0 2.8 %collective-permute-done.5 = bf16[2,256,256]{2,1,0:T(8,128)(2,1)S(1)} collective-permute-done((bf16[2,256,256]{2,1,0:T(8,128)(2,1)S(1)}, bf16[2,256,256]{2,1,0:T(8,128)(2,1)S(1)}, u32[]{:S(2)}, u32[]{:S(2)}) %collective-permute-start.5) | collective-permute-done | bytes 262176 | tf_op jit(solution)/shard_map/ppermute | solution.py:432
  37.8 2.7 %collective-permute-done.4 = bf16[2,256,256]{2,1,0:T(8,128)(2,1)S(1)} collective-permute-done((bf16[2,256,256]{2,1,0:T(8,128)(2,1)S(1)}, bf16[2,256,256]{2,1,0:T(8,128)(2,1)S(1)}, u32[]{:S(2)}, u32[]{:S(2)}) %collective-permute-start.4) | collective-permute-done | bytes 262176 | tf_op jit(solution)/shard_map/ppermute | solution.py:432
  40.5 0.1 pad_maximum_fusion.refs_4_
  40.7 0.0 copy-start.5
  40.7 0.7 collective-permute-start.7
  41.4 1.7 %collective-permute-start.8 = (bf16[4,2,256,256]{3,2,1,0:T(8,128)(2,1)S(1)}, bf16[4,2,256,256]{3,2,1,0:T(8,128)(2,1)}, u32[]{:S(2)}, u32[]{:S(2)}) collective-permute-start(bf16[4,2,256,256]{3,2,1,0:T(8,128)(2,1)S(1)} %pad_maximum_fusion.refs_4_), channel_id=1, source_target_pairs={{32,128},{33,193},{34,130},{35,195},{36,132},{37,197},{38,134},{39... | collective-permute-start | bytes 3145736 | tf_op jit(solution)/shard_map/ppermute | solution.py:432
  43.1 4.9 %collective-permute-start.9 = (bf16[4,2,256,256]{3,2,1,0:T(8,128)(2,1)S(1)}, bf16[4,2,256,256]{3,2,1,0:T(8,128)(2,1)}, u32[]{:S(2)}, u32[]{:S(2)}) collective-permute-start(bf16[4,2,256,256]{3,2,1,0:T(8,128)(2,1)S(1)} %pad_maximum_fusion.refs_4_), channel_id=1, source_target_pairs={{1,65},{3,67},{5,69},{7,71},{9,73},{11,75},{13,77},{15,79},{48,80}... | collective-permute-start | bytes 3145736 | tf_op jit(solution)/shard_map/ppermute | solution.py:432
  48.0 11.1 %shard_map.75.refs_8_ = bf16[17,2,512,512]{3,2,1,0:T(8,128)(2,1)} custom-call(f32[2,17]{1,0:T(2,128)} %constant.38.clone.scales, f32[4,256,256]{2,1,0:T(8,128)} %constant.39.clone.base), custom_call_target="tpu_custom_call" | custom-call | tf_op jit(solution)/shard_map/pallas_call | solution.py:49
  59.1 0.0 copy-done.5
  59.1 0.0 collective-permute-done.7.refs_5_
  59.2 0.0 collective-permute-done.8.refs_6_
  59.2 0.0 collective-permute-done.9.refs_7_
  59.2 0.9 copy-done.6
  60.1 1.8 %shard_map.76 = (bf16[4,2,128,256]{3,2,1,0:T(8,128)(2,1)}, bf16[4,2,128,256]{3,2,1,0:T(8,128)(2,1)}, bf16[4,2,128,256]{3,2,1,0:T(8,128)(2,1)}, bf16[4,2,128,256]...) custom-call(s32[48]{0:T(128)} %copy-done.3, ...), custom_call_target="tpu_custom_call" | custom-call | tf_op jit(solution)/shard_map/pallas_call | solution.py:234
  61.9 1.3 collective-permute-start.10
  63.2 0.7 collective-permute-start.11
  64.0 0.7 collective-permute-start.12
  64.7 0.7 constant_dynamic-slice_fusion
  65.4 0.6 slice.33
  67.9 1.3 collective-permute-start.17
  69.2 0.7 collective-permute-start.18
  69.9 42.1 %collective-permute-done.10 = bf16[4,2,128,256]{3,2,1,0:T(8,128)(2,1)S(1)} collective-permute-done((bf16[4,2,128,256]{3,2,1,0:T(8,128)(2,1)}, bf16[4,2,128,256]{3,2,1,0:T(8,128)(2,1)S(1)}, u32[]{:S(2)}, u32[]{:S(2)}) %collective-permute-start.10) | collective-permute-done | bytes 524320 | tf_op jit(solution)/shard_map/ppermute | solution.py:432
  112.0 0.7 collective-permute-start.19
  112.6 0.0 collective-permute-done.11
  112.7 0.0 collective-permute-done.12
  112.7 1.2 select_select_fusion.1
  113.9 7.0 %collective-permute-start.15 = (bf16[2,128,256]{2,1,0:T(8,128)(2,1)S(1)}, bf16[2,128,256]{2,1,0:T(8,128)(2,1)S(1)}, u32[]{:S(2)}, u32[]{:S(2)}) collective-permute-start(bf16[2,128,256]{2,1,0:T(8,128)(2,1)S(1)} %get-tuple-element.46), channel_id=1, source_target_pairs={{0,48},{1,241},{2,50},{3,243},{4,52},{5,245},{6,54},{7,247},{8,56}... | collective-permute-start | bytes 393224 | tf_op jit(solution)/shard_map/ppermute | solution.py:432
  120.9 0.4 collective-permute-start.14
  121.3 5.4 %collective-permute-done.15 = bf16[2,128,256]{2,1,0:T(8,128)(2,1)S(1)} collective-permute-done((bf16[2,128,256]{2,1,0:T(8,128)(2,1)S(1)}, bf16[2,128,256]{2,1,0:T(8,128)(2,1)S(1)}, u32[]{:S(2)}, u32[]{:S(2)}) %collective-permute-start.15) | collective-permute-done | bytes 131104 | tf_op jit(solution)/shard_map/ppermute | solution.py:432
  126.7 0.7 collective-permute-start.13
  127.4 0.0 collective-permute-done.14
  127.4 4.7 %collective-permute-done.13 = bf16[2,128,256]{2,1,0:T(8,128)(2,1)S(1)} collective-permute-done((bf16[2,128,256]{2,1,0:T(8,128)(2,1)S(1)}, bf16[2,128,256]{2,1,0:T(8,128)(2,1)S(1)}, u32[]{:S(2)}, u32[]{:S(2)}) %collective-permute-start.13) | collective-permute-done | bytes 131104 | tf_op jit(solution)/shard_map/ppermute | solution.py:432
  132.1 0.1 pad_maximum_fusion.1
  132.1 4.7 %collective-permute-start.16 = (bf16[4,2,128,256]{3,2,1,0:T(8,128)(2,1)S(1)}, bf16[4,2,128,256]{3,2,1,0:T(8,128)(2,1)S(1)}, u32[]{:S(2)}, u32[]{:S(2)}) collective-permute-start(bf16[4,2,128,256]{3,2,1,0:T(8,128)(2,1)S(1)} %pad_maximum_fusion.1), channel_id=1, source_target_pairs={{0,15},{1,0},{2,1},{3,2},{4,3},{5,4},{6,5},{7,6},{8,7},{9,8},{10,9... | collective-permute-start | bytes 1572872 | tf_op jit(solution)/shard_map/ppermute | solution.py:372
  136.8 0.0 collective-permute-start.23
  136.8 0.0 collective-permute-done.17
  136.8 0.0 collective-permute-done.18
  136.8 0.0 collective-permute-done.19
  136.8 0.1 select_select_fusion
  137.0 3.3 %collective-permute-start.20 = (bf16[2,128,256]{2,1,0:T(8,128)(2,1)S(1)}, bf16[2,128,256]{2,1,0:T(8,128)(2,1)S(1)}, u32[]{:S(2)}, u32[]{:S(2)}) collective-permute-start(bf16[2,128,256]{2,1,0:T(8,128)(2,1)S(1)} %get-tuple-element.43), channel_id=1, source_target_pairs={{0,16},{1,17},{2,18},{3,19},{4,20},{5,21},{6,22},{7,23},{8,24},{9,... | collective-permute-start | bytes 393224 | tf_op jit(solution)/shard_map/ppermute | solution.py:432
  140.3 5.0 %collective-permute-start.21 = (bf16[2,128,256]{2,1,0:T(8,128)(2,1)S(1)}, bf16[2,128,256]{2,1,0:T(8,128)(2,1)S(1)}, u32[]{:S(2)}, u32[]{:S(2)}) collective-permute-start(bf16[2,128,256]{2,1,0:T(8,128)(2,1)S(1)} %get-tuple-element.42), channel_id=1, source_target_pairs={{0,32},{1,225},{2,34},{3,227},{4,36},{5,229},{6,38},{7,231},{8,40}... | collective-permute-start | bytes 393224 | tf_op jit(solution)/shard_map/ppermute | solution.py:432
  145.3 2.6 %collective-permute-start.22 = (bf16[2,128,256]{2,1,0:T(8,128)(2,1)S(1)}, bf16[2,128,256]{2,1,0:T(8,128)(2,1)S(1)}, u32[]{:S(2)}, u32[]{:S(2)}) collective-permute-start(bf16[2,128,256]{2,1,0:T(8,128)(2,1)S(1)} %get-tuple-element.41), channel_id=1, source_target_pairs={{0,48},{1,241},{2,50},{3,243},{4,52},{5,245},{6,54},{7,247},{8,56}... | collective-permute-start | bytes 393224 | tf_op jit(solution)/shard_map/ppermute | solution.py:432
  147.9 2.1 %collective-permute-done.20.m1 = bf16[2,128,256]{2,1,0:T(8,128)(2,1)S(1)} collective-permute-done((bf16[2,128,256]{2,1,0:T(8,128)(2,1)S(1)}, bf16[2,128,256]{2,1,0:T(8,128)(2,1)S(1)}, u32[]{:S(2)}, u32[]{:S(2)}) %collective-permute-start.20) | collective-permute-done | bytes 131104 | tf_op jit(solution)/shard_map/ppermute | solution.py:432
  150.0 0.0 collective-permute-done.21.m2
  150.0 2.7 %collective-permute-done.22.m3 = bf16[2,128,256]{2,1,0:T(8,128)(2,1)S(1)} collective-permute-done((bf16[2,128,256]{2,1,0:T(8,128)(2,1)S(1)}, bf16[2,128,256]{2,1,0:T(8,128)(2,1)S(1)}, u32[]{:S(2)}, u32[]{:S(2)}) %collective-permute-start.22) | collective-permute-done | bytes 131104 | tf_op jit(solution)/shard_map/ppermute | solution.py:432
  152.7 0.0 collective-permute-done.16.from_own
  152.7 0.0 collective-permute-done.23.from_far
  152.7 3.0 %shard_map.77 = f32[2,128,2048]{2,1,0:T(8,128)} custom-call(s32[48]{0:T(128)S(1)} %copy-done.4, s32[4,2]{1,0:T(4,128)S(1)} %copy.11.places.own_places, s32[4,2]{1,0:T(4,128)S(1)} %copy-done.2, s32[4,2]{1,0:T(4,128)S(1)} %collective-permute-done.1.far_places, bf16[4,2,128,256]{3,2,1,0:T(8,128)(2,1)S(1)} %collective-permute-done.16.from_own, ...), custom_call_target="tpu_custom_call" | custom-call | tf_op jit(solution)/shard_map/pallas_call | solution.py:361
  (15 shorter events, 0.1 us)
Async XLA Ops:
  3.9 18.2 %collective-permute-start.2 = (bf16[2,128,2048]{2,1,0:T(8,128)(2,1)S(1)}, bf16[2,128,2048]{2,1,0:T(8,128)(2,1)S(1)}, u32[]{:S(2)}, u32[]{:S(2)}) collective-permute-start(bf16[2,128,2048]{2,1,0:T(8,128)(2,1)S(1)} %get-tuple-element.23.tile), channel_id=1, source_target_pairs={{0,15},{1,0},{2,1},{3,2},{4,3},{5,4},{6,5},{7,6},{8,7},{9,8},{10,9... | collective-permute-start | bytes 3145736 | tf_op jit(solution)/shard_map/ppermute | solution.py:372
  7.2 14.9 %collective-permute-start.3 = (bf16[6,2,128,256]{3,2,1,0:T(8,128)(2,1)}, bf16[6,2,128,256]{3,2,1,0:T(8,128)(2,1)S(1)}, u32[]{:S(2)}, u32[]{:S(2)}) collective-permute-start(bf16[6,2,128,256]{3,2,1,0:T(8,128)(2,1)} %get-tuple-element.24), channel_id=1, source_target_pairs={{0,1},{1,2},{2,3},{3,4},{4,5},{5,6},{6,7},{7,8},{8,9},{9,10},{10,1... | collective-permute-start | bytes 2359304 | tf_op jit(solution)/shard_map/ppermute | solution.py:372
  7.2 9.3 %collective-permute-start = (s32[4,2]{1,0:T(4,128)S(1)}, s32[4,2]{1,0:T(4,128)S(1)}, u32[]{:S(2)}, u32[]{:S(2)}) collective-permute-start(s32[4,2]{1,0:T(4,128)S(1)} %copy.11.places.own_places), channel_id=1, source_target_pairs={{0,1},{1,2},{2,3},{3,4},{4,5},{5,6},{6,7},{7,8},{8,9},{9,10},{10,1... | collective-permute-start | bytes 104 | tf_op jit(solution)/shard_map/ppermute | solution.py:372
  7.2 14.9 %collective-permute-start.1 = (s32[4,2]{1,0:T(4,128)S(1)}, s32[4,2]{1,0:T(4,128)S(1)}, u32[]{:S(2)}, u32[]{:S(2)}) collective-permute-start(s32[4,2]{1,0:T(4,128)S(1)} %copy.11.places.own_places), channel_id=1, source_target_pairs={{0,2},{1,3},{2,4},{3,5},{4,6},{5,7},{6,8},{7,9},{8,10},{9,11},{10,... | collective-permute-start | bytes 104 | tf_op jit(solution)/shard_map/ppermute | solution.py:372
  9.0 31.7 %copy-start.3 = (s32[48]{0:T(128)}, s32[48]{0:T(128)S(1)}, u32[]{:S(2)}) copy-start(s32[48]{0:T(128)S(1)} %fusion.1.plan.refs_0_) | copy-start | bytes 580
  16.5 24.2 %copy-start.1 = (s32[4,2]{1,0:T(4,128)}, s32[4,2]{1,0:T(4,128)S(1)}, u32[]{:S(2)}) copy-start(s32[4,2]{1,0:T(4,128)S(1)} %collective-permute-done.places.refs_1_.mid_places) | copy-start | bytes 100
  22.1 18.6 %copy-start = (bf16[6,2,128,256]{3,2,1,0:T(8,128)(2,1)}, bf16[6,2,128,256]{3,2,1,0:T(8,128)(2,1)S(1)}, u32[]{:S(2)}) copy-start(bf16[6,2,128,256]{3,2,1,0:T(8,128)(2,1)S(1)} %collective-permute-done.3.behind.refs_3_) | copy-start | bytes 2359300
  23.0 12.0 %collective-permute-start.6 = (bf16[2,256,256]{2,1,0:T(8,128)(2,1)S(1)}, bf16[2,256,256]{2,1,0:T(8,128)(2,1)S(1)}, u32[]{:S(2)}, u32[]{:S(2)}) collective-permute-start(bf16[2,256,256]{2,1,0:T(8,128)(2,1)S(1)} %get-tuple-element.32), channel_id=1, source_target_pairs={{0,48},{1,241},{2,50},{3,243},{4,52},{5,245},{6,54},{7,247},{8,56}... | collective-permute-start | bytes 786440 | tf_op jit(solution)/shard_map/ppermute | solution.py:432
  31.0 6.8 %collective-permute-start.5 = (bf16[2,256,256]{2,1,0:T(8,128)(2,1)S(1)}, bf16[2,256,256]{2,1,0:T(8,128)(2,1)S(1)}, u32[]{:S(2)}, u32[]{:S(2)}) collective-permute-start(bf16[2,256,256]{2,1,0:T(8,128)(2,1)S(1)} %get-tuple-element.31), channel_id=1, source_target_pairs={{0,32},{1,225},{2,34},{3,227},{4,36},{5,229},{6,38},{7,231},{8,40}... | collective-permute-start | bytes 786440 | tf_op jit(solution)/shard_map/ppermute | solution.py:432
  31.0 9.5 %collective-permute-start.4 = (bf16[2,256,256]{2,1,0:T(8,128)(2,1)S(1)}, bf16[2,256,256]{2,1,0:T(8,128)(2,1)S(1)}, u32[]{:S(2)}, u32[]{:S(2)}) collective-permute-start(bf16[2,256,256]{2,1,0:T(8,128)(2,1)S(1)} %get-tuple-element.30), channel_id=1, source_target_pairs={{0,16},{1,17},{2,18},{3,19},{4,20},{5,21},{6,22},{7,23},{8,24},{9,... | collective-permute-start | bytes 786440 | tf_op jit(solution)/shard_map/ppermute | solution.py:432
  40.7 18.5 %copy-start.5 = (bf16[4,2,256,256]{3,2,1,0:T(8,128)(2,1)}, bf16[4,2,256,256]{3,2,1,0:T(8,128)(2,1)S(1)}, u32[]{:S(2)}) copy-start(bf16[4,2,256,256]{3,2,1,0:T(8,128)(2,1)S(1)} %pad_maximum_fusion.refs_4_) | copy-start | bytes 3145732
  40.7 18.4 %collective-permute-start.7 = (bf16[4,2,256,256]{3,2,1,0:T(8,128)(2,1)S(1)}, bf16[4,2,256,256]{3,2,1,0:T(8,128)(2,1)S(1)}, u32[]{:S(2)}, u32[]{:S(2)}) collective-permute-start(bf16[4,2,256,256]{3,2,1,0:T(8,128)(2,1)S(1)} %pad_maximum_fusion.refs_4_), channel_id=1, source_target_pairs={{16,208},{18,210},{20,212},{22,214},{24,216},{26,218},{28,220},{30... | collective-permute-start | bytes 3145736 | tf_op jit(solution)/shard_map/ppermute | solution.py:432
  41.4 17.7 %collective-permute-start.8 = (bf16[4,2,256,256]{3,2,1,0:T(8,128)(2,1)S(1)}, bf16[4,2,256,256]{3,2,1,0:T(8,128)(2,1)}, u32[]{:S(2)}, u32[]{:S(2)}) collective-permute-start(bf16[4,2,256,256]{3,2,1,0:T(8,128)(2,1)S(1)} %pad_maximum_fusion.refs_4_), channel_id=1, source_target_pairs={{32,128},{33,193},{34,130},{35,195},{36,132},{37,197},{38,134},{39... | collective-permute-start | bytes 3145736 | tf_op jit(solution)/shard_map/ppermute | solution.py:432
  43.1 16.1 %collective-permute-start.9 = (bf16[4,2,256,256]{3,2,1,0:T(8,128)(2,1)S(1)}, bf16[4,2,256,256]{3,2,1,0:T(8,128)(2,1)}, u32[]{:S(2)}, u32[]{:S(2)}) collective-permute-start(bf16[4,2,256,256]{3,2,1,0:T(8,128)(2,1)S(1)} %pad_maximum_fusion.refs_4_), channel_id=1, source_target_pairs={{1,65},{3,67},{5,69},{7,71},{9,73},{11,75},{13,77},{15,79},{48,80}... | collective-permute-start | bytes 3145736 | tf_op jit(solution)/shard_map/ppermute | solution.py:432
  59.2 1.0 copy-start.6
  61.9 50.0 %collective-permute-start.10 = (bf16[4,2,128,256]{3,2,1,0:T(8,128)(2,1)}, bf16[4,2,128,256]{3,2,1,0:T(8,128)(2,1)S(1)}, u32[]{:S(2)}, u32[]{:S(2)}) collective-permute-start(bf16[4,2,128,256]{3,2,1,0:T(8,128)(2,1)} %get-tuple-element.33), channel_id=1, source_target_pairs={{0,224},{2,226},{4,228},{6,230},{8,232},{10,234},{12,236},{14,238}... | collective-permute-start | bytes 1572872 | tf_op jit(solution)/shard_map/ppermute | solution.py:432
  63.2 49.4 %collective-permute-start.11 = (bf16[4,2,128,256]{3,2,1,0:T(8,128)(2,1)}, bf16[4,2,128,256]{3,2,1,0:T(8,128)(2,1)S(1)}, u32[]{:S(2)}, u32[]{:S(2)}) collective-permute-start(bf16[4,2,128,256]{3,2,1,0:T(8,128)(2,1)} %get-tuple-element.34), channel_id=1, source_target_pairs={{0,160},{2,162},{4,164},{6,166},{8,168},{10,170},{12,172},{14,174}... | collective-permute-start | bytes 1572872 | tf_op jit(solution)/shard_map/ppermute | solution.py:432
  64.0 48.7 %collective-permute-start.12 = (bf16[4,2,128,256]{3,2,1,0:T(8,128)(2,1)}, bf16[4,2,128,256]{3,2,1,0:T(8,128)(2,1)S(1)}, u32[]{:S(2)}, u32[]{:S(2)}) collective-permute-start(bf16[4,2,128,256]{3,2,1,0:T(8,128)(2,1)} %get-tuple-element.35), channel_id=1, source_target_pairs={{0,64},{2,66},{4,68},{6,70},{8,72},{10,74},{12,76},{14,78},{17,49}... | collective-permute-start | bytes 1572872 | tf_op jit(solution)/shard_map/ppermute | solution.py:432
  67.9 68.9 %collective-permute-start.17 = (bf16[4,2,128,256]{3,2,1,0:T(8,128)(2,1)}, bf16[4,2,128,256]{3,2,1,0:T(8,128)(2,1)S(1)}, u32[]{:S(2)}, u32[]{:S(2)}) collective-permute-start(bf16[4,2,128,256]{3,2,1,0:T(8,128)(2,1)} %get-tuple-element.37), channel_id=1, source_target_pairs={{0,224},{2,226},{4,228},{6,230},{8,232},{10,234},{12,236},{14,238}... | collective-permute-start | bytes 1572872 | tf_op jit(solution)/shard_map/ppermute | solution.py:432
  69.2 67.6 %collective-permute-start.18 = (bf16[4,2,128,256]{3,2,1,0:T(8,128)(2,1)}, bf16[4,2,128,256]{3,2,1,0:T(8,128)(2,1)S(1)}, u32[]{:S(2)}, u32[]{:S(2)}) collective-permute-start(bf16[4,2,128,256]{3,2,1,0:T(8,128)(2,1)} %get-tuple-element.38), channel_id=1, source_target_pairs={{0,160},{2,162},{4,164},{6,166},{8,168},{10,170},{12,172},{14,174}... | collective-permute-start | bytes 1572872 | tf_op jit(solution)/shard_map/ppermute | solution.py:432
  112.0 24.9 %collective-permute-start.19 = (bf16[4,2,128,256]{3,2,1,0:T(8,128)(2,1)}, bf16[4,2,128,256]{3,2,1,0:T(8,128)(2,1)S(1)}, u32[]{:S(2)}, u32[]{:S(2)}) collective-permute-start(bf16[4,2,128,256]{3,2,1,0:T(8,128)(2,1)} %get-tuple-element.39), channel_id=1, source_target_pairs={{0,64},{2,66},{4,68},{6,70},{8,72},{10,74},{12,76},{14,78},{17,49}... | collective-permute-start | bytes 1572872 | tf_op jit(solution)/shard_map/ppermute | solution.py:432
  112.7 24.2 %copy-start.7 = (bf16[4,2,128,256]{3,2,1,0:T(8,128)(2,1)S(1)}, bf16[4,2,128,256]{3,2,1,0:T(8,128)(2,1)}, u32[]{:S(2)}) copy-start(bf16[4,2,128,256]{3,2,1,0:T(8,128)(2,1)} %get-tuple-element.40) | copy-start | bytes 1572868
  113.9 12.8 %collective-permute-start.15 = (bf16[2,128,256]{2,1,0:T(8,128)(2,1)S(1)}, bf16[2,128,256]{2,1,0:T(8,128)(2,1)S(1)}, u32[]{:S(2)}, u32[]{:S(2)}) collective-permute-start(bf16[2,128,256]{2,1,0:T(8,128)(2,1)S(1)} %get-tuple-element.46), channel_id=1, source_target_pairs={{0,48},{1,241},{2,50},{3,243},{4,52},{5,245},{6,54},{7,247},{8,56}... | collective-permute-start | bytes 393224 | tf_op jit(solution)/shard_map/ppermute | solution.py:432
  120.9 6.5 %collective-permute-start.14 = (bf16[2,128,256]{2,1,0:T(8,128)(2,1)S(1)}, bf16[2,128,256]{2,1,0:T(8,128)(2,1)S(1)}, u32[]{:S(2)}, u32[]{:S(2)}) collective-permute-start(bf16[2,128,256]{2,1,0:T(8,128)(2,1)S(1)} %get-tuple-element.47), channel_id=1, source_target_pairs={{0,32},{1,225},{2,34},{3,227},{4,36},{5,229},{6,38},{7,231},{8,40}... | collective-permute-start | bytes 393224 | tf_op jit(solution)/shard_map/ppermute | solution.py:432
  126.7 5.3 %collective-permute-start.13 = (bf16[2,128,256]{2,1,0:T(8,128)(2,1)S(1)}, bf16[2,128,256]{2,1,0:T(8,128)(2,1)S(1)}, u32[]{:S(2)}, u32[]{:S(2)}) collective-permute-start(bf16[2,128,256]{2,1,0:T(8,128)(2,1)S(1)} %get-tuple-element.48), channel_id=1, source_target_pairs={{0,16},{1,17},{2,18},{3,19},{4,20},{5,21},{6,22},{7,23},{8,24},{9,... | collective-permute-start | bytes 393224 | tf_op jit(solution)/shard_map/ppermute | solution.py:432
  132.1 20.6 %copy-start.2 = (s32[4,2]{1,0:T(4,128)S(1)}, s32[4,2]{1,0:T(4,128)}, u32[]{:S(2)}) copy-start(s32[4,2]{1,0:T(4,128)} %copy-done.1) | copy-start | bytes 100
  132.1 20.6 %copy-start.4 = (s32[48]{0:T(128)S(1)}, s32[48]{0:T(128)}, u32[]{:S(2)}) copy-start(s32[48]{0:T(128)} %copy-done.3) | copy-start | bytes 580
  132.1 20.6 %collective-permute-start.16 = (bf16[4,2,128,256]{3,2,1,0:T(8,128)(2,1)S(1)}, bf16[4,2,128,256]{3,2,1,0:T(8,128)(2,1)S(1)}, u32[]{:S(2)}, u32[]{:S(2)}) collective-permute-start(bf16[4,2,128,256]{3,2,1,0:T(8,128)(2,1)S(1)} %pad_maximum_fusion.1), channel_id=1, source_target_pairs={{0,15},{1,0},{2,1},{3,2},{4,3},{5,4},{6,5},{7,6},{8,7},{9,8},{10,9... | collective-permute-start | bytes 1572872 | tf_op jit(solution)/shard_map/ppermute | solution.py:372
  136.8 15.9 %collective-permute-start.23 = (bf16[4,2,128,256]{3,2,1,0:T(8,128)(2,1)S(1)}, bf16[4,2,128,256]{3,2,1,0:T(8,128)(2,1)S(1)}, u32[]{:S(2)}, u32[]{:S(2)}) collective-permute-start(bf16[4,2,128,256]{3,2,1,0:T(8,128)(2,1)S(1)} %pad_maximum_fusion.1), channel_id=1, source_target_pairs={{0,1},{1,2},{2,3},{3,4},{4,5},{5,6},{6,7},{7,8},{8,9},{9,10},{10,1... | collective-permute-start | bytes 1572872 | tf_op jit(solution)/shard_map/ppermute | solution.py:372
  137.0 13.0 %collective-permute-start.20 = (bf16[2,128,256]{2,1,0:T(8,128)(2,1)S(1)}, bf16[2,128,256]{2,1,0:T(8,128)(2,1)S(1)}, u32[]{:S(2)}, u32[]{:S(2)}) collective-permute-start(bf16[2,128,256]{2,1,0:T(8,128)(2,1)S(1)} %get-tuple-element.43), channel_id=1, source_target_pairs={{0,16},{1,17},{2,18},{3,19},{4,20},{5,21},{6,22},{7,23},{8,24},{9,... | collective-permute-start | bytes 393224 | tf_op jit(solution)/shard_map/ppermute | solution.py:432
  140.3 9.7 %collective-permute-start.21 = (bf16[2,128,256]{2,1,0:T(8,128)(2,1)S(1)}, bf16[2,128,256]{2,1,0:T(8,128)(2,1)S(1)}, u32[]{:S(2)}, u32[]{:S(2)}) collective-permute-start(bf16[2,128,256]{2,1,0:T(8,128)(2,1)S(1)} %get-tuple-element.42), channel_id=1, source_target_pairs={{0,32},{1,225},{2,34},{3,227},{4,36},{5,229},{6,38},{7,231},{8,40}... | collective-permute-start | bytes 393224 | tf_op jit(solution)/shard_map/ppermute | solution.py:432
  145.3 7.4 %collective-permute-start.22 = (bf16[2,128,256]{2,1,0:T(8,128)(2,1)S(1)}, bf16[2,128,256]{2,1,0:T(8,128)(2,1)S(1)}, u32[]{:S(2)}, u32[]{:S(2)}) collective-permute-start(bf16[2,128,256]{2,1,0:T(8,128)(2,1)S(1)} %get-tuple-element.41), channel_id=1, source_target_pairs={{0,48},{1,241},{2,50},{3,243},{4,52},{5,245},{6,54},{7,247},{8,56}... | collective-permute-start | bytes 393224 | tf_op jit(solution)/shard_map/ppermute | solution.py:432

commit v7 on v6

--- a/solution.py
+++ b/solution.py
@@ -55,13 +55,13 @@
     )(jnp.asarray(scales), jnp.asarray(base_tables(n)))
 
 
-def chain_kernel(*refs, n, slices, rows):
+def chain_kernel(*refs, n, slices):
     accs = [pltpu.ACC(c)((size, n), F32)
             for size in (FIRST, SECOND) for _ in range(2) for c in range(2) for _ in range(n // size)]
-    pl.run_scoped(lambda *scoped: chain_body(*refs, *scoped, n=n, slices=slices, rows=rows), *accs)
-
-
-def chain_body(plan, places, probe, behind, *refs, n, slices, rows):
+    pl.run_scoped(lambda *scoped: chain_body(*refs, *scoped, n=n, slices=slices), *accs)
+
+
+def chain_body(plan, wave, behind, *refs, n, slices):
     ins, tabs_hbm, near_out, far_out = refs[0:4], refs[4], refs[5:9], refs[9:13]
     (patch, tabs, inc, lhs0, lhs1, mid0, mid1, outv, target, term, psem, tsem, osem, gsem) = refs[13:27]
     accs = list(refs[27:])
@@ -168,17 +168,11 @@
                 def _():
                     pltpu.make_async_copy(ins[r].at[plan[ENTRY + s]], patch.at[s], psem.at[s]).start()
         table_copy(slices).start()
-        row_shift = lax.rem(places[plan[POSITION], 0], rows)
-        col_shift = lax.rem(places[plan[POSITION], 1], n)
+        patch_wait(0)
+        table_copy(0).wait()
         for m in range(2):
-            for c in range(2):
-                x = pltpu.roll(probe[m, c], row_shift, 0)
-                term[c] = pltpu.roll(x, col_shift, 1).astype(BF).astype(F32)
-            if m == 0:
-                patch_wait(0)
-                table_copy(0).wait()
             for i in range(count):
-                enter(0, m, i, term[0, span(i, SECOND)], term[1, span(i, SECOND)])
+                enter(0, m, i, wave[m, 0, span(i, SECOND)].astype(F32), wave[m, 1, span(i, SECOND)].astype(F32))
             first(m, 0, 0)
         run(turn(0))
 
@@ -227,14 +221,14 @@
                 pltpu.make_async_copy(outv.at[s, :, pl.ds(h * half, half)], near_out[0].at[0], osem.at[h, s]).wait()
 
 
-def chain(plan, places, probe, behind, messages, tables, rows):
-    n = probe.shape[-1]
+def chain(plan, wave, behind, messages, tables):
+    n = wave.shape[-1]
     slices = tables.shape[0] - 1
     piece = jax.ShapeDtypeStruct((slices // 4, 2, n // 2, n), BF)
     return pl.pallas_call(
-        functools.partial(chain_kernel, n=n, slices=slices, rows=rows),
+        functools.partial(chain_kernel, n=n, slices=slices),
         out_shape=(piece,) * 8,
-        in_specs=[SMEM, SMEM, VMEM] + [ANY] * 6,
+        in_specs=[SMEM, VMEM] + [ANY] * 6,
         out_specs=(ANY,) * 8,
         scratch_shapes=[
             pltpu.VMEM((slices, 2, n, n), BF),
@@ -253,7 +247,7 @@
             pltpu.SemaphoreType.DMA,
         ],
         compiler_params=pltpu.CompilerParams(vmem_limit_bytes=58 << 20),
-    )(plan, places, probe, behind, *messages, tables)
+    )(plan, wave, behind, *messages, tables)
 
 
 def window(ref, lead, offset, n):
@@ -266,26 +260,17 @@
     return jnp.where(lane >= offset % n, first, second)
 
 
-def own_windows_kernel(places, tile_hbm, measured, tile_bf, wins, tile, target, sems, *, n, ahead_at, parts=4):
-    rows = tile_hbm.shape[1]
-    size = rows // parts
-    copies = [pltpu.make_async_copy(tile_hbm.at[:, pl.ds(q * size, size)], tile.at[:, pl.ds(q * size, size)], sems.at[q])
-              for q in range(parts)]
-    for copy in copies:
-        copy.start()
+def own_windows_kernel(places, tile, measured, wins, target, sem, *, n, ahead_at):
+    rows = tile.shape[1]
     me = lax.axis_index("lat") % 2 * 16 + lax.axis_index("depth")
     which = jnp.int32(0)
     for at, position in enumerate(ahead_at):
         which = jnp.where(me == at, jnp.int32(position), which)
-    wanted = pltpu.make_async_copy(measured.at[which], target, sems.at[parts])
+    wanted = pltpu.make_async_copy(measured.at[which], target, sem)
     wanted.start()
-    for q, copy in enumerate(copies):
-        copy.wait()
-        part = pl.ds(q * size, size)
-        tile_bf[:, part] = tile[:, part].astype(BF)
-        for p in range(places.shape[0]):
-            for c in range(2):
-                wins[p, c, part] = window(tile.at[:, part], c, places[p, 1], n).astype(BF)
+    for p in range(places.shape[0]):
+        for c in range(2):
+            wins[p, c] = window(tile, c, places[p, 1], n).astype(BF)
     wanted.wait()
     for c in range(2):
         x = target[c * rows:(c + 1) * rows]
@@ -296,16 +281,34 @@
 
 def own_windows(places, tile, measured, n):
     count = places.shape[0]
-    hbm = functools.partial(pltpu.with_memory_space_constraint, memory_space=pltpu.HBM)
     ahead_at = tuple(int(x) for x in make_plan()[:, :, OTHER].ravel())
     return pl.pallas_call(
         functools.partial(own_windows_kernel, n=n, ahead_at=ahead_at),
-        out_shape=(jax.ShapeDtypeStruct(tile.shape, BF), jax.ShapeDtypeStruct((count + 2, 2, tile.shape[1], n), BF)),
-        in_specs=[SMEM, ANY, ANY],
-        out_specs=(VMEM, VMEM),
-        scratch_shapes=[pltpu.VMEM(tile.shape, F32), pltpu.VMEM((n, n), F32), pltpu.SemaphoreType.DMA((5,))],
+        out_shape=jax.ShapeDtypeStruct((count + 2, 2, tile.shape[1], n), BF),
+        in_specs=[SMEM, VMEM, ANY],
+        out_specs=VMEM,
+        scratch_shapes=[pltpu.VMEM((n, n), F32), pltpu.SemaphoreType.DMA],
         compiler_params=pltpu.CompilerParams(vmem_limit_bytes=40 << 20),
-    )(places, hbm(tile), hbm(measured))
+    )(places, tile, pltpu.with_memory_space_constraint(measured, pltpu.HBM))
+
+
+def roll_kernel(plan, places, probe, out, *, rows, n):
+    row_shift = lax.rem(places[plan[POSITION], 0], rows)
+    col_shift = lax.rem(places[plan[POSITION], 1], n)
+    for m in range(probe.shape[0]):
+        for c in range(2):
+            x = pltpu.roll(probe[m, c], row_shift, 0)
+            out[m, c] = pltpu.roll(x, col_shift, 1).astype(BF)
+
+
+def roll_probe(plan, places, probe, rows):
+    return pl.pallas_call(
+        functools.partial(roll_kernel, rows=rows, n=probe.shape[-1]),
+        out_shape=jax.ShapeDtypeStruct(probe.shape, BF),
+        in_specs=[SMEM, SMEM, VMEM],
+        out_specs=VMEM,
+        compiler_params=pltpu.CompilerParams(vmem_limit_bytes=40 << 20),
+    )(plan, places, probe)
 
 
 def merge_kernel(plan, places, behind, tile, ahead, *outs, n):
@@ -330,41 +333,59 @@
     )(plan, places, behind, tile, ahead)
 
 
-def gather_kernel(plan, own_places, mid_places, far_places, from_own, m0, m1, m2, m3, from_far, out, *, n):
+def add_window(out, places, p, c, term, n):
+    width = out.shape[-1]
+    offset = places[p, 1]
+    start = pl.multiple_of((offset // n) * n, n)
+    after = pl.multiple_of(jnp.minimum(start + n, width - n), n)
+    here = lax.broadcasted_iota(jnp.int32, term.shape, 1) >= offset % n
+    out[c, :, pl.ds(start, n)] += jnp.where(here, term, 0.0)
+    out[c, :, pl.ds(after, n)] += jnp.where(here, 0.0, term)
+
+
+def halo_terms_kernel(plan, own_places, far_places, from_own, from_far, out, *, n):
     rows = out.shape[1]
-    width = out.shape[-1]
     row = lax.broadcasted_iota(jnp.int32, (rows, n), 0)
-    lane = lax.broadcasted_iota(jnp.int32, (rows, n), 1)
     out[...] = jnp.zeros_like(out)
-    mids = (m0, m1, m2, m3)
-    for places, kind, order in ((own_places, 0, OTHER), (mid_places, 1, ORDER), (far_places, 2, OTHER)):
-        for k in range(4):
-            p = plan[order + k]
-            shift = places[p, 0] % rows
-            offset = places[p, 1]
-            start = pl.multiple_of((offset // n) * n, n)
-            after = pl.multiple_of(jnp.minimum(start + n, width - n), n)
-            for c in range(2):
-                if kind == 0:
-                    term = jnp.where(row >= shift, from_own[k, c].astype(F32), 0.0)
-                elif kind == 1:
-                    term = mids[k][c].astype(F32)
-                else:
-                    term = jnp.where(row < shift, from_far[k, c].astype(F32), 0.0)
-                here = lane >= offset % n
-                out[c, :, pl.ds(start, n)] += jnp.where(here, term, 0.0)
-                out[c, :, pl.ds(after, n)] += jnp.where(here, 0.0, term)
-
-
-def gather_terms(plan, own_places, mid_places, far_places, from_own, mids, from_far, rows, width):
-    n = from_own.shape[-1]
-    return pl.pallas_call(
-        functools.partial(gather_kernel, n=n),
+    for k in range(4):
+        p = plan[OTHER + k]
+        for c in range(2):
+            term = jnp.where(row >= own_places[p, 0] % rows, from_own[k, c].astype(F32), 0.0)
+            add_window(out, own_places, p, c, term, n)
+            term = jnp.where(row < far_places[p, 0] % rows, from_far[k, c].astype(F32), 0.0)
+            add_window(out, far_places, p, c, term, n)
+
+
+def halo_terms(plan, own_places, far_places, from_own, from_far, width):
+    _, _, rows, n = from_own.shape
+    return pl.pallas_call(
+        functools.partial(halo_terms_kernel, n=n),
         out_shape=jax.ShapeDtypeStruct((2, rows, width), F32),
-        in_specs=[SMEM] * 4 + [VMEM] * 6,
+        in_specs=[SMEM] * 3 + [VMEM] * 2,
         out_specs=VMEM,
         compiler_params=pltpu.CompilerParams(vmem_limit_bytes=40 << 20),
-    )(plan, own_places, mid_places, far_places, from_own, *mids, from_far)
+    )(plan, own_places, far_places, from_own, from_far)
+
+
+def own_terms_kernel(plan, places, total, m0, m1, m2, m3, out_hbm, out, sems, *, n):
+    out[...] = total[...]
+    for c in range(2):
+        for k, ref in enumerate((m0, m1, m2, m3)):
+            add_window(out, places, plan[ORDER + k], c, ref[c].astype(F32), n)
+        pltpu.make_async_copy(out.at[c], out_hbm.at[c], sems.at[c]).start()
+    for c in range(2):
+        pltpu.make_async_copy(out.at[c], out_hbm.at[c], sems.at[c]).wait()
+
+
+def own_terms(plan, places, total, mids):
+    return pl.pallas_call(
+        functools.partial(own_terms_kernel, n=mids[0].shape[-1]),
+        out_shape=jax.ShapeDtypeStruct(total.shape, F32),
+        in_specs=[SMEM] * 2 + [VMEM] * 5,
+        out_specs=ANY,
+        scratch_shapes=[pltpu.VMEM(total.shape, F32), pltpu.SemaphoreType.DMA((2,))],
+        compiler_params=pltpu.CompilerParams(vmem_limit_bytes=40 << 20),
+    )(plan, places, total, *mids)
 
 
 def shifted(block, distance):
@@ -460,8 +481,9 @@
     plan = lax.dynamic_slice(jnp.asarray(make_plan()), (m % 2, d, 0), (1, 1, 48)).reshape(48)
     tile = object_slices[0]
 
-    tile_bf, mine = own_windows(positions, tile, measured, n)
+    tile_bf = tile.astype(BF)
     ahead = shifted(tile_bf, -1)
+    mine = own_windows(positions, tile_bf, measured, n)
     behind = shifted(mine, 1)
     mid_places = shifted(positions, 1)
     far_places = shifted(positions, 2)
@@ -471,7 +493,8 @@
     message = jnp.stack([parts[0]] + [within(parts[k], k) for k in (1, 2, 3)])
     messages = [message] + [towards(message, k) for k in (1, 2, 3)]
     tables = make_tables(n, depth_size)
-    terms = chain(plan, mid_places, probe, behind, messages, tables, rows)
+    wave = roll_probe(plan, mid_places, probe, rows)
+    terms = chain(plan, wave, behind, messages, tables)
 
     def home(pieces):
         block = pieces[0]
@@ -485,8 +508,8 @@
     mids = [far_block[0]] + [within(far_block[k], k) for k in (1, 2, 3)]
     from_own = shifted(mixed, -1)
     from_far = shifted(mixed, 1)
-    total = gather_terms(plan, positions, mid_places, far_places, from_own, mids, from_far, rows, width)
-    return total[None]
+    total = halo_terms(plan, positions, far_places, from_own, from_far, width)
+    return own_terms(plan, mid_places, total, mids)[None]
 
 
 def solution(mesh):

time: 158 us -> 157 us (level)
  waiting for transfers between devices: 79.2 us -> 76.3 us
  other arithmetic: 1.5 us -> 3.35 us
    ppermute x18, waiting for transfers between devices: 66.2 us -> 63.2 us  [permute(): return lax.ppermute(block, ('depth', 'lat'), pairs)]
    convert_element_type x0 -> x1, other arithmetic: none -> 1.74 us  [on_device(): tile_bf = tile.astype(BF)]
    pallas_call x2 -> x4, Pallas kernels: 4.8 us -> 6.17 us  [the longest x1 2.17 us: own_terms(): pl.pallas_call(functools.partial(own_terms_kernel, n=mids[0].shape[-1]),...]
  transfers between devices with their start and end apart: 24 -> 24, of which waited for: 10 -> 9; matrix products, arithmetic and copies ran while one was open for 2% -> 2% of each run, Pallas kernels for 7% -> 10%
where the time goes in v7:
time: 157 us; the launch traced here: 156 us
  waiting for transfers between devices  76.3 us (49%)
  starting transfers between devices  49.8 us (32%)
  Pallas kernels  20.7 us (13%)
  other arithmetic  3.35 us (2%)
  local copies, waits for them, and re-layouts  2.96 us (2%)
  between operations  2.37 us (2%)
    ppermute x18, waiting for transfers between devices, permute(): return lax.ppermute(block, ('depth', 'lat'), pairs)  63.2 us
    ppermute x18, starting transfers between devices, permute(): return lax.ppermute(block, ('depth', 'lat'), pairs)  41 us
    ppermute x6, waiting for transfers between devices, shifted(): lax.ppermute(block, 'lat', [(i, (i + distance) % size) for i in range(siz...  13.1 us
    pallas_call x1, Pallas kernels, make_tables(): pl.pallas_call(functools.partial(tables_kernel, n=n, slices=slices), grid...  11.1 us
    ppermute x6, starting transfers between devices, shifted(): lax.ppermute(block, 'lat', [(i, (i + distance) % size) for i in range(siz...  8.86 us
  transfers between devices with their start and end apart: 24, of which 9 were waited for; matrix products, arithmetic and copies ran while one was open for 2% of the time, Pallas kernels for 10%

profile of v7, /device:TPU:1, one launch (start us, length us, event | category | flops | bytes accessed | tf_op | source)
XLA Modules:
  0.0 155.5 jit_solution(235788491463190633)
XLA Ops:
  0.0 1.7 %convert_bitcast_fusion.tile = bf16[2,128,2048]{2,1,0:T(8,128)(2,1)S(1)} fusion(f32[1,2,128,2048]{3,2,1,0:T(8,128)} %param.7), kind=kLoop, calls=%fused_computation.1 | loop fusion | flops 524288 | bytes 3145728 | tf_op jit(solution)/shard_map/convert_element_type | solution.py:484
  1.8 3.3 %collective-permute-start.2 = (bf16[2,128,2048]{2,1,0:T(8,128)(2,1)S(1)}, bf16[2,128,2048]{2,1,0:T(8,128)(2,1)S(1)}, u32[]{:S(2)}, u32[]{:S(2)}) collective-permute-start(bf16[2,128,2048]{2,1,0:T(8,128)(2,1)S(1)} %convert_bitcast_fusion.tile), channel_id=1, source_target_pairs={{0,15},{1,0},{2,1},{3,2},{4,3},{5,4},{6,5},{7,6},{8,7},{9,8},{10,9... | collective-permute-start | bytes 3145736 | tf_op jit(solution)/shard_map/ppermute | solution.py:393
  5.1 0.1 copy.8.places.own_places
  5.2 2.5 %shard_map.73 = bf16[6,2,128,256]{3,2,1,0:T(8,128)(2,1)} custom-call(s32[4,2]{1,0:T(4,128)S(1)} %copy.8.places.own_places, bf16[2,128,2048]{2,1,0:T(8,128)(2,1)S(1)} %convert_bitcast_fusion.tile, f32[4,256,256]{2,1,0:T(8,128)} %measured.1), custom_call_target="tpu_custom_call" | custom-call | tf_op jit(solution)/shard_map/pallas_call | solution.py:285
  7.6 0.1 collective-permute-start.3
  7.7 0.1 collective-permute-start
  7.8 1.0 collective-permute-start.1
  8.8 0.7 fusion.1.plan.refs_0_
  9.5 7.5 %collective-permute-done.places = s32[4,2]{1,0:T(4,128)S(1)} collective-permute-done((s32[4,2]{1,0:T(4,128)S(1)}, s32[4,2]{1,0:T(4,128)S(1)}, u32[]{:S(2)}, u32[]{:S(2)}) %collective-permute-start) | collective-permute-done | bytes 64 | tf_op jit(solution)/shard_map/ppermute | solution.py:393
  17.0 5.6 %collective-permute-done.1.far_places = s32[4,2]{1,0:T(4,128)S(1)} collective-permute-done((s32[4,2]{1,0:T(4,128)S(1)}, s32[4,2]{1,0:T(4,128)S(1)}, u32[]{:S(2)}, u32[]{:S(2)}) %collective-permute-start.1) | collective-permute-done | bytes 64 | tf_op jit(solution)/shard_map/ppermute | solution.py:393
  22.6 0.0 collective-permute-done.3.behind.refs_2_
  22.6 0.0 collective-permute-done.2.ahead
  22.6 0.9 shard_map.75
  23.5 8.0 %collective-permute-start.6 = (bf16[2,256,256]{2,1,0:T(8,128)(2,1)S(1)}, bf16[2,256,256]{2,1,0:T(8,128)(2,1)S(1)}, u32[]{:S(2)}, u32[]{:S(2)}) collective-permute-start(bf16[2,256,256]{2,1,0:T(8,128)(2,1)S(1)} %get-tuple-element.28), channel_id=1, source_target_pairs={{0,48},{1,241},{2,50},{3,243},{4,52},{5,245},{6,54},{7,247},{8,56}... | collective-permute-start | bytes 786440 | tf_op jit(solution)/shard_map/ppermute | solution.py:453
  31.5 0.0 collective-permute-start.5
  31.5 0.4 collective-permute-start.4
  31.9 3.6 %collective-permute-done.6 = bf16[2,256,256]{2,1,0:T(8,128)(2,1)S(1)} collective-permute-done((bf16[2,256,256]{2,1,0:T(8,128)(2,1)S(1)}, bf16[2,256,256]{2,1,0:T(8,128)(2,1)S(1)}, u32[]{:S(2)}, u32[]{:S(2)}) %collective-permute-start.6) | collective-permute-done | bytes 262176 | tf_op jit(solution)/shard_map/ppermute | solution.py:453
  35.5 2.8 %collective-permute-done.5 = bf16[2,256,256]{2,1,0:T(8,128)(2,1)S(1)} collective-permute-done((bf16[2,256,256]{2,1,0:T(8,128)(2,1)S(1)}, bf16[2,256,256]{2,1,0:T(8,128)(2,1)S(1)}, u32[]{:S(2)}, u32[]{:S(2)}) %collective-permute-start.5) | collective-permute-done | bytes 262176 | tf_op jit(solution)/shard_map/ppermute | solution.py:453
  38.3 2.7 %collective-permute-done.4 = bf16[2,256,256]{2,1,0:T(8,128)(2,1)S(1)} collective-permute-done((bf16[2,256,256]{2,1,0:T(8,128)(2,1)S(1)}, bf16[2,256,256]{2,1,0:T(8,128)(2,1)S(1)}, u32[]{:S(2)}, u32[]{:S(2)}) %collective-permute-start.4) | collective-permute-done | bytes 262176 | tf_op jit(solution)/shard_map/ppermute | solution.py:453
  41.1 0.1 pad_maximum_fusion.refs_3_
  41.2 0.0 copy-start.5
  41.2 0.0 copy-start.2
  41.2 1.8 %collective-permute-start.7 = (bf16[4,2,256,256]{3,2,1,0:T(8,128)(2,1)S(1)}, bf16[4,2,256,256]{3,2,1,0:T(8,128)(2,1)}, u32[]{:S(2)}, u32[]{:S(2)}) collective-permute-start(bf16[4,2,256,256]{3,2,1,0:T(8,128)(2,1)S(1)} %pad_maximum_fusion.refs_3_), channel_id=1, source_target_pairs={{16,208},{18,210},{20,212},{22,214},{24,216},{26,218},{28,220},{30... | collective-permute-start | bytes 3145736 | tf_op jit(solution)/shard_map/ppermute | solution.py:453
  43.0 1.7 %collective-permute-start.8 = (bf16[4,2,256,256]{3,2,1,0:T(8,128)(2,1)S(1)}, bf16[4,2,256,256]{3,2,1,0:T(8,128)(2,1)}, u32[]{:S(2)}, u32[]{:S(2)}) collective-permute-start(bf16[4,2,256,256]{3,2,1,0:T(8,128)(2,1)S(1)} %pad_maximum_fusion.refs_3_), channel_id=1, source_target_pairs={{32,128},{33,193},{34,130},{35,195},{36,132},{37,197},{38,134},{39... | collective-permute-start | bytes 3145736 | tf_op jit(solution)/shard_map/ppermute | solution.py:453
  44.6 4.0 %collective-permute-start.9 = (bf16[4,2,256,256]{3,2,1,0:T(8,128)(2,1)S(1)}, bf16[4,2,256,256]{3,2,1,0:T(8,128)(2,1)}, u32[]{:S(2)}, u32[]{:S(2)}) collective-permute-start(bf16[4,2,256,256]{3,2,1,0:T(8,128)(2,1)S(1)} %pad_maximum_fusion.refs_3_), channel_id=1, source_target_pairs={{1,65},{3,67},{5,69},{7,71},{9,73},{11,75},{13,77},{15,79},{48,80}... | collective-permute-start | bytes 3145736 | tf_op jit(solution)/shard_map/ppermute | solution.py:453
  48.7 11.1 %shard_map.76.refs_7_ = bf16[17,2,512,512]{3,2,1,0:T(8,128)(2,1)} custom-call(f32[2,17]{1,0:T(2,128)} %constant.38.clone.scales, f32[4,256,256]{2,1,0:T(8,128)} %constant.39.clone.base), custom_call_target="tpu_custom_call" | custom-call | tf_op jit(solution)/shard_map/pallas_call | solution.py:49
  59.8 1.0 shard_map.74.refs_1_
  60.8 0.8 copy-done.1
  61.6 0.0 collective-permute-done.7.refs_4_
  61.6 0.0 collective-permute-done.8.refs_5_
  61.6 0.0 collective-permute-done.9.refs_6_
  61.6 1.7 %shard_map.77 = (bf16[4,2,128,256]{3,2,1,0:T(8,128)(2,1)}, bf16[4,2,128,256]{3,2,1,0:T(8,128)(2,1)}, bf16[4,2,128,256]{3,2,1,0:T(8,128)(2,1)}, bf16[4,2,128,256]...) custom-call(s32[48]{0:T(128)} %copy-done.3, ...), custom_call_target="tpu_custom_call" | custom-call | tf_op jit(solution)/shard_map/pallas_call | solution.py:228
  63.3 1.3 collective-permute-start.10
  64.6 0.7 collective-permute-start.11
  65.3 0.7 collective-permute-start.12
  66.0 0.7 constant_dynamic-slice_fusion
  66.7 0.6 slice.33
  69.2 1.3 collective-permute-start.18
  70.5 0.7 collective-permute-start.19
  71.2 40.8 %collective-permute-done.10 = bf16[4,2,128,256]{3,2,1,0:T(8,128)(2,1)S(1)} collective-permute-done((bf16[4,2,128,256]{3,2,1,0:T(8,128)(2,1)}, bf16[4,2,128,256]{3,2,1,0:T(8,128)(2,1)S(1)}, u32[]{:S(2)}, u32[]{:S(2)}) %collective-permute-start.10) | collective-permute-done | bytes 524320 | tf_op jit(solution)/shard_map/ppermute | solution.py:453
  112.0 0.7 collective-permute-start.20
  112.7 0.0 collective-permute-done.11
  112.7 0.0 collective-permute-done.12
  112.7 1.2 select_select_fusion.1
  114.0 7.4 %collective-permute-start.15 = (bf16[2,128,256]{2,1,0:T(8,128)(2,1)S(1)}, bf16[2,128,256]{2,1,0:T(8,128)(2,1)S(1)}, u32[]{:S(2)}, u32[]{:S(2)}) collective-permute-start(bf16[2,128,256]{2,1,0:T(8,128)(2,1)S(1)} %get-tuple-element.42), channel_id=1, source_target_pairs={{0,48},{1,241},{2,50},{3,243},{4,52},{5,245},{6,54},{7,247},{8,56}... | collective-permute-start | bytes 393224 | tf_op jit(solution)/shard_map/ppermute | solution.py:453
  121.4 1.3 collective-permute-start.14
  122.7 4.8 %collective-permute-done.15 = bf16[2,128,256]{2,1,0:T(8,128)(2,1)S(1)} collective-permute-done((bf16[2,128,256]{2,1,0:T(8,128)(2,1)S(1)}, bf16[2,128,256]{2,1,0:T(8,128)(2,1)S(1)}, u32[]{:S(2)}, u32[]{:S(2)}) %collective-permute-start.15) | collective-permute-done | bytes 131104 | tf_op jit(solution)/shard_map/ppermute | solution.py:453
  127.5 0.2 collective-permute-start.13
  127.7 0.0 collective-permute-done.14
  127.7 5.1 %collective-permute-done.13 = bf16[2,128,256]{2,1,0:T(8,128)(2,1)S(1)} collective-permute-done((bf16[2,128,256]{2,1,0:T(8,128)(2,1)S(1)}, bf16[2,128,256]{2,1,0:T(8,128)(2,1)S(1)}, u32[]{:S(2)}, u32[]{:S(2)}) %collective-permute-start.13) | collective-permute-done | bytes 131104 | tf_op jit(solution)/shard_map/ppermute | solution.py:453
  132.8 0.1 pad_maximum_fusion.1
  132.9 4.4 %collective-permute-start.16 = (bf16[4,2,128,256]{3,2,1,0:T(8,128)(2,1)S(1)}, bf16[4,2,128,256]{3,2,1,0:T(8,128)(2,1)S(1)}, u32[]{:S(2)}, u32[]{:S(2)}) collective-permute-start(bf16[4,2,128,256]{3,2,1,0:T(8,128)(2,1)S(1)} %pad_maximum_fusion.1), channel_id=1, source_target_pairs={{0,15},{1,0},{2,1},{3,2},{4,3},{5,4},{6,5},{7,6},{8,7},{9,8},{10,9... | collective-permute-start | bytes 1572872 | tf_op jit(solution)/shard_map/ppermute | solution.py:393
  137.3 0.0 collective-permute-start.17
  137.3 0.0 collective-permute-done.18
  137.3 0.0 collective-permute-done.19
  137.3 0.2 select_select_fusion
  137.5 3.3 %collective-permute-start.21 = (bf16[2,128,256]{2,1,0:T(8,128)(2,1)S(1)}, bf16[2,128,256]{2,1,0:T(8,128)(2,1)S(1)}, u32[]{:S(2)}, u32[]{:S(2)}) collective-permute-start(bf16[2,128,256]{2,1,0:T(8,128)(2,1)S(1)} %get-tuple-element.39), channel_id=1, source_target_pairs={{0,16},{1,17},{2,18},{3,19},{4,20},{5,21},{6,22},{7,23},{8,24},{9,... | collective-permute-start | bytes 393224 | tf_op jit(solution)/shard_map/ppermute | solution.py:453
  140.8 4.9 %collective-permute-start.22 = (bf16[2,128,256]{2,1,0:T(8,128)(2,1)S(1)}, bf16[2,128,256]{2,1,0:T(8,128)(2,1)S(1)}, u32[]{:S(2)}, u32[]{:S(2)}) collective-permute-start(bf16[2,128,256]{2,1,0:T(8,128)(2,1)S(1)} %get-tuple-element.38), channel_id=1, source_target_pairs={{0,32},{1,225},{2,34},{3,227},{4,36},{5,229},{6,38},{7,231},{8,40}... | collective-permute-start | bytes 393224 | tf_op jit(solution)/shard_map/ppermute | solution.py:453
  145.8 2.6 %collective-permute-start.23 = (bf16[2,128,256]{2,1,0:T(8,128)(2,1)S(1)}, bf16[2,128,256]{2,1,0:T(8,128)(2,1)S(1)}, u32[]{:S(2)}, u32[]{:S(2)}) collective-permute-start(bf16[2,128,256]{2,1,0:T(8,128)(2,1)S(1)} %get-tuple-element.37), channel_id=1, source_target_pairs={{0,48},{1,241},{2,50},{3,243},{4,52},{5,245},{6,54},{7,247},{8,56}... | collective-permute-start | bytes 393224 | tf_op jit(solution)/shard_map/ppermute | solution.py:453
  148.4 0.0 collective-permute-done.16.from_own
  148.4 0.0 collective-permute-done.17.from_far
  148.4 1.4 shard_map.78.total
  149.8 3.5 %collective-permute-done.23.m3 = bf16[2,128,256]{2,1,0:T(8,128)(2,1)S(1)} collective-permute-done((bf16[2,128,256]{2,1,0:T(8,128)(2,1)S(1)}, bf16[2,128,256]{2,1,0:T(8,128)(2,1)S(1)}, u32[]{:S(2)}, u32[]{:S(2)}) %collective-permute-start.23) | collective-permute-done | bytes 131104 | tf_op jit(solution)/shard_map/ppermute | solution.py:453
  153.2 2.2 %shard_map.79 = f32[2,128,2048]{2,1,0:T(8,128)} custom-call(s32[48]{0:T(128)S(1)} %copy-done.4, s32[4,2]{1,0:T(4,128)S(1)} %collective-permute-done.places, f32[2,128,2048]{2,1,0:T(8,128)S(1)} %shard_map.78.total, bf16[2,128,256]{2,1,0:T(8,128)(2,1)S(1)} %get-tuple-element.40.m0, bf16[2,128,256]{2,1,0:T(8,128)(2,1)S(1)} %collective-permute-done.21.m1, ...), custom_call_target="tpu_custom_call" | custom-call | tf_op jit(solution)/shard_map/pallas_call | solution.py:381
  (18 shorter events, 0.1 us)
Async XLA Ops:
  0.0 5.1 %copy-start.7 = (s32[4,2]{0,1:T(2,128)S(1)}, s32[4,2]{0,1:T(2,128)}, u32[]{:S(2)}) copy-start(s32[4,2]{0,1:T(2,128)} %param.9) | copy-start | bytes 100
  1.8 20.8 %collective-permute-start.2 = (bf16[2,128,2048]{2,1,0:T(8,128)(2,1)S(1)}, bf16[2,128,2048]{2,1,0:T(8,128)(2,1)S(1)}, u32[]{:S(2)}, u32[]{:S(2)}) collective-permute-start(bf16[2,128,2048]{2,1,0:T(8,128)(2,1)S(1)} %convert_bitcast_fusion.tile), channel_id=1, source_target_pairs={{0,15},{1,0},{2,1},{3,2},{4,3},{5,4},{6,5},{7,6},{8,7},{9,8},{10,9... | collective-permute-start | bytes 3145736 | tf_op jit(solution)/shard_map/ppermute | solution.py:393
  7.6 14.9 %collective-permute-start.3 = (bf16[6,2,128,256]{3,2,1,0:T(8,128)(2,1)}, bf16[6,2,128,256]{3,2,1,0:T(8,128)(2,1)S(1)}, u32[]{:S(2)}, u32[]{:S(2)}) collective-permute-start(bf16[6,2,128,256]{3,2,1,0:T(8,128)(2,1)} %shard_map.73), channel_id=1, source_target_pairs={{0,1},{1,2},{2,3},{3,4},{4,5},{5,6},{6,7},{7,8},{8,9},{9,10},{10,1... | collective-permute-start | bytes 2359304 | tf_op jit(solution)/shard_map/ppermute | solution.py:393
  7.7 9.3 %collective-permute-start = (s32[4,2]{1,0:T(4,128)S(1)}, s32[4,2]{1,0:T(4,128)S(1)}, u32[]{:S(2)}, u32[]{:S(2)}) collective-permute-start(s32[4,2]{1,0:T(4,128)S(1)} %copy.8.places.own_places), channel_id=1, source_target_pairs={{0,1},{1,2},{2,3},{3,4},{4,5},{5,6},{6,7},{7,8},{8,9},{9,10},{10,1... | collective-permute-start | bytes 104 | tf_op jit(solution)/shard_map/ppermute | solution.py:393
  7.8 14.8 %collective-permute-start.1 = (s32[4,2]{1,0:T(4,128)S(1)}, s32[4,2]{1,0:T(4,128)S(1)}, u32[]{:S(2)}, u32[]{:S(2)}) collective-permute-start(s32[4,2]{1,0:T(4,128)S(1)} %copy.8.places.own_places), channel_id=1, source_target_pairs={{0,2},{1,3},{2,4},{3,5},{4,6},{5,7},{6,8},{7,9},{8,10},{9,11},{10,... | collective-permute-start | bytes 104 | tf_op jit(solution)/shard_map/ppermute | solution.py:393
  9.5 50.3 %copy-start.3 = (s32[48]{0:T(128)}, s32[48]{0:T(128)S(1)}, u32[]{:S(2)}) copy-start(s32[48]{0:T(128)S(1)} %fusion.1.plan.refs_0_) | copy-start | bytes 580
  22.6 18.6 %copy-start = (bf16[6,2,128,256]{3,2,1,0:T(8,128)(2,1)}, bf16[6,2,128,256]{3,2,1,0:T(8,128)(2,1)S(1)}, u32[]{:S(2)}) copy-start(bf16[6,2,128,256]{3,2,1,0:T(8,128)(2,1)S(1)} %collective-permute-done.3.behind.refs_2_) | copy-start | bytes 2359300
  23.5 12.0 %collective-permute-start.6 = (bf16[2,256,256]{2,1,0:T(8,128)(2,1)S(1)}, bf16[2,256,256]{2,1,0:T(8,128)(2,1)S(1)}, u32[]{:S(2)}, u32[]{:S(2)}) collective-permute-start(bf16[2,256,256]{2,1,0:T(8,128)(2,1)S(1)} %get-tuple-element.28), channel_id=1, source_target_pairs={{0,48},{1,241},{2,50},{3,243},{4,52},{5,245},{6,54},{7,247},{8,56}... | collective-permute-start | bytes 786440 | tf_op jit(solution)/shard_map/ppermute | solution.py:453
  31.5 6.8 %collective-permute-start.5 = (bf16[2,256,256]{2,1,0:T(8,128)(2,1)S(1)}, bf16[2,256,256]{2,1,0:T(8,128)(2,1)S(1)}, u32[]{:S(2)}, u32[]{:S(2)}) collective-permute-start(bf16[2,256,256]{2,1,0:T(8,128)(2,1)S(1)} %get-tuple-element.27), channel_id=1, source_target_pairs={{0,32},{1,225},{2,34},{3,227},{4,36},{5,229},{6,38},{7,231},{8,40}... | collective-permute-start | bytes 786440 | tf_op jit(solution)/shard_map/ppermute | solution.py:453
  31.5 9.5 %collective-permute-start.4 = (bf16[2,256,256]{2,1,0:T(8,128)(2,1)S(1)}, bf16[2,256,256]{2,1,0:T(8,128)(2,1)S(1)}, u32[]{:S(2)}, u32[]{:S(2)}) collective-permute-start(bf16[2,256,256]{2,1,0:T(8,128)(2,1)S(1)} %get-tuple-element.26), channel_id=1, source_target_pairs={{0,16},{1,17},{2,18},{3,19},{4,20},{5,21},{6,22},{7,23},{8,24},{9,... | collective-permute-start | bytes 786440 | tf_op jit(solution)/shard_map/ppermute | solution.py:453
  41.2 18.6 %copy-start.5 = (bf16[4,2,256,256]{3,2,1,0:T(8,128)(2,1)}, bf16[4,2,256,256]{3,2,1,0:T(8,128)(2,1)S(1)}, u32[]{:S(2)}) copy-start(bf16[4,2,256,256]{3,2,1,0:T(8,128)(2,1)S(1)} %pad_maximum_fusion.refs_3_) | copy-start | bytes 3145732
  41.2 18.6 %copy-start.2 = (f32[2,2,256,256]{3,2,1,0:T(8,128)S(1)}, f32[2,2,256,256]{3,2,1,0:T(8,128)}, u32[]{:S(2)}) copy-start(f32[2,2,256,256]{3,2,1,0:T(8,128)} %probe.1) | copy-start | bytes 3145732
  41.2 20.4 %collective-permute-start.7 = (bf16[4,2,256,256]{3,2,1,0:T(8,128)(2,1)S(1)}, bf16[4,2,256,256]{3,2,1,0:T(8,128)(2,1)}, u32[]{:S(2)}, u32[]{:S(2)}) collective-permute-start(bf16[4,2,256,256]{3,2,1,0:T(8,128)(2,1)S(1)} %pad_maximum_fusion.refs_3_), channel_id=1, source_target_pairs={{16,208},{18,210},{20,212},{22,214},{24,216},{26,218},{28,220},{30... | collective-permute-start | bytes 3145736 | tf_op jit(solution)/shard_map/ppermute | solution.py:453
  43.0 18.6 %collective-permute-start.8 = (bf16[4,2,256,256]{3,2,1,0:T(8,128)(2,1)S(1)}, bf16[4,2,256,256]{3,2,1,0:T(8,128)(2,1)}, u32[]{:S(2)}, u32[]{:S(2)}) collective-permute-start(bf16[4,2,256,256]{3,2,1,0:T(8,128)(2,1)S(1)} %pad_maximum_fusion.refs_3_), channel_id=1, source_target_pairs={{32,128},{33,193},{34,130},{35,195},{36,132},{37,197},{38,134},{39... | collective-permute-start | bytes 3145736 | tf_op jit(solution)/shard_map/ppermute | solution.py:453
  44.6 17.0 %collective-permute-start.9 = (bf16[4,2,256,256]{3,2,1,0:T(8,128)(2,1)S(1)}, bf16[4,2,256,256]{3,2,1,0:T(8,128)(2,1)}, u32[]{:S(2)}, u32[]{:S(2)}) collective-permute-start(bf16[4,2,256,256]{3,2,1,0:T(8,128)(2,1)S(1)} %pad_maximum_fusion.refs_3_), channel_id=1, source_target_pairs={{1,65},{3,67},{5,69},{7,71},{9,73},{11,75},{13,77},{15,79},{48,80}... | collective-permute-start | bytes 3145736 | tf_op jit(solution)/shard_map/ppermute | solution.py:453
  60.8 0.8 copy-start.1
  63.3 48.7 %collective-permute-start.10 = (bf16[4,2,128,256]{3,2,1,0:T(8,128)(2,1)}, bf16[4,2,128,256]{3,2,1,0:T(8,128)(2,1)S(1)}, u32[]{:S(2)}, u32[]{:S(2)}) collective-permute-start(bf16[4,2,128,256]{3,2,1,0:T(8,128)(2,1)} %get-tuple-element.29), channel_id=1, source_target_pairs={{0,224},{2,226},{4,228},{6,230},{8,232},{10,234},{12,236},{14,238}... | collective-permute-start | bytes 1572872 | tf_op jit(solution)/shard_map/ppermute | solution.py:453
  64.6 48.1 %collective-permute-start.11 = (bf16[4,2,128,256]{3,2,1,0:T(8,128)(2,1)}, bf16[4,2,128,256]{3,2,1,0:T(8,128)(2,1)S(1)}, u32[]{:S(2)}, u32[]{:S(2)}) collective-permute-start(bf16[4,2,128,256]{3,2,1,0:T(8,128)(2,1)} %get-tuple-element.30), channel_id=1, source_target_pairs={{0,160},{2,162},{4,164},{6,166},{8,168},{10,170},{12,172},{14,174}... | collective-permute-start | bytes 1572872 | tf_op jit(solution)/shard_map/ppermute | solution.py:453
  65.3 47.4 %collective-permute-start.12 = (bf16[4,2,128,256]{3,2,1,0:T(8,128)(2,1)}, bf16[4,2,128,256]{3,2,1,0:T(8,128)(2,1)S(1)}, u32[]{:S(2)}, u32[]{:S(2)}) collective-permute-start(bf16[4,2,128,256]{3,2,1,0:T(8,128)(2,1)} %get-tuple-element.31), channel_id=1, source_target_pairs={{0,64},{2,66},{4,68},{6,70},{8,72},{10,74},{12,76},{14,78},{17,49}... | collective-permute-start | bytes 1572872 | tf_op jit(solution)/shard_map/ppermute | solution.py:453
  69.2 68.1 %collective-permute-start.18 = (bf16[4,2,128,256]{3,2,1,0:T(8,128)(2,1)}, bf16[4,2,128,256]{3,2,1,0:T(8,128)(2,1)S(1)}, u32[]{:S(2)}, u32[]{:S(2)}) collective-permute-start(bf16[4,2,128,256]{3,2,1,0:T(8,128)(2,1)} %get-tuple-element.33), channel_id=1, source_target_pairs={{0,224},{2,226},{4,228},{6,230},{8,232},{10,234},{12,236},{14,238}... | collective-permute-start | bytes 1572872 | tf_op jit(solution)/shard_map/ppermute | solution.py:453
  70.5 66.8 %collective-permute-start.19 = (bf16[4,2,128,256]{3,2,1,0:T(8,128)(2,1)}, bf16[4,2,128,256]{3,2,1,0:T(8,128)(2,1)S(1)}, u32[]{:S(2)}, u32[]{:S(2)}) collective-permute-start(bf16[4,2,128,256]{3,2,1,0:T(8,128)(2,1)} %get-tuple-element.34), channel_id=1, source_target_pairs={{0,160},{2,162},{4,164},{6,166},{8,168},{10,170},{12,172},{14,174}... | collective-permute-start | bytes 1572872 | tf_op jit(solution)/shard_map/ppermute | solution.py:453
  112.0 25.3 %collective-permute-start.20 = (bf16[4,2,128,256]{3,2,1,0:T(8,128)(2,1)}, bf16[4,2,128,256]{3,2,1,0:T(8,128)(2,1)S(1)}, u32[]{:S(2)}, u32[]{:S(2)}) collective-permute-start(bf16[4,2,128,256]{3,2,1,0:T(8,128)(2,1)} %get-tuple-element.35), channel_id=1, source_target_pairs={{0,64},{2,66},{4,68},{6,70},{8,72},{10,74},{12,76},{14,78},{17,49}... | collective-permute-start | bytes 1572872 | tf_op jit(solution)/shard_map/ppermute | solution.py:453
  112.7 24.6 %copy-start.6 = (bf16[4,2,128,256]{3,2,1,0:T(8,128)(2,1)S(1)}, bf16[4,2,128,256]{3,2,1,0:T(8,128)(2,1)}, u32[]{:S(2)}) copy-start(bf16[4,2,128,256]{3,2,1,0:T(8,128)(2,1)} %get-tuple-element.36) | copy-start | bytes 1572868
  114.0 13.5 %collective-permute-start.15 = (bf16[2,128,256]{2,1,0:T(8,128)(2,1)S(1)}, bf16[2,128,256]{2,1,0:T(8,128)(2,1)S(1)}, u32[]{:S(2)}, u32[]{:S(2)}) collective-permute-start(bf16[2,128,256]{2,1,0:T(8,128)(2,1)S(1)} %get-tuple-element.42), channel_id=1, source_target_pairs={{0,48},{1,241},{2,50},{3,243},{4,52},{5,245},{6,54},{7,247},{8,56}... | collective-permute-start | bytes 393224 | tf_op jit(solution)/shard_map/ppermute | solution.py:453
  121.4 6.3 %collective-permute-start.14 = (bf16[2,128,256]{2,1,0:T(8,128)(2,1)S(1)}, bf16[2,128,256]{2,1,0:T(8,128)(2,1)S(1)}, u32[]{:S(2)}, u32[]{:S(2)}) collective-permute-start(bf16[2,128,256]{2,1,0:T(8,128)(2,1)S(1)} %get-tuple-element.43), channel_id=1, source_target_pairs={{0,32},{1,225},{2,34},{3,227},{4,36},{5,229},{6,38},{7,231},{8,40}... | collective-permute-start | bytes 393224 | tf_op jit(solution)/shard_map/ppermute | solution.py:453
  127.5 5.3 %collective-permute-start.13 = (bf16[2,128,256]{2,1,0:T(8,128)(2,1)S(1)}, bf16[2,128,256]{2,1,0:T(8,128)(2,1)S(1)}, u32[]{:S(2)}, u32[]{:S(2)}) collective-permute-start(bf16[2,128,256]{2,1,0:T(8,128)(2,1)S(1)} %get-tuple-element.44), channel_id=1, source_target_pairs={{0,16},{1,17},{2,18},{3,19},{4,20},{5,21},{6,22},{7,23},{8,24},{9,... | collective-permute-start | bytes 393224 | tf_op jit(solution)/shard_map/ppermute | solution.py:453
  132.9 15.5 %copy-start.4 = (s32[48]{0:T(128)S(1)}, s32[48]{0:T(128)}, u32[]{:S(2)}) copy-start(s32[48]{0:T(128)} %copy-done.3) | copy-start | bytes 580
  132.9 15.5 %collective-permute-start.16 = (bf16[4,2,128,256]{3,2,1,0:T(8,128)(2,1)S(1)}, bf16[4,2,128,256]{3,2,1,0:T(8,128)(2,1)S(1)}, u32[]{:S(2)}, u32[]{:S(2)}) collective-permute-start(bf16[4,2,128,256]{3,2,1,0:T(8,128)(2,1)S(1)} %pad_maximum_fusion.1), channel_id=1, source_target_pairs={{0,15},{1,0},{2,1},{3,2},{4,3},{5,4},{6,5},{7,6},{8,7},{9,8},{10,9... | collective-permute-start | bytes 1572872 | tf_op jit(solution)/shard_map/ppermute | solution.py:393
  137.3 11.1 %collective-permute-start.17 = (bf16[4,2,128,256]{3,2,1,0:T(8,128)(2,1)S(1)}, bf16[4,2,128,256]{3,2,1,0:T(8,128)(2,1)S(1)}, u32[]{:S(2)}, u32[]{:S(2)}) collective-permute-start(bf16[4,2,128,256]{3,2,1,0:T(8,128)(2,1)S(1)} %pad_maximum_fusion.1), channel_id=1, source_target_pairs={{0,1},{1,2},{2,3},{3,4},{4,5},{5,6},{6,7},{7,8},{8,9},{9,10},{10,1... | collective-permute-start | bytes 1572872 | tf_op jit(solution)/shard_map/ppermute | solution.py:393
  137.5 12.2 %collective-permute-start.21 = (bf16[2,128,256]{2,1,0:T(8,128)(2,1)S(1)}, bf16[2,128,256]{2,1,0:T(8,128)(2,1)S(1)}, u32[]{:S(2)}, u32[]{:S(2)}) collective-permute-start(bf16[2,128,256]{2,1,0:T(8,128)(2,1)S(1)} %get-tuple-element.39), channel_id=1, source_target_pairs={{0,16},{1,17},{2,18},{3,19},{4,20},{5,21},{6,22},{7,23},{8,24},{9,... | collective-permute-start | bytes 393224 | tf_op jit(solution)/shard_map/ppermute | solution.py:453
  140.8 8.9 %collective-permute-start.22 = (bf16[2,128,256]{2,1,0:T(8,128)(2,1)S(1)}, bf16[2,128,256]{2,1,0:T(8,128)(2,1)S(1)}, u32[]{:S(2)}, u32[]{:S(2)}) collective-permute-start(bf16[2,128,256]{2,1,0:T(8,128)(2,1)S(1)} %get-tuple-element.38), channel_id=1, source_target_pairs={{0,32},{1,225},{2,34},{3,227},{4,36},{5,229},{6,38},{7,231},{8,40}... | collective-permute-start | bytes 393224 | tf_op jit(solution)/shard_map/ppermute | solution.py:453
  145.8 7.4 %collective-permute-start.23 = (bf16[2,128,256]{2,1,0:T(8,128)(2,1)S(1)}, bf16[2,128,256]{2,1,0:T(8,128)(2,1)S(1)}, u32[]{:S(2)}, u32[]{:S(2)}) collective-permute-start(bf16[2,128,256]{2,1,0:T(8,128)(2,1)S(1)} %get-tuple-element.37), channel_id=1, source_target_pairs={{0,48},{1,241},{2,50},{3,243},{4,52},{5,245},{6,54},{7,247},{8,56}... | collective-permute-start | bytes 393224 | tf_op jit(solution)/shard_map/ppermute | solution.py:453

commit v8 on v7

--- a/solution.py
+++ b/solution.py
@@ -61,7 +61,7 @@
     pl.run_scoped(lambda *scoped: chain_body(*refs, *scoped, n=n, slices=slices), *accs)
 
 
-def chain_body(plan, wave, behind, *refs, n, slices):
+def chain_body(plan, wave, wanted, *refs, n, slices):
     ins, tabs_hbm, near_out, far_out = refs[0:4], refs[4], refs[5:9], refs[9:13]
     (patch, tabs, inc, lhs0, lhs1, mid0, mid1, outv, target, term, psem, tsem, osem, gsem) = refs[13:27]
     accs = list(refs[27:])
@@ -159,7 +159,7 @@
 
     @pl.when(plan[HANDLER] == 1)
     def _():
-        target_copy = pltpu.make_async_copy(behind.at[pl.ds(behind.shape[0] - 2, 2)], target, gsem)
+        target_copy = pltpu.make_async_copy(wanted, target, gsem)
         target_copy.start()
         for s in range(slices):
             table_copy(s).start()
@@ -191,9 +191,7 @@
         for i in range(count):
             ar, ai = pop(0, i)
             br, bi = pop(1, i)
-            h, at = divmod(i * SECOND, half)
-            wanted = target[0, h, pl.ds(at, SECOND)].astype(F32) + target[1, h, pl.ds(at, SECOND)].astype(F32)
-            resid = (ar * ar + ai * ai) + (br * br + bi * bi) - wanted
+            resid = (ar * ar + ai * ai) + (br * br + bi * bi) - target[span(i, SECOND)]
             put(0, i, resid * ar, resid * ai)
             put(1, i, resid * br, resid * bi)
         first(0, slices, 1)
@@ -221,7 +219,7 @@
                 pltpu.make_async_copy(outv.at[s, :, pl.ds(h * half, half)], near_out[0].at[0], osem.at[h, s]).wait()
 
 
-def chain(plan, wave, behind, messages, tables):
+def chain(plan, wave, wanted, messages, tables):
     n = wave.shape[-1]
     slices = tables.shape[0] - 1
     piece = jax.ShapeDtypeStruct((slices // 4, 2, n // 2, n), BF)
@@ -239,7 +237,7 @@
             pltpu.VMEM((n, 2 * n), BF),
             pltpu.VMEM((n, 2 * n), BF),
             pltpu.VMEM((slices, 2, n, n), BF),
-            pltpu.VMEM((2, 2, n // 2, n), BF),
+            pltpu.VMEM((n, n), F32),
             pltpu.VMEM((2, n, n), F32),
             pltpu.SemaphoreType.DMA((slices,)),
             pltpu.SemaphoreType.DMA((slices + 1,)),
@@ -247,7 +245,7 @@
             pltpu.SemaphoreType.DMA,
         ],
         compiler_params=pltpu.CompilerParams(vmem_limit_bytes=58 << 20),
-    )(plan, wave, behind, *messages, tables)
+    )(plan, wave, wanted, *messages, tables)
 
 
 def window(ref, lead, offset, n):
@@ -260,36 +258,20 @@
     return jnp.where(lane >= offset % n, first, second)
 
 
-def own_windows_kernel(places, tile, measured, wins, target, sem, *, n, ahead_at):
-    rows = tile.shape[1]
-    me = lax.axis_index("lat") % 2 * 16 + lax.axis_index("depth")
-    which = jnp.int32(0)
-    for at, position in enumerate(ahead_at):
-        which = jnp.where(me == at, jnp.int32(position), which)
-    wanted = pltpu.make_async_copy(measured.at[which], target, sem)
-    wanted.start()
+def own_windows_kernel(places, tile, wins, *, n):
     for p in range(places.shape[0]):
         for c in range(2):
             wins[p, c] = window(tile, c, places[p, 1], n).astype(BF)
-    wanted.wait()
-    for c in range(2):
-        x = target[c * rows:(c + 1) * rows]
-        high = x.astype(BF)
-        wins[places.shape[0], c] = high
-        wins[places.shape[0] + 1, c] = (x - high.astype(F32)).astype(BF)
-
-
-def own_windows(places, tile, measured, n):
-    count = places.shape[0]
-    ahead_at = tuple(int(x) for x in make_plan()[:, :, OTHER].ravel())
-    return pl.pallas_call(
-        functools.partial(own_windows_kernel, n=n, ahead_at=ahead_at),
-        out_shape=jax.ShapeDtypeStruct((count + 2, 2, tile.shape[1], n), BF),
-        in_specs=[SMEM, VMEM, ANY],
+
+
+def own_windows(places, tile, n):
+    return pl.pallas_call(
+        functools.partial(own_windows_kernel, n=n),
+        out_shape=jax.ShapeDtypeStruct((places.shape[0], 2, tile.shape[1], n), BF),
+        in_specs=[SMEM, VMEM],
         out_specs=VMEM,
-        scratch_shapes=[pltpu.VMEM((n, n), F32), pltpu.SemaphoreType.DMA],
         compiler_params=pltpu.CompilerParams(vmem_limit_bytes=40 << 20),
-    )(places, tile, pltpu.with_memory_space_constraint(measured, pltpu.HBM))
+    )(places, tile)
 
 
 def roll_kernel(plan, places, probe, out, *, rows, n):
@@ -483,18 +465,21 @@
 
     tile_bf = tile.astype(BF)
     ahead = shifted(tile_bf, -1)
-    mine = own_windows(positions, tile_bf, measured, n)
+    mine = own_windows(positions, tile_bf, n)
     behind = shifted(mine, 1)
     mid_places = shifted(positions, 1)
     far_places = shifted(positions, 2)
     mid_places, far_places, ahead, behind = lax.optimization_barrier((mid_places, far_places, ahead, behind))
     parts = merge(plan, mid_places, behind, tile_bf, ahead, n)
 
+    measured, parts = lax.optimization_barrier((measured, parts))
+    target = shifted(lax.dynamic_index_in_dim(measured, plan[OTHER], 0, False), 1)
+
     message = jnp.stack([parts[0]] + [within(parts[k], k) for k in (1, 2, 3)])
     messages = [message] + [towards(message, k) for k in (1, 2, 3)]
     tables = make_tables(n, depth_size)
     wave = roll_probe(plan, mid_places, probe, rows)
-    terms = chain(plan, wave, behind, messages, tables)
+    terms = tuple(chain(plan, wave, target, messages, tables))
 
     def home(pieces):
         block = pieces[0]
@@ -503,8 +488,10 @@
         return block
 
     near_block = home(terms[:4])
-    far_block = home(terms[4:])
-    mixed = jnp.stack([near_block[0]] + [within(near_block[k], k) for k in (1, 2, 3)])
+    near_got = [within(near_block[k], k) for k in (1, 2, 3)]
+    late, near_got[2] = lax.optimization_barrier((terms[7], near_got[2]))
+    far_block = home(terms[4:7] + (late,))
+    mixed = jnp.stack([near_block[0]] + near_got)
     mids = [far_block[0]] + [within(far_block[k], k) for k in (1, 2, 3)]
     from_own = shifted(mixed, -1)
     from_far = shifted(mixed, 1)

time: 157 us -> 160 us (1.019)
  waiting for transfers between devices: 76.3 us -> 78.3 us
  between operations: 2.37 us -> 4.3 us
    ppermute x18, starting transfers between devices: 41 us -> 35.9 us  [permute(): return lax.ppermute(block, ('depth', 'lat'), pairs)]
    ppermute x18, waiting for transfers between devices: 63.2 us -> 67.9 us  [permute(): return lax.ppermute(block, ('depth', 'lat'), pairs)]
    ppermute x6 -> x7, starting transfers between devices: 8.86 us -> 12.8 us  [shifted(): lax.ppermute(block, 'lat', [(i, (i + distance) % size) for i in range(siz...]
    ppermute x6 -> x7, waiting for transfers between devices: 13.1 us -> 10.4 us  [shifted(): lax.ppermute(block, 'lat', [(i, (i + distance) % size) for i in range(siz...]
  transfers between devices with their start and end apart: 24 -> 25, of which waited for: 9 -> 10; matrix products, arithmetic and copies ran while one was open for 2% -> 2% of each run, Pallas kernels for 10% -> 9%
where the time goes in v8:
time: 160 us; the launch traced here: 159 us
  waiting for transfers between devices  78.3 us (49%)
  starting transfers between devices  48.6 us (30%)
  Pallas kernels  20.2 us (13%)
  local copies, waits for them, and re-layouts  4.46 us (3%)
  between operations  4.3 us (3%)
  other arithmetic  3.39 us (2%)
    ppermute x18, waiting for transfers between devices, permute(): return lax.ppermute(block, ('depth', 'lat'), pairs)  67.9 us
    ppermute x18, starting transfers between devices, permute(): return lax.ppermute(block, ('depth', 'lat'), pairs)  35.9 us
    ppermute x7, starting transfers between devices, shifted(): lax.ppermute(block, 'lat', [(i, (i + distance) % size) for i in range(siz...  12.8 us
    pallas_call x1, Pallas kernels, make_tables(): pl.pallas_call(functools.partial(tables_kernel, n=n, slices=slices), grid...  11.1 us
    ppermute x7, waiting for transfers between devices, shifted(): lax.ppermute(block, 'lat', [(i, (i + distance) % size) for i in range(siz...  10.4 us
  transfers between devices with their start and end apart: 25, of which 10 were waited for; matrix products, arithmetic and copies ran while one was open for 2% of the time, Pallas kernels for 9%

profile of v8, /device:TPU:1, one launch (start us, length us, event | category | flops | bytes accessed | tf_op | source)
XLA Modules:
  0.0 159.3 jit_solution(8140891067597095343)
XLA Ops:
  0.0 1.8 %convert_bitcast_fusion.tile = bf16[2,128,2048]{2,1,0:T(8,128)(2,1)S(1)} fusion(f32[1,2,128,2048]{3,2,1,0:T(8,128)} %param.7), kind=kLoop, calls=%fused_computation.1 | loop fusion | flops 524288 | bytes 3145728 | tf_op jit(solution)/shard_map/convert_element_type | solution.py:466
  1.8 3.3 %collective-permute-start.2 = (bf16[2,128,2048]{2,1,0:T(8,128)(2,1)S(1)}, bf16[2,128,2048]{2,1,0:T(8,128)(2,1)S(1)}, u32[]{:S(2)}, u32[]{:S(2)}) collective-permute-start(bf16[2,128,2048]{2,1,0:T(8,128)(2,1)S(1)} %convert_bitcast_fusion.tile), channel_id=1, source_target_pairs={{0,15},{1,0},{2,1},{3,2},{4,3},{5,4},{6,5},{7,6},{8,7},{9,8},{10,9... | collective-permute-start | bytes 3145736 | tf_op jit(solution)/shard_map/ppermute | solution.py:375
  5.2 0.1 copy.8.places.own_places
  5.3 1.5 shard_map.73
  6.8 0.0 collective-permute-start.3
  6.8 0.0 collective-permute-start
  6.8 1.1 collective-permute-start.1
  7.8 0.7 fusion.2.plan.refs_0_
  8.5 4.7 %collective-permute-done.places = s32[4,2]{1,0:T(4,128)S(1)} collective-permute-done((s32[4,2]{1,0:T(4,128)S(1)}, s32[4,2]{1,0:T(4,128)S(1)}, u32[]{:S(2)}, u32[]{:S(2)}) %collective-permute-start) | collective-permute-done | bytes 64 | tf_op jit(solution)/shard_map/ppermute | solution.py:375
  13.2 5.7 %collective-permute-done.1.far_places = s32[4,2]{1,0:T(4,128)S(1)} collective-permute-done((s32[4,2]{1,0:T(4,128)S(1)}, s32[4,2]{1,0:T(4,128)S(1)}, u32[]{:S(2)}, u32[]{:S(2)}) %collective-permute-start.1) | collective-permute-done | bytes 64 | tf_op jit(solution)/shard_map/ppermute | solution.py:375
  18.9 0.0 collective-permute-done.3.behind
  18.9 0.0 collective-permute-done.2.ahead
  18.9 1.4 shard_map.75
  20.3 8.0 %collective-permute-start.7 = (bf16[2,256,256]{2,1,0:T(8,128)(2,1)S(1)}, bf16[2,256,256]{2,1,0:T(8,128)(2,1)S(1)}, u32[]{:S(2)}, u32[]{:S(2)}) collective-permute-start(bf16[2,256,256]{2,1,0:T(8,128)(2,1)S(1)} %get-tuple-element.40), channel_id=1, source_target_pairs={{0,48},{1,241},{2,50},{3,243},{4,52},{5,245},{6,54},{7,247},{8,56}... | collective-permute-start | bytes 786440 | tf_op jit(solution)/shard_map/ppermute | solution.py:435
  28.3 0.0 collective-permute-start.6
  28.3 0.4 collective-permute-start.5
  28.7 3.6 %collective-permute-done.7 = bf16[2,256,256]{2,1,0:T(8,128)(2,1)S(1)} collective-permute-done((bf16[2,256,256]{2,1,0:T(8,128)(2,1)S(1)}, bf16[2,256,256]{2,1,0:T(8,128)(2,1)S(1)}, u32[]{:S(2)}, u32[]{:S(2)}) %collective-permute-start.7) | collective-permute-done | bytes 262176 | tf_op jit(solution)/shard_map/ppermute | solution.py:435
  32.3 2.8 %collective-permute-done.6 = bf16[2,256,256]{2,1,0:T(8,128)(2,1)S(1)} collective-permute-done((bf16[2,256,256]{2,1,0:T(8,128)(2,1)S(1)}, bf16[2,256,256]{2,1,0:T(8,128)(2,1)S(1)}, u32[]{:S(2)}, u32[]{:S(2)}) %collective-permute-start.6) | collective-permute-done | bytes 262176 | tf_op jit(solution)/shard_map/ppermute | solution.py:435
  35.1 2.7 %collective-permute-done.5 = bf16[2,256,256]{2,1,0:T(8,128)(2,1)S(1)} collective-permute-done((bf16[2,256,256]{2,1,0:T(8,128)(2,1)S(1)}, bf16[2,256,256]{2,1,0:T(8,128)(2,1)S(1)}, u32[]{:S(2)}, u32[]{:S(2)}) %collective-permute-start.5) | collective-permute-done | bytes 262176 | tf_op jit(solution)/shard_map/ppermute | solution.py:435
  37.9 0.1 pad_maximum_fusion.refs_3_
  38.0 0.0 copy-start.5
  38.0 1.6 %collective-permute-start.8 = (bf16[4,2,256,256]{3,2,1,0:T(8,128)(2,1)S(1)}, bf16[4,2,256,256]{3,2,1,0:T(8,128)(2,1)}, u32[]{:S(2)}, u32[]{:S(2)}) collective-permute-start(bf16[4,2,256,256]{3,2,1,0:T(8,128)(2,1)S(1)} %pad_maximum_fusion.refs_3_), channel_id=1, source_target_pairs={{16,208},{18,210},{20,212},{22,214},{24,216},{26,218},{28,220},{30... | collective-permute-start | bytes 3145736 | tf_op jit(solution)/shard_map/ppermute | solution.py:435
  39.6 1.6 %collective-permute-start.9 = (bf16[4,2,256,256]{3,2,1,0:T(8,128)(2,1)S(1)}, bf16[4,2,256,256]{3,2,1,0:T(8,128)(2,1)}, u32[]{:S(2)}, u32[]{:S(2)}) collective-permute-start(bf16[4,2,256,256]{3,2,1,0:T(8,128)(2,1)S(1)} %pad_maximum_fusion.refs_3_), channel_id=1, source_target_pairs={{32,128},{33,193},{34,130},{35,195},{36,132},{37,197},{38,134},{39... | collective-permute-start | bytes 3145736 | tf_op jit(solution)/shard_map/ppermute | solution.py:435
  41.3 4.0 %collective-permute-start.10 = (bf16[4,2,256,256]{3,2,1,0:T(8,128)(2,1)S(1)}, bf16[4,2,256,256]{3,2,1,0:T(8,128)(2,1)}, u32[]{:S(2)}, u32[]{:S(2)}) collective-permute-start(bf16[4,2,256,256]{3,2,1,0:T(8,128)(2,1)S(1)} %pad_maximum_fusion.refs_3_), channel_id=1, source_target_pairs={{1,65},{3,67},{5,69},{7,71},{9,73},{11,75},{13,77},{15,79},{48,80}... | collective-permute-start | bytes 3145736 | tf_op jit(solution)/shard_map/ppermute | solution.py:435
  45.3 0.7 constant_dynamic-slice_fusion
  46.0 0.7 fusion.1
  48.7 0.7 dynamic-slice_bitcast_fusion
  49.4 0.0 collective-permute-start.4
  49.4 11.1 %shard_map.76.refs_7_ = bf16[17,2,512,512]{3,2,1,0:T(8,128)(2,1)} custom-call(f32[2,17]{1,0:T(2,128)} %constant.43.clone.scales, f32[4,256,256]{2,1,0:T(8,128)} %constant.44.clone.base), custom_call_target="tpu_custom_call" | custom-call | tf_op jit(solution)/shard_map/pallas_call | solution.py:49
  60.6 1.0 shard_map.74.refs_1_
  61.6 0.8 copy-done.1
  62.4 0.0 collective-permute-done.4.refs_2_
  62.4 0.0 collective-permute-done.8.refs_4_
  62.4 0.0 collective-permute-done.9.refs_5_
  62.5 0.7 copy-done.7
  63.1 1.6 %shard_map.77 = (bf16[4,2,128,256]{3,2,1,0:T(8,128)(2,1)}, bf16[4,2,128,256]{3,2,1,0:T(8,128)(2,1)}, bf16[4,2,128,256]{3,2,1,0:T(8,128)(2,1)}, bf16[4,2,128,256]...) custom-call(s32[48]{0:T(128)} %copy-done.3, ...), custom_call_target="tpu_custom_call" | custom-call | tf_op jit(solution)/shard_map/pallas_call | solution.py:226
  64.8 1.4 collective-permute-start.11
  66.2 0.7 collective-permute-start.12
  66.9 0.7 collective-permute-start.13
  69.5 39.5 %collective-permute-done.11 = bf16[4,2,128,256]{3,2,1,0:T(8,128)(2,1)S(1)} collective-permute-done((bf16[4,2,128,256]{3,2,1,0:T(8,128)(2,1)}, bf16[4,2,128,256]{3,2,1,0:T(8,128)(2,1)S(1)}, u32[]{:S(2)}, u32[]{:S(2)}) %collective-permute-start.11) | collective-permute-done | bytes 524320 | tf_op jit(solution)/shard_map/ppermute | solution.py:435
  109.0 0.0 collective-permute-done.12
  109.0 1.2 select_select_fusion.1
  110.3 8.1 %collective-permute-start.16 = (bf16[2,128,256]{2,1,0:T(8,128)(2,1)S(1)}, bf16[2,128,256]{2,1,0:T(8,128)(2,1)S(1)}, u32[]{:S(2)}, u32[]{:S(2)}) collective-permute-start(bf16[2,128,256]{2,1,0:T(8,128)(2,1)S(1)} %get-tuple-element.56), channel_id=1, source_target_pairs={{0,48},{1,241},{2,50},{3,243},{4,52},{5,245},{6,54},{7,247},{8,56}... | collective-permute-start | bytes 393224 | tf_op jit(solution)/shard_map/ppermute | solution.py:435
  118.4 0.7 collective-permute-start.20
  119.1 0.7 collective-permute-start.21
  119.8 4.7 %collective-permute-done.16 = bf16[2,128,256]{2,1,0:T(8,128)(2,1)S(1)} collective-permute-done((bf16[2,128,256]{2,1,0:T(8,128)(2,1)S(1)}, bf16[2,128,256]{2,1,0:T(8,128)(2,1)S(1)}, u32[]{:S(2)}, u32[]{:S(2)}) %collective-permute-start.16) | collective-permute-done | bytes 131104 | tf_op jit(solution)/shard_map/ppermute | solution.py:435
  124.4 1.3 collective-permute-start.19
  125.7 0.1 collective-permute-start.15
  125.8 1.0 collective-permute-start.14
  126.9 5.9 %collective-permute-done.15 = bf16[2,128,256]{2,1,0:T(8,128)(2,1)S(1)} collective-permute-done((bf16[2,128,256]{2,1,0:T(8,128)(2,1)S(1)}, bf16[2,128,256]{2,1,0:T(8,128)(2,1)S(1)}, u32[]{:S(2)}, u32[]{:S(2)}) %collective-permute-start.15) | collective-permute-done | bytes 131104 | tf_op jit(solution)/shard_map/ppermute | solution.py:435
  132.8 0.1 pad_maximum_fusion.1
  132.9 8.4 %collective-permute-start.17 = (bf16[4,2,128,256]{3,2,1,0:T(8,128)(2,1)S(1)}, bf16[4,2,128,256]{3,2,1,0:T(8,128)(2,1)S(1)}, u32[]{:S(2)}, u32[]{:S(2)}) collective-permute-start(bf16[4,2,128,256]{3,2,1,0:T(8,128)(2,1)S(1)} %pad_maximum_fusion.1), channel_id=1, source_target_pairs={{0,15},{1,0},{2,1},{3,2},{4,3},{5,4},{6,5},{7,6},{8,7},{9,8},{10,9... | collective-permute-start | bytes 1572872 | tf_op jit(solution)/shard_map/ppermute | solution.py:375
  141.3 0.0 collective-permute-done.20
  141.3 0.0 collective-permute-done.21
  141.3 1.4 collective-permute-done.19
  142.7 0.2 select_select_fusion
  142.9 0.1 collective-permute-start.22
  143.0 1.8 %collective-permute-start.23 = (bf16[2,128,256]{2,1,0:T(8,128)(2,1)S(1)}, bf16[2,128,256]{2,1,0:T(8,128)(2,1)S(1)}, u32[]{:S(2)}, u32[]{:S(2)}) collective-permute-start(bf16[2,128,256]{2,1,0:T(8,128)(2,1)S(1)} %get-tuple-element.52), channel_id=1, source_target_pairs={{0,32},{1,225},{2,34},{3,227},{4,36},{5,229},{6,38},{7,231},{8,40}... | collective-permute-start | bytes 393224 | tf_op jit(solution)/shard_map/ppermute | solution.py:435
  144.8 3.5 %collective-permute-start.24 = (bf16[2,128,256]{2,1,0:T(8,128)(2,1)S(1)}, bf16[2,128,256]{2,1,0:T(8,128)(2,1)S(1)}, u32[]{:S(2)}, u32[]{:S(2)}) collective-permute-start(bf16[2,128,256]{2,1,0:T(8,128)(2,1)S(1)} %get-tuple-element.51), channel_id=1, source_target_pairs={{0,48},{1,241},{2,50},{3,243},{4,52},{5,245},{6,54},{7,247},{8,56}... | collective-permute-start | bytes 393224 | tf_op jit(solution)/shard_map/ppermute | solution.py:435
  148.4 0.0 collective-permute-done.17.from_own
  148.4 0.0 collective-permute-done.18.from_far
  148.4 1.3 shard_map.78.total
  149.7 7.2 %collective-permute-done.22.m1 = bf16[2,128,256]{2,1,0:T(8,128)(2,1)S(1)} collective-permute-done((bf16[2,128,256]{2,1,0:T(8,128)(2,1)S(1)}, bf16[2,128,256]{2,1,0:T(8,128)(2,1)S(1)}, u32[]{:S(2)}, u32[]{:S(2)}) %collective-permute-start.22) | collective-permute-done | bytes 131104 | tf_op jit(solution)/shard_map/ppermute | solution.py:435
  156.9 2.2 %shard_map.79 = f32[2,128,2048]{2,1,0:T(8,128)} custom-call(s32[48]{0:T(128)S(1)} %copy-done.4, s32[4,2]{1,0:T(4,128)S(1)} %collective-permute-done.places, f32[2,128,2048]{2,1,0:T(8,128)S(1)} %shard_map.78.total, bf16[2,128,256]{2,1,0:T(8,128)(2,1)S(1)} %get-tuple-element.54.m0, bf16[2,128,256]{2,1,0:T(8,128)(2,1)S(1)} %collective-permute-done.22.m1, ...), custom_call_target="tpu_custom_call" | custom-call | tf_op jit(solution)/shard_map/pallas_call | solution.py:363
  (29 shorter events, 0.1 us)
Async XLA Ops:
  0.0 48.7 %copy-start = (f32[4,256,256]{2,1,0:T(8,128)S(1)}, f32[4,256,256]{2,1,0:T(8,128)}, u32[]{:S(2)}) copy-start(f32[4,256,256]{2,1,0:T(8,128)} %param.10) | copy-start | bytes 3145732
  0.0 5.2 %copy-start.8 = (s32[4,2]{0,1:T(2,128)S(1)}, s32[4,2]{0,1:T(2,128)}, u32[]{:S(2)}) copy-start(s32[4,2]{0,1:T(2,128)} %param.9) | copy-start | bytes 100
  1.8 17.1 %collective-permute-start.2 = (bf16[2,128,2048]{2,1,0:T(8,128)(2,1)S(1)}, bf16[2,128,2048]{2,1,0:T(8,128)(2,1)S(1)}, u32[]{:S(2)}, u32[]{:S(2)}) collective-permute-start(bf16[2,128,2048]{2,1,0:T(8,128)(2,1)S(1)} %convert_bitcast_fusion.tile), channel_id=1, source_target_pairs={{0,15},{1,0},{2,1},{3,2},{4,3},{5,4},{6,5},{7,6},{8,7},{9,8},{10,9... | collective-permute-start | bytes 3145736 | tf_op jit(solution)/shard_map/ppermute | solution.py:375
  6.8 12.1 %collective-permute-start.3 = (bf16[4,2,128,256]{3,2,1,0:T(8,128)(2,1)}, bf16[4,2,128,256]{3,2,1,0:T(8,128)(2,1)}, u32[]{:S(2)}, u32[]{:S(2)}) collective-permute-start(bf16[4,2,128,256]{3,2,1,0:T(8,128)(2,1)} %shard_map.73), channel_id=1, source_target_pairs={{0,1},{1,2},{2,3},{3,4},{4,5},{5,6},{6,7},{7,8},{8,9},{9,10},{10,1... | collective-permute-start | bytes 1572872 | tf_op jit(solution)/shard_map/ppermute | solution.py:375
  6.8 6.5 %collective-permute-start = (s32[4,2]{1,0:T(4,128)S(1)}, s32[4,2]{1,0:T(4,128)S(1)}, u32[]{:S(2)}, u32[]{:S(2)}) collective-permute-start(s32[4,2]{1,0:T(4,128)S(1)} %copy.8.places.own_places), channel_id=1, source_target_pairs={{0,1},{1,2},{2,3},{3,4},{4,5},{5,6},{6,7},{7,8},{8,9},{9,10},{10,1... | collective-permute-start | bytes 104 | tf_op jit(solution)/shard_map/ppermute | solution.py:375
  6.8 12.1 %collective-permute-start.1 = (s32[4,2]{1,0:T(4,128)S(1)}, s32[4,2]{1,0:T(4,128)S(1)}, u32[]{:S(2)}, u32[]{:S(2)}) collective-permute-start(s32[4,2]{1,0:T(4,128)S(1)} %copy.8.places.own_places), channel_id=1, source_target_pairs={{0,2},{1,3},{2,4},{3,5},{4,6},{5,7},{6,8},{7,9},{8,10},{9,11},{10,... | collective-permute-start | bytes 104 | tf_op jit(solution)/shard_map/ppermute | solution.py:375
  8.5 52.0 %copy-start.3 = (s32[48]{0:T(128)}, s32[48]{0:T(128)S(1)}, u32[]{:S(2)}) copy-start(s32[48]{0:T(128)S(1)} %fusion.2.plan.refs_0_) | copy-start | bytes 580
  20.3 12.0 %collective-permute-start.7 = (bf16[2,256,256]{2,1,0:T(8,128)(2,1)S(1)}, bf16[2,256,256]{2,1,0:T(8,128)(2,1)S(1)}, u32[]{:S(2)}, u32[]{:S(2)}) collective-permute-start(bf16[2,256,256]{2,1,0:T(8,128)(2,1)S(1)} %get-tuple-element.40), channel_id=1, source_target_pairs={{0,48},{1,241},{2,50},{3,243},{4,52},{5,245},{6,54},{7,247},{8,56}... | collective-permute-start | bytes 786440 | tf_op jit(solution)/shard_map/ppermute | solution.py:435
  28.3 6.8 %collective-permute-start.6 = (bf16[2,256,256]{2,1,0:T(8,128)(2,1)S(1)}, bf16[2,256,256]{2,1,0:T(8,128)(2,1)S(1)}, u32[]{:S(2)}, u32[]{:S(2)}) collective-permute-start(bf16[2,256,256]{2,1,0:T(8,128)(2,1)S(1)} %get-tuple-element.39), channel_id=1, source_target_pairs={{0,32},{1,225},{2,34},{3,227},{4,36},{5,229},{6,38},{7,231},{8,40}... | collective-permute-start | bytes 786440 | tf_op jit(solution)/shard_map/ppermute | solution.py:435
  28.3 9.5 %collective-permute-start.5 = (bf16[2,256,256]{2,1,0:T(8,128)(2,1)S(1)}, bf16[2,256,256]{2,1,0:T(8,128)(2,1)S(1)}, u32[]{:S(2)}, u32[]{:S(2)}) collective-permute-start(bf16[2,256,256]{2,1,0:T(8,128)(2,1)S(1)} %get-tuple-element.38), channel_id=1, source_target_pairs={{0,16},{1,17},{2,18},{3,19},{4,20},{5,21},{6,22},{7,23},{8,24},{9,... | collective-permute-start | bytes 786440 | tf_op jit(solution)/shard_map/ppermute | solution.py:435
  38.0 22.6 %copy-start.5 = (bf16[4,2,256,256]{3,2,1,0:T(8,128)(2,1)}, bf16[4,2,256,256]{3,2,1,0:T(8,128)(2,1)S(1)}, u32[]{:S(2)}) copy-start(bf16[4,2,256,256]{3,2,1,0:T(8,128)(2,1)S(1)} %pad_maximum_fusion.refs_3_) | copy-start | bytes 3145732
  38.0 24.4 %collective-permute-start.8 = (bf16[4,2,256,256]{3,2,1,0:T(8,128)(2,1)S(1)}, bf16[4,2,256,256]{3,2,1,0:T(8,128)(2,1)}, u32[]{:S(2)}, u32[]{:S(2)}) collective-permute-start(bf16[4,2,256,256]{3,2,1,0:T(8,128)(2,1)S(1)} %pad_maximum_fusion.refs_3_), channel_id=1, source_target_pairs={{16,208},{18,210},{20,212},{22,214},{24,216},{26,218},{28,220},{30... | collective-permute-start | bytes 3145736 | tf_op jit(solution)/shard_map/ppermute | solution.py:435
  39.6 22.8 %collective-permute-start.9 = (bf16[4,2,256,256]{3,2,1,0:T(8,128)(2,1)S(1)}, bf16[4,2,256,256]{3,2,1,0:T(8,128)(2,1)}, u32[]{:S(2)}, u32[]{:S(2)}) collective-permute-start(bf16[4,2,256,256]{3,2,1,0:T(8,128)(2,1)S(1)} %pad_maximum_fusion.refs_3_), channel_id=1, source_target_pairs={{32,128},{33,193},{34,130},{35,195},{36,132},{37,197},{38,134},{39... | collective-permute-start | bytes 3145736 | tf_op jit(solution)/shard_map/ppermute | solution.py:435
  41.3 21.2 %collective-permute-start.10 = (bf16[4,2,256,256]{3,2,1,0:T(8,128)(2,1)S(1)}, bf16[4,2,256,256]{3,2,1,0:T(8,128)(2,1)}, u32[]{:S(2)}, u32[]{:S(2)}) collective-permute-start(bf16[4,2,256,256]{3,2,1,0:T(8,128)(2,1)S(1)} %pad_maximum_fusion.refs_3_), channel_id=1, source_target_pairs={{1,65},{3,67},{5,69},{7,71},{9,73},{11,75},{13,77},{15,79},{48,80}... | collective-permute-start | bytes 3145736 | tf_op jit(solution)/shard_map/ppermute | solution.py:435
  49.4 11.2 %copy-start.2 = (f32[2,2,256,256]{3,2,1,0:T(8,128)S(1)}, f32[2,2,256,256]{3,2,1,0:T(8,128)}, u32[]{:S(2)}) copy-start(f32[2,2,256,256]{3,2,1,0:T(8,128)} %probe.1) | copy-start | bytes 3145732
  49.4 13.0 %collective-permute-start.4 = (f32[256,256]{1,0:T(8,128)}, f32[256,256]{1,0:T(8,128)S(1)}, u32[]{:S(2)}, u32[]{:S(2)}) collective-permute-start(f32[256,256]{1,0:T(8,128)} %dynamic-slice_bitcast_fusion), channel_id=1, source_target_pairs={{0,1},{1,2},{2,3},{3,4},{4,5},{5,6},{6,7},{7,8},{8,9},{9,10},{10,1... | collective-permute-start | bytes 786440 | tf_op jit(solution)/shard_map/ppermute | solution.py:375
  61.6 0.8 copy-start.1
  62.4 0.7 copy-start.7
  64.8 53.6 %copy-start.11 = (bf16[4,2,128,256]{3,2,1,0:T(8,128)(2,1)S(1)}, bf16[4,2,128,256]{3,2,1,0:T(8,128)(2,1)}, u32[]{:S(2)}) copy-start(bf16[4,2,128,256]{3,2,1,0:T(8,128)(2,1)} %get-tuple-element.48) | copy-start | bytes 1572868
  64.8 54.3 %copy-start.10 = (bf16[4,2,128,256]{3,2,1,0:T(8,128)(2,1)S(1)}, bf16[4,2,128,256]{3,2,1,0:T(8,128)(2,1)}, u32[]{:S(2)}) copy-start(bf16[4,2,128,256]{3,2,1,0:T(8,128)(2,1)} %get-tuple-element.49) | copy-start | bytes 1572868
  64.8 59.7 %copy-start.9 = (bf16[4,2,128,256]{3,2,1,0:T(8,128)(2,1)S(1)}, bf16[4,2,128,256]{3,2,1,0:T(8,128)(2,1)}, u32[]{:S(2)}) copy-start(bf16[4,2,128,256]{3,2,1,0:T(8,128)(2,1)} %get-tuple-element.47) | copy-start | bytes 1572868
  64.8 44.2 %collective-permute-start.11 = (bf16[4,2,128,256]{3,2,1,0:T(8,128)(2,1)}, bf16[4,2,128,256]{3,2,1,0:T(8,128)(2,1)S(1)}, u32[]{:S(2)}, u32[]{:S(2)}) collective-permute-start(bf16[4,2,128,256]{3,2,1,0:T(8,128)(2,1)} %get-tuple-element.41), channel_id=1, source_target_pairs={{0,224},{2,226},{4,228},{6,230},{8,232},{10,234},{12,236},{14,238}... | collective-permute-start | bytes 1572872 | tf_op jit(solution)/shard_map/ppermute | solution.py:435
  66.2 42.8 %collective-permute-start.12 = (bf16[4,2,128,256]{3,2,1,0:T(8,128)(2,1)}, bf16[4,2,128,256]{3,2,1,0:T(8,128)(2,1)S(1)}, u32[]{:S(2)}, u32[]{:S(2)}) collective-permute-start(bf16[4,2,128,256]{3,2,1,0:T(8,128)(2,1)} %get-tuple-element.42), channel_id=1, source_target_pairs={{0,160},{2,162},{4,164},{6,166},{8,168},{10,170},{12,172},{14,174}... | collective-permute-start | bytes 1572872 | tf_op jit(solution)/shard_map/ppermute | solution.py:435
  66.9 42.1 %collective-permute-start.13 = (bf16[4,2,128,256]{3,2,1,0:T(8,128)(2,1)}, bf16[4,2,128,256]{3,2,1,0:T(8,128)(2,1)S(1)}, u32[]{:S(2)}, u32[]{:S(2)}) collective-permute-start(bf16[4,2,128,256]{3,2,1,0:T(8,128)(2,1)} %get-tuple-element.43), channel_id=1, source_target_pairs={{0,64},{2,66},{4,68},{6,70},{8,72},{10,74},{12,76},{14,78},{17,49}... | collective-permute-start | bytes 1572872 | tf_op jit(solution)/shard_map/ppermute | solution.py:435
  109.0 33.7 %copy-start.6 = (bf16[4,2,128,256]{3,2,1,0:T(8,128)(2,1)S(1)}, bf16[4,2,128,256]{3,2,1,0:T(8,128)(2,1)}, u32[]{:S(2)}) copy-start(bf16[4,2,128,256]{3,2,1,0:T(8,128)(2,1)} %get-tuple-element.50) | copy-start | bytes 1572868
  110.3 14.2 %collective-permute-start.16 = (bf16[2,128,256]{2,1,0:T(8,128)(2,1)S(1)}, bf16[2,128,256]{2,1,0:T(8,128)(2,1)S(1)}, u32[]{:S(2)}, u32[]{:S(2)}) collective-permute-start(bf16[2,128,256]{2,1,0:T(8,128)(2,1)S(1)} %get-tuple-element.56), channel_id=1, source_target_pairs={{0,48},{1,241},{2,50},{3,243},{4,52},{5,245},{6,54},{7,247},{8,56}... | collective-permute-start | bytes 393224 | tf_op jit(solution)/shard_map/ppermute | solution.py:435
  118.4 22.9 %collective-permute-start.20 = (bf16[4,2,128,256]{3,2,1,0:T(8,128)(2,1)S(1)}, bf16[4,2,128,256]{3,2,1,0:T(8,128)(2,1)S(1)}, u32[]{:S(2)}, u32[]{:S(2)}) collective-permute-start(bf16[4,2,128,256]{3,2,1,0:T(8,128)(2,1)S(1)} %copy-done.11), channel_id=1, source_target_pairs={{0,160},{2,162},{4,164},{6,166},{8,168},{10,170},{12,172},{14,174}... | collective-permute-start | bytes 1572872 | tf_op jit(solution)/shard_map/ppermute | solution.py:435
  119.1 22.2 %collective-permute-start.21 = (bf16[4,2,128,256]{3,2,1,0:T(8,128)(2,1)S(1)}, bf16[4,2,128,256]{3,2,1,0:T(8,128)(2,1)S(1)}, u32[]{:S(2)}, u32[]{:S(2)}) collective-permute-start(bf16[4,2,128,256]{3,2,1,0:T(8,128)(2,1)S(1)} %copy-done.10), channel_id=1, source_target_pairs={{0,64},{2,66},{4,68},{6,70},{8,72},{10,74},{12,76},{14,78},{17,49}... | collective-permute-start | bytes 1572872 | tf_op jit(solution)/shard_map/ppermute | solution.py:435
  124.4 18.3 %collective-permute-start.19 = (bf16[4,2,128,256]{3,2,1,0:T(8,128)(2,1)S(1)}, bf16[4,2,128,256]{3,2,1,0:T(8,128)(2,1)S(1)}, u32[]{:S(2)}, u32[]{:S(2)}) collective-permute-start(bf16[4,2,128,256]{3,2,1,0:T(8,128)(2,1)S(1)} %copy-done.9), channel_id=1, source_target_pairs={{0,224},{2,226},{4,228},{6,230},{8,232},{10,234},{12,236},{14,238}... | collective-permute-start | bytes 1572872 | tf_op jit(solution)/shard_map/ppermute | solution.py:435
  125.7 7.1 %collective-permute-start.15 = (bf16[2,128,256]{2,1,0:T(8,128)(2,1)S(1)}, bf16[2,128,256]{2,1,0:T(8,128)(2,1)S(1)}, u32[]{:S(2)}, u32[]{:S(2)}) collective-permute-start(bf16[2,128,256]{2,1,0:T(8,128)(2,1)S(1)} %get-tuple-element.57), channel_id=1, source_target_pairs={{0,32},{1,225},{2,34},{3,227},{4,36},{5,229},{6,38},{7,231},{8,40}... | collective-permute-start | bytes 393224 | tf_op jit(solution)/shard_map/ppermute | solution.py:435
  125.8 7.0 %collective-permute-start.14 = (bf16[2,128,256]{2,1,0:T(8,128)(2,1)S(1)}, bf16[2,128,256]{2,1,0:T(8,128)(2,1)S(1)}, u32[]{:S(2)}, u32[]{:S(2)}) collective-permute-start(bf16[2,128,256]{2,1,0:T(8,128)(2,1)S(1)} %get-tuple-element.58), channel_id=1, source_target_pairs={{0,16},{1,17},{2,18},{3,19},{4,20},{5,21},{6,22},{7,23},{8,24},{9,... | collective-permute-start | bytes 393224 | tf_op jit(solution)/shard_map/ppermute | solution.py:435
  132.9 15.5 %copy-start.4 = (s32[48]{0:T(128)S(1)}, s32[48]{0:T(128)}, u32[]{:S(2)}) copy-start(s32[48]{0:T(128)} %copy-done.3) | copy-start | bytes 580
  132.9 15.5 %collective-permute-start.17 = (bf16[4,2,128,256]{3,2,1,0:T(8,128)(2,1)S(1)}, bf16[4,2,128,256]{3,2,1,0:T(8,128)(2,1)S(1)}, u32[]{:S(2)}, u32[]{:S(2)}) collective-permute-start(bf16[4,2,128,256]{3,2,1,0:T(8,128)(2,1)S(1)} %pad_maximum_fusion.1), channel_id=1, source_target_pairs={{0,15},{1,0},{2,1},{3,2},{4,3},{5,4},{6,5},{7,6},{8,7},{9,8},{10,9... | collective-permute-start | bytes 1572872 | tf_op jit(solution)/shard_map/ppermute | solution.py:375
  141.3 7.1 %collective-permute-start.18 = (bf16[4,2,128,256]{3,2,1,0:T(8,128)(2,1)S(1)}, bf16[4,2,128,256]{3,2,1,0:T(8,128)(2,1)S(1)}, u32[]{:S(2)}, u32[]{:S(2)}) collective-permute-start(bf16[4,2,128,256]{3,2,1,0:T(8,128)(2,1)S(1)} %pad_maximum_fusion.1), channel_id=1, source_target_pairs={{0,1},{1,2},{2,3},{3,4},{4,5},{5,6},{6,7},{7,8},{8,9},{9,10},{10,1... | collective-permute-start | bytes 1572872 | tf_op jit(solution)/shard_map/ppermute | solution.py:375
  142.9 14.0 %collective-permute-start.22 = (bf16[2,128,256]{2,1,0:T(8,128)(2,1)S(1)}, bf16[2,128,256]{2,1,0:T(8,128)(2,1)S(1)}, u32[]{:S(2)}, u32[]{:S(2)}) collective-permute-start(bf16[2,128,256]{2,1,0:T(8,128)(2,1)S(1)} %get-tuple-element.53), channel_id=1, source_target_pairs={{0,16},{1,17},{2,18},{3,19},{4,20},{5,21},{6,22},{7,23},{8,24},{9,... | collective-permute-start | bytes 393224 | tf_op jit(solution)/shard_map/ppermute | solution.py:435
  143.0 13.9 %collective-permute-start.23 = (bf16[2,128,256]{2,1,0:T(8,128)(2,1)S(1)}, bf16[2,128,256]{2,1,0:T(8,128)(2,1)S(1)}, u32[]{:S(2)}, u32[]{:S(2)}) collective-permute-start(bf16[2,128,256]{2,1,0:T(8,128)(2,1)S(1)} %get-tuple-element.52), channel_id=1, source_target_pairs={{0,32},{1,225},{2,34},{3,227},{4,36},{5,229},{6,38},{7,231},{8,40}... | collective-permute-start | bytes 393224 | tf_op jit(solution)/shard_map/ppermute | solution.py:435
  144.8 12.1 %collective-permute-start.24 = (bf16[2,128,256]{2,1,0:T(8,128)(2,1)S(1)}, bf16[2,128,256]{2,1,0:T(8,128)(2,1)S(1)}, u32[]{:S(2)}, u32[]{:S(2)}) collective-permute-start(bf16[2,128,256]{2,1,0:T(8,128)(2,1)S(1)} %get-tuple-element.51), channel_id=1, source_target_pairs={{0,48},{1,241},{2,50},{3,243},{4,52},{5,245},{6,54},{7,247},{8,56}... | collective-permute-start | bytes 393224 | tf_op jit(solution)/shard_map/ppermute | solution.py:435

commit v9 on v8

--- a/solution.py
+++ b/solution.py
@@ -479,19 +479,18 @@
     messages = [message] + [towards(message, k) for k in (1, 2, 3)]
     tables = make_tables(n, depth_size)
     wave = roll_probe(plan, mid_places, probe, rows)
+    wave, source = lax.optimization_barrier((wave, [plan[SOURCE] == k for k in (1, 2, 3)]))
     terms = tuple(chain(plan, wave, target, messages, tables))
 
     def home(pieces):
         block = pieces[0]
         for k in (1, 2, 3):
-            block = jnp.where(plan[SOURCE] == k, away(pieces[k], k), block)
+            block = jnp.where(source[k - 1], away(pieces[k], k), block)
         return block
 
     near_block = home(terms[:4])
-    near_got = [within(near_block[k], k) for k in (1, 2, 3)]
-    late, near_got[2] = lax.optimization_barrier((terms[7], near_got[2]))
-    far_block = home(terms[4:7] + (late,))
-    mixed = jnp.stack([near_block[0]] + near_got)
+    far_block = home(terms[4:])
+    mixed = jnp.stack([near_block[0]] + [within(near_block[k], k) for k in (1, 2, 3)])
     mids = [far_block[0]] + [within(far_block[k], k) for k in (1, 2, 3)]
     from_own = shifted(mixed, -1)
     from_far = shifted(mixed, 1)

time: 160 us -> 154 us (0.963)
  waiting for transfers between devices: 78.3 us -> 69.3 us
  starting transfers between devices: 48.6 us -> 52.2 us
    ppermute x18, waiting for transfers between devices: 67.9 us -> 59.2 us  [permute(): return lax.ppermute(block, ('depth', 'lat'), pairs)]
    ppermute x18, starting transfers between devices: 35.9 us -> 38.9 us  [permute(): return lax.ppermute(block, ('depth', 'lat'), pairs)]
  transfers between devices with their start and end apart: 25 -> 25, of which waited for: 10 -> 9; matrix products, arithmetic and copies ran while one was open for 2% -> 3% of each run, Pallas kernels for 9% -> 10%
where the time goes in v9:
time: 154 us
  waiting for transfers between devices  69.3 us (45%)
  starting transfers between devices  52.2 us (34%)
  Pallas kernels  20.2 us (13%)
  local copies, waits for them, and re-layouts  4.43 us (3%)
  between operations  4.39 us (3%)
  other arithmetic  3.44 us (2%)
    ppermute x18, waiting for transfers between devices, permute(): return lax.ppermute(block, ('depth', 'lat'), pairs)  59.2 us
    ppermute x18, starting transfers between devices, permute(): return lax.ppermute(block, ('depth', 'lat'), pairs)  38.9 us
    ppermute x7, starting transfers between devices, shifted(): lax.ppermute(block, 'lat', [(i, (i + distance) % size) for i in range(siz...  13.3 us
    pallas_call x1, Pallas kernels, make_tables(): pl.pallas_call(functools.partial(tables_kernel, n=n, slices=slices), grid...  11.2 us
    ppermute x7, waiting for transfers between devices, shifted(): lax.ppermute(block, 'lat', [(i, (i + distance) % size) for i in range(siz...  10.1 us
  transfers between devices with their start and end apart: 25, of which 9 were waited for; matrix products, arithmetic and copies ran while one was open for 3% of the time, Pallas kernels for 10%

profile of v9, /device:TPU:1, one launch (start us, length us, event | category | flops | bytes accessed | tf_op | source)
XLA Modules:
  0.0 153.9 jit_solution(5060374362241104926)
XLA Ops:
  0.0 1.8 %convert_bitcast_fusion.tile = bf16[2,128,2048]{2,1,0:T(8,128)(2,1)S(1)} fusion(f32[1,2,128,2048]{3,2,1,0:T(8,128)} %param.7), kind=kLoop, calls=%fused_computation.1 | loop fusion | flops 524288 | bytes 3145728 | tf_op jit(solution)/shard_map/convert_element_type | solution.py:466
  1.8 3.3 %collective-permute-start.2 = (bf16[2,128,2048]{2,1,0:T(8,128)(2,1)S(1)}, bf16[2,128,2048]{2,1,0:T(8,128)(2,1)S(1)}, u32[]{:S(2)}, u32[]{:S(2)}) collective-permute-start(bf16[2,128,2048]{2,1,0:T(8,128)(2,1)S(1)} %convert_bitcast_fusion.tile), channel_id=1, source_target_pairs={{0,15},{1,0},{2,1},{3,2},{4,3},{5,4},{6,5},{7,6},{8,7},{9,8},{10,9... | collective-permute-start | bytes 3145736 | tf_op jit(solution)/shard_map/ppermute | solution.py:375
  5.2 0.1 copy.8.places.own_places
  5.3 1.5 shard_map.73
  6.8 0.0 collective-permute-start.3
  6.8 0.6 collective-permute-start.1
  7.4 0.8 collective-permute-start
  8.1 0.7 fusion.2.plan.refs_0_
  8.8 10.1 %collective-permute-done.1.far_places = s32[4,2]{1,0:T(4,128)S(1)} collective-permute-done((s32[4,2]{1,0:T(4,128)S(1)}, s32[4,2]{1,0:T(4,128)S(1)}, u32[]{:S(2)}, u32[]{:S(2)}) %collective-permute-start.1) | collective-permute-done | bytes 64 | tf_op jit(solution)/shard_map/ppermute | solution.py:375
  18.9 0.0 collective-permute-done.3.behind
  18.9 0.0 collective-permute-done.2.ahead
  18.9 1.4 shard_map.75
  20.3 2.7 %collective-permute-start.5 = (bf16[2,256,256]{2,1,0:T(8,128)(2,1)S(1)}, bf16[2,256,256]{2,1,0:T(8,128)(2,1)S(1)}, u32[]{:S(2)}, u32[]{:S(2)}) collective-permute-start(bf16[2,256,256]{2,1,0:T(8,128)(2,1)S(1)} %get-tuple-element.42), channel_id=1, source_target_pairs={{0,16},{1,17},{2,18},{3,19},{4,20},{5,21},{6,22},{7,23},{8,24},{9,... | collective-permute-start | bytes 786440 | tf_op jit(solution)/shard_map/ppermute | solution.py:435
  23.1 5.6 %collective-permute-start.6 = (bf16[2,256,256]{2,1,0:T(8,128)(2,1)S(1)}, bf16[2,256,256]{2,1,0:T(8,128)(2,1)S(1)}, u32[]{:S(2)}, u32[]{:S(2)}) collective-permute-start(bf16[2,256,256]{2,1,0:T(8,128)(2,1)S(1)} %get-tuple-element.43), channel_id=1, source_target_pairs={{0,32},{1,225},{2,34},{3,227},{4,36},{5,229},{6,38},{7,231},{8,40}... | collective-permute-start | bytes 786440 | tf_op jit(solution)/shard_map/ppermute | solution.py:435
  28.6 0.1 collective-permute-start.7
  28.7 0.7 collective-permute-done.5
  29.4 3.2 %collective-permute-done.6 = bf16[2,256,256]{2,1,0:T(8,128)(2,1)S(1)} collective-permute-done((bf16[2,256,256]{2,1,0:T(8,128)(2,1)S(1)}, bf16[2,256,256]{2,1,0:T(8,128)(2,1)S(1)}, u32[]{:S(2)}, u32[]{:S(2)}) %collective-permute-start.6) | collective-permute-done | bytes 262176 | tf_op jit(solution)/shard_map/ppermute | solution.py:435
  32.7 4.8 %collective-permute-done.7 = bf16[2,256,256]{2,1,0:T(8,128)(2,1)S(1)} collective-permute-done((bf16[2,256,256]{2,1,0:T(8,128)(2,1)S(1)}, bf16[2,256,256]{2,1,0:T(8,128)(2,1)S(1)}, u32[]{:S(2)}, u32[]{:S(2)}) %collective-permute-start.7) | collective-permute-done | bytes 262176 | tf_op jit(solution)/shard_map/ppermute | solution.py:435
  37.5 0.1 pad_maximum_fusion.refs_3_
  37.6 0.0 copy-start.5
  37.6 3.5 %collective-permute-start.10 = (bf16[4,2,256,256]{3,2,1,0:T(8,128)(2,1)S(1)}, bf16[4,2,256,256]{3,2,1,0:T(8,128)(2,1)}, u32[]{:S(2)}, u32[]{:S(2)}) collective-permute-start(bf16[4,2,256,256]{3,2,1,0:T(8,128)(2,1)S(1)} %pad_maximum_fusion.refs_3_), channel_id=1, source_target_pairs={{1,65},{3,67},{5,69},{7,71},{9,73},{11,75},{13,77},{15,79},{48,80}... | collective-permute-start | bytes 3145736 | tf_op jit(solution)/shard_map/ppermute | solution.py:435
  41.1 1.6 %collective-permute-start.9 = (bf16[4,2,256,256]{3,2,1,0:T(8,128)(2,1)S(1)}, bf16[4,2,256,256]{3,2,1,0:T(8,128)(2,1)}, u32[]{:S(2)}, u32[]{:S(2)}) collective-permute-start(bf16[4,2,256,256]{3,2,1,0:T(8,128)(2,1)S(1)} %pad_maximum_fusion.refs_3_), channel_id=1, source_target_pairs={{32,128},{33,193},{34,130},{35,195},{36,132},{37,197},{38,134},{39... | collective-permute-start | bytes 3145736 | tf_op jit(solution)/shard_map/ppermute | solution.py:435
  42.7 1.6 %collective-permute-start.8 = (bf16[4,2,256,256]{3,2,1,0:T(8,128)(2,1)S(1)}, bf16[4,2,256,256]{3,2,1,0:T(8,128)(2,1)}, u32[]{:S(2)}, u32[]{:S(2)}) collective-permute-start(bf16[4,2,256,256]{3,2,1,0:T(8,128)(2,1)S(1)} %pad_maximum_fusion.refs_3_), channel_id=1, source_target_pairs={{16,208},{18,210},{20,212},{22,214},{24,216},{26,218},{28,220},{30... | collective-permute-start | bytes 3145736 | tf_op jit(solution)/shard_map/ppermute | solution.py:435
  44.4 0.7 constant_dynamic-slice_fusion
  45.1 0.7 fusion.1
  47.8 0.7 dynamic-slice_bitcast_fusion
  48.5 0.0 collective-permute-start.4
  50.5 0.0 copy-start.2
  50.5 11.2 %shard_map.76.refs_7_ = bf16[17,2,512,512]{3,2,1,0:T(8,128)(2,1)} custom-call(f32[2,17]{1,0:T(2,128)} %constant.43.clone.scales, f32[4,256,256]{2,1,0:T(8,128)} %constant.44.clone.base), custom_call_target="tpu_custom_call" | custom-call | tf_op jit(solution)/shard_map/pallas_call | solution.py:49
  61.7 1.0 shard_map.74.refs_1_
  62.7 0.8 copy-done.1
  63.4 0.0 collective-permute-done.4.refs_2_
  63.5 0.0 collective-permute-done.10.refs_6_
  63.5 0.0 collective-permute-done.8.refs_4_
  63.5 0.7 copy-done.7
  64.1 1.6 %shard_map.77 = (bf16[4,2,128,256]{3,2,1,0:T(8,128)(2,1)}, bf16[4,2,128,256]{3,2,1,0:T(8,128)(2,1)}, bf16[4,2,128,256]{3,2,1,0:T(8,128)(2,1)}, bf16[4,2,128,256]...) custom-call(s32[48]{0:T(128)} %copy-done.3, ...), custom_call_target="tpu_custom_call" | custom-call | tf_op jit(solution)/shard_map/pallas_call | solution.py:226
  65.8 1.3 collective-permute-start.11
  67.1 0.7 collective-permute-start.12
  67.8 0.7 collective-permute-start.13
  68.5 1.3 collective-permute-start.19
  69.8 0.7 collective-permute-start.20
  70.5 36.8 %collective-permute-done.11 = bf16[4,2,128,256]{3,2,1,0:T(8,128)(2,1)S(1)} collective-permute-done((bf16[4,2,128,256]{3,2,1,0:T(8,128)(2,1)}, bf16[4,2,128,256]{3,2,1,0:T(8,128)(2,1)S(1)}, u32[]{:S(2)}, u32[]{:S(2)}) %collective-permute-start.11) | collective-permute-done | bytes 524320 | tf_op jit(solution)/shard_map/ppermute | solution.py:435
  107.3 0.7 collective-permute-start.21
  108.0 0.0 collective-permute-done.13
  108.0 1.2 select_select_fusion.1
  109.3 6.0 %collective-permute-start.16 = (bf16[2,128,256]{2,1,0:T(8,128)(2,1)S(1)}, bf16[2,128,256]{2,1,0:T(8,128)(2,1)S(1)}, u32[]{:S(2)}, u32[]{:S(2)}) collective-permute-start(bf16[2,128,256]{2,1,0:T(8,128)(2,1)S(1)} %get-tuple-element.60), channel_id=1, source_target_pairs={{0,48},{1,241},{2,50},{3,243},{4,52},{5,245},{6,54},{7,247},{8,56}... | collective-permute-start | bytes 393224 | tf_op jit(solution)/shard_map/ppermute | solution.py:435
  115.3 1.7 %collective-permute-start.15 = (bf16[2,128,256]{2,1,0:T(8,128)(2,1)S(1)}, bf16[2,128,256]{2,1,0:T(8,128)(2,1)S(1)}, u32[]{:S(2)}, u32[]{:S(2)}) collective-permute-start(bf16[2,128,256]{2,1,0:T(8,128)(2,1)S(1)} %get-tuple-element.61), channel_id=1, source_target_pairs={{0,32},{1,225},{2,34},{3,227},{4,36},{5,229},{6,38},{7,231},{8,40}... | collective-permute-start | bytes 393224 | tf_op jit(solution)/shard_map/ppermute | solution.py:435
  116.9 3.3 %collective-permute-done.16 = bf16[2,128,256]{2,1,0:T(8,128)(2,1)S(1)} collective-permute-done((bf16[2,128,256]{2,1,0:T(8,128)(2,1)S(1)}, bf16[2,128,256]{2,1,0:T(8,128)(2,1)S(1)}, u32[]{:S(2)}, u32[]{:S(2)}) %collective-permute-start.16) | collective-permute-done | bytes 131104 | tf_op jit(solution)/shard_map/ppermute | solution.py:435
  120.2 5.3 %collective-permute-start.14 = (bf16[2,128,256]{2,1,0:T(8,128)(2,1)S(1)}, bf16[2,128,256]{2,1,0:T(8,128)(2,1)S(1)}, u32[]{:S(2)}, u32[]{:S(2)}) collective-permute-start(bf16[2,128,256]{2,1,0:T(8,128)(2,1)S(1)} %get-tuple-element.62), channel_id=1, source_target_pairs={{0,16},{1,17},{2,18},{3,19},{4,20},{5,21},{6,22},{7,23},{8,24},{9,... | collective-permute-start | bytes 393224 | tf_op jit(solution)/shard_map/ppermute | solution.py:435
  125.5 0.0 collective-permute-done.15
  125.5 2.6 %collective-permute-done.14 = bf16[2,128,256]{2,1,0:T(8,128)(2,1)S(1)} collective-permute-done((bf16[2,128,256]{2,1,0:T(8,128)(2,1)S(1)}, bf16[2,128,256]{2,1,0:T(8,128)(2,1)S(1)}, u32[]{:S(2)}, u32[]{:S(2)}) %collective-permute-start.14) | collective-permute-done | bytes 131104 | tf_op jit(solution)/shard_map/ppermute | solution.py:435
  128.2 0.1 pad_maximum_fusion.1
  128.3 5.0 %collective-permute-start.18 = (bf16[4,2,128,256]{3,2,1,0:T(8,128)(2,1)S(1)}, bf16[4,2,128,256]{3,2,1,0:T(8,128)(2,1)S(1)}, u32[]{:S(2)}, u32[]{:S(2)}) collective-permute-start(bf16[4,2,128,256]{3,2,1,0:T(8,128)(2,1)S(1)} %pad_maximum_fusion.1), channel_id=1, source_target_pairs={{0,1},{1,2},{2,3},{3,4},{4,5},{5,6},{6,7},{7,8},{8,9},{9,10},{10,1... | collective-permute-start | bytes 1572872 | tf_op jit(solution)/shard_map/ppermute | solution.py:375
  133.2 3.6 %collective-permute-start.17 = (bf16[4,2,128,256]{3,2,1,0:T(8,128)(2,1)S(1)}, bf16[4,2,128,256]{3,2,1,0:T(8,128)(2,1)S(1)}, u32[]{:S(2)}, u32[]{:S(2)}) collective-permute-start(bf16[4,2,128,256]{3,2,1,0:T(8,128)(2,1)S(1)} %pad_maximum_fusion.1), channel_id=1, source_target_pairs={{0,15},{1,0},{2,1},{3,2},{4,3},{5,4},{6,5},{7,6},{8,7},{9,8},{10,9... | collective-permute-start | bytes 1572872 | tf_op jit(solution)/shard_map/ppermute | solution.py:375
  136.9 0.0 collective-permute-done.19
  136.9 0.0 collective-permute-done.20
  136.9 0.2 select_select_fusion
  137.1 1.8 %collective-permute-start.24 = (bf16[2,128,256]{2,1,0:T(8,128)(2,1)S(1)}, bf16[2,128,256]{2,1,0:T(8,128)(2,1)S(1)}, u32[]{:S(2)}, u32[]{:S(2)}) collective-permute-start(bf16[2,128,256]{2,1,0:T(8,128)(2,1)S(1)} %get-tuple-element.55), channel_id=1, source_target_pairs={{0,48},{1,241},{2,50},{3,243},{4,52},{5,245},{6,54},{7,247},{8,56}... | collective-permute-start | bytes 393224 | tf_op jit(solution)/shard_map/ppermute | solution.py:435
  138.9 0.7 collective-permute-start.23
  139.5 3.0 %collective-permute-start.22 = (bf16[2,128,256]{2,1,0:T(8,128)(2,1)S(1)}, bf16[2,128,256]{2,1,0:T(8,128)(2,1)S(1)}, u32[]{:S(2)}, u32[]{:S(2)}) collective-permute-start(bf16[2,128,256]{2,1,0:T(8,128)(2,1)S(1)} %get-tuple-element.57), channel_id=1, source_target_pairs={{0,16},{1,17},{2,18},{3,19},{4,20},{5,21},{6,22},{7,23},{8,24},{9,... | collective-permute-start | bytes 393224 | tf_op jit(solution)/shard_map/ppermute | solution.py:435
  142.5 1.3 shard_map.78.total
  143.9 2.2 %collective-permute-done.24.m3 = bf16[2,128,256]{2,1,0:T(8,128)(2,1)S(1)} collective-permute-done((bf16[2,128,256]{2,1,0:T(8,128)(2,1)S(1)}, bf16[2,128,256]{2,1,0:T(8,128)(2,1)S(1)}, u32[]{:S(2)}, u32[]{:S(2)}) %collective-permute-start.24) | collective-permute-done | bytes 131104 | tf_op jit(solution)/shard_map/ppermute | solution.py:435
  146.1 5.5 %collective-permute-done.22.m1 = bf16[2,128,256]{2,1,0:T(8,128)(2,1)S(1)} collective-permute-done((bf16[2,128,256]{2,1,0:T(8,128)(2,1)S(1)}, bf16[2,128,256]{2,1,0:T(8,128)(2,1)S(1)}, u32[]{:S(2)}, u32[]{:S(2)}) %collective-permute-start.22) | collective-permute-done | bytes 131104 | tf_op jit(solution)/shard_map/ppermute | solution.py:435
  151.6 2.2 %shard_map.79 = f32[2,128,2048]{2,1,0:T(8,128)} custom-call(s32[48]{0:T(128)S(1)} %copy-done.4, s32[4,2]{1,0:T(4,128)S(1)} %collective-permute-done.places, f32[2,128,2048]{2,1,0:T(8,128)S(1)} %shard_map.78.total, bf16[2,128,256]{2,1,0:T(8,128)(2,1)S(1)} %get-tuple-element.58.m0, bf16[2,128,256]{2,1,0:T(8,128)(2,1)S(1)} %collective-permute-done.22.m1, ...), custom_call_target="tpu_custom_call" | custom-call | tf_op jit(solution)/shard_map/pallas_call | solution.py:363
  (23 shorter events, 0.1 us)
Async XLA Ops:
  0.0 47.8 %copy-start = (f32[4,256,256]{2,1,0:T(8,128)S(1)}, f32[4,256,256]{2,1,0:T(8,128)}, u32[]{:S(2)}) copy-start(f32[4,256,256]{2,1,0:T(8,128)} %param.10) | copy-start | bytes 3145732
  0.0 5.2 %copy-start.8 = (s32[4,2]{0,1:T(2,128)S(1)}, s32[4,2]{0,1:T(2,128)}, u32[]{:S(2)}) copy-start(s32[4,2]{0,1:T(2,128)} %param.9) | copy-start | bytes 100
  1.8 17.1 %collective-permute-start.2 = (bf16[2,128,2048]{2,1,0:T(8,128)(2,1)S(1)}, bf16[2,128,2048]{2,1,0:T(8,128)(2,1)S(1)}, u32[]{:S(2)}, u32[]{:S(2)}) collective-permute-start(bf16[2,128,2048]{2,1,0:T(8,128)(2,1)S(1)} %convert_bitcast_fusion.tile), channel_id=1, source_target_pairs={{0,15},{1,0},{2,1},{3,2},{4,3},{5,4},{6,5},{7,6},{8,7},{9,8},{10,9... | collective-permute-start | bytes 3145736 | tf_op jit(solution)/shard_map/ppermute | solution.py:375
  6.8 12.1 %collective-permute-start.3 = (bf16[4,2,128,256]{3,2,1,0:T(8,128)(2,1)}, bf16[4,2,128,256]{3,2,1,0:T(8,128)(2,1)}, u32[]{:S(2)}, u32[]{:S(2)}) collective-permute-start(bf16[4,2,128,256]{3,2,1,0:T(8,128)(2,1)} %shard_map.73), channel_id=1, source_target_pairs={{0,1},{1,2},{2,3},{3,4},{4,5},{5,6},{6,7},{7,8},{8,9},{9,10},{10,1... | collective-permute-start | bytes 1572872 | tf_op jit(solution)/shard_map/ppermute | solution.py:375
  6.8 12.1 %collective-permute-start.1 = (s32[4,2]{1,0:T(4,128)S(1)}, s32[4,2]{1,0:T(4,128)S(1)}, u32[]{:S(2)}, u32[]{:S(2)}) collective-permute-start(s32[4,2]{1,0:T(4,128)S(1)} %copy.8.places.own_places), channel_id=1, source_target_pairs={{0,2},{1,3},{2,4},{3,5},{4,6},{5,7},{6,8},{7,9},{8,10},{9,11},{10,... | collective-permute-start | bytes 104 | tf_op jit(solution)/shard_map/ppermute | solution.py:375
  7.4 11.5 %collective-permute-start = (s32[4,2]{1,0:T(4,128)S(1)}, s32[4,2]{1,0:T(4,128)S(1)}, u32[]{:S(2)}, u32[]{:S(2)}) collective-permute-start(s32[4,2]{1,0:T(4,128)S(1)} %copy.8.places.own_places), channel_id=1, source_target_pairs={{0,1},{1,2},{2,3},{3,4},{4,5},{5,6},{6,7},{7,8},{8,9},{9,10},{10,1... | collective-permute-start | bytes 104 | tf_op jit(solution)/shard_map/ppermute | solution.py:375
  8.8 52.8 %copy-start.3 = (s32[48]{0:T(128)}, s32[48]{0:T(128)S(1)}, u32[]{:S(2)}) copy-start(s32[48]{0:T(128)S(1)} %fusion.2.plan.refs_0_) | copy-start | bytes 580
  20.3 9.1 %collective-permute-start.5 = (bf16[2,256,256]{2,1,0:T(8,128)(2,1)S(1)}, bf16[2,256,256]{2,1,0:T(8,128)(2,1)S(1)}, u32[]{:S(2)}, u32[]{:S(2)}) collective-permute-start(bf16[2,256,256]{2,1,0:T(8,128)(2,1)S(1)} %get-tuple-element.42), channel_id=1, source_target_pairs={{0,16},{1,17},{2,18},{3,19},{4,20},{5,21},{6,22},{7,23},{8,24},{9,... | collective-permute-start | bytes 786440 | tf_op jit(solution)/shard_map/ppermute | solution.py:435
  23.1 9.6 %collective-permute-start.6 = (bf16[2,256,256]{2,1,0:T(8,128)(2,1)S(1)}, bf16[2,256,256]{2,1,0:T(8,128)(2,1)S(1)}, u32[]{:S(2)}, u32[]{:S(2)}) collective-permute-start(bf16[2,256,256]{2,1,0:T(8,128)(2,1)S(1)} %get-tuple-element.43), channel_id=1, source_target_pairs={{0,32},{1,225},{2,34},{3,227},{4,36},{5,229},{6,38},{7,231},{8,40}... | collective-permute-start | bytes 786440 | tf_op jit(solution)/shard_map/ppermute | solution.py:435
  28.6 8.8 %collective-permute-start.7 = (bf16[2,256,256]{2,1,0:T(8,128)(2,1)S(1)}, bf16[2,256,256]{2,1,0:T(8,128)(2,1)S(1)}, u32[]{:S(2)}, u32[]{:S(2)}) collective-permute-start(bf16[2,256,256]{2,1,0:T(8,128)(2,1)S(1)} %get-tuple-element.44), channel_id=1, source_target_pairs={{0,48},{1,241},{2,50},{3,243},{4,52},{5,245},{6,54},{7,247},{8,56}... | collective-permute-start | bytes 786440 | tf_op jit(solution)/shard_map/ppermute | solution.py:435
  37.6 24.0 %copy-start.5 = (bf16[4,2,256,256]{3,2,1,0:T(8,128)(2,1)}, bf16[4,2,256,256]{3,2,1,0:T(8,128)(2,1)S(1)}, u32[]{:S(2)}) copy-start(bf16[4,2,256,256]{3,2,1,0:T(8,128)(2,1)S(1)} %pad_maximum_fusion.refs_3_) | copy-start | bytes 3145732
  37.6 25.8 %collective-permute-start.10 = (bf16[4,2,256,256]{3,2,1,0:T(8,128)(2,1)S(1)}, bf16[4,2,256,256]{3,2,1,0:T(8,128)(2,1)}, u32[]{:S(2)}, u32[]{:S(2)}) collective-permute-start(bf16[4,2,256,256]{3,2,1,0:T(8,128)(2,1)S(1)} %pad_maximum_fusion.refs_3_), channel_id=1, source_target_pairs={{1,65},{3,67},{5,69},{7,71},{9,73},{11,75},{13,77},{15,79},{48,80}... | collective-permute-start | bytes 3145736 | tf_op jit(solution)/shard_map/ppermute | solution.py:435
  41.1 22.4 %collective-permute-start.9 = (bf16[4,2,256,256]{3,2,1,0:T(8,128)(2,1)S(1)}, bf16[4,2,256,256]{3,2,1,0:T(8,128)(2,1)}, u32[]{:S(2)}, u32[]{:S(2)}) collective-permute-start(bf16[4,2,256,256]{3,2,1,0:T(8,128)(2,1)S(1)} %pad_maximum_fusion.refs_3_), channel_id=1, source_target_pairs={{32,128},{33,193},{34,130},{35,195},{36,132},{37,197},{38,134},{39... | collective-permute-start | bytes 3145736 | tf_op jit(solution)/shard_map/ppermute | solution.py:435
  42.7 20.7 %collective-permute-start.8 = (bf16[4,2,256,256]{3,2,1,0:T(8,128)(2,1)S(1)}, bf16[4,2,256,256]{3,2,1,0:T(8,128)(2,1)}, u32[]{:S(2)}, u32[]{:S(2)}) collective-permute-start(bf16[4,2,256,256]{3,2,1,0:T(8,128)(2,1)S(1)} %pad_maximum_fusion.refs_3_), channel_id=1, source_target_pairs={{16,208},{18,210},{20,212},{22,214},{24,216},{26,218},{28,220},{30... | collective-permute-start | bytes 3145736 | tf_op jit(solution)/shard_map/ppermute | solution.py:435
  48.5 14.9 %collective-permute-start.4 = (f32[256,256]{1,0:T(8,128)}, f32[256,256]{1,0:T(8,128)S(1)}, u32[]{:S(2)}, u32[]{:S(2)}) collective-permute-start(f32[256,256]{1,0:T(8,128)} %dynamic-slice_bitcast_fusion), channel_id=1, source_target_pairs={{0,1},{1,2},{2,3},{3,4},{4,5},{5,6},{6,7},{7,8},{8,9},{9,10},{10,1... | collective-permute-start | bytes 786440 | tf_op jit(solution)/shard_map/ppermute | solution.py:375
  50.5 11.2 %copy-start.2 = (f32[2,2,256,256]{3,2,1,0:T(8,128)S(1)}, f32[2,2,256,256]{3,2,1,0:T(8,128)}, u32[]{:S(2)}) copy-start(f32[2,2,256,256]{3,2,1,0:T(8,128)} %probe.1) | copy-start | bytes 3145732
  62.6 0.8 copy-start.1
  63.4 0.7 copy-start.7
  65.8 41.5 %collective-permute-start.11 = (bf16[4,2,128,256]{3,2,1,0:T(8,128)(2,1)}, bf16[4,2,128,256]{3,2,1,0:T(8,128)(2,1)S(1)}, u32[]{:S(2)}, u32[]{:S(2)}) collective-permute-start(bf16[4,2,128,256]{3,2,1,0:T(8,128)(2,1)} %get-tuple-element.45), channel_id=1, source_target_pairs={{0,224},{2,226},{4,228},{6,230},{8,232},{10,234},{12,236},{14,238}... | collective-permute-start | bytes 1572872 | tf_op jit(solution)/shard_map/ppermute | solution.py:435
  67.1 40.9 %collective-permute-start.12 = (bf16[4,2,128,256]{3,2,1,0:T(8,128)(2,1)}, bf16[4,2,128,256]{3,2,1,0:T(8,128)(2,1)S(1)}, u32[]{:S(2)}, u32[]{:S(2)}) collective-permute-start(bf16[4,2,128,256]{3,2,1,0:T(8,128)(2,1)} %get-tuple-element.47), channel_id=1, source_target_pairs={{0,160},{2,162},{4,164},{6,166},{8,168},{10,170},{12,172},{14,174}... | collective-permute-start | bytes 1572872 | tf_op jit(solution)/shard_map/ppermute | solution.py:435
  67.8 40.2 %collective-permute-start.13 = (bf16[4,2,128,256]{3,2,1,0:T(8,128)(2,1)}, bf16[4,2,128,256]{3,2,1,0:T(8,128)(2,1)S(1)}, u32[]{:S(2)}, u32[]{:S(2)}) collective-permute-start(bf16[4,2,128,256]{3,2,1,0:T(8,128)(2,1)} %get-tuple-element.49), channel_id=1, source_target_pairs={{0,64},{2,66},{4,68},{6,70},{8,72},{10,74},{12,76},{14,78},{17,49}... | collective-permute-start | bytes 1572872 | tf_op jit(solution)/shard_map/ppermute | solution.py:435
  68.5 68.4 %collective-permute-start.19 = (bf16[4,2,128,256]{3,2,1,0:T(8,128)(2,1)}, bf16[4,2,128,256]{3,2,1,0:T(8,128)(2,1)S(1)}, u32[]{:S(2)}, u32[]{:S(2)}) collective-permute-start(bf16[4,2,128,256]{3,2,1,0:T(8,128)(2,1)} %get-tuple-element.51), channel_id=1, source_target_pairs={{0,224},{2,226},{4,228},{6,230},{8,232},{10,234},{12,236},{14,238}... | collective-permute-start | bytes 1572872 | tf_op jit(solution)/shard_map/ppermute | solution.py:435
  69.8 67.1 %collective-permute-start.20 = (bf16[4,2,128,256]{3,2,1,0:T(8,128)(2,1)}, bf16[4,2,128,256]{3,2,1,0:T(8,128)(2,1)S(1)}, u32[]{:S(2)}, u32[]{:S(2)}) collective-permute-start(bf16[4,2,128,256]{3,2,1,0:T(8,128)(2,1)} %get-tuple-element.52), channel_id=1, source_target_pairs={{0,160},{2,162},{4,164},{6,166},{8,168},{10,170},{12,172},{14,174}... | collective-permute-start | bytes 1572872 | tf_op jit(solution)/shard_map/ppermute | solution.py:435
  107.3 29.6 %collective-permute-start.21 = (bf16[4,2,128,256]{3,2,1,0:T(8,128)(2,1)}, bf16[4,2,128,256]{3,2,1,0:T(8,128)(2,1)S(1)}, u32[]{:S(2)}, u32[]{:S(2)}) collective-permute-start(bf16[4,2,128,256]{3,2,1,0:T(8,128)(2,1)} %get-tuple-element.53), channel_id=1, source_target_pairs={{0,64},{2,66},{4,68},{6,70},{8,72},{10,74},{12,76},{14,78},{17,49}... | collective-permute-start | bytes 1572872 | tf_op jit(solution)/shard_map/ppermute | solution.py:435
  108.0 28.9 %copy-start.6 = (bf16[4,2,128,256]{3,2,1,0:T(8,128)(2,1)S(1)}, bf16[4,2,128,256]{3,2,1,0:T(8,128)(2,1)}, u32[]{:S(2)}) copy-start(bf16[4,2,128,256]{3,2,1,0:T(8,128)(2,1)} %get-tuple-element.54) | copy-start | bytes 1572868
  109.3 10.9 %collective-permute-start.16 = (bf16[2,128,256]{2,1,0:T(8,128)(2,1)S(1)}, bf16[2,128,256]{2,1,0:T(8,128)(2,1)S(1)}, u32[]{:S(2)}, u32[]{:S(2)}) collective-permute-start(bf16[2,128,256]{2,1,0:T(8,128)(2,1)S(1)} %get-tuple-element.60), channel_id=1, source_target_pairs={{0,48},{1,241},{2,50},{3,243},{4,52},{5,245},{6,54},{7,247},{8,56}... | collective-permute-start | bytes 393224 | tf_op jit(solution)/shard_map/ppermute | solution.py:435
  115.3 10.3 %collective-permute-start.15 = (bf16[2,128,256]{2,1,0:T(8,128)(2,1)S(1)}, bf16[2,128,256]{2,1,0:T(8,128)(2,1)S(1)}, u32[]{:S(2)}, u32[]{:S(2)}) collective-permute-start(bf16[2,128,256]{2,1,0:T(8,128)(2,1)S(1)} %get-tuple-element.61), channel_id=1, source_target_pairs={{0,32},{1,225},{2,34},{3,227},{4,36},{5,229},{6,38},{7,231},{8,40}... | collective-permute-start | bytes 393224 | tf_op jit(solution)/shard_map/ppermute | solution.py:435
  120.2 8.0 %collective-permute-start.14 = (bf16[2,128,256]{2,1,0:T(8,128)(2,1)S(1)}, bf16[2,128,256]{2,1,0:T(8,128)(2,1)S(1)}, u32[]{:S(2)}, u32[]{:S(2)}) collective-permute-start(bf16[2,128,256]{2,1,0:T(8,128)(2,1)S(1)} %get-tuple-element.62), channel_id=1, source_target_pairs={{0,16},{1,17},{2,18},{3,19},{4,20},{5,21},{6,22},{7,23},{8,24},{9,... | collective-permute-start | bytes 393224 | tf_op jit(solution)/shard_map/ppermute | solution.py:435
  128.2 14.3 %copy-start.4 = (s32[48]{0:T(128)S(1)}, s32[48]{0:T(128)}, u32[]{:S(2)}) copy-start(s32[48]{0:T(128)} %copy-done.3) | copy-start | bytes 580
  128.3 14.3 %collective-permute-start.18 = (bf16[4,2,128,256]{3,2,1,0:T(8,128)(2,1)S(1)}, bf16[4,2,128,256]{3,2,1,0:T(8,128)(2,1)S(1)}, u32[]{:S(2)}, u32[]{:S(2)}) collective-permute-start(bf16[4,2,128,256]{3,2,1,0:T(8,128)(2,1)S(1)} %pad_maximum_fusion.1), channel_id=1, source_target_pairs={{0,1},{1,2},{2,3},{3,4},{4,5},{5,6},{6,7},{7,8},{8,9},{9,10},{10,1... | collective-permute-start | bytes 1572872 | tf_op jit(solution)/shard_map/ppermute | solution.py:375
  133.2 9.3 %collective-permute-start.17 = (bf16[4,2,128,256]{3,2,1,0:T(8,128)(2,1)S(1)}, bf16[4,2,128,256]{3,2,1,0:T(8,128)(2,1)S(1)}, u32[]{:S(2)}, u32[]{:S(2)}) collective-permute-start(bf16[4,2,128,256]{3,2,1,0:T(8,128)(2,1)S(1)} %pad_maximum_fusion.1), channel_id=1, source_target_pairs={{0,15},{1,0},{2,1},{3,2},{4,3},{5,4},{6,5},{7,6},{8,7},{9,8},{10,9... | collective-permute-start | bytes 1572872 | tf_op jit(solution)/shard_map/ppermute | solution.py:375
  137.1 9.0 %collective-permute-start.24 = (bf16[2,128,256]{2,1,0:T(8,128)(2,1)S(1)}, bf16[2,128,256]{2,1,0:T(8,128)(2,1)S(1)}, u32[]{:S(2)}, u32[]{:S(2)}) collective-permute-start(bf16[2,128,256]{2,1,0:T(8,128)(2,1)S(1)} %get-tuple-element.55), channel_id=1, source_target_pairs={{0,48},{1,241},{2,50},{3,243},{4,52},{5,245},{6,54},{7,247},{8,56}... | collective-permute-start | bytes 393224 | tf_op jit(solution)/shard_map/ppermute | solution.py:435
  138.9 7.2 %collective-permute-start.23 = (bf16[2,128,256]{2,1,0:T(8,128)(2,1)S(1)}, bf16[2,128,256]{2,1,0:T(8,128)(2,1)S(1)}, u32[]{:S(2)}, u32[]{:S(2)}) collective-permute-start(bf16[2,128,256]{2,1,0:T(8,128)(2,1)S(1)} %get-tuple-element.56), channel_id=1, source_target_pairs={{0,32},{1,225},{2,34},{3,227},{4,36},{5,229},{6,38},{7,231},{8,40}... | collective-permute-start | bytes 393224 | tf_op jit(solution)/shard_map/ppermute | solution.py:435
  139.5 12.1 %collective-permute-start.22 = (bf16[2,128,256]{2,1,0:T(8,128)(2,1)S(1)}, bf16[2,128,256]{2,1,0:T(8,128)(2,1)S(1)}, u32[]{:S(2)}, u32[]{:S(2)}) collective-permute-start(bf16[2,128,256]{2,1,0:T(8,128)(2,1)S(1)} %get-tuple-element.57), channel_id=1, source_target_pairs={{0,16},{1,17},{2,18},{3,19},{4,20},{5,21},{6,22},{7,23},{8,24},{9,... | collective-permute-start | bytes 393224 | tf_op jit(solution)/shard_map/ppermute | solution.py:435

commit v10 on v9

--- a/solution.py
+++ b/solution.py
@@ -468,23 +468,24 @@
     mine = own_windows(positions, tile_bf, n)
     behind = shifted(mine, 1)
     mid_places = shifted(positions, 1)
-    far_places = shifted(positions, 2)
-    mid_places, far_places, ahead, behind = lax.optimization_barrier((mid_places, far_places, ahead, behind))
+    mid_places, ahead, behind = lax.optimization_barrier((mid_places, ahead, behind))
     parts = merge(plan, mid_places, behind, tile_bf, ahead, n)
 
-    measured, parts = lax.optimization_barrier((measured, parts))
+    measured, late_positions, parts = lax.optimization_barrier((measured, positions, parts))
+    far_places = shifted(late_positions, 2)
     target = shifted(lax.dynamic_index_in_dim(measured, plan[OTHER], 0, False), 1)
 
     message = jnp.stack([parts[0]] + [within(parts[k], k) for k in (1, 2, 3)])
-    messages = [message] + [towards(message, k) for k in (1, 2, 3)]
+    messages = {0: message} | {k: towards(message, k) for k in (2, 1, 3)}
+    messages = [messages[k] for k in range(4)]
     tables = make_tables(n, depth_size)
     wave = roll_probe(plan, mid_places, probe, rows)
-    wave, source = lax.optimization_barrier((wave, [plan[SOURCE] == k for k in (1, 2, 3)]))
+    wave, source, far_places = lax.optimization_barrier((wave, [plan[SOURCE] == k for k in (1, 2, 3)], far_places))
     terms = tuple(chain(plan, wave, target, messages, tables))
 
     def home(pieces):
         block = pieces[0]
-        for k in (1, 2, 3):
+        for k in (2, 1, 3):
             block = jnp.where(source[k - 1], away(pieces[k], k), block)
         return block
 

time: 154 us -> 150 us (0.974)
  starting transfers between devices: 52.2 us -> 49.3 us
  waiting for transfers between devices: 69.3 us -> 67.6 us
    ppermute x7, starting transfers between devices: 13.3 us -> 5.18 us  [shifted(): lax.ppermute(block, 'lat', [(i, (i + distance) % size) for i in range(siz...]
    ppermute x18, waiting for transfers between devices: 59.2 us -> 53 us  [permute(): return lax.ppermute(block, ('depth', 'lat'), pairs)]
    ppermute x18, starting transfers between devices: 38.9 us -> 44.1 us  [permute(): return lax.ppermute(block, ('depth', 'lat'), pairs)]
    ppermute x7, waiting for transfers between devices: 10.1 us -> 14.6 us  [shifted(): lax.ppermute(block, 'lat', [(i, (i + distance) % size) for i in range(siz...]
  transfers between devices with their start and end apart: 25 -> 25, of which waited for: 9 -> 12; matrix products, arithmetic and copies ran while one was open for 3% -> 3% of each run, Pallas kernels for 10% -> 10%
where the time goes in v10:
time: 150 us
  waiting for transfers between devices  67.6 us (45%)
  starting transfers between devices  49.3 us (33%)
  Pallas kernels  20.3 us (14%)
  other arithmetic  4.43 us (3%)
  between operations  4.19 us (3%)
  local copies, waits for them, and re-layouts  3.8 us (3%)
    ppermute x18, waiting for transfers between devices, permute(): return lax.ppermute(block, ('depth', 'lat'), pairs)  53 us
    ppermute x18, starting transfers between devices, permute(): return lax.ppermute(block, ('depth', 'lat'), pairs)  44.1 us
    ppermute x7, waiting for transfers between devices, shifted(): lax.ppermute(block, 'lat', [(i, (i + distance) % size) for i in range(siz...  14.6 us
    pallas_call x1, Pallas kernels, make_tables(): pl.pallas_call(functools.partial(tables_kernel, n=n, slices=slices), grid...  11.2 us
    ppermute x7, starting transfers between devices, shifted(): lax.ppermute(block, 'lat', [(i, (i + distance) % size) for i in range(siz...  5.18 us
  transfers between devices with their start and end apart: 25, of which 12 were waited for; matrix products, arithmetic and copies ran while one was open for 3% of the time, Pallas kernels for 10%

profile of v10, /device:TPU:1, one launch (start us, length us, event | category | flops | bytes accessed | tf_op | source)
XLA Modules:
  0.0 149.7 jit_solution(2017394576889161750)
XLA Ops:
  0.0 1.8 %convert_bitcast_fusion.tile = bf16[2,128,2048]{2,1,0:T(8,128)(2,1)S(1)} fusion(f32[1,2,128,2048]{3,2,1,0:T(8,128)} %param.7), kind=kLoop, calls=%fused_computation.1 | loop fusion | flops 524288 | bytes 3145728 | tf_op jit(solution)/shard_map/convert_element_type | solution.py:466
  1.8 3.3 %collective-permute-start.1 = (bf16[2,128,2048]{2,1,0:T(8,128)(2,1)S(1)}, bf16[2,128,2048]{2,1,0:T(8,128)(2,1)S(1)}, u32[]{:S(2)}, u32[]{:S(2)}) collective-permute-start(bf16[2,128,2048]{2,1,0:T(8,128)(2,1)S(1)} %convert_bitcast_fusion.tile), channel_id=1, source_target_pairs={{0,15},{1,0},{2,1},{3,2},{4,3},{5,4},{6,5},{7,6},{8,7},{9,8},{10,9... | collective-permute-start | bytes 3145736 | tf_op jit(solution)/shard_map/ppermute | solution.py:375
  5.2 0.1 copy.8.places.own_places
  5.3 1.5 %shard_map.73 = bf16[4,2,128,256]{3,2,1,0:T(8,128)(2,1)} custom-call(s32[4,2]{1,0:T(4,128)S(1)} %copy.8.places.own_places, bf16[2,128,2048]{2,1,0:T(8,128)(2,1)S(1)} %convert_bitcast_fusion.tile), custom_call_target="tpu_custom_call" | custom-call | tf_op jit(solution)/shard_map/pallas_call | solution.py:268
  6.8 0.0 collective-permute-start.2
  6.8 0.0 collective-permute-start
  6.8 0.7 fusion.2.plan.refs_0_
  7.5 5.7 %collective-permute-done.places = s32[4,2]{1,0:T(4,128)S(1)} collective-permute-done((s32[4,2]{1,0:T(4,128)S(1)}, s32[4,2]{1,0:T(4,128)S(1)}, u32[]{:S(2)}, u32[]{:S(2)}) %collective-permute-start) | collective-permute-done | bytes 64 | tf_op jit(solution)/shard_map/ppermute | solution.py:375
  13.2 0.0 collective-permute-done.2.behind
  13.2 4.2 %collective-permute-done.1.ahead = bf16[2,128,2048]{2,1,0:T(8,128)(2,1)S(1)} collective-permute-done((bf16[2,128,2048]{2,1,0:T(8,128)(2,1)S(1)}, bf16[2,128,2048]{2,1,0:T(8,128)(2,1)S(1)}, u32[]{:S(2)}, u32[]{:S(2)}) %collective-permute-start.1) | collective-permute-done | bytes 1048608 | tf_op jit(solution)/shard_map/ppermute | solution.py:375
  17.4 1.4 shard_map.75
  18.8 3.0 %collective-permute-start.5 = (bf16[2,256,256]{2,1,0:T(8,128)(2,1)S(1)}, bf16[2,256,256]{2,1,0:T(8,128)(2,1)S(1)}, u32[]{:S(2)}, u32[]{:S(2)}) collective-permute-start(bf16[2,256,256]{2,1,0:T(8,128)(2,1)S(1)} %get-tuple-element.44), channel_id=1, source_target_pairs={{0,16},{1,17},{2,18},{3,19},{4,20},{5,21},{6,22},{7,23},{8,24},{9,... | collective-permute-start | bytes 786440 | tf_op jit(solution)/shard_map/ppermute | solution.py:435
  21.8 5.6 %collective-permute-start.6 = (bf16[2,256,256]{2,1,0:T(8,128)(2,1)S(1)}, bf16[2,256,256]{2,1,0:T(8,128)(2,1)S(1)}, u32[]{:S(2)}, u32[]{:S(2)}) collective-permute-start(bf16[2,256,256]{2,1,0:T(8,128)(2,1)S(1)} %get-tuple-element.45), channel_id=1, source_target_pairs={{0,32},{1,225},{2,34},{3,227},{4,36},{5,229},{6,38},{7,231},{8,40}... | collective-permute-start | bytes 786440 | tf_op jit(solution)/shard_map/ppermute | solution.py:435
  27.4 4.0 %collective-permute-done.6 = bf16[2,256,256]{2,1,0:T(8,128)(2,1)S(1)} collective-permute-done((bf16[2,256,256]{2,1,0:T(8,128)(2,1)S(1)}, bf16[2,256,256]{2,1,0:T(8,128)(2,1)S(1)}, u32[]{:S(2)}, u32[]{:S(2)}) %collective-permute-start.6) | collective-permute-done | bytes 262176 | tf_op jit(solution)/shard_map/ppermute | solution.py:435
  31.5 5.0 %collective-permute-done.7 = bf16[2,256,256]{2,1,0:T(8,128)(2,1)S(1)} collective-permute-done((bf16[2,256,256]{2,1,0:T(8,128)(2,1)S(1)}, bf16[2,256,256]{2,1,0:T(8,128)(2,1)S(1)}, u32[]{:S(2)}, u32[]{:S(2)}) %collective-permute-start.7) | collective-permute-done | bytes 262176 | tf_op jit(solution)/shard_map/ppermute | solution.py:435
  36.5 1.1 pad_maximum_fusion.refs_3_
  37.6 2.3 %collective-permute-start.10 = (bf16[4,2,256,256]{3,2,1,0:T(8,128)(2,1)}, bf16[4,2,256,256]{3,2,1,0:T(8,128)(2,1)}, u32[]{:S(2)}, u32[]{:S(2)}) collective-permute-start(bf16[4,2,256,256]{3,2,1,0:T(8,128)(2,1)} %pad_maximum_fusion.refs_3_), channel_id=1, source_target_pairs={{1,65},{3,67},{5,69},{7,71},{9,73},{11,75},{13,77},{15,79},{48,80}... | collective-permute-start | bytes 3145736 | tf_op jit(solution)/shard_map/ppermute | solution.py:435
  39.9 1.7 %collective-permute-start.9 = (bf16[4,2,256,256]{3,2,1,0:T(8,128)(2,1)}, bf16[4,2,256,256]{3,2,1,0:T(8,128)(2,1)}, u32[]{:S(2)}, u32[]{:S(2)}) collective-permute-start(bf16[4,2,256,256]{3,2,1,0:T(8,128)(2,1)} %pad_maximum_fusion.refs_3_), channel_id=1, source_target_pairs={{32,128},{33,193},{34,130},{35,195},{36,132},{37,197},{38,134},{39... | collective-permute-start | bytes 3145736 | tf_op jit(solution)/shard_map/ppermute | solution.py:435
  41.5 1.6 %collective-permute-start.8 = (bf16[4,2,256,256]{3,2,1,0:T(8,128)(2,1)}, bf16[4,2,256,256]{3,2,1,0:T(8,128)(2,1)}, u32[]{:S(2)}, u32[]{:S(2)}) collective-permute-start(bf16[4,2,256,256]{3,2,1,0:T(8,128)(2,1)} %pad_maximum_fusion.refs_3_), channel_id=1, source_target_pairs={{16,208},{18,210},{20,212},{22,214},{24,216},{26,218},{28,220},{30... | collective-permute-start | bytes 3145736 | tf_op jit(solution)/shard_map/ppermute | solution.py:435
  43.2 0.7 constant_dynamic-slice_fusion
  43.9 0.7 fusion.1
  46.5 0.1 collective-permute-start.4
  48.4 0.0 copy-start.2
  48.4 11.2 %shard_map.76.refs_7_ = bf16[17,2,512,512]{3,2,1,0:T(8,128)(2,1)} custom-call(f32[2,17]{1,0:T(2,128)} %constant.43.clone.scales, f32[4,256,256]{2,1,0:T(8,128)} %constant.44.clone.base), custom_call_target="tpu_custom_call" | custom-call | tf_op jit(solution)/shard_map/pallas_call | solution.py:49
  59.6 0.1 copy.10
  59.7 1.2 collective-permute-start.3
  60.9 1.0 shard_map.74.refs_1_
  61.9 0.8 copy-done.1
  62.7 2.4 %collective-permute-done.3.far_places = s32[4,2]{1,0:T(4,128)S(1)} collective-permute-done((s32[4,2]{1,0:T(4,128)S(1)}, s32[4,2]{1,0:T(4,128)S(1)}, u32[]{:S(2)}, u32[]{:S(2)}) %collective-permute-start.3) | collective-permute-done | bytes 64 | tf_op jit(solution)/shard_map/ppermute | solution.py:375
  65.1 0.0 collective-permute-done.4.refs_2_
  65.1 0.0 collective-permute-done.10.refs_6_
  65.1 0.0 collective-permute-done.8.refs_4_
  65.2 0.7 copy-done.6
  65.8 1.6 %shard_map.77 = (bf16[4,2,128,256]{3,2,1,0:T(8,128)(2,1)}, bf16[4,2,128,256]{3,2,1,0:T(8,128)(2,1)}, bf16[4,2,128,256]{3,2,1,0:T(8,128)(2,1)}, bf16[4,2,128,256]...) custom-call(s32[48]{0:T(128)} %copy-done.3, ...), custom_call_target="tpu_custom_call" | custom-call | tf_op jit(solution)/shard_map/pallas_call | solution.py:226
  67.5 1.3 collective-permute-start.11
  68.8 0.7 collective-permute-start.12
  69.5 0.7 collective-permute-start.13
  70.2 1.3 collective-permute-start.19
  71.5 0.7 collective-permute-start.20
  72.2 31.8 %collective-permute-done.11 = bf16[4,2,128,256]{3,2,1,0:T(8,128)(2,1)S(1)} collective-permute-done((bf16[4,2,128,256]{3,2,1,0:T(8,128)(2,1)}, bf16[4,2,128,256]{3,2,1,0:T(8,128)(2,1)S(1)}, u32[]{:S(2)}, u32[]{:S(2)}) %collective-permute-start.11) | collective-permute-done | bytes 524320 | tf_op jit(solution)/shard_map/ppermute | solution.py:435
  104.0 0.7 collective-permute-start.21
  104.7 0.0 collective-permute-done.13
  104.7 1.3 select_select_fusion.1
  106.0 12.9 %collective-permute-start.16 = (bf16[2,128,256]{2,1,0:T(8,128)(2,1)S(1)}, bf16[2,128,256]{2,1,0:T(8,128)(2,1)S(1)}, u32[]{:S(2)}, u32[]{:S(2)}) collective-permute-start(bf16[2,128,256]{2,1,0:T(8,128)(2,1)S(1)} %get-tuple-element.62), channel_id=1, source_target_pairs={{0,48},{1,241},{2,50},{3,243},{4,52},{5,245},{6,54},{7,247},{8,56}... | collective-permute-start | bytes 393224 | tf_op jit(solution)/shard_map/ppermute | solution.py:435
  118.9 1.8 %collective-permute-start.15 = (bf16[2,128,256]{2,1,0:T(8,128)(2,1)S(1)}, bf16[2,128,256]{2,1,0:T(8,128)(2,1)S(1)}, u32[]{:S(2)}, u32[]{:S(2)}) collective-permute-start(bf16[2,128,256]{2,1,0:T(8,128)(2,1)S(1)} %get-tuple-element.63), channel_id=1, source_target_pairs={{0,32},{1,225},{2,34},{3,227},{4,36},{5,229},{6,38},{7,231},{8,40}... | collective-permute-start | bytes 393224 | tf_op jit(solution)/shard_map/ppermute | solution.py:435
  120.7 3.8 %collective-permute-done.16 = bf16[2,128,256]{2,1,0:T(8,128)(2,1)S(1)} collective-permute-done((bf16[2,128,256]{2,1,0:T(8,128)(2,1)S(1)}, bf16[2,128,256]{2,1,0:T(8,128)(2,1)S(1)}, u32[]{:S(2)}, u32[]{:S(2)}) %collective-permute-start.16) | collective-permute-done | bytes 131104 | tf_op jit(solution)/shard_map/ppermute | solution.py:435
  124.5 4.0 %collective-permute-start.14 = (bf16[2,128,256]{2,1,0:T(8,128)(2,1)S(1)}, bf16[2,128,256]{2,1,0:T(8,128)(2,1)S(1)}, u32[]{:S(2)}, u32[]{:S(2)}) collective-permute-start(bf16[2,128,256]{2,1,0:T(8,128)(2,1)S(1)} %get-tuple-element.64), channel_id=1, source_target_pairs={{0,16},{1,17},{2,18},{3,19},{4,20},{5,21},{6,22},{7,23},{8,24},{9,... | collective-permute-start | bytes 393224 | tf_op jit(solution)/shard_map/ppermute | solution.py:435
  128.5 0.1 collective-permute-done.15
  128.6 2.2 %collective-permute-done.14 = bf16[2,128,256]{2,1,0:T(8,128)(2,1)S(1)} collective-permute-done((bf16[2,128,256]{2,1,0:T(8,128)(2,1)S(1)}, bf16[2,128,256]{2,1,0:T(8,128)(2,1)S(1)}, u32[]{:S(2)}, u32[]{:S(2)}) %collective-permute-start.14) | collective-permute-done | bytes 131104 | tf_op jit(solution)/shard_map/ppermute | solution.py:435
  130.9 0.1 pad_maximum_fusion.1
  130.9 0.1 collective-permute-start.18
  131.0 0.5 collective-permute-start.17
  131.5 0.0 collective-permute-done.19
  131.5 0.0 collective-permute-done.20
  131.5 0.0 collective-permute-done.21
  131.5 0.1 select_select_fusion
  131.7 4.9 %collective-permute-start.24 = (bf16[2,128,256]{2,1,0:T(8,128)(2,1)S(1)}, bf16[2,128,256]{2,1,0:T(8,128)(2,1)S(1)}, u32[]{:S(2)}, u32[]{:S(2)}) collective-permute-start(bf16[2,128,256]{2,1,0:T(8,128)(2,1)S(1)} %get-tuple-element.57), channel_id=1, source_target_pairs={{0,48},{1,241},{2,50},{3,243},{4,52},{5,245},{6,54},{7,247},{8,56}... | collective-permute-start | bytes 393224 | tf_op jit(solution)/shard_map/ppermute | solution.py:435
  136.7 0.5 collective-permute-start.23
  137.2 0.6 collective-permute-start.22
  137.7 2.3 %collective-permute-done.17.from_own = bf16[4,2,128,256]{3,2,1,0:T(8,128)(2,1)S(1)} collective-permute-done((bf16[4,2,128,256]{3,2,1,0:T(8,128)(2,1)S(1)}, bf16[4,2,128,256]{3,2,1,0:T(8,128)(2,1)S(1)}, u32[]{:S(2)}, u32[]{:S(2)}) %collective-permute-start.17) | collective-permute-done | bytes 524320 | tf_op jit(solution)/shard_map/ppermute | solution.py:375
  140.0 1.3 shard_map.78.total
  141.4 0.6 collective-permute-done.23.m2
  142.0 5.3 %collective-permute-done.22.m1 = bf16[2,128,256]{2,1,0:T(8,128)(2,1)S(1)} collective-permute-done((bf16[2,128,256]{2,1,0:T(8,128)(2,1)S(1)}, bf16[2,128,256]{2,1,0:T(8,128)(2,1)S(1)}, u32[]{:S(2)}, u32[]{:S(2)}) %collective-permute-start.22) | collective-permute-done | bytes 131104 | tf_op jit(solution)/shard_map/ppermute | solution.py:435
  147.3 2.2 %shard_map.79 = f32[2,128,2048]{2,1,0:T(8,128)} custom-call(s32[48]{0:T(128)S(1)} %copy-done.4, s32[4,2]{1,0:T(4,128)S(1)} %collective-permute-done.places, f32[2,128,2048]{2,1,0:T(8,128)S(1)} %shard_map.78.total, bf16[2,128,256]{2,1,0:T(8,128)(2,1)S(1)} %get-tuple-element.60.m0, bf16[2,128,256]{2,1,0:T(8,128)(2,1)S(1)} %collective-permute-done.22.m1, ...), custom_call_target="tpu_custom_call" | custom-call | tf_op jit(solution)/shard_map/pallas_call | solution.py:363
  (22 shorter events, 0.1 us)
Async XLA Ops:
  0.0 46.4 %copy-start = (f32[4,256,256]{2,1,0:T(8,128)S(1)}, f32[4,256,256]{2,1,0:T(8,128)}, u32[]{:S(2)}) copy-start(f32[4,256,256]{2,1,0:T(8,128)} %param.10) | copy-start | bytes 3145732
  0.0 5.2 %copy-start.7 = (s32[4,2]{0,1:T(2,128)S(1)}, s32[4,2]{0,1:T(2,128)}, u32[]{:S(2)}) copy-start(s32[4,2]{0,1:T(2,128)} %param.9) | copy-start | bytes 100
  1.8 15.6 %collective-permute-start.1 = (bf16[2,128,2048]{2,1,0:T(8,128)(2,1)S(1)}, bf16[2,128,2048]{2,1,0:T(8,128)(2,1)S(1)}, u32[]{:S(2)}, u32[]{:S(2)}) collective-permute-start(bf16[2,128,2048]{2,1,0:T(8,128)(2,1)S(1)} %convert_bitcast_fusion.tile), channel_id=1, source_target_pairs={{0,15},{1,0},{2,1},{3,2},{4,3},{5,4},{6,5},{7,6},{8,7},{9,8},{10,9... | collective-permute-start | bytes 3145736 | tf_op jit(solution)/shard_map/ppermute | solution.py:375
  6.8 6.4 %collective-permute-start.2 = (bf16[4,2,128,256]{3,2,1,0:T(8,128)(2,1)}, bf16[4,2,128,256]{3,2,1,0:T(8,128)(2,1)}, u32[]{:S(2)}, u32[]{:S(2)}) collective-permute-start(bf16[4,2,128,256]{3,2,1,0:T(8,128)(2,1)} %shard_map.73), channel_id=1, source_target_pairs={{0,1},{1,2},{2,3},{3,4},{4,5},{5,6},{6,7},{7,8},{8,9},{9,10},{10,1... | collective-permute-start | bytes 1572872 | tf_op jit(solution)/shard_map/ppermute | solution.py:375
  6.8 6.4 %collective-permute-start = (s32[4,2]{1,0:T(4,128)S(1)}, s32[4,2]{1,0:T(4,128)S(1)}, u32[]{:S(2)}, u32[]{:S(2)}) collective-permute-start(s32[4,2]{1,0:T(4,128)S(1)} %copy.8.places.own_places), channel_id=1, source_target_pairs={{0,1},{1,2},{2,3},{3,4},{4,5},{5,6},{6,7},{7,8},{8,9},{9,10},{10,1... | collective-permute-start | bytes 104 | tf_op jit(solution)/shard_map/ppermute | solution.py:375
  7.5 53.5 %copy-start.3 = (s32[48]{0:T(128)}, s32[48]{0:T(128)S(1)}, u32[]{:S(2)}) copy-start(s32[48]{0:T(128)S(1)} %fusion.2.plan.refs_0_) | copy-start | bytes 580
  18.8 8.6 %collective-permute-start.5 = (bf16[2,256,256]{2,1,0:T(8,128)(2,1)S(1)}, bf16[2,256,256]{2,1,0:T(8,128)(2,1)S(1)}, u32[]{:S(2)}, u32[]{:S(2)}) collective-permute-start(bf16[2,256,256]{2,1,0:T(8,128)(2,1)S(1)} %get-tuple-element.44), channel_id=1, source_target_pairs={{0,16},{1,17},{2,18},{3,19},{4,20},{5,21},{6,22},{7,23},{8,24},{9,... | collective-permute-start | bytes 786440 | tf_op jit(solution)/shard_map/ppermute | solution.py:435
  21.8 9.6 %collective-permute-start.6 = (bf16[2,256,256]{2,1,0:T(8,128)(2,1)S(1)}, bf16[2,256,256]{2,1,0:T(8,128)(2,1)S(1)}, u32[]{:S(2)}, u32[]{:S(2)}) collective-permute-start(bf16[2,256,256]{2,1,0:T(8,128)(2,1)S(1)} %get-tuple-element.45), channel_id=1, source_target_pairs={{0,32},{1,225},{2,34},{3,227},{4,36},{5,229},{6,38},{7,231},{8,40}... | collective-permute-start | bytes 786440 | tf_op jit(solution)/shard_map/ppermute | solution.py:435
  27.4 9.1 %collective-permute-start.7 = (bf16[2,256,256]{2,1,0:T(8,128)(2,1)S(1)}, bf16[2,256,256]{2,1,0:T(8,128)(2,1)S(1)}, u32[]{:S(2)}, u32[]{:S(2)}) collective-permute-start(bf16[2,256,256]{2,1,0:T(8,128)(2,1)S(1)} %get-tuple-element.46), channel_id=1, source_target_pairs={{0,48},{1,241},{2,50},{3,243},{4,52},{5,245},{6,54},{7,247},{8,56}... | collective-permute-start | bytes 786440 | tf_op jit(solution)/shard_map/ppermute | solution.py:435
  37.6 27.5 %collective-permute-start.10 = (bf16[4,2,256,256]{3,2,1,0:T(8,128)(2,1)}, bf16[4,2,256,256]{3,2,1,0:T(8,128)(2,1)}, u32[]{:S(2)}, u32[]{:S(2)}) collective-permute-start(bf16[4,2,256,256]{3,2,1,0:T(8,128)(2,1)} %pad_maximum_fusion.refs_3_), channel_id=1, source_target_pairs={{1,65},{3,67},{5,69},{7,71},{9,73},{11,75},{13,77},{15,79},{48,80}... | collective-permute-start | bytes 3145736 | tf_op jit(solution)/shard_map/ppermute | solution.py:435
  39.9 25.2 %collective-permute-start.9 = (bf16[4,2,256,256]{3,2,1,0:T(8,128)(2,1)}, bf16[4,2,256,256]{3,2,1,0:T(8,128)(2,1)}, u32[]{:S(2)}, u32[]{:S(2)}) collective-permute-start(bf16[4,2,256,256]{3,2,1,0:T(8,128)(2,1)} %pad_maximum_fusion.refs_3_), channel_id=1, source_target_pairs={{32,128},{33,193},{34,130},{35,195},{36,132},{37,197},{38,134},{39... | collective-permute-start | bytes 3145736 | tf_op jit(solution)/shard_map/ppermute | solution.py:435
  41.5 23.6 %collective-permute-start.8 = (bf16[4,2,256,256]{3,2,1,0:T(8,128)(2,1)}, bf16[4,2,256,256]{3,2,1,0:T(8,128)(2,1)}, u32[]{:S(2)}, u32[]{:S(2)}) collective-permute-start(bf16[4,2,256,256]{3,2,1,0:T(8,128)(2,1)} %pad_maximum_fusion.refs_3_), channel_id=1, source_target_pairs={{16,208},{18,210},{20,212},{22,214},{24,216},{26,218},{28,220},{30... | collective-permute-start | bytes 3145736 | tf_op jit(solution)/shard_map/ppermute | solution.py:435
  46.5 18.7 %collective-permute-start.4 = (f32[256,256]{1,0:T(8,128)S(1)}, f32[256,256]{1,0:T(8,128)S(1)}, u32[]{:S(2)}, u32[]{:S(2)}) collective-permute-start(f32[256,256]{1,0:T(8,128)S(1)} %dynamic-slice_bitcast_fusion), channel_id=1, source_target_pairs={{0,1},{1,2},{2,3},{3,4},{4,5},{5,6},{6,7},{7,8},{8,9},{9,10},{10,1... | collective-permute-start | bytes 786440 | tf_op jit(solution)/shard_map/ppermute | solution.py:375
  48.4 12.5 %copy-start.2 = (f32[2,2,256,256]{3,2,1,0:T(8,128)S(1)}, f32[2,2,256,256]{3,2,1,0:T(8,128)}, u32[]{:S(2)}) copy-start(f32[2,2,256,256]{3,2,1,0:T(8,128)} %probe.1) | copy-start | bytes 3145732
  59.7 5.4 %collective-permute-start.3 = (s32[4,2]{1,0:T(4,128)S(1)}, s32[4,2]{1,0:T(4,128)S(1)}, u32[]{:S(2)}, u32[]{:S(2)}) collective-permute-start(s32[4,2]{1,0:T(4,128)S(1)} %copy.10), channel_id=1, source_target_pairs={{0,2},{1,3},{2,4},{3,5},{4,6},{5,7},{6,8},{7,9},{8,10},{9,11},{10,... | collective-permute-start | bytes 104 | tf_op jit(solution)/shard_map/ppermute | solution.py:375
  61.9 0.8 copy-start.1
  65.1 0.7 copy-start.6
  67.5 36.5 %collective-permute-start.11 = (bf16[4,2,128,256]{3,2,1,0:T(8,128)(2,1)}, bf16[4,2,128,256]{3,2,1,0:T(8,128)(2,1)S(1)}, u32[]{:S(2)}, u32[]{:S(2)}) collective-permute-start(bf16[4,2,128,256]{3,2,1,0:T(8,128)(2,1)} %get-tuple-element.47), channel_id=1, source_target_pairs={{0,224},{2,226},{4,228},{6,230},{8,232},{10,234},{12,236},{14,238}... | collective-permute-start | bytes 1572872 | tf_op jit(solution)/shard_map/ppermute | solution.py:435
  68.8 35.9 %collective-permute-start.12 = (bf16[4,2,128,256]{3,2,1,0:T(8,128)(2,1)}, bf16[4,2,128,256]{3,2,1,0:T(8,128)(2,1)S(1)}, u32[]{:S(2)}, u32[]{:S(2)}) collective-permute-start(bf16[4,2,128,256]{3,2,1,0:T(8,128)(2,1)} %get-tuple-element.49), channel_id=1, source_target_pairs={{0,64},{2,66},{4,68},{6,70},{8,72},{10,74},{12,76},{14,78},{17,49}... | collective-permute-start | bytes 1572872 | tf_op jit(solution)/shard_map/ppermute | solution.py:435
  69.5 35.2 %collective-permute-start.13 = (bf16[4,2,128,256]{3,2,1,0:T(8,128)(2,1)}, bf16[4,2,128,256]{3,2,1,0:T(8,128)(2,1)S(1)}, u32[]{:S(2)}, u32[]{:S(2)}) collective-permute-start(bf16[4,2,128,256]{3,2,1,0:T(8,128)(2,1)} %get-tuple-element.51), channel_id=1, source_target_pairs={{0,160},{2,162},{4,164},{6,166},{8,168},{10,170},{12,172},{14,174}... | collective-permute-start | bytes 1572872 | tf_op jit(solution)/shard_map/ppermute | solution.py:435
  70.2 61.4 %collective-permute-start.19 = (bf16[4,2,128,256]{3,2,1,0:T(8,128)(2,1)}, bf16[4,2,128,256]{3,2,1,0:T(8,128)(2,1)S(1)}, u32[]{:S(2)}, u32[]{:S(2)}) collective-permute-start(bf16[4,2,128,256]{3,2,1,0:T(8,128)(2,1)} %get-tuple-element.53), channel_id=1, source_target_pairs={{0,224},{2,226},{4,228},{6,230},{8,232},{10,234},{12,236},{14,238}... | collective-permute-start | bytes 1572872 | tf_op jit(solution)/shard_map/ppermute | solution.py:435
  71.5 60.1 %collective-permute-start.20 = (bf16[4,2,128,256]{3,2,1,0:T(8,128)(2,1)}, bf16[4,2,128,256]{3,2,1,0:T(8,128)(2,1)S(1)}, u32[]{:S(2)}, u32[]{:S(2)}) collective-permute-start(bf16[4,2,128,256]{3,2,1,0:T(8,128)(2,1)} %get-tuple-element.54), channel_id=1, source_target_pairs={{0,64},{2,66},{4,68},{6,70},{8,72},{10,74},{12,76},{14,78},{17,49}... | collective-permute-start | bytes 1572872 | tf_op jit(solution)/shard_map/ppermute | solution.py:435
  104.0 27.5 %collective-permute-start.21 = (bf16[4,2,128,256]{3,2,1,0:T(8,128)(2,1)}, bf16[4,2,128,256]{3,2,1,0:T(8,128)(2,1)S(1)}, u32[]{:S(2)}, u32[]{:S(2)}) collective-permute-start(bf16[4,2,128,256]{3,2,1,0:T(8,128)(2,1)} %get-tuple-element.55), channel_id=1, source_target_pairs={{0,160},{2,162},{4,164},{6,166},{8,168},{10,170},{12,172},{14,174}... | collective-permute-start | bytes 1572872 | tf_op jit(solution)/shard_map/ppermute | solution.py:435
  104.7 26.8 %copy-start.5 = (bf16[4,2,128,256]{3,2,1,0:T(8,128)(2,1)S(1)}, bf16[4,2,128,256]{3,2,1,0:T(8,128)(2,1)}, u32[]{:S(2)}) copy-start(bf16[4,2,128,256]{3,2,1,0:T(8,128)(2,1)} %get-tuple-element.56) | copy-start | bytes 1572868
  106.0 18.5 %collective-permute-start.16 = (bf16[2,128,256]{2,1,0:T(8,128)(2,1)S(1)}, bf16[2,128,256]{2,1,0:T(8,128)(2,1)S(1)}, u32[]{:S(2)}, u32[]{:S(2)}) collective-permute-start(bf16[2,128,256]{2,1,0:T(8,128)(2,1)S(1)} %get-tuple-element.62), channel_id=1, source_target_pairs={{0,48},{1,241},{2,50},{3,243},{4,52},{5,245},{6,54},{7,247},{8,56}... | collective-permute-start | bytes 393224 | tf_op jit(solution)/shard_map/ppermute | solution.py:435
  118.9 9.7 %collective-permute-start.15 = (bf16[2,128,256]{2,1,0:T(8,128)(2,1)S(1)}, bf16[2,128,256]{2,1,0:T(8,128)(2,1)S(1)}, u32[]{:S(2)}, u32[]{:S(2)}) collective-permute-start(bf16[2,128,256]{2,1,0:T(8,128)(2,1)S(1)} %get-tuple-element.63), channel_id=1, source_target_pairs={{0,32},{1,225},{2,34},{3,227},{4,36},{5,229},{6,38},{7,231},{8,40}... | collective-permute-start | bytes 393224 | tf_op jit(solution)/shard_map/ppermute | solution.py:435
  124.5 6.3 %collective-permute-start.14 = (bf16[2,128,256]{2,1,0:T(8,128)(2,1)S(1)}, bf16[2,128,256]{2,1,0:T(8,128)(2,1)S(1)}, u32[]{:S(2)}, u32[]{:S(2)}) collective-permute-start(bf16[2,128,256]{2,1,0:T(8,128)(2,1)S(1)} %get-tuple-element.64), channel_id=1, source_target_pairs={{0,16},{1,17},{2,18},{3,19},{4,20},{5,21},{6,22},{7,23},{8,24},{9,... | collective-permute-start | bytes 393224 | tf_op jit(solution)/shard_map/ppermute | solution.py:435
  130.9 9.1 %copy-start.4 = (s32[48]{0:T(128)S(1)}, s32[48]{0:T(128)}, u32[]{:S(2)}) copy-start(s32[48]{0:T(128)} %copy-done.3) | copy-start | bytes 580
  130.9 6.8 %collective-permute-start.18 = (bf16[4,2,128,256]{3,2,1,0:T(8,128)(2,1)S(1)}, bf16[4,2,128,256]{3,2,1,0:T(8,128)(2,1)S(1)}, u32[]{:S(2)}, u32[]{:S(2)}) collective-permute-start(bf16[4,2,128,256]{3,2,1,0:T(8,128)(2,1)S(1)} %pad_maximum_fusion.1), channel_id=1, source_target_pairs={{0,1},{1,2},{2,3},{3,4},{4,5},{5,6},{6,7},{7,8},{8,9},{9,10},{10,1... | collective-permute-start | bytes 1572872 | tf_op jit(solution)/shard_map/ppermute | solution.py:375
  131.0 9.0 %collective-permute-start.17 = (bf16[4,2,128,256]{3,2,1,0:T(8,128)(2,1)S(1)}, bf16[4,2,128,256]{3,2,1,0:T(8,128)(2,1)S(1)}, u32[]{:S(2)}, u32[]{:S(2)}) collective-permute-start(bf16[4,2,128,256]{3,2,1,0:T(8,128)(2,1)S(1)} %pad_maximum_fusion.1), channel_id=1, source_target_pairs={{0,15},{1,0},{2,1},{3,2},{4,3},{5,4},{6,5},{7,6},{8,7},{9,8},{10,9... | collective-permute-start | bytes 1572872 | tf_op jit(solution)/shard_map/ppermute | solution.py:375
  131.7 9.6 %collective-permute-start.24 = (bf16[2,128,256]{2,1,0:T(8,128)(2,1)S(1)}, bf16[2,128,256]{2,1,0:T(8,128)(2,1)S(1)}, u32[]{:S(2)}, u32[]{:S(2)}) collective-permute-start(bf16[2,128,256]{2,1,0:T(8,128)(2,1)S(1)} %get-tuple-element.57), channel_id=1, source_target_pairs={{0,48},{1,241},{2,50},{3,243},{4,52},{5,245},{6,54},{7,247},{8,56}... | collective-permute-start | bytes 393224 | tf_op jit(solution)/shard_map/ppermute | solution.py:435
  136.7 5.3 %collective-permute-start.23 = (bf16[2,128,256]{2,1,0:T(8,128)(2,1)S(1)}, bf16[2,128,256]{2,1,0:T(8,128)(2,1)S(1)}, u32[]{:S(2)}, u32[]{:S(2)}) collective-permute-start(bf16[2,128,256]{2,1,0:T(8,128)(2,1)S(1)} %get-tuple-element.58), channel_id=1, source_target_pairs={{0,32},{1,225},{2,34},{3,227},{4,36},{5,229},{6,38},{7,231},{8,40}... | collective-permute-start | bytes 393224 | tf_op jit(solution)/shard_map/ppermute | solution.py:435
  137.2 10.1 %collective-permute-start.22 = (bf16[2,128,256]{2,1,0:T(8,128)(2,1)S(1)}, bf16[2,128,256]{2,1,0:T(8,128)(2,1)S(1)}, u32[]{:S(2)}, u32[]{:S(2)}) collective-permute-start(bf16[2,128,256]{2,1,0:T(8,128)(2,1)S(1)} %get-tuple-element.59), channel_id=1, source_target_pairs={{0,16},{1,17},{2,18},{3,19},{4,20},{5,21},{6,22},{7,23},{8,24},{9,... | collective-permute-start | bytes 393224 | tf_op jit(solution)/shard_map/ppermute | solution.py:435

commit v11 on v10

--- a/solution.py
+++ b/solution.py
@@ -62,7 +62,7 @@
 
 
 def chain_body(plan, wave, wanted, *refs, n, slices):
-    ins, tabs_hbm, near_out, far_out = refs[0:4], refs[4], refs[5:9], refs[9:13]
+    ins, tabs_hbm, near_out, far_out = refs[3::-1], refs[4], refs[5:9], refs[9:13]
     (patch, tabs, inc, lhs0, lhs1, mid0, mid1, outv, target, term, psem, tsem, osem, gsem) = refs[13:27]
     accs = list(refs[27:])
     first_acc = [[[accs.pop(0) for _ in range(n // FIRST)] for _ in range(2)] for _ in range(2)]
@@ -245,7 +245,7 @@
             pltpu.SemaphoreType.DMA,
         ],
         compiler_params=pltpu.CompilerParams(vmem_limit_bytes=58 << 20),
-    )(plan, wave, wanted, *messages, tables)
+    )(plan, wave, wanted, *messages[::-1], tables)
 
 
 def window(ref, lead, offset, n):
@@ -476,8 +476,7 @@
     target = shifted(lax.dynamic_index_in_dim(measured, plan[OTHER], 0, False), 1)
 
     message = jnp.stack([parts[0]] + [within(parts[k], k) for k in (1, 2, 3)])
-    messages = {0: message} | {k: towards(message, k) for k in (2, 1, 3)}
-    messages = [messages[k] for k in range(4)]
+    messages = [message] + [towards(message, k) for k in (1, 2, 3)]
     tables = make_tables(n, depth_size)
     wave = roll_probe(plan, mid_places, probe, rows)
     wave, source, far_places = lax.optimization_barrier((wave, [plan[SOURCE] == k for k in (1, 2, 3)], far_places))

time: 150 us -> 156 us (1.040)
  starting transfers between devices: 49.3 us -> 55.2 us
    ppermute x18, starting transfers between devices: 44.1 us -> 47.3 us  [permute(): return lax.ppermute(block, ('depth', 'lat'), pairs)]
    ppermute x7, starting transfers between devices: 5.18 us -> 7.9 us  [shifted(): lax.ppermute(block, 'lat', [(i, (i + distance) % size) for i in range(siz...]
  transfers between devices with their start and end apart: 25 -> 25, of which waited for: 12 -> 11; matrix products, arithmetic and copies ran while one was open for 3% -> 2% of each run, Pallas kernels for 10% -> 10%
where the time goes in v11:
time: 156 us; the launch traced here: 155 us
  waiting for transfers between devices  67.5 us (43%)
  starting transfers between devices  55.2 us (35%)
  Pallas kernels  20.3 us (13%)
  other arithmetic  4.43 us (3%)
  between operations  4.19 us (3%)
  local copies, waits for them, and re-layouts  3.8 us (2%)
    ppermute x18, waiting for transfers between devices, permute(): return lax.ppermute(block, ('depth', 'lat'), pairs)  54.3 us
    ppermute x18, starting transfers between devices, permute(): return lax.ppermute(block, ('depth', 'lat'), pairs)  47.3 us
    ppermute x7, waiting for transfers between devices, shifted(): lax.ppermute(block, 'lat', [(i, (i + distance) % size) for i in range(siz...  13.2 us
    pallas_call x1, Pallas kernels, make_tables(): pl.pallas_call(functools.partial(tables_kernel, n=n, slices=slices), grid...  11.2 us
    ppermute x7, starting transfers between devices, shifted(): lax.ppermute(block, 'lat', [(i, (i + distance) % size) for i in range(siz...  7.9 us
  transfers between devices with their start and end apart: 25, of which 11 were waited for; matrix products, arithmetic and copies ran while one was open for 2% of the time, Pallas kernels for 10%

profile of v11, /device:TPU:1, one launch (start us, length us, event | category | flops | bytes accessed | tf_op | source)
XLA Modules:
  0.0 155.4 jit_solution(11437749122409153598)
XLA Ops:
  0.0 1.8 %convert_bitcast_fusion.tile = bf16[2,128,2048]{2,1,0:T(8,128)(2,1)S(1)} fusion(f32[1,2,128,2048]{3,2,1,0:T(8,128)} %param.7), kind=kLoop, calls=%fused_computation.1 | loop fusion | flops 524288 | bytes 3145728 | tf_op jit(solution)/shard_map/convert_element_type | solution.py:466
  1.8 3.3 %collective-permute-start.1 = (bf16[2,128,2048]{2,1,0:T(8,128)(2,1)S(1)}, bf16[2,128,2048]{2,1,0:T(8,128)(2,1)S(1)}, u32[]{:S(2)}, u32[]{:S(2)}) collective-permute-start(bf16[2,128,2048]{2,1,0:T(8,128)(2,1)S(1)} %convert_bitcast_fusion.tile), channel_id=1, source_target_pairs={{0,15},{1,0},{2,1},{3,2},{4,3},{5,4},{6,5},{7,6},{8,7},{9,8},{10,9... | collective-permute-start | bytes 3145736 | tf_op jit(solution)/shard_map/ppermute | solution.py:375
  5.2 0.1 copy.8.places.own_places
  5.3 1.5 shard_map.73
  6.8 0.0 collective-permute-start.2
  6.8 0.0 collective-permute-start
  6.8 0.7 fusion.2.plan.refs_0_
  7.5 5.7 %collective-permute-done.places = s32[4,2]{1,0:T(4,128)S(1)} collective-permute-done((s32[4,2]{1,0:T(4,128)S(1)}, s32[4,2]{1,0:T(4,128)S(1)}, u32[]{:S(2)}, u32[]{:S(2)}) %collective-permute-start) | collective-permute-done | bytes 64 | tf_op jit(solution)/shard_map/ppermute | solution.py:375
  13.2 0.0 collective-permute-done.2.behind
  13.2 4.2 %collective-permute-done.1.ahead = bf16[2,128,2048]{2,1,0:T(8,128)(2,1)S(1)} collective-permute-done((bf16[2,128,2048]{2,1,0:T(8,128)(2,1)S(1)}, bf16[2,128,2048]{2,1,0:T(8,128)(2,1)S(1)}, u32[]{:S(2)}, u32[]{:S(2)}) %collective-permute-start.1) | collective-permute-done | bytes 1048608 | tf_op jit(solution)/shard_map/ppermute | solution.py:375
  17.4 1.4 shard_map.75
  18.8 3.0 %collective-permute-start.5 = (bf16[2,256,256]{2,1,0:T(8,128)(2,1)S(1)}, bf16[2,256,256]{2,1,0:T(8,128)(2,1)S(1)}, u32[]{:S(2)}, u32[]{:S(2)}) collective-permute-start(bf16[2,256,256]{2,1,0:T(8,128)(2,1)S(1)} %get-tuple-element.44), channel_id=1, source_target_pairs={{0,16},{1,17},{2,18},{3,19},{4,20},{5,21},{6,22},{7,23},{8,24},{9,... | collective-permute-start | bytes 786440 | tf_op jit(solution)/shard_map/ppermute | solution.py:435
  21.8 5.6 %collective-permute-start.6 = (bf16[2,256,256]{2,1,0:T(8,128)(2,1)S(1)}, bf16[2,256,256]{2,1,0:T(8,128)(2,1)S(1)}, u32[]{:S(2)}, u32[]{:S(2)}) collective-permute-start(bf16[2,256,256]{2,1,0:T(8,128)(2,1)S(1)} %get-tuple-element.45), channel_id=1, source_target_pairs={{0,32},{1,225},{2,34},{3,227},{4,36},{5,229},{6,38},{7,231},{8,40}... | collective-permute-start | bytes 786440 | tf_op jit(solution)/shard_map/ppermute | solution.py:435
  27.4 0.0 collective-permute-done.5
  27.4 4.0 %collective-permute-done.6 = bf16[2,256,256]{2,1,0:T(8,128)(2,1)S(1)} collective-permute-done((bf16[2,256,256]{2,1,0:T(8,128)(2,1)S(1)}, bf16[2,256,256]{2,1,0:T(8,128)(2,1)S(1)}, u32[]{:S(2)}, u32[]{:S(2)}) %collective-permute-start.6) | collective-permute-done | bytes 262176 | tf_op jit(solution)/shard_map/ppermute | solution.py:435
  31.5 5.0 %collective-permute-done.7 = bf16[2,256,256]{2,1,0:T(8,128)(2,1)S(1)} collective-permute-done((bf16[2,256,256]{2,1,0:T(8,128)(2,1)S(1)}, bf16[2,256,256]{2,1,0:T(8,128)(2,1)S(1)}, u32[]{:S(2)}, u32[]{:S(2)}) %collective-permute-start.7) | collective-permute-done | bytes 262176 | tf_op jit(solution)/shard_map/ppermute | solution.py:435
  36.5 1.1 pad_maximum_fusion.refs_6_
  37.6 1.6 %collective-permute-start.10 = (bf16[4,2,256,256]{3,2,1,0:T(8,128)(2,1)}, bf16[4,2,256,256]{3,2,1,0:T(8,128)(2,1)}, u32[]{:S(2)}, u32[]{:S(2)}) collective-permute-start(bf16[4,2,256,256]{3,2,1,0:T(8,128)(2,1)} %pad_maximum_fusion.refs_6_), channel_id=1, source_target_pairs={{16,208},{18,210},{20,212},{22,214},{24,216},{26,218},{28,220},{30... | collective-permute-start | bytes 3145736 | tf_op jit(solution)/shard_map/ppermute | solution.py:435
  39.3 1.7 %collective-permute-start.9 = (bf16[4,2,256,256]{3,2,1,0:T(8,128)(2,1)}, bf16[4,2,256,256]{3,2,1,0:T(8,128)(2,1)}, u32[]{:S(2)}, u32[]{:S(2)}) collective-permute-start(bf16[4,2,256,256]{3,2,1,0:T(8,128)(2,1)} %pad_maximum_fusion.refs_6_), channel_id=1, source_target_pairs={{32,128},{33,193},{34,130},{35,195},{36,132},{37,197},{38,134},{39... | collective-permute-start | bytes 3145736 | tf_op jit(solution)/shard_map/ppermute | solution.py:435
  40.9 2.3 %collective-permute-start.8 = (bf16[4,2,256,256]{3,2,1,0:T(8,128)(2,1)}, bf16[4,2,256,256]{3,2,1,0:T(8,128)(2,1)}, u32[]{:S(2)}, u32[]{:S(2)}) collective-permute-start(bf16[4,2,256,256]{3,2,1,0:T(8,128)(2,1)} %pad_maximum_fusion.refs_6_), channel_id=1, source_target_pairs={{1,65},{3,67},{5,69},{7,71},{9,73},{11,75},{13,77},{15,79},{48,80}... | collective-permute-start | bytes 3145736 | tf_op jit(solution)/shard_map/ppermute | solution.py:435
  43.2 0.7 constant_dynamic-slice_fusion
  43.9 0.7 fusion.1
  46.5 0.1 collective-permute-start.4
  48.4 0.0 copy-start.2
  48.4 11.2 %shard_map.76.refs_7_ = bf16[17,2,512,512]{3,2,1,0:T(8,128)(2,1)} custom-call(f32[2,17]{1,0:T(2,128)} %constant.43.clone.scales, f32[4,256,256]{2,1,0:T(8,128)} %constant.44.clone.base), custom_call_target="tpu_custom_call" | custom-call | tf_op jit(solution)/shard_map/pallas_call | solution.py:49
  59.6 0.1 copy.10
  59.7 0.5 collective-permute-start.3
  60.3 1.0 shard_map.74.refs_1_
  61.3 0.8 copy-done.1
  62.1 3.0 %collective-permute-done.3.far_places = s32[4,2]{1,0:T(4,128)S(1)} collective-permute-done((s32[4,2]{1,0:T(4,128)S(1)}, s32[4,2]{1,0:T(4,128)S(1)}, u32[]{:S(2)}, u32[]{:S(2)}) %collective-permute-start.3) | collective-permute-done | bytes 64 | tf_op jit(solution)/shard_map/ppermute | solution.py:375
  65.1 0.0 collective-permute-done.4.refs_2_
  65.1 0.0 collective-permute-done.9.refs_4_
  65.1 0.0 collective-permute-done.8.refs_3_
  65.1 0.7 copy-done.6
  65.8 1.6 %shard_map.77 = (bf16[4,2,128,256]{3,2,1,0:T(8,128)(2,1)}, bf16[4,2,128,256]{3,2,1,0:T(8,128)(2,1)}, bf16[4,2,128,256]{3,2,1,0:T(8,128)(2,1)}, bf16[4,2,128,256]...) custom-call(s32[48]{0:T(128)} %copy-done.3, ...), custom_call_target="tpu_custom_call" | custom-call | tf_op jit(solution)/shard_map/pallas_call | solution.py:226
  67.5 1.3 collective-permute-start.11
  68.8 0.7 collective-permute-start.12
  69.5 0.7 collective-permute-start.13
  70.2 1.3 collective-permute-start.19
  71.5 0.7 collective-permute-start.20
  72.2 31.9 %collective-permute-done.11 = bf16[4,2,128,256]{3,2,1,0:T(8,128)(2,1)S(1)} collective-permute-done((bf16[4,2,128,256]{3,2,1,0:T(8,128)(2,1)}, bf16[4,2,128,256]{3,2,1,0:T(8,128)(2,1)S(1)}, u32[]{:S(2)}, u32[]{:S(2)}) %collective-permute-start.11) | collective-permute-done | bytes 524320 | tf_op jit(solution)/shard_map/ppermute | solution.py:435
  104.1 0.7 collective-permute-start.21
  104.8 0.0 collective-permute-done.13
  104.8 1.3 select_select_fusion.1
  106.2 12.8 %collective-permute-start.16 = (bf16[2,128,256]{2,1,0:T(8,128)(2,1)S(1)}, bf16[2,128,256]{2,1,0:T(8,128)(2,1)S(1)}, u32[]{:S(2)}, u32[]{:S(2)}) collective-permute-start(bf16[2,128,256]{2,1,0:T(8,128)(2,1)S(1)} %get-tuple-element.62), channel_id=1, source_target_pairs={{0,48},{1,241},{2,50},{3,243},{4,52},{5,245},{6,54},{7,247},{8,56}... | collective-permute-start | bytes 393224 | tf_op jit(solution)/shard_map/ppermute | solution.py:435
  119.0 2.2 %collective-permute-start.15 = (bf16[2,128,256]{2,1,0:T(8,128)(2,1)S(1)}, bf16[2,128,256]{2,1,0:T(8,128)(2,1)S(1)}, u32[]{:S(2)}, u32[]{:S(2)}) collective-permute-start(bf16[2,128,256]{2,1,0:T(8,128)(2,1)S(1)} %get-tuple-element.63), channel_id=1, source_target_pairs={{0,32},{1,225},{2,34},{3,227},{4,36},{5,229},{6,38},{7,231},{8,40}... | collective-permute-start | bytes 393224 | tf_op jit(solution)/shard_map/ppermute | solution.py:435
  121.2 3.8 %collective-permute-done.16 = bf16[2,128,256]{2,1,0:T(8,128)(2,1)S(1)} collective-permute-done((bf16[2,128,256]{2,1,0:T(8,128)(2,1)S(1)}, bf16[2,128,256]{2,1,0:T(8,128)(2,1)S(1)}, u32[]{:S(2)}, u32[]{:S(2)}) %collective-permute-start.16) | collective-permute-done | bytes 131104 | tf_op jit(solution)/shard_map/ppermute | solution.py:435
  125.0 4.3 %collective-permute-start.14 = (bf16[2,128,256]{2,1,0:T(8,128)(2,1)S(1)}, bf16[2,128,256]{2,1,0:T(8,128)(2,1)S(1)}, u32[]{:S(2)}, u32[]{:S(2)}) collective-permute-start(bf16[2,128,256]{2,1,0:T(8,128)(2,1)S(1)} %get-tuple-element.64), channel_id=1, source_target_pairs={{0,16},{1,17},{2,18},{3,19},{4,20},{5,21},{6,22},{7,23},{8,24},{9,... | collective-permute-start | bytes 393224 | tf_op jit(solution)/shard_map/ppermute | solution.py:435
  129.3 0.0 collective-permute-done.15
  129.3 2.4 %collective-permute-done.14 = bf16[2,128,256]{2,1,0:T(8,128)(2,1)S(1)} collective-permute-done((bf16[2,128,256]{2,1,0:T(8,128)(2,1)S(1)}, bf16[2,128,256]{2,1,0:T(8,128)(2,1)S(1)}, u32[]{:S(2)}, u32[]{:S(2)}) %collective-permute-start.14) | collective-permute-done | bytes 131104 | tf_op jit(solution)/shard_map/ppermute | solution.py:435
  131.7 0.1 pad_maximum_fusion.1
  131.7 3.9 %collective-permute-start.18 = (bf16[4,2,128,256]{3,2,1,0:T(8,128)(2,1)S(1)}, bf16[4,2,128,256]{3,2,1,0:T(8,128)(2,1)S(1)}, u32[]{:S(2)}, u32[]{:S(2)}) collective-permute-start(bf16[4,2,128,256]{3,2,1,0:T(8,128)(2,1)S(1)} %pad_maximum_fusion.1), channel_id=1, source_target_pairs={{0,1},{1,2},{2,3},{3,4},{4,5},{5,6},{6,7},{7,8},{8,9},{9,10},{10,1... | collective-permute-start | bytes 1572872 | tf_op jit(solution)/shard_map/ppermute | solution.py:375
  135.7 0.0 collective-permute-done.20
  135.7 0.0 collective-permute-done.21
  135.7 0.1 select_select_fusion
  135.9 5.2 %collective-permute-start.24 = (bf16[2,128,256]{2,1,0:T(8,128)(2,1)S(1)}, bf16[2,128,256]{2,1,0:T(8,128)(2,1)S(1)}, u32[]{:S(2)}, u32[]{:S(2)}) collective-permute-start(bf16[2,128,256]{2,1,0:T(8,128)(2,1)S(1)} %get-tuple-element.57), channel_id=1, source_target_pairs={{0,48},{1,241},{2,50},{3,243},{4,52},{5,245},{6,54},{7,247},{8,56}... | collective-permute-start | bytes 393224 | tf_op jit(solution)/shard_map/ppermute | solution.py:435
  141.1 0.7 collective-permute-start.23
  141.8 2.6 %collective-permute-start.22 = (bf16[2,128,256]{2,1,0:T(8,128)(2,1)S(1)}, bf16[2,128,256]{2,1,0:T(8,128)(2,1)S(1)}, u32[]{:S(2)}, u32[]{:S(2)}) collective-permute-start(bf16[2,128,256]{2,1,0:T(8,128)(2,1)S(1)} %get-tuple-element.59), channel_id=1, source_target_pairs={{0,16},{1,17},{2,18},{3,19},{4,20},{5,21},{6,22},{7,23},{8,24},{9,... | collective-permute-start | bytes 393224 | tf_op jit(solution)/shard_map/ppermute | solution.py:435
  144.4 0.2 collective-permute-done.17.from_own
  144.6 1.3 shard_map.78.total
  145.9 0.0 collective-permute-done.24.m3
  146.0 0.5 collective-permute-done.23.m2
  146.4 6.6 %collective-permute-done.22.m1 = bf16[2,128,256]{2,1,0:T(8,128)(2,1)S(1)} collective-permute-done((bf16[2,128,256]{2,1,0:T(8,128)(2,1)S(1)}, bf16[2,128,256]{2,1,0:T(8,128)(2,1)S(1)}, u32[]{:S(2)}, u32[]{:S(2)}) %collective-permute-start.22) | collective-permute-done | bytes 131104 | tf_op jit(solution)/shard_map/ppermute | solution.py:435
  153.1 2.2 %shard_map.79 = f32[2,128,2048]{2,1,0:T(8,128)} custom-call(s32[48]{0:T(128)S(1)} %copy-done.4, s32[4,2]{1,0:T(4,128)S(1)} %collective-permute-done.places, f32[2,128,2048]{2,1,0:T(8,128)S(1)} %shard_map.78.total, bf16[2,128,256]{2,1,0:T(8,128)(2,1)S(1)} %get-tuple-element.60.m0, bf16[2,128,256]{2,1,0:T(8,128)(2,1)S(1)} %collective-permute-done.22.m1, ...), custom_call_target="tpu_custom_call" | custom-call | tf_op jit(solution)/shard_map/pallas_call | solution.py:363
  (22 shorter events, 0.1 us)
Async XLA Ops:
  0.0 46.4 %copy-start = (f32[4,256,256]{2,1,0:T(8,128)S(1)}, f32[4,256,256]{2,1,0:T(8,128)}, u32[]{:S(2)}) copy-start(f32[4,256,256]{2,1,0:T(8,128)} %param.10) | copy-start | bytes 3145732
  0.0 5.2 %copy-start.7 = (s32[4,2]{0,1:T(2,128)S(1)}, s32[4,2]{0,1:T(2,128)}, u32[]{:S(2)}) copy-start(s32[4,2]{0,1:T(2,128)} %param.9) | copy-start | bytes 100
  1.8 15.6 %collective-permute-start.1 = (bf16[2,128,2048]{2,1,0:T(8,128)(2,1)S(1)}, bf16[2,128,2048]{2,1,0:T(8,128)(2,1)S(1)}, u32[]{:S(2)}, u32[]{:S(2)}) collective-permute-start(bf16[2,128,2048]{2,1,0:T(8,128)(2,1)S(1)} %convert_bitcast_fusion.tile), channel_id=1, source_target_pairs={{0,15},{1,0},{2,1},{3,2},{4,3},{5,4},{6,5},{7,6},{8,7},{9,8},{10,9... | collective-permute-start | bytes 3145736 | tf_op jit(solution)/shard_map/ppermute | solution.py:375
  6.8 6.4 %collective-permute-start.2 = (bf16[4,2,128,256]{3,2,1,0:T(8,128)(2,1)}, bf16[4,2,128,256]{3,2,1,0:T(8,128)(2,1)}, u32[]{:S(2)}, u32[]{:S(2)}) collective-permute-start(bf16[4,2,128,256]{3,2,1,0:T(8,128)(2,1)} %shard_map.73), channel_id=1, source_target_pairs={{0,1},{1,2},{2,3},{3,4},{4,5},{5,6},{6,7},{7,8},{8,9},{9,10},{10,1... | collective-permute-start | bytes 1572872 | tf_op jit(solution)/shard_map/ppermute | solution.py:375
  6.8 6.4 %collective-permute-start = (s32[4,2]{1,0:T(4,128)S(1)}, s32[4,2]{1,0:T(4,128)S(1)}, u32[]{:S(2)}, u32[]{:S(2)}) collective-permute-start(s32[4,2]{1,0:T(4,128)S(1)} %copy.8.places.own_places), channel_id=1, source_target_pairs={{0,1},{1,2},{2,3},{3,4},{4,5},{5,6},{6,7},{7,8},{8,9},{9,10},{10,1... | collective-permute-start | bytes 104 | tf_op jit(solution)/shard_map/ppermute | solution.py:375
  7.5 52.8 %copy-start.3 = (s32[48]{0:T(128)}, s32[48]{0:T(128)S(1)}, u32[]{:S(2)}) copy-start(s32[48]{0:T(128)S(1)} %fusion.2.plan.refs_0_) | copy-start | bytes 580
  18.8 8.6 %collective-permute-start.5 = (bf16[2,256,256]{2,1,0:T(8,128)(2,1)S(1)}, bf16[2,256,256]{2,1,0:T(8,128)(2,1)S(1)}, u32[]{:S(2)}, u32[]{:S(2)}) collective-permute-start(bf16[2,256,256]{2,1,0:T(8,128)(2,1)S(1)} %get-tuple-element.44), channel_id=1, source_target_pairs={{0,16},{1,17},{2,18},{3,19},{4,20},{5,21},{6,22},{7,23},{8,24},{9,... | collective-permute-start | bytes 786440 | tf_op jit(solution)/shard_map/ppermute | solution.py:435
  21.8 9.6 %collective-permute-start.6 = (bf16[2,256,256]{2,1,0:T(8,128)(2,1)S(1)}, bf16[2,256,256]{2,1,0:T(8,128)(2,1)S(1)}, u32[]{:S(2)}, u32[]{:S(2)}) collective-permute-start(bf16[2,256,256]{2,1,0:T(8,128)(2,1)S(1)} %get-tuple-element.45), channel_id=1, source_target_pairs={{0,32},{1,225},{2,34},{3,227},{4,36},{5,229},{6,38},{7,231},{8,40}... | collective-permute-start | bytes 786440 | tf_op jit(solution)/shard_map/ppermute | solution.py:435
  27.4 9.1 %collective-permute-start.7 = (bf16[2,256,256]{2,1,0:T(8,128)(2,1)S(1)}, bf16[2,256,256]{2,1,0:T(8,128)(2,1)S(1)}, u32[]{:S(2)}, u32[]{:S(2)}) collective-permute-start(bf16[2,256,256]{2,1,0:T(8,128)(2,1)S(1)} %get-tuple-element.46), channel_id=1, source_target_pairs={{0,48},{1,241},{2,50},{3,243},{4,52},{5,245},{6,54},{7,247},{8,56}... | collective-permute-start | bytes 786440 | tf_op jit(solution)/shard_map/ppermute | solution.py:435
  37.6 27.5 %collective-permute-start.10 = (bf16[4,2,256,256]{3,2,1,0:T(8,128)(2,1)}, bf16[4,2,256,256]{3,2,1,0:T(8,128)(2,1)}, u32[]{:S(2)}, u32[]{:S(2)}) collective-permute-start(bf16[4,2,256,256]{3,2,1,0:T(8,128)(2,1)} %pad_maximum_fusion.refs_6_), channel_id=1, source_target_pairs={{16,208},{18,210},{20,212},{22,214},{24,216},{26,218},{28,220},{30... | collective-permute-start | bytes 3145736 | tf_op jit(solution)/shard_map/ppermute | solution.py:435
  39.3 25.9 %collective-permute-start.9 = (bf16[4,2,256,256]{3,2,1,0:T(8,128)(2,1)}, bf16[4,2,256,256]{3,2,1,0:T(8,128)(2,1)}, u32[]{:S(2)}, u32[]{:S(2)}) collective-permute-start(bf16[4,2,256,256]{3,2,1,0:T(8,128)(2,1)} %pad_maximum_fusion.refs_6_), channel_id=1, source_target_pairs={{32,128},{33,193},{34,130},{35,195},{36,132},{37,197},{38,134},{39... | collective-permute-start | bytes 3145736 | tf_op jit(solution)/shard_map/ppermute | solution.py:435
  40.9 24.2 %collective-permute-start.8 = (bf16[4,2,256,256]{3,2,1,0:T(8,128)(2,1)}, bf16[4,2,256,256]{3,2,1,0:T(8,128)(2,1)}, u32[]{:S(2)}, u32[]{:S(2)}) collective-permute-start(bf16[4,2,256,256]{3,2,1,0:T(8,128)(2,1)} %pad_maximum_fusion.refs_6_), channel_id=1, source_target_pairs={{1,65},{3,67},{5,69},{7,71},{9,73},{11,75},{13,77},{15,79},{48,80}... | collective-permute-start | bytes 3145736 | tf_op jit(solution)/shard_map/ppermute | solution.py:435
  46.5 18.6 %collective-permute-start.4 = (f32[256,256]{1,0:T(8,128)S(1)}, f32[256,256]{1,0:T(8,128)S(1)}, u32[]{:S(2)}, u32[]{:S(2)}) collective-permute-start(f32[256,256]{1,0:T(8,128)S(1)} %dynamic-slice_bitcast_fusion), channel_id=1, source_target_pairs={{0,1},{1,2},{2,3},{3,4},{4,5},{5,6},{6,7},{7,8},{8,9},{9,10},{10,1... | collective-permute-start | bytes 786440 | tf_op jit(solution)/shard_map/ppermute | solution.py:375
  48.4 11.9 %copy-start.2 = (f32[2,2,256,256]{3,2,1,0:T(8,128)S(1)}, f32[2,2,256,256]{3,2,1,0:T(8,128)}, u32[]{:S(2)}) copy-start(f32[2,2,256,256]{3,2,1,0:T(8,128)} %probe.1) | copy-start | bytes 3145732
  59.7 5.4 %collective-permute-start.3 = (s32[4,2]{1,0:T(4,128)S(1)}, s32[4,2]{1,0:T(4,128)S(1)}, u32[]{:S(2)}, u32[]{:S(2)}) collective-permute-start(s32[4,2]{1,0:T(4,128)S(1)} %copy.10), channel_id=1, source_target_pairs={{0,2},{1,3},{2,4},{3,5},{4,6},{5,7},{6,8},{7,9},{8,10},{9,11},{10,... | collective-permute-start | bytes 104 | tf_op jit(solution)/shard_map/ppermute | solution.py:375
  61.3 0.8 copy-start.1
  65.1 0.7 copy-start.6
  67.5 36.7 %collective-permute-start.11 = (bf16[4,2,128,256]{3,2,1,0:T(8,128)(2,1)}, bf16[4,2,128,256]{3,2,1,0:T(8,128)(2,1)S(1)}, u32[]{:S(2)}, u32[]{:S(2)}) collective-permute-start(bf16[4,2,128,256]{3,2,1,0:T(8,128)(2,1)} %get-tuple-element.47), channel_id=1, source_target_pairs={{0,224},{2,226},{4,228},{6,230},{8,232},{10,234},{12,236},{14,238}... | collective-permute-start | bytes 1572872 | tf_op jit(solution)/shard_map/ppermute | solution.py:435
  68.8 36.0 %collective-permute-start.12 = (bf16[4,2,128,256]{3,2,1,0:T(8,128)(2,1)}, bf16[4,2,128,256]{3,2,1,0:T(8,128)(2,1)S(1)}, u32[]{:S(2)}, u32[]{:S(2)}) collective-permute-start(bf16[4,2,128,256]{3,2,1,0:T(8,128)(2,1)} %get-tuple-element.49), channel_id=1, source_target_pairs={{0,64},{2,66},{4,68},{6,70},{8,72},{10,74},{12,76},{14,78},{17,49}... | collective-permute-start | bytes 1572872 | tf_op jit(solution)/shard_map/ppermute | solution.py:435
  69.5 35.4 %collective-permute-start.13 = (bf16[4,2,128,256]{3,2,1,0:T(8,128)(2,1)}, bf16[4,2,128,256]{3,2,1,0:T(8,128)(2,1)S(1)}, u32[]{:S(2)}, u32[]{:S(2)}) collective-permute-start(bf16[4,2,128,256]{3,2,1,0:T(8,128)(2,1)} %get-tuple-element.51), channel_id=1, source_target_pairs={{0,160},{2,162},{4,164},{6,166},{8,168},{10,170},{12,172},{14,174}... | collective-permute-start | bytes 1572872 | tf_op jit(solution)/shard_map/ppermute | solution.py:435
  70.2 65.5 %collective-permute-start.19 = (bf16[4,2,128,256]{3,2,1,0:T(8,128)(2,1)}, bf16[4,2,128,256]{3,2,1,0:T(8,128)(2,1)S(1)}, u32[]{:S(2)}, u32[]{:S(2)}) collective-permute-start(bf16[4,2,128,256]{3,2,1,0:T(8,128)(2,1)} %get-tuple-element.53), channel_id=1, source_target_pairs={{0,224},{2,226},{4,228},{6,230},{8,232},{10,234},{12,236},{14,238}... | collective-permute-start | bytes 1572872 | tf_op jit(solution)/shard_map/ppermute | solution.py:435
  71.5 64.2 %collective-permute-start.20 = (bf16[4,2,128,256]{3,2,1,0:T(8,128)(2,1)}, bf16[4,2,128,256]{3,2,1,0:T(8,128)(2,1)S(1)}, u32[]{:S(2)}, u32[]{:S(2)}) collective-permute-start(bf16[4,2,128,256]{3,2,1,0:T(8,128)(2,1)} %get-tuple-element.54), channel_id=1, source_target_pairs={{0,64},{2,66},{4,68},{6,70},{8,72},{10,74},{12,76},{14,78},{17,49}... | collective-permute-start | bytes 1572872 | tf_op jit(solution)/shard_map/ppermute | solution.py:435
  104.1 31.6 %collective-permute-start.21 = (bf16[4,2,128,256]{3,2,1,0:T(8,128)(2,1)}, bf16[4,2,128,256]{3,2,1,0:T(8,128)(2,1)S(1)}, u32[]{:S(2)}, u32[]{:S(2)}) collective-permute-start(bf16[4,2,128,256]{3,2,1,0:T(8,128)(2,1)} %get-tuple-element.55), channel_id=1, source_target_pairs={{0,160},{2,162},{4,164},{6,166},{8,168},{10,170},{12,172},{14,174}... | collective-permute-start | bytes 1572872 | tf_op jit(solution)/shard_map/ppermute | solution.py:435
  104.8 30.9 %copy-start.5 = (bf16[4,2,128,256]{3,2,1,0:T(8,128)(2,1)S(1)}, bf16[4,2,128,256]{3,2,1,0:T(8,128)(2,1)}, u32[]{:S(2)}) copy-start(bf16[4,2,128,256]{3,2,1,0:T(8,128)(2,1)} %get-tuple-element.56) | copy-start | bytes 1572868
  106.2 18.8 %collective-permute-start.16 = (bf16[2,128,256]{2,1,0:T(8,128)(2,1)S(1)}, bf16[2,128,256]{2,1,0:T(8,128)(2,1)S(1)}, u32[]{:S(2)}, u32[]{:S(2)}) collective-permute-start(bf16[2,128,256]{2,1,0:T(8,128)(2,1)S(1)} %get-tuple-element.62), channel_id=1, source_target_pairs={{0,48},{1,241},{2,50},{3,243},{4,52},{5,245},{6,54},{7,247},{8,56}... | collective-permute-start | bytes 393224 | tf_op jit(solution)/shard_map/ppermute | solution.py:435
  119.0 10.4 %collective-permute-start.15 = (bf16[2,128,256]{2,1,0:T(8,128)(2,1)S(1)}, bf16[2,128,256]{2,1,0:T(8,128)(2,1)S(1)}, u32[]{:S(2)}, u32[]{:S(2)}) collective-permute-start(bf16[2,128,256]{2,1,0:T(8,128)(2,1)S(1)} %get-tuple-element.63), channel_id=1, source_target_pairs={{0,32},{1,225},{2,34},{3,227},{4,36},{5,229},{6,38},{7,231},{8,40}... | collective-permute-start | bytes 393224 | tf_op jit(solution)/shard_map/ppermute | solution.py:435
  125.0 6.7 %collective-permute-start.14 = (bf16[2,128,256]{2,1,0:T(8,128)(2,1)S(1)}, bf16[2,128,256]{2,1,0:T(8,128)(2,1)S(1)}, u32[]{:S(2)}, u32[]{:S(2)}) collective-permute-start(bf16[2,128,256]{2,1,0:T(8,128)(2,1)S(1)} %get-tuple-element.64), channel_id=1, source_target_pairs={{0,16},{1,17},{2,18},{3,19},{4,20},{5,21},{6,22},{7,23},{8,24},{9,... | collective-permute-start | bytes 393224 | tf_op jit(solution)/shard_map/ppermute | solution.py:435
  131.7 12.9 %copy-start.4 = (s32[48]{0:T(128)S(1)}, s32[48]{0:T(128)}, u32[]{:S(2)}) copy-start(s32[48]{0:T(128)} %copy-done.3) | copy-start | bytes 580
  131.7 12.6 %collective-permute-start.18 = (bf16[4,2,128,256]{3,2,1,0:T(8,128)(2,1)S(1)}, bf16[4,2,128,256]{3,2,1,0:T(8,128)(2,1)S(1)}, u32[]{:S(2)}, u32[]{:S(2)}) collective-permute-start(bf16[4,2,128,256]{3,2,1,0:T(8,128)(2,1)S(1)} %pad_maximum_fusion.1), channel_id=1, source_target_pairs={{0,1},{1,2},{2,3},{3,4},{4,5},{5,6},{6,7},{7,8},{8,9},{9,10},{10,1... | collective-permute-start | bytes 1572872 | tf_op jit(solution)/shard_map/ppermute | solution.py:375
  135.7 8.9 %collective-permute-start.17 = (bf16[4,2,128,256]{3,2,1,0:T(8,128)(2,1)S(1)}, bf16[4,2,128,256]{3,2,1,0:T(8,128)(2,1)S(1)}, u32[]{:S(2)}, u32[]{:S(2)}) collective-permute-start(bf16[4,2,128,256]{3,2,1,0:T(8,128)(2,1)S(1)} %pad_maximum_fusion.1), channel_id=1, source_target_pairs={{0,15},{1,0},{2,1},{3,2},{4,3},{5,4},{6,5},{7,6},{8,7},{9,8},{10,9... | collective-permute-start | bytes 1572872 | tf_op jit(solution)/shard_map/ppermute | solution.py:375
  135.9 10.0 %collective-permute-start.24 = (bf16[2,128,256]{2,1,0:T(8,128)(2,1)S(1)}, bf16[2,128,256]{2,1,0:T(8,128)(2,1)S(1)}, u32[]{:S(2)}, u32[]{:S(2)}) collective-permute-start(bf16[2,128,256]{2,1,0:T(8,128)(2,1)S(1)} %get-tuple-element.57), channel_id=1, source_target_pairs={{0,48},{1,241},{2,50},{3,243},{4,52},{5,245},{6,54},{7,247},{8,56}... | collective-permute-start | bytes 393224 | tf_op jit(solution)/shard_map/ppermute | solution.py:435
  141.1 5.3 %collective-permute-start.23 = (bf16[2,128,256]{2,1,0:T(8,128)(2,1)S(1)}, bf16[2,128,256]{2,1,0:T(8,128)(2,1)S(1)}, u32[]{:S(2)}, u32[]{:S(2)}) collective-permute-start(bf16[2,128,256]{2,1,0:T(8,128)(2,1)S(1)} %get-tuple-element.58), channel_id=1, source_target_pairs={{0,32},{1,225},{2,34},{3,227},{4,36},{5,229},{6,38},{7,231},{8,40}... | collective-permute-start | bytes 393224 | tf_op jit(solution)/shard_map/ppermute | solution.py:435
  141.8 11.3 %collective-permute-start.22 = (bf16[2,128,256]{2,1,0:T(8,128)(2,1)S(1)}, bf16[2,128,256]{2,1,0:T(8,128)(2,1)S(1)}, u32[]{:S(2)}, u32[]{:S(2)}) collective-permute-start(bf16[2,128,256]{2,1,0:T(8,128)(2,1)S(1)} %get-tuple-element.59), channel_id=1, source_target_pairs={{0,16},{1,17},{2,18},{3,19},{4,20},{5,21},{6,22},{7,23},{8,24},{9,... | collective-permute-start | bytes 393224 | tf_op jit(solution)/shard_map/ppermute | solution.py:435
